TPU v7x, 32 devices: a whole 2x2x4 slice. The times are simulated.
32 devices in a mesh: dp: 4 (over z), gx: 4 (over y, core), gy: 2 (over x).
Axes of the slice: x: 2, y: 2, z: 4, core: 2. Of those that a mesh axis runs over, the one named last changes fastest.
Arguments:
- inputs: bfloat16 [8, 1024, 2048], P('dp', 'gx', 'gy'), may hold values from -6 to 6
- segments: int32 [8, 1024], P('dp'), may hold values from 0 to 3, never falling along the last dimension, each value on 1 to 512 neighbouring positions
- norm_gain: float32 [2048], replicated, may hold values from 0.5 to 1.5
- w_query: bfloat16 [2048, 2048], P('gy', 'gx'), may hold values from -0.125 to 0.125
- w_key: bfloat16 [2048, 2048], P('gy', 'gx'), may hold values from -0.125 to 0.125
- w_value: bfloat16 [2048, 2048], P('gy', 'gx'), may hold values from -0.125 to 0.125
- w_beta: bfloat16 [2048, 16], P('gy', 'gx'), may hold values from -0.125 to 0.125
- w_gate_head: bfloat16 [2048, 2048], P('gy', 'gx'), may hold values from -0.125 to 0.125
- conv_kernel: float32 [3, 4, 2048], replicated, may hold values from -1 to 1
- head_gain: float32 [128], replicated, may hold values from 0.5 to 1.5
- w_out: bfloat16 [2048, 2048], P('gx', 'gy'), may hold values from -0.25 to 0.25
- mlp_gain: float32 [2048], replicated, may hold values from 0.5 to 1.5
- w_gate: bfloat16 [2048, 5632], P('gy', 'gx'), may hold values from -0.125 to 0.125
- w_up: bfloat16 [2048, 5632], P('gy', 'gx'), may hold values from -0.125 to 0.125
- w_down: bfloat16 [5632, 2048], P('gx', 'gy'), may hold values from -0.15625 to 0.15625
- grad_y: bfloat16 [8, 1024, 2048], P('dp', 'gx', 'gy'), may hold values from -6 to 6
Outputs:
- layer_out: bfloat16 [8, 1024, 2048], P('dp', 'gx', 'gy')
- grad_inputs: bfloat16 [8, 1024, 2048], P('dp', 'gx', 'gy')
- grad_norm_gain: float32 [2048], replicated
- grad_query: float32 [2048, 2048], P(('gy', 'dp'), 'gx')
- grad_key: float32 [2048, 2048], P(('gy', 'dp'), 'gx')
- grad_value: float32 [2048, 2048], P(('gy', 'dp'), 'gx')
- grad_beta: float32 [2048, 16], P(('gy', 'dp'), 'gx')
- grad_gate_head: float32 [2048, 2048], P(('gy', 'dp'), 'gx')
- grad_conv: float32 [3, 4, 2048], replicated
- grad_head_gain: float32 [128], replicated
- grad_out: float32 [2048, 2048], P(('gx', 'dp'), 'gy')
- grad_mlp_gain: float32 [2048], replicated
- grad_gate: float32 [2048, 5632], P(('gy', 'dp'), 'gx')
- grad_up: float32 [2048, 5632], P(('gy', 'dp'), 'gx')
- grad_down: float32 [5632, 2048], P(('gx', 'dp'), 'gy')
Inputs may be any that keep to these rules, and one draw needn't show every extreme that they name: `segments`: within each sequence the document number starts at 0 and never falls; a document has 1 to 512 tokens, and one of them exactly that many.
All inputs are finite; a program needn't handle non-finite values.
Results may differ from a plain program's by a relative error of at most 0.024.
Values may be sent and summed in bfloat16 or wider, within the bound.
A program may use at most 256 MiB of HBM per device.

v0:
```python
import jax
import jax.numpy as jnp
from jax import lax
from jax.sharding import PartitionSpec as P

BLOCK = 64


EPS = 1e-06
HEAD_EPS = 0.01
HIGH_ACCURACY = lax.Precision.HIGHEST


def causal_mix(raw_rows, kernel, segment):
    length = raw_rows.shape[0]
    mixed_sum = jnp.zeros(raw_rows.shape, jnp.float32)
    for offset in range(kernel.shape[0]):
        moved_rows = jnp.pad(raw_rows, ((offset, 0), (0, 0)))[:length]
        moved_seg = jnp.pad(segment, (offset, 0), constant_values=-1)[:length]
        keep_mask = (moved_seg == segment).astype(jnp.float32)[:, None]
        mixed_sum = mixed_sum + kernel[offset][None, :] * moved_rows * keep_mask
    return mixed_sum


def unit_norm(value_in):
    return value_in * lax.rsqrt(jnp.sum(value_in * value_in, axis=-1, keepdims=True) + EPS)


def block_step(carry_in, block_data):
    state_now, last_doc = carry_in
    query_rows, key_rows, value_rows, beta_rows, segment = block_data
    block_size = segment.shape[0]
    same_doc = (segment[:, None] == segment[None, :]).astype(jnp.float32)
    strict = jnp.tril(jnp.ones((block_size, block_size), jnp.float32), -1)
    inclusive = jnp.tril(jnp.ones((block_size, block_size), jnp.float32))
    key_inner = jnp.einsum("hid,hjd->hij", key_rows, key_rows, precision=HIGH_ACCURACY)
    system = (
        beta_rows[:, :, None] * key_inner * (same_doc * strict)[None]
        + jnp.eye(block_size, dtype=jnp.float32)[None]
    )
    stacked = beta_rows[:, :, None] * jnp.concatenate([key_rows, value_rows], axis=-1)
    solved = lax.linalg.triangular_solve(
        system, stacked, left_side=True, lower=True, unit_diagonal=True
    )
    dim_key = key_rows.shape[-1]
    weight_rows = solved[..., :dim_key]
    update_rows = solved[..., dim_key:]
    carried = (segment == last_doc).astype(jnp.float32)
    fresh_rows = update_rows - carried[None, :, None] * jnp.einsum(
        "hid,hed->hie", weight_rows, state_now, precision=HIGH_ACCURACY
    )
    scores = (
        jnp.einsum("hid,hjd->hij", query_rows, key_rows, precision=HIGH_ACCURACY)
        * (same_doc * inclusive)[None]
    )
    output = carried[None, :, None] * jnp.einsum(
        "hid,hed->hie", query_rows, state_now, precision=HIGH_ACCURACY
    )
    output = output + jnp.einsum("hij,hje->hie", scores, fresh_rows, precision=HIGH_ACCURACY)
    tail_doc = (segment == segment[-1]).astype(jnp.float32)
    new_state = carried[-1] * state_now + jnp.einsum(
        "hje,hjd->hed", fresh_rows * tail_doc[None, :, None], key_rows, precision=HIGH_ACCURACY
    )
    return ((new_state, segment[-1]), output)


def delta_rule(query_rows, key_rows, value_rows, beta_rows, segment):
    length, head_count, dim_key = query_rows.shape
    steps_count = length // BLOCK

    def blocked(array_in):
        return array_in.reshape(steps_count, BLOCK, head_count, -1).transpose(0, 2, 1, 3)

    start_carry = (jnp.zeros((head_count, dim_key, dim_key), jnp.float32), jnp.array(-1, jnp.int32))
    block_inputs = (
        blocked(query_rows),
        blocked(key_rows),
        blocked(value_rows),
        beta_rows.reshape(steps_count, BLOCK, head_count).transpose(0, 2, 1),
        segment.reshape(steps_count, BLOCK),
    )
    final_carry, outputs = lax.scan(jax.checkpoint(block_step), start_carry, block_inputs)
    return outputs.transpose(0, 2, 1, 3).reshape(length, head_count, dim_key)


def mixer(query_raw, key_raw, value_raw, gate_raw, beta_raw, conv_kernel, head_gain, segment):
    length = query_raw.shape[0]
    head_count = beta_raw.shape[-1]
    dim_key = query_raw.shape[-1] // head_count

    def heads_of(value_in):
        return value_in.reshape(length, head_count, dim_key)

    query_rows = unit_norm(heads_of(jax.nn.silu(causal_mix(query_raw, conv_kernel[0], segment))))
    key_rows = unit_norm(heads_of(jax.nn.silu(causal_mix(key_raw, conv_kernel[1], segment))))
    value_rows = heads_of(jax.nn.silu(causal_mix(value_raw, conv_kernel[2], segment)))
    beta_rows = jax.nn.sigmoid(beta_raw)
    delta_out = delta_rule(query_rows, key_rows, value_rows, beta_rows, segment)
    normed = (
        delta_out
        * lax.rsqrt(jnp.mean(delta_out * delta_out, axis=-1, keepdims=True) + HEAD_EPS)
        * head_gain
    )
    return (normed * heads_of(jax.nn.silu(gate_raw))).reshape(length, head_count * dim_key)


def local_product(row_total, weight_matrix):
    return jnp.einsum("pnj,ju->pnu", row_total, weight_matrix, preferred_element_type=jnp.float32)


def back_product(gradient_tree, weight_matrix):
    return jnp.einsum(
        "par,br->pab", gradient_tree, weight_matrix, preferred_element_type=jnp.float32
    )


def weight_product(row_total, gradient_tree):
    return jnp.einsum("zut,zue->te", row_total, gradient_tree, preferred_element_type=jnp.float32)


def gather_rows(value_in):
    return lax.all_gather(value_in, "gx", axis=1, tiled=True)


def sum_rows(value_in):
    return lax.psum_scatter(
        value_in.astype(jnp.bfloat16), "gx", scatter_dimension=1, tiled=True
    ).astype(jnp.float32)


def gather_units(value_in):
    return lax.all_gather(value_in, "gy", axis=2, tiled=True)


def sum_units(value_in):
    return lax.psum_scatter(
        value_in.astype(jnp.bfloat16), "gy", scatter_dimension=2, tiled=True
    ).astype(jnp.float32)


def feature_sum(value_in):
    return lax.psum(value_in, "gy")


def norm_rate(value_in, width):
    squares = feature_sum(jnp.sum(value_in * value_in, axis=-1, keepdims=True))
    return lax.rsqrt(squares / width + EPS)


def norm_back(value_in, rate, gain, incoming, width):
    scaled = gain * incoming
    inner = feature_sum(jnp.sum(value_in * scaled, axis=-1, keepdims=True))
    grad_value = rate * scaled - value_in * (rate * rate * rate) * inner / width
    grad_gain = jnp.sum(incoming * value_in * rate, axis=(0, 1))
    return (grad_value, grad_gain)


def shards(
    inputs,
    segments,
    norm_gain,
    w_query,
    w_key,
    w_value,
    w_beta,
    w_gate_head,
    conv_kernel,
    head_gain,
    w_out,
    mlp_gain,
    w_gate,
    w_up,
    w_down,
    grad_y,
):
    feat_local = inputs.shape[2]
    feat_total = feat_local * lax.axis_size("gy")
    row_index = lax.axis_index("gy")
    block_index = lax.axis_index("gx")
    gain_first = lax.dynamic_slice_in_dim(norm_gain, row_index * feat_local, feat_local)
    gain_second = lax.dynamic_slice_in_dim(mlp_gain, row_index * feat_local, feat_local)
    inputs_wide = inputs.astype(jnp.float32)
    rate_first = norm_rate(inputs_wide, feat_total)
    normed = (inputs_wide * rate_first * gain_first).astype(jnp.bfloat16)
    normed_all = gather_rows(normed)
    query_raw, key_raw, value_raw, gate_raw, beta_raw = (
        lax.psum_scatter(local_product(normed_all, w_query), "gy", scatter_dimension=2, tiled=True),
        lax.psum_scatter(local_product(normed_all, w_key), "gy", scatter_dimension=2, tiled=True),
        lax.psum_scatter(local_product(normed_all, w_value), "gy", scatter_dimension=2, tiled=True),
        lax.psum_scatter(
            local_product(normed_all, w_gate_head), "gy", scatter_dimension=2, tiled=True
        ),
        lax.psum_scatter(local_product(normed_all, w_beta), "gy", scatter_dimension=2, tiled=True),
    )
    width_local = query_raw.shape[2]
    conv_start = (block_index * lax.axis_size("gy") + row_index) * width_local
    conv_local = lax.dynamic_slice_in_dim(conv_kernel, conv_start, width_local, 2)
    mixer_many = jax.vmap(mixer, in_axes=(0, 0, 0, 0, 0, None, None, 0))

    def local_mix(query_in, key_in, value_in, gate_input, beta_in, kernel_in, gain_in):
        return mixer_many(
            query_in, key_in, value_in, gate_input, beta_in, kernel_in, gain_in, segments
        )

    mixed, mix_back = jax.vjp(
        local_mix, query_raw, key_raw, value_raw, gate_raw, beta_raw, conv_local, head_gain
    )
    mixed_all = gather_units(mixed.astype(jnp.bfloat16))
    middle = inputs_wide + sum_rows(local_product(mixed_all, w_out))
    rate_second = norm_rate(middle, feat_total)
    second = (middle * rate_second * gain_second).astype(jnp.bfloat16)
    second_all = gather_rows(second)
    gate_val, up_val = (
        lax.psum_scatter(
            local_product(second_all, w_gate).astype(jnp.bfloat16),
            "gy",
            scatter_dimension=2,
            tiled=True,
        ).astype(jnp.float32),
        lax.psum_scatter(
            local_product(second_all, w_up).astype(jnp.bfloat16),
            "gy",
            scatter_dimension=2,
            tiled=True,
        ).astype(jnp.float32),
    )
    sig_gate = jax.nn.sigmoid(gate_val)
    act_gate = gate_val * sig_gate
    hidden_state = (act_gate * up_val).astype(jnp.bfloat16)
    hidden_all = gather_units(hidden_state)
    layer_out = (middle + sum_rows(local_product(hidden_all, w_down))).astype(jnp.bfloat16)
    cot_all = gather_rows(grad_y)
    grad_down = weight_product(hidden_all, cot_all)
    grad_hidden = sum_units(back_product(cot_all, w_down))
    grad_up_val = (grad_hidden * act_gate).astype(jnp.bfloat16)
    grad_gate_val = (grad_hidden * up_val * sig_gate * (1.0 + gate_val * (1.0 - sig_gate))).astype(
        jnp.bfloat16
    )
    gate_grad_all, up_grad_all = (
        lax.all_gather(grad_gate_val, "gy", axis=2, tiled=True),
        lax.all_gather(grad_up_val, "gy", axis=2, tiled=True),
    )
    grad_gate = weight_product(second_all, gate_grad_all)
    grad_up = weight_product(second_all, up_grad_all)
    grad_second = sum_rows(back_product(gate_grad_all, w_gate) + back_product(up_grad_all, w_up))
    norm_term_two, grad_gain_two = norm_back(
        middle, rate_second, gain_second, grad_second, feat_total
    )
    grad_middle = grad_y.astype(jnp.float32) + norm_term_two
    mid_all = gather_rows(grad_middle.astype(jnp.bfloat16))
    grad_out = weight_product(mixed_all, mid_all)
    grad_mixed = sum_units(back_product(mid_all, w_out))
    (
        grad_query_raw,
        grad_key_raw,
        grad_value_raw,
        grad_gate_raw,
        grad_beta_raw,
        grad_conv_local,
        grad_head_gain,
    ) = mix_back(grad_mixed)
    query_grads, key_grads, value_grads, gate_grads, beta_grads = (
        lax.all_gather(grad_query_raw.astype(jnp.bfloat16), "gy", axis=2, tiled=True),
        lax.all_gather(grad_key_raw.astype(jnp.bfloat16), "gy", axis=2, tiled=True),
        lax.all_gather(grad_value_raw.astype(jnp.bfloat16), "gy", axis=2, tiled=True),
        lax.all_gather(grad_gate_raw.astype(jnp.bfloat16), "gy", axis=2, tiled=True),
        lax.all_gather(grad_beta_raw.astype(jnp.bfloat16), "gy", axis=2, tiled=True),
    )
    grad_query = weight_product(normed_all, query_grads)
    grad_key = weight_product(normed_all, key_grads)
    grad_value = weight_product(normed_all, value_grads)
    grad_gate_head = weight_product(normed_all, gate_grads)
    grad_beta = weight_product(normed_all, beta_grads)
    grad_normed = sum_rows(
        back_product(query_grads, w_query)
        + back_product(key_grads, w_key)
        + back_product(value_grads, w_value)
        + back_product(gate_grads, w_gate_head)
        + back_product(beta_grads, w_beta)
    )
    norm_term_one, grad_gain_one = norm_back(
        inputs_wide, rate_first, gain_first, grad_normed, feat_total
    )
    grad_inputs = (grad_middle + norm_term_one).astype(jnp.bfloat16)
    gain_one_full = lax.dynamic_update_slice_in_dim(
        jnp.zeros(norm_gain.shape, jnp.float32), grad_gain_one, row_index * feat_local, 0
    )
    gain_two_full = lax.dynamic_update_slice_in_dim(
        jnp.zeros(mlp_gain.shape, jnp.float32), grad_gain_two, row_index * feat_local, 0
    )
    conv_full = lax.dynamic_update_slice_in_dim(
        jnp.zeros(conv_kernel.shape, jnp.float32), grad_conv_local, conv_start, 2
    )
    gain_one_sum, gain_two_sum, conv_sum, head_sum = lax.psum(
        (gain_one_full, gain_two_full, conv_full, grad_head_gain), ("dp", "gx", "gy")
    )
    (
        sum_query,
        sum_key,
        summed_value,
        sum_beta,
        summed_head_gate,
        sum_out,
        sum_gate,
        sum_up,
        sum_down,
    ) = (
        lax.psum_scatter(
            grad_query.astype(jnp.bfloat16), "dp", scatter_dimension=0, tiled=True
        ).astype(jnp.float32),
        lax.psum_scatter(
            grad_key.astype(jnp.bfloat16), "dp", scatter_dimension=0, tiled=True
        ).astype(jnp.float32),
        lax.psum_scatter(
            grad_value.astype(jnp.bfloat16), "dp", scatter_dimension=0, tiled=True
        ).astype(jnp.float32),
        lax.psum_scatter(
            grad_beta.astype(jnp.bfloat16), "dp", scatter_dimension=0, tiled=True
        ).astype(jnp.float32),
        lax.psum_scatter(
            grad_gate_head.astype(jnp.bfloat16), "dp", scatter_dimension=0, tiled=True
        ).astype(jnp.float32),
        lax.psum_scatter(
            grad_out.astype(jnp.bfloat16), "dp", scatter_dimension=0, tiled=True
        ).astype(jnp.float32),
        lax.psum_scatter(
            grad_gate.astype(jnp.bfloat16), "dp", scatter_dimension=0, tiled=True
        ).astype(jnp.float32),
        lax.psum_scatter(
            grad_up.astype(jnp.bfloat16), "dp", scatter_dimension=0, tiled=True
        ).astype(jnp.float32),
        lax.psum_scatter(
            grad_down.astype(jnp.bfloat16), "dp", scatter_dimension=0, tiled=True
        ).astype(jnp.float32),
    )
    return (
        layer_out,
        grad_inputs,
        gain_one_sum,
        sum_query,
        sum_key,
        summed_value,
        sum_beta,
        summed_head_gate,
        conv_sum,
        head_sum,
        sum_out,
        gain_two_sum,
        sum_gate,
        sum_up,
        sum_down,
    )


def solution(mesh):
    placed = (
        P("dp", "gx", "gy"),
        P("dp", None),
        P(),
        P("gy", "gx"),
        P("gy", "gx"),
        P("gy", "gx"),
        P("gy", "gx"),
        P("gy", "gx"),
        P(),
        P(),
        P("gx", "gy"),
        P(),
        P("gy", "gx"),
        P("gy", "gx"),
        P("gx", "gy"),
        P("dp", "gx", "gy"),
    )
    return jax.shard_map(
        shards,
        mesh=mesh,
        in_specs=placed,
        out_specs=(
            P("dp", "gx", "gy"),
            P("dp", "gx", "gy"),
            P(),
            P(("gy", "dp"), "gx"),
            P(("gy", "dp"), "gx"),
            P(("gy", "dp"), "gx"),
            P(("gy", "dp"), "gx"),
            P(("gy", "dp"), "gx"),
            P(),
            P(),
            P(("gx", "dp"), "gy"),
            P(),
            P(("gy", "dp"), "gx"),
            P(("gy", "dp"), "gx"),
            P(("gx", "dp"), "gy"),
        ),
        check_vma=False,
    )
```

profile of v0, /device:TPU:0, one launch (start us, length us, event | category | flops | bytes accessed | tf_op | source)
XLA Modules:
  0.0 2902.1 jit_solution(2783570189085170164)
XLA Ops:
  19.2 36.4 %all-gather.13.cloned.1.call-done = bf16[2,1024,1024]{2,1,0:T(8,128)(2,1)} async-done(((bf16[2,256,1024]{2,1,0:T(8,128)(2,1)}), bf16[2,1024,1024]{2,1,0:T(8,128)(2,1)}) %all-gather.13.cloned.1.call-update) | async-done | bytes 4194320 | tf_op jit(solution)/shard_map/all_gather | solution.py:122
  101.3 16.2 reduce-scatter.27.cloned.1.call-done
  117.6 56.7 %reduce-scatter.29.cloned.1.call-done = f32[2,1024,256]{2,1,0:T(8,128)} async-done(((f32[2,1024,512]{2,1,0:T(8,128)}), f32[2,1024,256]{2,1,0:T(8,128)}) %reduce-scatter.29.cloned.1.call-update) | async-done | bytes 2097168 | tf_op jit(solution)/shard_map/reduce_scatter | solution.py:187
  195.1 35.7 %reduce-scatter.25.cloned.1.call-done = f32[2,1024,256]{2,1,0:T(8,128)} async-done(((f32[2,1024,512]{2,1,0:T(8,128)}), f32[2,1024,256]{2,1,0:T(8,128)}) %reduce-scatter.25.cloned.1.call-update) | async-done | bytes 2097168 | tf_op jit(solution)/shard_map/reduce_scatter | solution.py:188
  271.9 564.2 %while.42 = (s32[]{:T(128)}, f32[2,2,128,128]{3,2,1,0:T(8,128)S(1)}, s32[2]{0:T(128)S(1)}, f32[16,2,2,64,128]{4,3,2,1,0:T(8,128)}, f32[16,2,2,128,128]{4,3,2,1,0...) while((s32[]{:T(128)}, ...), condition=%wide.region_9.11_spmd.clone, body=%wide.region_8.10_spmd.clone.sunk | while | flops 277672512 | bytes 4869610 | solution.py:82
  276.0 21.0 custom-call.27
  311.3 21.0 custom-call.27
  346.5 21.0 custom-call.27
  381.7 21.0 custom-call.27
  417.0 21.0 custom-call.27
  452.2 21.0 custom-call.27
  487.4 21.0 custom-call.27
  522.7 21.0 custom-call.27
  557.9 21.0 custom-call.27
  593.1 21.0 custom-call.27
  628.4 21.0 custom-call.27
  663.6 21.0 custom-call.27
  698.9 21.0 custom-call.27
  734.1 21.0 custom-call.27
  769.4 21.0 custom-call.27
  804.6 21.0 custom-call.27
  862.2 33.3 %all-gather.15.cloned.1.call-done = bf16[2,1024,512]{2,1,0:T(8,128)(2,1)} async-done(((bf16[2,1024,256]{2,1,0:T(8,128)(2,1)}), bf16[2,1024,512]{2,1,0:T(8,128)(2,1)}) %all-gather.15.cloned.1.call-update) | async-done | bytes 2097168 | tf_op jit(solution)/shard_map/all_gather | solution.py:132
  902.5 43.8 %reduce-scatter.33.cloned.1.call-done = bf16[2,256,1024]{2,1,0:T(8,128)(2,1)} async-done(((bf16[2,1024,1024]{2,1,0:T(8,128)(2,1)}), bf16[2,256,1024]{2,1,0:T(8,128)(2,1)}) %reduce-scatter.33.cloned.1.call-update) | async-done | bytes 1048592 | tf_op jit(solution)/shard_map/reduce_scatter | solution.py:126
  956.4 26.1 all-gather.21.cloned.1.call-done
  993.4 25.9 all-gather.17.cloned.1.call-done
  1040.6 52.3 %reduce-scatter.41.cloned.1.call-done = bf16[2,1024,704]{1,2,0:T(8,128)(2,1)} async-done(((bf16[2,1024,1408]{1,2,0:T(8,128)(2,1)}), bf16[2,1024,704]{1,2,0:T(8,128)(2,1)}) %reduce-scatter.41.cloned.1.call-update) | async-done | bytes 2883600 | tf_op jit(solution)/shard_map/reduce_scatter | solution.py:136
  1092.9 73.7 %reduce-scatter.35.cloned.1.call-done = bf16[2,1024,704]{1,2,0:T(8,128)(2,1)} async-done(((bf16[2,1024,1408]{1,2,0:T(8,128)(2,1)}), bf16[2,1024,704]{1,2,0:T(8,128)(2,1)}) %reduce-scatter.35.cloned.1.call-update) | async-done | bytes 2883600 | tf_op jit(solution)/shard_map/reduce_scatter | solution.py:214
  1166.6 73.7 %reduce-scatter.37.cloned.1.call-done = bf16[2,1024,704]{1,2,0:T(8,128)(2,1)} async-done(((bf16[2,1024,1408]{1,2,0:T(8,128)(2,1)}), bf16[2,1024,704]{1,2,0:T(8,128)(2,1)}) %reduce-scatter.37.cloned.1.call-update) | async-done | bytes 2883600 | tf_op jit(solution)/shard_map/reduce_scatter | solution.py:220
  1249.4 74.0 %all-gather.25.cloned.1.call-done = bf16[2,1024,1408]{1,2,0:T(8,128)(2,1)} async-done(((bf16[2,1024,704]{1,2,0:T(8,128)(2,1)}), bf16[2,1024,1408]{1,2,0:T(8,128)(2,1)}) %all-gather.25.cloned.1.call-update) | async-done | bytes 5767184 | tf_op jit(solution)/shard_map/all_gather | solution.py:241
  1334.7 64.6 %all-gather.23.cloned.1.call-done = bf16[2,1024,1408]{1,2,0:T(8,128)(2,1)} async-done(((bf16[2,1024,704]{1,2,0:T(8,128)(2,1)}), bf16[2,1024,1408]{1,2,0:T(8,128)(2,1)}) %all-gather.23.cloned.1.call-update) | async-done | bytes 5767184 | tf_op jit(solution)/shard_map/all_gather | solution.py:240
  1412.1 44.6 %reduce-scatter.43.cloned.1.call-done = bf16[2,256,1024]{2,1,0:T(8,128)(2,1)} async-done(((bf16[2,1024,1024]{2,1,0:T(8,128)(2,1)}), bf16[2,256,1024]{2,1,0:T(8,128)(2,1)}) %reduce-scatter.43.cloned.1.call-update) | async-done | bytes 1048592 | tf_op jit(solution)/shard_map/reduce_scatter | solution.py:126
  1467.8 34.6 %all-gather.27.cloned.1.call-done = bf16[2,1024,1024]{2,1,0:T(8,128)(2,1)} async-done(((bf16[2,256,1024]{2,1,0:T(8,128)(2,1)}), bf16[2,1024,1024]{2,1,0:T(8,128)(2,1)}) %all-gather.27.cloned.1.call-update) | async-done | bytes 4194320 | tf_op jit(solution)/shard_map/all_gather | solution.py:122
  1560.2 565.1 %while.43 = (s32[]{:T(128)}, f32[2,2,128,128]{3,2,1,0:T(8,128)S(1)}, f32[16,2,2,64,128]{4,3,2,1,0:T(8,128)}, f32[16,2,2,64,128]{4,3,2,1,0:T(8,128)}, f32[16,2,2,...) while((s32[]{:T(128)}, ...), condition=%wide.region_27.29_spmd.clone, body=%wide.region_24.28_spmd.clone.sunk | while | flops 718696768 | bytes 13274147 | solution.py:82
  1567.4 19.7 custom-call.29
  1602.7 19.7 custom-call.29
  1638.0 19.7 custom-call.29
  1673.3 19.7 custom-call.29
  1708.6 19.7 custom-call.29
  1744.0 19.7 custom-call.29
  1779.2 19.7 custom-call.29
  1814.6 19.7 custom-call.29
  1849.9 19.7 custom-call.29
  1885.2 19.7 custom-call.29
  1920.5 19.7 custom-call.29
  1955.8 19.7 custom-call.29
  1991.2 19.7 custom-call.29
  2026.5 19.7 custom-call.29
  2061.8 19.7 custom-call.29
  2097.1 19.7 custom-call.29
  2168.5 20.1 multiply_reduce_fusion.6
  2271.0 28.7 all-gather.33.cloned.1.call-done
  2306.0 28.9 all-gather.35.cloned.1.call-done
  2395.8 55.9 %reduce-scatter.61.cloned.1.call-done = bf16[256,1408]{1,0:T(8,128)(2,1)} async-done(((bf16[1024,1408]{1,0:T(8,128)(2,1)}), bf16[256,1408]{1,0:T(8,128)(2,1)}) %reduce-scatter.61.cloned.1.call-update) | async-done | bytes 720912 | tf_op jit(solution)/shard_map/reduce_scatter | solution.py:329
  2454.0 56.1 %reduce-scatter.63.cloned.1.call-done = bf16[352,1024]{1,0:T(8,128)(2,1)} async-done(((bf16[1408,1024]{1,0:T(8,128)(2,1)}), bf16[352,1024]{1,0:T(8,128)(2,1)}) %reduce-scatter.63.cloned.1.call-update) | async-done | bytes 720912 | tf_op jit(solution)/shard_map/reduce_scatter | solution.py:332
  2512.7 26.6 reduce-scatter.57.cloned.1.call-done
  2541.8 18.6 reduce-scatter.65.cloned.1.call-done
  2561.9 26.1 reduce-scatter.51.cloned.1.call-done
  2589.9 26.4 reduce-scatter.49.cloned.1.call-done
  2618.1 26.7 reduce-scatter.53.cloned.1.call-done
  2646.7 27.0 reduce-scatter.55.cloned.1.call-done
  2675.5 43.9 %reduce-scatter.47.cloned.1.call-done = bf16[2,256,1024]{2,1,0:T(8,128)(2,1)} async-done(((bf16[2,1024,1024]{2,1,0:T(8,128)(2,1)}), bf16[2,256,1024]{2,1,0:T(8,128)(2,1)}) %reduce-scatter.47.cloned.1.call-update) | async-done | bytes 1048592 | tf_op jit(solution)/shard_map/reduce_scatter | solution.py:126
  2726.4 40.1 %reduce-scatter.39.cloned.1.call-done = bf16[2,256,1024]{2,1,0:T(8,128)(2,1)} async-done(((bf16[2,1024,1024]{2,1,0:T(8,128)(2,1)}), bf16[2,256,1024]{2,1,0:T(8,128)(2,1)}) %reduce-scatter.39.cloned.1.call-update) | async-done | bytes 1048592 | tf_op jit(solution)/shard_map/reduce_scatter | solution.py:126
  2771.7 39.8 %all-reduce.39 = (f32[2048]{0:T(1024)}, f32[128]{0:T(128)}, f32[2048]{0:T(1024)}) all-reduce(f32[2048]{0:T(1024)S(1)} %dynamic_update_slice.58, f32[128]{0:T(128)S(1)} %copy-done.76, f32[2048]{0:T(1024)S(1)} %dynamic_update_slice.60), channel_id=1, replica_groups=mesh['dp'=4,'gx'=4,'gy'=2] {'dp','gx','gy'}, use_global_device_ids=true, to_apply=%region_34.36 | all-reduce | flops 4224 | bytes 33792 | tf_op jit(solution)/shard_map/psum | solution.py:294
  2811.5 81.7 %all-reduce.42.cloned.1.call-done = f32[3,4,2048]{2,1,0:T(4,128)} async-done(((f32[3,4,2048]{2,1,0:T(4,128)}), f32[3,4,2048]{2,1,0:T(4,128)}) %all-reduce.42.cloned.1.call-update) | async-done | bytes 98320 | tf_op jit(solution)/shard_map/psum | solution.py:294
  (1349 shorter events, 990.7 us)
Async XLA Ops:
  7.2 1022.7 %copy-start = (bf16[1024,1408]{1,0:T(8,128)(2,1)S(1)}, bf16[1024,1408]{1,0:T(8,128)(2,1)}, u32[]{:S(2)}) copy-start(bf16[1024,1408]{1,0:T(8,128)(2,1)} %param.35) | copy-start | bytes 8650756
  7.2 48.4 %all-gather.13.cloned.1.call-start = ((), (), s32[]{:S(2)}) async-start(), calls=%async_computation.21 | async-start | bytes 5242880 | tf_op jit(solution)/shard_map/all_gather | solution.py:122
  15.3 47.0 %copy-start.41 = (f32[2,256]{1,0:T(2,128)}, f32[2,256]{1,0:T(2,128)S(1)}, u32[]{:S(2)}) copy-start(f32[2,256]{1,0:T(2,128)S(1)} %get-tuple-element.743) | copy-start | bytes 6148
  19.2 98.4 %reduce-scatter.27.cloned.1.call-start = ((), (), s32[]{:S(2)}) async-start(), calls=%async_computation.23 | async-start | bytes 6291456 | tf_op jit(solution)/shard_map/reduce_scatter | solution.py:189
  62.4 111.9 %reduce-scatter.29.cloned.1.call-start = ((), (), s32[]{:S(2)}) async-start(), calls=%async_computation.24 | async-start | bytes 6291456 | tf_op jit(solution)/shard_map/reduce_scatter | solution.py:187
  69.4 161.4 %reduce-scatter.25.cloned.1.call-start = ((), (), s32[]{:S(2)}) async-start(), calls=%async_computation.22 | async-start | bytes 6291456 | tf_op jit(solution)/shard_map/reduce_scatter | solution.py:188
  76.3 781.4 %reduce-scatter.31.cloned.1.call-start = ((), (), s32[]{:S(2)}) async-start(), calls=%async_computation.25 | async-start | bytes 6291456 | tf_op jit(solution)/shard_map/reduce_scatter | solution.py:190
  80.4 93.9 %copy-start.48 = (f32[1,1,256]{2,1,0:T(1,128)}, f32[1,1,256]{2,1,0:T(1,128)S(1)}, u32[]{:S(2)}) copy-start(f32[1,1,256]{2,1,0:T(1,128)S(1)} %get-tuple-element.725) | copy-start | bytes 3076
  80.4 93.9 %copy-start.50 = (f32[1,1,256]{2,1,0:T(1,128)}, f32[1,1,256]{2,1,0:T(1,128)S(1)}, u32[]{:S(2)}) copy-start(f32[1,1,256]{2,1,0:T(1,128)S(1)} %get-tuple-element.719) | copy-start | bytes 3076
  80.4 93.9 %copy-start.52 = (f32[1,1,256]{2,1,0:T(1,128)}, f32[1,1,256]{2,1,0:T(1,128)S(1)}, u32[]{:S(2)}) copy-start(f32[1,1,256]{2,1,0:T(1,128)S(1)} %get-tuple-element.720) | copy-start | bytes 3076
  80.4 93.9 %copy-start.54 = (f32[1,1,256]{2,1,0:T(1,128)}, f32[1,1,256]{2,1,0:T(1,128)S(1)}, u32[]{:S(2)}) copy-start(f32[1,1,256]{2,1,0:T(1,128)S(1)} %get-tuple-element.721) | copy-start | bytes 3076
  80.5 93.9 %copy-start.56 = (f32[1,1,256]{2,1,0:T(1,128)}, f32[1,1,256]{2,1,0:T(1,128)S(1)}, u32[]{:S(2)}) copy-start(f32[1,1,256]{2,1,0:T(1,128)S(1)} %get-tuple-element.722) | copy-start | bytes 3076
  80.5 93.9 %copy-start.58 = (f32[1,1,256]{2,1,0:T(1,128)}, f32[1,1,256]{2,1,0:T(1,128)S(1)}, u32[]{:S(2)}) copy-start(f32[1,1,256]{2,1,0:T(1,128)S(1)} %get-tuple-element.723) | copy-start | bytes 3076
  80.5 93.9 %copy-start.60 = (f32[1,1,256]{2,1,0:T(1,128)}, f32[1,1,256]{2,1,0:T(1,128)S(1)}, u32[]{:S(2)}) copy-start(f32[1,1,256]{2,1,0:T(1,128)S(1)} %get-tuple-element.724) | copy-start | bytes 3076
  80.5 93.9 %copy-start.62 = (f32[1,1,256]{2,1,0:T(1,128)}, f32[1,1,256]{2,1,0:T(1,128)S(1)}, u32[]{:S(2)}) copy-start(f32[1,1,256]{2,1,0:T(1,128)S(1)} %get-tuple-element.730) | copy-start | bytes 3076
  80.5 150.3 %copy-start.64 = (f32[1,1,256]{2,1,0:T(1,128)}, f32[1,1,256]{2,1,0:T(1,128)S(1)}, u32[]{:S(2)}) copy-start(f32[1,1,256]{2,1,0:T(1,128)S(1)} %get-tuple-element.729) | copy-start | bytes 3076
  80.5 150.3 %copy-start.66 = (f32[1,1,256]{2,1,0:T(1,128)}, f32[1,1,256]{2,1,0:T(1,128)S(1)}, u32[]{:S(2)}) copy-start(f32[1,1,256]{2,1,0:T(1,128)S(1)} %get-tuple-element.726) | copy-start | bytes 3076
  80.5 150.3 %copy-start.68 = (f32[1,1,256]{2,1,0:T(1,128)}, f32[1,1,256]{2,1,0:T(1,128)S(1)}, u32[]{:S(2)}) copy-start(f32[1,1,256]{2,1,0:T(1,128)S(1)} %get-tuple-element.727) | copy-start | bytes 3076
  80.5 150.3 %copy-start.70 = (f32[1,1,256]{2,1,0:T(1,128)}, f32[1,1,256]{2,1,0:T(1,128)S(1)}, u32[]{:S(2)}) copy-start(f32[1,1,256]{2,1,0:T(1,128)S(1)} %get-tuple-element.728) | copy-start | bytes 3076
  81.2 149.6 %copy-start.20 = (f32[2,1024]{1,0:T(2,128)}, f32[2,1024]{1,0:T(2,128)S(1)}, u32[]{:S(2)}) copy-start(f32[2,1024]{1,0:T(2,128)S(1)} %get-tuple-element.739) | copy-start | bytes 24580
  81.2 149.6 %copy-start.22 = (f32[2,1024]{1,0:T(2,128)}, f32[2,1024]{1,0:T(2,128)S(1)}, u32[]{:S(2)}) copy-start(f32[2,1024]{1,0:T(2,128)S(1)} %get-tuple-element.740) | copy-start | bytes 24580
  81.2 149.6 %copy-start.24 = (f32[2,1024]{1,0:T(2,128)}, f32[2,1024]{1,0:T(2,128)S(1)}, u32[]{:S(2)}) copy-start(f32[2,1024]{1,0:T(2,128)S(1)} %get-tuple-element.741) | copy-start | bytes 24580
  101.1 794.4 %all-gather.15.cloned.1.call-start = ((), (), s32[]{:S(2)}) async-start(), calls=%async_computation.26 | async-start | bytes 3145728 | tf_op jit(solution)/shard_map/all_gather | solution.py:132
  862.2 84.2 %reduce-scatter.33.cloned.1.call-start = ((), (), s32[]{:S(2)}) async-start(), calls=%async_computation.27 | async-start | bytes 5242880 | tf_op jit(solution)/shard_map/reduce_scatter | solution.py:126
  901.7 80.8 %all-gather.21.cloned.1.call-start = ((), (), s32[]{:S(2)}) async-start(), calls=%async_computation.33 | async-start | bytes 5242880 | tf_op jit(solution)/shard_map/all_gather | solution.py:122
  902.4 116.8 %all-gather.17.cloned.1.call-start = ((), (), s32[]{:S(2)}) async-start(), calls=%async_computation.28 | async-start | bytes 5242880 | tf_op jit(solution)/shard_map/all_gather | solution.py:122
  902.5 561.8 %copy-start.32 = (f32[1024]{0:T(1024)}, f32[1024]{0:T(1024)S(1)}, u32[]{:S(2)}) copy-start(f32[1024]{0:T(1024)S(1)} %dynamic_slice.103) | copy-start | bytes 12292
  953.3 511.1 %copy-start.36 = (f32[2,256]{1,0:T(2,128)}, f32[2,256]{1,0:T(2,128)S(1)}, u32[]{:S(2)}) copy-start(f32[2,256]{1,0:T(2,128)S(1)} %get-tuple-element.745) | copy-start | bytes 6148
  953.3 511.1 %copy-start.43 = (f32[2,256]{1,0:T(2,128)}, f32[2,256]{1,0:T(2,128)S(1)}, u32[]{:S(2)}) copy-start(f32[2,256]{1,0:T(2,128)S(1)} %get-tuple-element.744) | copy-start | bytes 6148
  956.4 136.5 %reduce-scatter.41.cloned.1.call-start = ((), (), s32[]{:S(2)}) async-start(), calls=%async_computation.34 | async-start | bytes 8650752 | tf_op jit(solution)/shard_map/reduce_scatter | solution.py:136
  993.3 173.3 %reduce-scatter.35.cloned.1.call-start = ((), (), s32[]{:S(2)}) async-start(), calls=%async_computation.29 | async-start | bytes 8650752 | tf_op jit(solution)/shard_map/reduce_scatter | solution.py:214
  1029.8 210.5 %reduce-scatter.37.cloned.1.call-start = ((), (), s32[]{:S(2)}) async-start(), calls=%async_computation.30 | async-start | bytes 8650752 | tf_op jit(solution)/shard_map/reduce_scatter | solution.py:220
  1040.5 282.8 %all-gather.25.cloned.1.call-start = ((), (), s32[]{:S(2)}) async-start(), calls=%async_computation.36 | async-start | bytes 8650752 | tf_op jit(solution)/shard_map/all_gather | solution.py:241
  1248.8 150.5 %all-gather.23.cloned.1.call-start = ((), (), s32[]{:S(2)}) async-start(), calls=%async_computation.35 | async-start | bytes 8650752 | tf_op jit(solution)/shard_map/all_gather | solution.py:240
  1249.3 207.4 %reduce-scatter.43.cloned.1.call-start = ((), (), s32[]{:S(2)}) async-start(), calls=%async_computation.37 | async-start | bytes 5242880 | tf_op jit(solution)/shard_map/reduce_scatter | solution.py:126
  1412.1 90.4 %all-gather.27.cloned.1.call-start = ((), (), s32[]{:S(2)}) async-start(), calls=%async_computation.38 | async-start | bytes 5242880 | tf_op jit(solution)/shard_map/all_gather | solution.py:122
  1467.8 72.9 %reduce-scatter.45.cloned.1.call-start = ((), (), s32[]{:S(2)}) async-start(), calls=%async_computation.39 | async-start | bytes 3145728 | tf_op jit(solution)/shard_map/reduce_scatter | solution.py:136
  1508.7 721.7 %all-gather.19.cloned.1.call-start = ((), (), s32[]{:S(2)}) async-start(), calls=%async_computation.31 | async-start | bytes 8650752 | tf_op jit(solution)/shard_map/all_gather | solution.py:132
  1525.8 731.0 %all-gather.31.cloned.1.call-start = ((), (), s32[]{:S(2)}) async-start(), calls=%async_computation.41 | async-start | bytes 3145728 | tf_op jit(solution)/shard_map/all_gather | solution.py:264
  2196.0 68.5 %all-gather.29.cloned.1.call-start = ((), (), s32[]{:S(2)}) async-start(), calls=%async_computation.40 | async-start | bytes 3145728 | tf_op jit(solution)/shard_map/all_gather | solution.py:263
  2201.3 98.5 %all-gather.33.cloned.1.call-start = ((), (), s32[]{:S(2)}) async-start(), calls=%async_computation.42 | async-start | bytes 3145728 | tf_op jit(solution)/shard_map/all_gather | solution.py:265
  2206.5 128.5 %all-gather.35.cloned.1.call-start = ((), (), s32[]{:S(2)}) async-start(), calls=%async_computation.43 | async-start | bytes 3145728 | tf_op jit(solution)/shard_map/all_gather | solution.py:266
  2207.2 186.2 %reduce-scatter.59.cloned.1.call-start = ((), (), s32[]{:S(2)}) async-start(), calls=%async_computation.51 | async-start | bytes 3604480 | tf_op jit(solution)/shard_map/reduce_scatter | solution.py:326
  2218.8 232.9 %reduce-scatter.61.cloned.1.call-start = ((), (), s32[]{:S(2)}) async-start(), calls=%async_computation.52 | async-start | bytes 3604480 | tf_op jit(solution)/shard_map/reduce_scatter | solution.py:329
  2230.3 279.8 %reduce-scatter.63.cloned.1.call-start = ((), (), s32[]{:S(2)}) async-start(), calls=%async_computation.53 | async-start | bytes 3604480 | tf_op jit(solution)/shard_map/reduce_scatter | solution.py:332
  2241.0 298.3 %reduce-scatter.57.cloned.1.call-start = ((), (), s32[]{:S(2)}) async-start(), calls=%async_computation.50 | async-start | bytes 1310720 | tf_op jit(solution)/shard_map/reduce_scatter | solution.py:323
  2248.2 312.2 %reduce-scatter.65.cloned.1.call-start = ((), (), s32[]{:S(2)}) async-start(), calls=%async_computation.54 | async-start | bytes 327680
  2256.7 331.4 %reduce-scatter.51.cloned.1.call-start = ((), (), s32[]{:S(2)}) async-start(), calls=%async_computation.46 | async-start | bytes 1310720 | tf_op jit(solution)/shard_map/reduce_scatter | solution.py:311
  2263.0 353.3 %reduce-scatter.49.cloned.1.call-start = ((), (), s32[]{:S(2)}) async-start(), calls=%async_computation.45 | async-start | bytes 1310720 | tf_op jit(solution)/shard_map/reduce_scatter | solution.py:308
  2270.8 374.1 %reduce-scatter.53.cloned.1.call-start = ((), (), s32[]{:S(2)}) async-start(), calls=%async_computation.47 | async-start | bytes 1310720 | tf_op jit(solution)/shard_map/reduce_scatter | solution.py:314
  2306.0 367.7 %reduce-scatter.55.cloned.1.call-start = ((), (), s32[]{:S(2)}) async-start(), calls=%async_computation.48 | async-start | bytes 1310720 | tf_op jit(solution)/shard_map/reduce_scatter | solution.py:320
  2341.2 378.2 %reduce-scatter.47.cloned.1.call-start = ((), (), s32[]{:S(2)}) async-start(), calls=%async_computation.44 | async-start | bytes 5242880 | tf_op jit(solution)/shard_map/reduce_scatter | solution.py:126
  2379.5 386.9 %reduce-scatter.39.cloned.1.call-start = ((), (), s32[]{:S(2)}) async-start(), calls=%async_computation.32 | async-start | bytes 5242880 | tf_op jit(solution)/shard_map/reduce_scatter | solution.py:126
  2392.4 500.8 %all-reduce.42.cloned.1.call-start = ((), (), s32[]{:S(2)}) async-start(), calls=%async_computation.49 | async-start | bytes 196608 | tf_op jit(solution)/shard_map/psum | solution.py:294
  2395.8 116.7 %copy-start.47 = (f32[1024]{0:T(1024)S(1)}, f32[1024]{0:T(1024)}, u32[]{:S(2)}) copy-start(f32[1024]{0:T(1024)} %get-tuple-element.601) | copy-start | bytes 12292
  2512.7 206.7 %copy-start.3 = (bf16[2,256,1024]{2,1,0:T(8,128)(2,1)S(1)}, bf16[2,256,1024]{2,1,0:T(8,128)(2,1)}, u32[]{:S(2)}) copy-start(bf16[2,256,1024]{2,1,0:T(8,128)(2,1)} %param.22) | copy-start | bytes 3145732
  2512.7 206.7 %copy-start.35 = (f32[1024]{0:T(1024)S(1)}, f32[1024]{0:T(1024)}, u32[]{:S(2)}) copy-start(f32[1024]{0:T(1024)} %copy-done.34) | copy-start | bytes 12292
  2512.7 206.7 %copy-start.42 = (f32[2,256]{1,0:T(2,128)S(1)}, f32[2,256]{1,0:T(2,128)}, u32[]{:S(2)}) copy-start(f32[2,256]{1,0:T(2,128)} %copy-done.41) | copy-start | bytes 6148
  2589.9 176.6 %copy-start.33 = (f32[1024]{0:T(1024)S(1)}, f32[1024]{0:T(1024)}, u32[]{:S(2)}) copy-start(f32[1024]{0:T(1024)} %copy-done.32) | copy-start | bytes 12292
  2589.9 176.6 %copy-start.37 = (f32[2,256]{1,0:T(2,128)S(1)}, f32[2,256]{1,0:T(2,128)}, u32[]{:S(2)}) copy-start(f32[2,256]{1,0:T(2,128)} %copy-done.36) | copy-start | bytes 6148
  2589.9 176.6 %copy-start.44 = (f32[2,256]{1,0:T(2,128)S(1)}, f32[2,256]{1,0:T(2,128)}, u32[]{:S(2)}) copy-start(f32[2,256]{1,0:T(2,128)} %copy-done.43) | copy-start | bytes 6148
  2589.9 176.6 %copy-start.46 = (f32[2,256]{1,0:T(2,128)S(1)}, f32[2,256]{1,0:T(2,128)}, u32[]{:S(2)}) copy-start(f32[2,256]{1,0:T(2,128)} %copy-done.45) | copy-start | bytes 6148
  2589.9 176.6 %copy-start.72 = (f32[2,256]{1,0:T(2,128)S(1)}, f32[2,256]{1,0:T(2,128)}, u32[]{:S(2)}) copy-start(f32[2,256]{1,0:T(2,128)} %get-tuple-element.742) | copy-start | bytes 6148
  2766.5 128.3 %copy-start.1 = (bf16[1024,1408]{1,0:T(8,128)(2,1)S(1)}, bf16[1024,1408]{1,0:T(8,128)(2,1)}, u32[]{:S(2)}) copy-start(bf16[1024,1408]{1,0:T(8,128)(2,1)} %param.35) | copy-start | bytes 8650756
  (58 other events, 484.5 us)
Sparse Core Ops, SparseCore 0:
  19.3 36.2 all-gather.12
  62.5 54.9 reduce-scatter.26
  120.0 54.3 reduce-scatter.28
  176.4 54.3 reduce-scatter.24
  233.0 54.2 reduce-scatter.30
  862.3 33.1 all-gather.14
  901.8 44.4 reduce-scatter.32
  948.0 34.4 all-gather.20
  984.7 34.4 all-gather.16
  1021.5 71.3 reduce-scatter.40
  1095.2 71.3 reduce-scatter.34
  1168.9 71.3 reduce-scatter.36
  1248.9 74.4 all-gather.24
  1324.8 74.4 all-gather.22
  1412.2 44.4 reduce-scatter.42
  1467.9 34.4 all-gather.26
  1508.8 31.8 reduce-scatter.44
  1542.0 74.5 all-gather.18
  2196.1 33.0 all-gather.30
  2231.2 33.2 all-gather.28
  2266.6 33.0 all-gather.32
  2301.8 33.0 all-gather.34
  2337.3 56.1 reduce-scatter.58
  2395.6 56.0 reduce-scatter.60
  2454.0 56.0 reduce-scatter.62
  2512.2 26.9 reduce-scatter.56
  2542.1 18.3 reduce-scatter.64
  2562.7 25.3 reduce-scatter.50
  2590.5 25.7 reduce-scatter.48
  2619.0 25.7 reduce-scatter.52
  2647.8 25.7 reduce-scatter.54
  2676.2 43.1 reduce-scatter.46
  2721.9 44.5 reduce-scatter.38
  2772.6 120.5 all-reduce.41
where the time goes:
time: 2920 us; the launch traced here: 2900 us
  waiting for transfers between devices  1200 us (41%)
  other arithmetic  837 us (29%)
  matrix products  513 us (18%)
  local copies, waits for them, and re-layouts  256 us (9%)
  blocking collectives  74.1 us (3%)
    another operation x128, other arithmetic, block_step(): lax.linalg.triangular_solve(system, stacked, left_side=True, lower=True,...  656 us
    reduce_scatter x4, waiting for transfers between devices, sum_rows(): lax.psum_scatter(value_in.astype(jnp.bfloat16), 'gx', scatter_dimension=1...  172 us
    all_gather x4, waiting for transfers between devices, gather_rows(): return lax.all_gather(value_in, 'gx', axis=1, tiled=True)  123 us
    squeeze x112, local copies, waits for them, and re-layouts, delta_rule(): lax.scan(jax.checkpoint(block_step), start_carry, block_inputs)  85.4 us
    psum x1, waiting for transfers between devices, shards(): lax.psum((gain_one_full, gain_two_full, conv_full, grad_head_gain), ('dp'...  81.7 us
    dot_general x9, matrix products, back_product(): jnp.einsum('par,br->pab', gradient_tree, weight_matrix, preferred_element...  79.2 us
    all_gather x1, waiting for transfers between devices, shards(): lax.all_gather(grad_up_val, 'gy', axis=2, tiled=True)  74 us
    reduce_scatter x1, waiting for transfers between devices, shards(): lax.psum_scatter(local_product(second_all, w_gate).astype(jnp.bfloat16),...  73.7 us
  transfers between devices with their start and end apart: 34, of which 31 were waited for; matrix products, arithmetic and copies ran while one was open for 53% of the time, Pallas kernels for 0%

commit v1 on v0

v1 whole, which is shorter than its diff:
```python
import jax, jax.numpy as jnp
from jax import lax
from jax.experimental import pallas as pl
from jax.experimental.pallas import tpu as pltpu
import functools
from jax.sharding import PartitionSpec as P
EPS = 1e-6
HEAD_EPS = 0.01
C = 128
bf = jnp.bfloat16
f32 = jnp.float32
GROUP = 8

def nn(a, b):
    return lax.dot_general(a.astype(bf), b.astype(bf), (((1,), (0,)), ((), ())), preferred_element_type=f32)
def nt(a, b):
    return lax.dot_general(a.astype(bf), b.astype(bf), (((1,), (1,)), ((), ())), preferred_element_type=f32)
def tn(a, b):
    return lax.dot_general(a.astype(bf), b.astype(bf), (((0,), (0,)), ((), ())), preferred_element_type=f32)

def level_masks(n):
    row = lax.broadcasted_iota(jnp.int32, (n, n), 0)
    col = lax.broadcasted_iota(jnp.int32, (n, n), 1)
    out = []
    size = 1
    while size < n:
        out.append(((row ^ col) & (-size) == size).astype(f32).astype(bf))
        size *= 2
    return (row == col).astype(f32).astype(bf), out

def inverse_many(many, eye, levels):
    totals = [eye - a * levels[0] for a in many]
    for mask in levels[1:]:
        inner = [nn(a * mask, t).astype(bf) for a, t in zip(many, totals)]
        outer = [nn(t, x).astype(bf) for t, x in zip(totals, inner)]
        totals = [t - x for t, x in zip(totals, outer)]
    return totals

def act_stage(x, prev, aux, w, norm):
    row8 = lax.broadcasted_iota(jnp.int32, (8, 128), 0)
    conv = x * w[0:1]
    sh = []
    for i in range(1, w.shape[0]):
        r = pltpu.roll(x, i, 0)
        p = pltpu.roll(prev, i, 0)
        head = jnp.where(row8 < i, p, r[:8])
        m = jnp.concatenate([head, r[8:]], axis=0) * aux[:, 2 + i:3 + i]
        sh.append(m)
        conv = conv + m * w[i:i + 1]
    s = jax.nn.sigmoid(conv)
    act = conv * s
    if norm:
        rate = lax.rsqrt(jnp.sum(act * act, axis=-1, keepdims=True) + EPS)
        return conv, s, act * rate, rate, sh
    return conv, s, act, None, sh

def masks(aux, segrow):
    n = aux.shape[0]
    row = lax.broadcasted_iota(jnp.int32, (n, n), 0)
    col = lax.broadcasted_iota(jnp.int32, (n, n), 1)
    same = aux[:, 0:1] == segrow
    return same & (row > col), same & (row >= col)

def beta_column(block, h):
    lane = lax.broadcasted_iota(jnp.int32, block.shape, 1)
    return jnp.sum(jnp.where(lane == h, jax.nn.sigmoid(block), 0.0), axis=1, keepdims=True)

def prev_rows(ref, lo):
    start = pl.multiple_of(jnp.maximum(lo - 8, 0), 8)
    return jnp.where(lo > 0, ref[0, pl.ds(start, 8), :].astype(f32), 0.0)

def fwd_kernel(q_ref, k_ref, v_ref, g_ref, b_ref, aux_ref, seg_ref, w_ref, gain_ref,
               mixed_ref, t_ref, w_out, p_ref, f_ref, s_ref, fresh_ref, o_ref,
               q_s, u_s, b_s):
    h = pl.program_id(1)
    length = q_ref.shape[1]
    steps = length // C
    eye, levels = level_masks(C)
    def stage_a(group, _):
        lows = [pl.multiple_of((group * GROUP + n) * C, C) for n in range(GROUP)]
        spans = [pl.ds(lo, C) for lo in lows]
        many, keys, right = [], [], []
        for lo, rows in zip(lows, spans):
            aux = aux_ref[0, rows, :]
            q = act_stage(q_ref[0, rows, :].astype(f32), prev_rows(q_ref, lo), aux, w_ref[0], True)[2]
            k = act_stage(k_ref[0, rows, :].astype(f32), prev_rows(k_ref, lo), aux, w_ref[1], True)[2]
            v = act_stage(v_ref[0, rows, :].astype(f32), prev_rows(v_ref, lo), aux, w_ref[2], False)[2]
            beta = beta_column(b_ref[0, rows, :].astype(f32), h)
            strict, inclusive = masks(aux, seg_ref[0, 0:1, rows])
            kb = k.astype(bf)
            qb = q.astype(bf)
            both = nt(jnp.concatenate([kb, qb], axis=0), kb)
            many.append(jnp.where(strict, beta * both[:C], 0.0).astype(bf))
            p_ref[0, 0, rows, :] = jnp.where(inclusive, both[C:], 0.0).astype(bf)
            q_s[rows, :] = qb
            keys.append((k * aux[:, 2:3]).astype(bf))
            right.append(jnp.concatenate([(beta * k).astype(bf), (beta * v).astype(bf)], axis=1))
        totals = inverse_many(many, eye, levels)
        wus = [nn(t, r) for t, r in zip(totals, right)]
        kwus = [tn(k, wu) for k, wu in zip(keys, wus)]
        for rows, t, wu, kwu in zip(spans, totals, wus, kwus):
            clast = aux_ref[0, rows, :][C - 1:C, 1:2]
            f_ref[0, 0, rows, :] = (clast * (eye.astype(f32) - kwu[:, :C])).astype(bf)
            b_s[rows, :] = kwu[:, C:]
            t_ref[0, 0, rows, :] = t
            w_out[0, 0, rows, :] = wu[:, :C].astype(bf)
            u_s[rows, :] = wu[:, C:]
        return 0
    lax.fori_loop(0, steps // GROUP, stage_a, 0)
    def scan(c, state):
        rows = pl.ds(pl.multiple_of(c * C, C), C)
        sb = state.astype(bf)
        s_ref[0, 0, rows, :] = sb
        return nn(f_ref[0, 0, rows, :], sb) + b_s[rows, :]
    lax.fori_loop(0, steps, scan, jnp.zeros((C, C), f32), unroll=True)
    def stage_c(c, _):
        rows = pl.ds(pl.multiple_of(c * C, C), C)
        aux = aux_ref[0, rows, :]
        carried = aux[:, 1:2]
        ws = nn(jnp.concatenate([w_out[0, 0, rows, :], q_s[rows, :]], axis=0), s_ref[0, 0, rows, :])
        fresh = (u_s[rows, :] - carried * ws[:C]).astype(bf)
        out = carried * ws[C:] + nn(p_ref[0, 0, rows, :], fresh)
        fresh_ref[0, 0, rows, :] = fresh
        o_ref[0, 0, rows, :] = out
        g = g_ref[0, rows, :].astype(f32)
        r = lax.rsqrt(jnp.mean(out * out, axis=-1, keepdims=True) + HEAD_EPS)
        mixed_ref[0, rows, :] = (out * r * gain_ref[0:1] * (g * jax.nn.sigmoid(g))).astype(bf)
        return 0
    lax.fori_loop(0, steps, stage_c, 0, unroll=4)

def specs(length, heads, off):
    return [pl.BlockSpec((1, length, 128), functools.partial(lambda t, b, h: (b, 0, t * heads + h), t)) for t in range(4)] + [
        pl.BlockSpec((1, length, 128), lambda b, h: (b, 0, 4 * heads))]

def mixer_fwd(raw, aux, segrow, conv, gain):
    nb, length, width = raw.shape
    heads = (width - 128) // 512
    per = pl.BlockSpec((1, 1, length, 128), lambda b, h: (b, h, 0, 0))
    sh = lambda d: jax.ShapeDtypeStruct((nb, heads, length, 128), d)
    return pl.pallas_call(
        fwd_kernel,
        grid=(nb, heads),
        in_specs=specs(length, heads, 0) + [
            pl.BlockSpec((1, length, aux.shape[2]), lambda b, h: (b, 0, 0)),
            pl.BlockSpec((1, 1, length), lambda b, h: (b, 0, 0)),
            pl.BlockSpec((3, conv.shape[1], 128), lambda b, h: (0, 0, h)),
            pl.BlockSpec((1, 128), lambda b, h: (0, 0)),
        ],
        out_specs=[pl.BlockSpec((1, length, 128), lambda b, h: (b, 0, h))] + [per] * 7,
        out_shape=[jax.ShapeDtypeStruct((nb, length, heads * 128), bf)] + [sh(bf)] * 6 + [sh(f32)],
        scratch_shapes=[pltpu.VMEM((length, 128), bf), pltpu.VMEM((length, 128), f32), pltpu.VMEM((length, 128), f32)],
        name="mixer_forward",
    )(raw, raw, raw, raw, raw, aux, segrow, conv, gain)

def bwd_kernel(q_ref, k_ref, v_ref, g_ref, b_ref, aux_ref, seg_ref, w_ref, gain_ref,
               t_ref, w_in, p_ref, f_ref, s_ref, fresh_ref, o_ref, dm_ref,
               draw_ref, dconv_ref, dgain_ref,
               do_s, pd_s, base_s, ds_s):
    h = pl.program_id(1)
    heads = pl.num_programs(1)
    length = q_ref.shape[1]
    steps = length // C
    gain = gain_ref[0:1]
    def stage_a(c, dgain):
        lo = pl.multiple_of(c * C, C)
        rows = pl.ds(lo, C)
        aux = aux_ref[0, rows, :]
        carried = aux[:, 1:2]
        q = act_stage(q_ref[0, rows, :].astype(f32), prev_rows(q_ref, lo), aux, w_ref[0], True)[2]
        out = o_ref[0, 0, rows, :]
        g = g_ref[0, rows, :].astype(f32)
        dm = dm_ref[0, rows, :].astype(f32)
        s = jax.nn.sigmoid(g)
        r = lax.rsqrt(jnp.mean(out * out, axis=-1, keepdims=True) + HEAD_EPS)
        scaled = out * r
        dn = dm * (g * s)
        dg = dm * scaled * gain * (s * (1.0 + g * (1.0 - s)))
        draw_ref[0, rows, pl.ds(pl.multiple_of((3 * heads + h) * 128, 128), 128)] = dg.astype(bf)
        e = dn * gain
        do = r * (e - scaled * jnp.mean(e * scaled, axis=-1, keepdims=True))
        pd = tn(p_ref[0, 0, rows, :], do)
        do_s[rows, :] = do
        pd_s[rows, :] = pd
        base_s[rows, :] = tn(jnp.concatenate([q.astype(bf), w_in[0, 0, rows, :]], axis=0),
                             jnp.concatenate([carried * do, -carried * pd], axis=0))
        return dgain + jnp.sum((dn * scaled).reshape(C // 8, 8, 128), axis=0)
    dgain = lax.fori_loop(0, steps, stage_a, jnp.zeros((8, 128), f32), unroll=2)
    dgain_ref[0, 0] = dgain
    def scan(j, state):
        c = steps - 1 - j
        rows = pl.ds(pl.multiple_of(c * C, C), C)
        sb = state.astype(bf)
        ds_s[rows, :] = sb
        return tn(f_ref[0, 0, rows, :], sb) + base_s[rows, :]
    lax.fori_loop(0, steps, scan, jnp.zeros((C, C), f32), unroll=True)
    row8 = lax.broadcasted_iota(jnp.int32, (8, 128), 0)
    lane = lax.broadcasted_iota(jnp.int32, (C, 128), 1)

    def conv_back(dconv, nxt, aux, w, raw, sh):
        d = dconv * w[0:1]
        dw = [jnp.sum((dconv * raw).reshape(C // 8, 8, 128), axis=0)]
        for i in range(1, w.shape[0]):
            r = pltpu.roll(dconv, C - i, 0)
            p = pltpu.roll(nxt, 8 - i, 0)
            tailrows = jnp.where(row8 >= 8 - i, p, r[C - 8:])
            m = jnp.concatenate([r[:C - 8], tailrows], axis=0) * aux[:, 5 + i:6 + i]
            d = d + m * w[i:i + 1]
            dw.append(jnp.sum((dconv * sh[i - 1]).reshape(C // 8, 8, 128), axis=0))
        return d, dw

    def stage_c(j, carry):
        nq, nk, nv, dws = carry
        c = steps - 1 - j
        lo = pl.multiple_of(c * C, C)
        rows = pl.ds(lo, C)
        aux = aux_ref[0, rows, :]
        carried = aux[:, 1:2]
        tail = aux[:, 2:3]
        xq = q_ref[0, rows, :].astype(f32)
        xk = k_ref[0, rows, :].astype(f32)
        xv = v_ref[0, rows, :].astype(f32)
        cq, sq, q, rq, shq = act_stage(xq, prev_rows(q_ref, lo), aux, w_ref[0], True)
        ck, sk, k, rk, shk = act_stage(xk, prev_rows(k_ref, lo), aux, w_ref[1], True)
        cv, sv, v, _, shv = act_stage(xv, prev_rows(v_ref, lo), aux, w_ref[2], False)
        bblock = b_ref[0, rows, :].astype(f32)
        beta = beta_column(bblock, h)
        strict, inclusive = masks(aux, seg_ref[0, 0:1, rows])
        kb = k.astype(bf)
        qb = q.astype(bf)
        st = s_ref[0, 0, rows, :]
        dst = ds_s[rows, :]
        fresh = fresh_ref[0, 0, rows, :]
        do = do_s[rows, :]
        gram = nt(kb, kb)
        kk = nn(kb, jnp.concatenate([dst, st], axis=1))
        dfresh = pd_s[rows, :] + tail * kk[:, :128]
        x = v - carried * kk[:, 128:]
        y = tn(t_ref[0, 0, rows, :], dfresh)
        dx = beta * y
        cdx = (carried * dx).astype(bf)
        yb = y.astype(bf)
        dob = do.astype(bf)
        both = nt(jnp.concatenate([dob, yb], axis=0), fresh)
        dp = jnp.where(inclusive, both[:C], 0.0)
        da = jnp.where(strict, -both[C:], 0.0)
        dbeta = jnp.sum(y * x, axis=-1, keepdims=True) + jnp.sum(da * gram, axis=-1, keepdims=True)
        dg = beta * da
        dgs = dg + dg.T
        through = nt(jnp.concatenate([carried * do, -(carried * dx)], axis=0), st)
        dpb = dp.astype(bf)
        dq = through[:C] + nn(dpb, kb)
        dk = through[C:] + tn(dpb, qb) + nt(tail * fresh.astype(f32), dst) + nn(dgs, kb)
        dv = dx
        db = dbeta * beta * (1.0 - beta)
        bl = pl.ds(4 * heads * 128, 128)
        @pl.when(h == 0)
        def _():
            draw_ref[0, rows, bl] = jnp.where(lane == 0, db, 0.0).astype(bf)
        @pl.when(h > 0)
        def _():
            old = draw_ref[0, rows, bl]
            draw_ref[0, rows, bl] = jnp.where(lane == h, db.astype(bf).astype(f32), old.astype(f32)).astype(bf)
        dq = rq * (dq - q * jnp.sum(q * dq, axis=-1, keepdims=True))
        dk = rk * (dk - k * jnp.sum(k * dk, axis=-1, keepdims=True))
        dcq = dq * (sq * (1.0 + cq * (1.0 - sq)))
        dck = dk * (sk * (1.0 + ck * (1.0 - sk)))
        dcv = dv * (sv * (1.0 + cv * (1.0 - sv)))
        rq_, wq = conv_back(dcq, nq, aux, w_ref[0], xq, shq)
        rk_, wk = conv_back(dck, nk, aux, w_ref[1], xk, shk)
        rv_, wv = conv_back(dcv, nv, aux, w_ref[2], xv, shv)
        for t, val in ((0, rq_), (1, rk_), (2, rv_)):
            draw_ref[0, rows, pl.ds(pl.multiple_of((t * heads + h) * 128, 128), 128)] = val.astype(bf)
        dws = tuple(a + b for a, b in zip(dws, wq + wk + wv))
        return dcq[:8], dck[:8], dcv[:8], dws
    z8 = jnp.zeros((8, 128), f32)
    taps = w_ref.shape[1]
    _, _, _, dws = lax.fori_loop(0, steps, stage_c, (z8, z8, z8, (z8,) * (3 * taps)), unroll=2)
    for n, d in enumerate(dws):
        dconv_ref[0, 0, n] = d

def mixer_bwd(raw, aux, segrow, conv, gain, saved, dmixed):
    nb, length, width = raw.shape
    heads = (width - 128) // 512
    taps = conv.shape[1]
    per = pl.BlockSpec((1, 1, length, 128), lambda b, h: (b, h, 0, 0))
    sh = lambda d: jax.ShapeDtypeStruct((nb, heads, length, 128), d)
    draw, dconv, dgain = pl.pallas_call(
        bwd_kernel,
        grid=(nb, heads),
        in_specs=specs(length, heads, 0) + [
            pl.BlockSpec((1, length, aux.shape[2]), lambda b, h: (b, 0, 0)),
            pl.BlockSpec((1, 1, length), lambda b, h: (b, 0, 0)),
            pl.BlockSpec((3, taps, 128), lambda b, h: (0, 0, h)),
            pl.BlockSpec((1, 128), lambda b, h: (0, 0)),
        ] + [per] * 7 + [pl.BlockSpec((1, length, 128), lambda b, h: (b, 0, h))],
        out_specs=[pl.BlockSpec((1, length, width), lambda b, h: (b, 0, 0)),
                   pl.BlockSpec((1, 1, 3 * taps, 8, 128), lambda b, h: (b, h, 0, 0, 0)),
                   pl.BlockSpec((1, 1, 8, 128), lambda b, h: (b, h, 0, 0))],
        out_shape=[jax.ShapeDtypeStruct((nb, length, width), bf),
                   jax.ShapeDtypeStruct((nb, heads, 3 * taps, 8, 128), f32),
                   jax.ShapeDtypeStruct((nb, heads, 8, 128), f32)],
        scratch_shapes=[pltpu.VMEM((length, 128), f32)] * 3 + [pltpu.VMEM((length, 128), bf)],
        name="mixer_backward",
    )(raw, raw, raw, raw, raw, aux, segrow, conv, gain, *saved, dmixed)
    dconv = jnp.sum(dconv, axis=(0, 3)).reshape(heads, 3, taps, 128).transpose(1, 2, 0, 3).reshape(3, taps, heads * 128)
    return draw, dconv, jnp.sum(dgain, axis=(0, 1, 2))

def make_aux(segments):
    nb, length = segments.shape
    seg = segments.astype(f32)
    blocks = seg.reshape(nb, length // C, C)
    last = blocks[:, :, -1:]
    before = jnp.concatenate([jnp.full((nb, 1, 1), -1.0, f32), last[:, :-1]], axis=1)
    carried = (blocks == before).astype(f32).reshape(nb, length)
    tail = (blocks == last).astype(f32).reshape(nb, length)
    cols = [seg, carried, tail]
    for i in range(1, 4):
        cols.append((jnp.pad(seg, ((0, 0), (i, 0)), constant_values=-1.0)[:, :length] == seg).astype(f32))
    for i in range(1, 4):
        cols.append((jnp.pad(seg, ((0, 0), (0, i)), constant_values=-1.0)[:, i:] == seg).astype(f32))
    cols += [jnp.zeros_like(seg)] * (16 - len(cols))
    return jnp.stack(cols, axis=-1), seg[:, None, :]


TOKENS = ("gy", "gx")
EVERY = ("dp", "gx", "gy")


def dot(a, b):
    return lax.dot_general(a, b, (((1,), (0,)), ((), ())), preferred_element_type=f32)


def dot_t(a, b):
    return lax.dot_general(a, b, (((1,), (1,)), ((), ())), preferred_element_type=f32)


def dot_w(a, b):
    return lax.dot_general(a, b, (((0,), (0,)), ((), ())), preferred_element_type=f32)


def swap(value):
    return lax.ppermute(value, "gy", [(0, 1), (1, 0)])


def in_order(mine, other, axis):
    first = lax.axis_index("gy") == 0
    return jnp.concatenate([jnp.where(first, mine, other), jnp.where(first, other, mine)], axis=axis)


def halves(value, axis):
    size = value.shape[axis] // 2
    mine = lax.axis_index("gy")
    return (
        lax.dynamic_slice_in_dim(value, mine * size, size, axis),
        lax.dynamic_slice_in_dim(value, (1 - mine) * size, size, axis),
    )


def gather_blocks(value):
    nb, rows, width = value.shape
    many = lax.all_gather(value, ("gx", "gy"), axis=0, tiled=False)
    ngx, ngy = lax.axis_size("gx"), lax.axis_size("gy")
    many = many.reshape(ngx, ngy, nb, rows, width)
    return many.transpose(2, 0, 3, 1, 4).reshape(nb, ngx * rows, ngy * width)


def gather_rows(value):
    return lax.all_gather(value, TOKENS, axis=0, tiled=True)


def scatter_rows(value):
    return lax.psum_scatter(value.astype(bf), TOKENS, scatter_dimension=0, tiled=True).astype(f32)


def to_final(own):
    mine, other = halves(own, 1)
    return in_order(mine[None], swap(other)[None], 0)


def rate_of(value):
    return lax.rsqrt(jnp.mean(value * value, axis=-1, keepdims=True) + EPS)


def norm_back(value, rate, gain, incoming):
    scaled = gain * incoming
    inner = jnp.mean(value * scaled, axis=-1, keepdims=True)
    return rate * scaled - value * (rate * rate * rate) * inner, jnp.sum(incoming * value * rate, axis=0)


def scatter_dp(value):
    return lax.psum_scatter(value.astype(bf), "dp", scatter_dimension=0, tiled=True)


def columns_grad(grad, ndp):
    rows, cols = grad.shape
    parts = grad.astype(bf).reshape(2, ndp, rows // (2 * ndp), cols).transpose(1, 0, 2, 3)
    summed = lax.psum_scatter(parts.reshape(rows, cols), "dp", scatter_dimension=0, tiled=True)
    mine, other = halves(summed, 0)
    return mine, swap(other)


def shards(
    inputs,
    segments,
    norm_gain,
    w_query,
    w_key,
    w_value,
    w_beta,
    w_gate_head,
    conv_kernel,
    head_gain,
    w_out,
    mlp_gain,
    w_gate,
    w_up,
    w_down,
    grad_y,
):
    ngx, ngy, ndp = lax.axis_size("gx"), lax.axis_size("gy"), lax.axis_size("dp")
    gx, gy = lax.axis_index("gx"), lax.axis_index("gy")
    x_all = gather_blocks(inputs)
    nb, length, feat = x_all.shape
    tokens = nb * length
    own_rows = tokens // (ngx * ngy)
    own_start = (gy * ngx + gx) * own_rows
    heads = w_beta.shape[1] // ngy
    width = w_query.shape[1] // ngy

    cat = [halves(w, 1) for w in (w_query, w_key, w_value, w_gate_head)]
    pad = ((0, 0), (0, 128 - heads))
    beta_mine, beta_other = halves(w_beta, 1)
    head_w = in_order(
        jnp.concatenate([m for m, _ in cat] + [jnp.pad(beta_mine, pad)], axis=1),
        swap(jnp.concatenate([o for _, o in cat] + [jnp.pad(beta_other, pad)], axis=1)),
        0,
    )

    def own_columns(w):
        mine, other = halves(w, 1)
        return in_order(mine, swap(other), 0)

    aux, segrow = make_aux(segments)
    x_flat = x_all.reshape(tokens, feat)
    x_wide = x_flat.astype(f32)
    rate_first = rate_of(x_wide)
    normed = (x_wide * rate_first * norm_gain).astype(bf)
    raw = dot(normed, head_w).reshape(nb, length, -1)
    conv_start = (gx * ngy + gy) * width
    conv_local = lax.dynamic_slice_in_dim(conv_kernel, conv_start, width, 2)
    gain_row = head_gain[None]
    mixed, *saved = mixer_fwd(raw, aux, segrow, conv_local, gain_row)
    mixed = mixed.reshape(tokens, width)

    out_blocks = lax.all_gather(w_out, ("gx", "gy"), axis=0, tiled=False)
    out_full = (
        out_blocks.reshape(ngx, ngy, ngy, width, -1).transpose(2, 0, 3, 1, 4).reshape(ngx * ngy * width, feat)
    )
    y_all = gather_blocks(grad_y).reshape(tokens, feat)
    gate_w = own_columns(w_gate)
    up_w = own_columns(w_up)
    down_mine, down_other = halves(w_down, 0)
    down_w = in_order(down_mine, swap(down_other), 1)

    mixed_own = lax.all_to_all(mixed, TOKENS, 0, 1, tiled=True)
    x_own = lax.dynamic_slice_in_dim(x_flat, own_start, own_rows, 0).astype(f32)
    middle = x_own + dot(mixed_own, out_full)
    rate_second = rate_of(middle)
    second = gather_rows((middle * rate_second * mlp_gain).astype(bf))
    gate_val = dot(second, gate_w)
    up_val = dot(second, up_w)
    grad_hidden = dot_t(y_all, down_w)
    sig = jax.nn.sigmoid(gate_val)
    act = gate_val * sig
    hidden = (act * up_val).astype(bf)
    grad_up_val = (grad_hidden * act).astype(bf)
    grad_gate_val = (grad_hidden * up_val * sig * (1.0 + gate_val * (1.0 - sig))).astype(bf)
    grad_second = scatter_rows(dot_t(grad_gate_val, gate_w) + dot_t(grad_up_val, up_w))
    norm_two, mlp_gain_grad = norm_back(middle, rate_second, mlp_gain, grad_second)
    y_own = lax.dynamic_slice_in_dim(y_all, own_start, own_rows, 0).astype(f32)
    grad_middle = y_own + norm_two
    mid_low = grad_middle.astype(bf)
    grad_mixed = lax.all_to_all(dot_t(mid_low, out_full).astype(bf), TOKENS, 1, 0, tiled=True)
    draw, conv_grad, gain_grad = mixer_bwd(
        raw, aux, segrow, conv_local, gain_row, saved, grad_mixed.reshape(nb, length, width)
    )
    draw = draw.reshape(tokens, -1)
    grad_normed = scatter_rows(dot_t(draw, head_w))
    rate_own = lax.dynamic_slice_in_dim(rate_first, own_start, own_rows, 0)
    norm_one, norm_gain_grad = norm_back(x_own, rate_own, norm_gain, grad_normed)
    grad_inputs = to_final((grad_middle + norm_one).astype(bf))

    layer_out = to_final((middle + scatter_rows(dot(hidden, down_w))).astype(bf))
    mid_all = gather_rows(mid_low)

    down_keep, down_send = halves(dot_w(hidden, y_all).astype(bf), 1)
    sum_down = scatter_dp(in_order(down_keep, swap(down_send), 0)).astype(f32)
    out_keep, out_send = halves(dot_w(mixed, mid_all).astype(bf), 1)
    sum_out = scatter_dp(in_order(out_keep, swap(out_send), 0)).astype(f32)

    def whole_columns(grad):
        mine, other = columns_grad(grad, ndp)
        return in_order(mine, other, 1).astype(f32)

    sum_gate = whole_columns(dot_w(second, grad_gate_val))
    sum_up = whole_columns(dot_w(second, grad_up_val))
    head_mine, head_other = columns_grad(dot_w(normed, draw), ndp)

    def head_part(i, n):
        return in_order(head_mine[:, i : i + n], head_other[:, i : i + n], 1).astype(f32)

    sum_query, sum_key, sum_value, sum_head_gate = (head_part(i * width, width) for i in range(4))
    sum_beta = head_part(4 * width, heads)

    conv_full = lax.dynamic_update_slice_in_dim(jnp.zeros(conv_kernel.shape, f32), conv_grad, conv_start, 2)
    norm_sum, mlp_sum, conv_sum, gain_sum = lax.psum((norm_gain_grad, mlp_gain_grad, conv_full, gain_grad), EVERY)
    return (
        layer_out,
        grad_inputs,
        norm_sum,
        sum_query,
        sum_key,
        sum_value,
        sum_beta,
        sum_head_gate,
        conv_sum,
        gain_sum,
        sum_out,
        mlp_sum,
        sum_gate,
        sum_up,
        sum_down,
    )


def solution(mesh):
    cols = P("gy", "gx")
    rows = P("gx", "gy")
    acts = P("dp", "gx", "gy")
    cols_out = P(("gy", "dp"), "gx")
    rows_out = P(("gx", "dp"), "gy")
    return jax.shard_map(
        shards,
        mesh=mesh,
        in_specs=(acts, P("dp", None), P(), cols, cols, cols, cols, cols, P(), P(), rows, P(), cols, cols, rows, acts),
        out_specs=(
            acts,
            acts,
            P(),
            cols_out,
            cols_out,
            cols_out,
            cols_out,
            cols_out,
            P(),
            P(),
            rows_out,
            P(),
            cols_out,
            cols_out,
            rows_out,
        ),
        check_vma=False,
    )
```

time: 2920 us -> 1240 us (0.42)
  other arithmetic: 837 us -> 129 us
  waiting for transfers between devices: 1200 us -> 528 us
  matrix products: 513 us -> 173 us
  Pallas kernels: 0 us -> 89.4 us
  local copies, waits for them, and re-layouts: 256 us -> 221 us
    another operation x144 -> x1, other arithmetic: 656 us -> 0.12 us  [make_aux(): return (jnp.stack(cols, axis=-1), seg[:, None, :])]
    reduce_scatter x20 -> x8, waiting for transfers between devices: 742 us -> 227 us  [the longest x3 211 us: scatter_rows(): lax.psum_scatter(value.astype(bf), TOKENS, scatter_dimension=0, tiled=True)]
    all_gather x12 -> x5, waiting for transfers between devices: 354 us -> 0.04 us  [the longest x2 0.02 us: gather_rows(): return lax.all_gather(value, TOKENS, axis=0, tiled=True)]
    dot_general x379 -> x15, matrix products: 458 us -> 173 us  [the longest x5 60.8 us: dot(): lax.dot_general(a, b, (((1,), (0,)), ((), ())), preferred_element_type=f32)]
    ppermute x0 -> x11, waiting for transfers between devices: none -> 215 us  [swap(): return lax.ppermute(value, 'gy', [(0, 1), (1, 0)])]
    pallas_call x0 -> x2, Pallas kernels: none -> 89.4 us  [the longest x1 56.5 us: mixer_bwd(): pl.pallas_call(bwd_kernel, grid=(nb, heads), in_specs=specs(length, heads...]
    squeeze x112 -> x0, local copies, waits for them, and re-layouts: 85.4 us -> none  [delta_rule(): lax.scan(jax.checkpoint(block_step), start_carry, block_inputs)]
    another operation x64 -> x0, matrix products: 54.8 us -> none  [block_step(): lax.linalg.triangular_solve(system, stacked, left_side=True, lower=True,...]
  transfers between devices with their start and end apart: 34 -> 27, of which waited for: 31 -> 13; matrix products, arithmetic and copies ran while one was open for 53% -> 38% of each run, Pallas kernels for 0% -> 7%
where the time goes in v1:
time: 1240 us; the launch traced here: 1230 us
  waiting for transfers between devices  528 us (43%)
  local copies, waits for them, and re-layouts  221 us (18%)
  matrix products  173 us (14%)
  other arithmetic  129 us (10%)
  Pallas kernels  89.4 us (7%)
  blocking collectives  48.2 us (4%)
  starting transfers between devices  24.8 us (2%)
  between operations  14.7 us (1%)
    ppermute x11, waiting for transfers between devices, swap(): return lax.ppermute(value, 'gy', [(0, 1), (1, 0)])  215 us
    reduce_scatter x3, waiting for transfers between devices, scatter_rows(): lax.psum_scatter(value.astype(bf), TOKENS, scatter_dimension=0, tiled=True)  211 us
    psum x1, waiting for transfers between devices, shards(): lax.psum((norm_gain_grad, mlp_gain_grad, conv_full, gain_grad), EVERY)  83.4 us
    unnamed x107, local copies, waits for them, and re-layouts  69 us
    dot_general x5, matrix products, dot(): lax.dot_general(a, b, (((1,), (0,)), ((), ())), preferred_element_type=f32)  60.8 us
    dot_general x5, matrix products, dot_t(): lax.dot_general(a, b, (((1,), (1,)), ((), ())), preferred_element_type=f32)  58.8 us
    pallas_call x1, Pallas kernels, mixer_bwd(): pl.pallas_call(bwd_kernel, grid=(nb, heads), in_specs=specs(length, heads...  56.5 us
    dot_general x5, matrix products, dot_w(): lax.dot_general(a, b, (((0,), (0,)), ((), ())), preferred_element_type=f32)  53.5 us
  transfers between devices with their start and end apart: 27, of which 13 were waited for; matrix products, arithmetic and copies ran while one was open for 38% of the time, Pallas kernels for 7%

profile of v1, /device:TPU:0, one launch (start us, length us, event | category | flops | bytes accessed | tf_op | source)
XLA Modules:
  0.0 1229.1 jit_solution(11310057124477497433)
XLA Ops:
  16.2 2.9 collective-permute-start
  34.0 8.6 stack.63.aux_ref
  44.0 60.4 %collective-permute-done = bf16[1024,1152]{1,0:T(8,128)(2,1)} collective-permute-done((bf16[1024,1152]{1,0:T(8,128)(2,1)}, bf16[1024,1152]{1,0:T(8,128)(2,1)}, u32[]{:S(2)}, u32[]{:S(2)}) %collective-permute-start) | collective-permute-done | bytes 2359328 | tf_op jit(solution)/shard_map/ppermute | solution.py:342
  104.4 5.0 broadcast_select_fusion.1
  109.4 22.3 %multiply_reduce_fusion = f32[2,4,256]{2,1,0:T(4,128)S(1)} fusion(bf16[4,2,2,256,1024]{4,3,2,1,0:T(8,128)(2,1)} %bitcast.135), kind=kLoop, calls=%fused_computation.3 | loop fusion | flops 12580864 | bytes 8396800 | tf_op jit(solution)/shard_map/reduce_sum | solution.py:381
  132.2 31.2 %fusion.46 = (bf16[4,2,2,256,1024]{4,1,3,0,2:T(2,128)(2,1)}, f32[2,4,256,2,1024]{4,3,2,1,0:T(2,128)}) fusion(bf16[4,2,2,256,1024]{4,3,2,1,0:T(8,128)(2,1)S(1)} %bitcast.137), kind=kLoop, calls=%fused_computation.172 | loop fusion | flops 4194304 | bytes 33554432 | tf_op jit(solution)/shard_map/reshape | solution.py:363
  163.4 22.3 %reshape.203 = f32[2,1024,2048]{2,1,0:T(8,128)} reshape(f32[2,4,256,2,1024]{4,3,2,1,0:T(2,128)} %get-tuple-element.125) | data formatting | bytes 33554432 | tf_op jit(solution)/shard_map/convert_element_type | solution.py:445
  185.7 19.1 %fusion.q_ref.k_ref.v_ref.g_ref.b_ref = f32[2,1024,1152]{2,1,0:T(8,128)} fusion(f32[2,1024,2048]{2,1,0:T(8,128)} %reshape.203, f32[2048]{0:T(1024)S(1)} %copy-done.28, f32[2,1024]{1,0:T(2,128)S(1)} %bitcast.169, bf16[1024,1152]{1,0:T(8,128)(2,1)} %get-tuple-element.127, bf16[1024,1152]{1,0:T(8,128)(2,1)} %get-tuple-element.126), kind=kOutput, calls=%fused_computation.4 | convolution fusion | flops 9685696512 | bytes 30949376 | tf_op jit(solution)/shard_map/dot_general | solution.py:330
  204.9 32.9 %mixer_forward.1 = (bf16[2,1024,256]{2,1,0:T(8,128)(2,1)}, bf16[2,2,1024,128]{3,2,1,0:T(8,128)(2,1)}, bf16[2,2,1024,128]{3,2,1,0:T(8,128)(2,1)}, bf16[2,2,1024,1...) custom-call(f32[2,1024,1152]{2,1,0:T(8,128)} %fusion.q_ref.k_ref.v_r, ...), custom_call_target="tpu_custom_call" | custom-call | tf_op jit(solution)/shard_map/mixer_forward/pallas_call | solution.py:140
  240.0 3.9 all-to-all-start
  244.1 16.5 %copy.152 = bf16[4,2,2,256,1024]{4,1,3,0,2:T(2,128)(2,1)} copy(bf16[4,2,2,256,1024]{4,3,2,1,0:T(8,128)(2,1)} %bitcast.156) | data formatting | bytes 16777216 | tf_op jit(solution)/shard_map/reshape | solution.py:457
  260.5 10.1 copy.181
  270.7 10.2 copy.176
  280.9 6.1 multiply_reduce_fusion.1
  288.3 2.6 constant_dynamic-slice_fusion.8
  292.8 5.3 constant_dynamic-slice_fusion.12
  298.1 3.0 copy.172
  301.1 5.2 constant_dynamic-slice_fusion.10
  306.3 2.6 copy.174
  315.1 28.9 %collective-permute-done.3 = bf16[704,1024]{1,0:T(8,128)(2,1)} collective-permute-done((bf16[704,1024]{1,0:T(8,128)(2,1)}, bf16[704,1024]{1,0:T(8,128)(2,1)}, u32[]{:S(2)}, u32[]{:S(2)}) %collective-permute-start.3) | collective-permute-done | bytes 1441824 | tf_op jit(solution)/shard_map/ppermute | solution.py:342
  344.0 4.2 broadcast_select_fusion.5
  348.2 42.0 %collective-permute-done.1 = bf16[1024,704]{0,1:T(8,128)(2,1)} collective-permute-done((bf16[1024,704]{0,1:T(8,128)(2,1)}, bf16[1024,704]{0,1:T(8,128)(2,1)}, u32[]{:S(2)}, u32[]{:S(2)}) %collective-permute-start.1) | collective-permute-done | bytes 1441824 | tf_op jit(solution)/shard_map/ppermute | solution.py:342
  390.2 3.1 broadcast_select_fusion.9
  393.3 27.3 %collective-permute-done.2 = bf16[1024,704]{0,1:T(8,128)(2,1)} collective-permute-done((bf16[1024,704]{0,1:T(8,128)(2,1)}, bf16[1024,704]{0,1:T(8,128)(2,1)}, u32[]{:S(2)}, u32[]{:S(2)}) %collective-permute-start.2) | collective-permute-done | bytes 1441824 | tf_op jit(solution)/shard_map/ppermute | solution.py:342
  420.6 3.1 broadcast_select_fusion.7
  423.7 16.5 %copy.157 = bf16[4,2,2,256,1024]{4,1,3,0,2:T(2,128)(2,1)} copy(bf16[4,2,2,256,1024]{4,3,2,1,0:T(8,128)(2,1)} %bitcast.155) | data formatting | bytes 16777216 | tf_op jit(solution)/shard_map/reshape | solution.py:363
  440.2 10.4 copy.182
  450.6 10.3 fusion.24
  461.0 11.1 fusion.27
  472.1 13.4 %fusion.5 = (bf16[2048,704]{0,1:T(8,128)(2,1)}, bf16[2048,704]{0,1:T(8,128)(2,1)}, bf16[2048,704]{0,1:T(8,128)(2,1)}) fusion(f32[704,2048]{1,0:T(8,128)} %fusion.24, f32[2048,704]{0,1:T(8,128)} %fusion.27, bf16[2048,2048]{1,0:T(8,128)(2,1)S(1)} %copy-done.39, bf16[1024,704]{0,1:T(8,128)(2,1)S(1)} %copy-done.16, bf16[1024,704]{0,1:T(8,128)(2,1)S(1)} %copy-done.15), kind=kOutput, calls=%fused_computation.15 | convolution fusion | flops 5932974080 | bytes 31457280 | tf_op jit(solution)/shard_map/dot_general | solution.py:330
  485.4 12.5 %fusion.25 = f32[2048,2048]{1,0:T(8,128)} fusion(bf16[2048,704]{0,1:T(8,128)(2,1)} %get-tuple-element.122, bf16[1024,704]{0,1:T(8,128)(2,1)S(1)} %copy-done.16, bf16[1024,704]{0,1:T(8,128)(2,1)S(1)} %copy-done.15), kind=kOutput, calls=%fused_computation.59 | convolution fusion | flops 5911347200 | bytes 22544384 | tf_op jit(solution)/shard_map/dot_general | solution.py:334
  497.9 13.0 %add_convert_fusion = bf16[2048,2048]{1,0:T(8,128)(2,1)} fusion(f32[2048,2048]{1,0:T(8,128)} %fusion.25, bf16[2048,704]{0,1:T(8,128)(2,1)S(1)} %copy-done.40, bf16[1024,704]{0,1:T(8,128)(2,1)S(1)} %copy-done.14, bf16[1024,704]{0,1:T(8,128)(2,1)S(1)} %copy-done.13), kind=kOutput, calls=%fused_computation.1 | convolution fusion | flops 5919735808 | bytes 30932992 | tf_op jit(solution)/shard_map/dot_general | solution.py:334
  511.0 72.5 %reduce-scatter.11.cloned.1.call-done = bf16[256,2048]{1,0:T(8,128)(2,1)} async-done(((bf16[2048,2048]{1,0:T(8,128)(2,1)}), bf16[256,2048]{1,0:T(8,128)(2,1)}) %reduce-scatter.11.cloned.1.call-update) | async-done | bytes 1048592 | tf_op jit(solution)/shard_map/reduce_scatter | solution.py:372
  586.0 2.9 fusion.45
  589.0 10.6 convolution_convert_fusion.4
  599.5 7.1 reshape.199
  606.6 5.9 copy.161
  612.6 10.7 convolution_convert_fusion.3
  623.3 7.1 reshape.201
  630.4 5.9 copy.162
  637.0 6.1 convolution_convert_fusion.7
  644.2 4.3 all-to-all-start.1
  648.5 17.2 %multiply_convert_fusion = bf16[2,4,256,2,1024]{4,3,2,1,0:T(2,128)(2,1)} fusion(f32[2,1024]{1,0:T(2,128)S(1)} %mul.297, f32[2,4,256]{2,1,0:T(4,128)S(1)} %copy-done.27, bf16[4,2,2,256,1024]{4,3,2,1,0:T(8,128)(2,1)} %bitcast.136), kind=kLoop, calls=%fused_computation | loop fusion | flops 16777216 | bytes 16793600 | tf_op jit(solution)/shard_map/convert_element_type | solution.py:447
  665.7 10.3 copy.183
  676.0 56.5 %mixer_backward.1 = (bf16[2,1024,1152]{2,1,0:T(8,128)(2,1)}, f32[2,2,12,8,128]{4,3,2,1,0:T(8,128)}, f32[2,2,8,128]{3,2,1,0:T(8,128)}) custom-call(f32[2,1024,1152]{2,1,0:T(8,128)} %fusion.q_ref.k_ref.v_ref.g_ref.b_ref, f32[2,1024,1152]{2,1,0:T(8,128)} %fusion.q_ref.k_ref.v_ref.g_ref.b_ref, f32[2,1024,1152]{2,1,0:T(8,128)} %fusion.q_ref.k_ref.v_ref.g_ref.b_ref, ...), custom_call_target="tpu_custom_call" | custom-call | tf_op jit(solution)/shard_map/mixer_backward/pallas_call | solution.py:287
  732.5 16.6 %convolution_convert_fusion = bf16[2048,1152]{1,0:T(8,128)(2,1)} fusion(bf16[2048,2048]{1,0:T(8,128)(2,1)} %bitcast.157, bf16[2048,1152]{1,0:T(8,128)(2,1)} %bitcast.174), kind=kOutput, calls=%fused_computation.8 | convolution fusion | flops 9666035712 | bytes 17825792 | tf_op jit(solution)/shard_map/dot_general | solution.py:338
  749.2 12.6 %copy.159 = bf16[4,2,256,1152]{2,1,0,3:T(2,128)(2,1)} copy(bf16[4,2,256,1152]{3,2,0,1:T(8,128)(2,1)} %bitcast.161) | data formatting | bytes 9437184 | tf_op jit(solution)/shard_map/transpose | solution.py:396
  761.8 8.8 reshape.195
  770.7 9.4 convolution_convert_fusion.5
  784.8 32.3 %collective-permute-done.10 = bf16[704,1024]{1,0:T(8,128)(2,1)} collective-permute-done((bf16[704,1024]{1,0:T(8,128)(2,1)}, bf16[704,1024]{1,0:T(8,128)(2,1)}, u32[]{:S(2)}, u32[]{:S(2)}) %collective-permute-start.10) | collective-permute-done | bytes 1441824 | tf_op jit(solution)/shard_map/ppermute | solution.py:342
  821.6 16.9 %convolution_convert_fusion.1 = bf16[2048,2048]{1,0:T(8,128)(2,1)} fusion(bf16[2048,1152]{1,0:T(8,128)(2,1)} %bitcast.175, bf16[1024,1152]{1,0:T(8,128)(2,1)} %get-tuple-element.127, bf16[1024,1152]{1,0:T(8,128)(2,1)} %get-tuple-element.126), kind=kOutput, calls=%fused_computation.9 | convolution fusion | flops 9677307904 | bytes 17825792 | tf_op jit(solution)/shard_map/dot_general | solution.py:334
  838.6 11.2 convolution_convert_fusion.2
  849.9 6.2 convolution_convert_fusion.6
  857.9 11.7 collective-permute-done.7
  877.8 6.5 collective-permute-done.8
  884.3 6.1 collective-permute-done.9
  890.4 2.7 broadcast_select_fusion.13
  900.1 16.3 %reduce-scatter.23.cloned.1.call-done = bf16[352,1024]{1,0:T(8,128)(2,1)} async-done(((bf16[1408,1024]{1,0:T(8,128)(2,1)}), bf16[352,1024]{1,0:T(8,128)(2,1)}) %reduce-scatter.23.cloned.1.call-update) | async-done | bytes 720912 | tf_op jit(solution)/shard_map/reduce_scatter | solution.py:391
  924.1 67.4 %reduce-scatter.13.cloned.1.call-done = bf16[256,2048]{1,0:T(8,128)(2,1)} async-done(((bf16[2048,2048]{1,0:T(8,128)(2,1)}), bf16[256,2048]{1,0:T(8,128)(2,1)}) %reduce-scatter.13.cloned.1.call-update) | async-done | bytes 1048592 | tf_op jit(solution)/shard_map/reduce_scatter | solution.py:372
  991.4 2.8 fusion.23
  994.8 71.2 %reduce-scatter.9.cloned.1.call-done = bf16[256,2048]{1,0:T(8,128)(2,1)} async-done(((bf16[2048,2048]{1,0:T(8,128)(2,1)}), bf16[256,2048]{1,0:T(8,128)(2,1)}) %reduce-scatter.9.cloned.1.call-update) | async-done | bytes 1048592 | tf_op jit(solution)/shard_map/reduce_scatter | solution.py:372
  1066.1 3.5 fusion.14
  1083.5 48.2 %all-reduce.9 = (f32[2048]{0:T(1024)}, f32[128]{0:T(128)}, f32[2048]{0:T(1024)}) all-reduce(f32[2048]{0:T(1024)S(1)} %copy-done.32, f32[128]{0:T(128)S(1)} %copy-done.38, f32[2048]{0:T(1024)S(1)} %copy-done.31), channel_id=1, replica_groups=mesh['dp'=4,'gx'=4,'gy'=2] {'dp','gx','gy'}, use_global_device_ids=true, to_apply=%region_8.9 | all-reduce | flops 4224 | bytes 33792 | tf_op jit(solution)/shard_map/psum | solution.py:516
  1137.4 83.4 %all-reduce.12.cloned.1.call-done = f32[3,4,2048]{2,1,0:T(4,128)} async-done(((f32[3,4,2048]{2,1,0:T(4,128)}), f32[3,4,2048]{2,1,0:T(4,128)}) %all-reduce.12.cloned.1.call-update) | async-done | bytes 98320 | tf_op jit(solution)/shard_map/psum | solution.py:516
  (216 shorter events, 97.8 us)
Async XLA Ops:
  7.2 35.4 %copy-start = (f32[3,4,2048]{2,1,0:T(4,128)S(1)}, f32[3,4,2048]{2,1,0:T(4,128)}, u32[]{:S(2)}) copy-start(f32[3,4,2048]{2,1,0:T(4,128)} %param.24) | copy-start | bytes 294916
  7.2 2.3 copy-start.37
  7.2 2.5 copy-start.17
  7.2 3.7 copy-start.18
  7.2 102.1 %all-gather.13.cloned.1.call-start = ((), (), s32[]{:S(2)}) async-start(), calls=%async_computation.21 | async-start | bytes 9437184 | tf_op jit(solution)/shard_map/all_gather | solution.py:361
  8.0 236.1 %all-gather.15.cloned.1.call-start = ((), (), s32[]{:S(2)}) async-start(), calls=%async_computation.22 | async-start | bytes 9437184 | tf_op jit(solution)/shard_map/all_gather | solution.py:455
  8.7 415.0 %all-gather.17.cloned.1.call-start = ((), (), s32[]{:S(2)}) async-start(), calls=%async_computation.23 | async-start | bytes 9437184 | tf_op jit(solution)/shard_map/all_gather | solution.py:361
  9.7 4.6 copy-start.19
  12.0 7.1 copy-start.33
  16.2 88.2 %collective-permute-start = (bf16[1024,1152]{1,0:T(8,128)(2,1)}, bf16[1024,1152]{1,0:T(8,128)(2,1)}, u32[]{:S(2)}, u32[]{:S(2)}) collective-permute-start(bf16[1024,1152]{1,0:T(8,128)(2,1)} %pad_dynamic-update-slice_fusion), channel_id=1, source_target_pairs={{0,1},{1,0},{2,3},{3,2},{4,5},{5,4},{6,7},{7,6},{8,9},{9,8},{10,11... | collective-permute-start | bytes 7077896 | tf_op jit(solution)/shard_map/ppermute | solution.py:342
  109.4 22.9 %copy-start.2 = (bf16[16,256,1024]{2,1,0:T(8,128)(2,1)S(1)}, bf16[16,256,1024]{2,1,0:T(8,128)(2,1)}, u32[]{:S(2)}) copy-start(bf16[16,256,1024]{2,1,0:T(8,128)(2,1)} %all-gather.13.cloned.1.call-done) | copy-start | bytes 25165828
  163.4 22.3 %copy-start.28 = (f32[2048]{0:T(1024)S(1)}, f32[2048]{0:T(1024)}, u32[]{:S(2)}) copy-start(f32[2048]{0:T(1024)} %param.18) | copy-start | bytes 24580
  240.0 40.9 %all-to-all-start = ((bf16[8,256,256]{1,2,0:T(8,128)(2,1)}), bf16[8,256,256]{1,2,0:T(8,128)(2,1)S(1)}, u32[]{:S(2)}, u32[]{:S(2)}) async-start(bf16[8,256,256]{1,2,0:T(8,128)(2,1)} %copy.151), calls=%async_computation | async-start | bytes 2097152 | tf_op jit(solution)/shard_map/all_to_all | solution.py:465
  244.0 217.0 %all-gather.9.cloned.1.call-start = ((), (), s32[]{:S(2)}) async-start(), calls=%async_computation.10 | async-start | bytes 9437184 | tf_op jit(solution)/shard_map/all_gather | solution.py:368
  280.9 6.1 copy-start.26
  287.0 299.0 %copy-start.34 = (f32[256]{0:T(256)}, f32[256]{0:T(256)S(1)}, u32[]{:S(2)}) copy-start(f32[256]{0:T(256)S(1)} %get-tuple-element.186) | copy-start | bytes 3076
  287.0 299.0 %copy-start.35 = (f32[256]{0:T(256)}, f32[256]{0:T(256)S(1)}, u32[]{:S(2)}) copy-start(f32[256]{0:T(256)S(1)} %get-tuple-element.185) | copy-start | bytes 3076
  288.2 295.2 %reduce-scatter.11.cloned.1.call-start = ((), (), s32[]{:S(2)}) async-start(), calls=%async_computation.12 | async-start | bytes 9437184 | tf_op jit(solution)/shard_map/reduce_scatter | solution.py:372
  290.9 53.1 %collective-permute-start.3 = (bf16[704,1024]{1,0:T(8,128)(2,1)}, bf16[704,1024]{1,0:T(8,128)(2,1)}, u32[]{:S(2)}, u32[]{:S(2)}) collective-permute-start(bf16[704,1024]{1,0:T(8,128)(2,1)} %constant_dynamic-slice_fusion.8), channel_id=1, source_target_pairs={{0,1},{1,0},{2,3},{3,2},{4,5},{5,4},{6,7},{7,6},{8,9},{9,8},{10,11... | collective-permute-start | bytes 4325384 | tf_op jit(solution)/shard_map/ppermute | solution.py:342
  301.0 89.1 %collective-permute-start.1 = (bf16[1024,704]{0,1:T(8,128)(2,1)}, bf16[1024,704]{0,1:T(8,128)(2,1)}, u32[]{:S(2)}, u32[]{:S(2)}) collective-permute-start(bf16[1024,704]{0,1:T(8,128)(2,1)} %copy.172), channel_id=1, source_target_pairs={{0,1},{1,0},{2,3},{3,2},{4,5},{5,4},{6,7},{7,6},{8,9},{9,8},{10,11... | collective-permute-start | bytes 4325384 | tf_op jit(solution)/shard_map/ppermute | solution.py:342
  308.9 111.7 %collective-permute-start.2 = (bf16[1024,704]{0,1:T(8,128)(2,1)}, bf16[1024,704]{0,1:T(8,128)(2,1)}, u32[]{:S(2)}, u32[]{:S(2)}) collective-permute-start(bf16[1024,704]{0,1:T(8,128)(2,1)} %copy.174), channel_id=1, source_target_pairs={{0,1},{1,0},{2,3},{3,2},{4,5},{5,4},{6,7},{7,6},{8,9},{9,8},{10,11... | collective-permute-start | bytes 4325384 | tf_op jit(solution)/shard_map/ppermute | solution.py:342
  315.1 75.0 %copy-start.4 = (bf16[1024,704]{0,1:T(8,128)(2,1)S(1)}, bf16[1024,704]{0,1:T(8,128)(2,1)}, u32[]{:S(2)}) copy-start(bf16[1024,704]{0,1:T(8,128)(2,1)} %copy.171) | copy-start | bytes 4325380
  440.2 10.4 copy-start.11
  440.2 10.4 copy-start.12
  450.6 10.3 copy-start.13
  461.0 11.1 copy-start.15
  461.0 11.1 copy-start.16
  461.0 11.1 copy-start.39
  485.4 12.5 %copy-start.14 = (bf16[1024,704]{0,1:T(8,128)(2,1)S(1)}, bf16[1024,704]{0,1:T(8,128)(2,1)}, u32[]{:S(2)}) copy-start(bf16[1024,704]{0,1:T(8,128)(2,1)} %get-tuple-element.133) | copy-start | bytes 4325380
  485.4 12.5 %copy-start.40 = (bf16[2048,704]{0,1:T(8,128)(2,1)S(1)}, bf16[2048,704]{0,1:T(8,128)(2,1)}, u32[]{:S(2)}) copy-start(bf16[2048,704]{0,1:T(8,128)(2,1)} %get-tuple-element.121) | copy-start | bytes 8650756
  510.9 339.0 %all-gather.11.cloned.1.call-start = ((), (), s32[]{:S(2)}) async-start(), calls=%async_computation.16 | async-start | bytes 9437184 | tf_op jit(solution)/shard_map/all_gather | solution.py:368
  583.4 2.5 copy-start.3
  586.0 2.9 copy-start.36
  588.9 282.1 %reduce-scatter.19.cloned.1.call-start = ((), (), s32[]{:S(2)}) async-start(), calls=%async_computation.18 | async-start | bytes 3932160 | tf_op jit(solution)/shard_map/reduce_scatter | solution.py:397
  612.5 261.2 %reduce-scatter.21.cloned.1.call-start = ((), (), s32[]{:S(2)}) async-start(), calls=%async_computation.19 | async-start | bytes 3932160 | tf_op jit(solution)/shard_map/reduce_scatter | solution.py:397
  643.1 5.4 copy-start.27
  644.2 31.9 %all-to-all-start.1 = ((bf16[256,8,256]{2,0,1:T(8,128)(2,1)}), bf16[256,8,256]{2,0,1:T(8,128)(2,1)}, u32[]{:S(2)}, u32[]{:S(2)}) async-start(bf16[256,8,256]{2,0,1:T(8,128)(2,1)} %bitcast.162), calls=%async_computation.3 | async-start | bytes 2097152 | tf_op jit(solution)/shard_map/all_to_all | solution.py:483
  648.4 244.6 %reduce-scatter.15.cloned.1.call-start = ((), (), s32[]{:S(2)}) async-start(), calls=%async_computation.14 | async-start | bytes 5898240 | tf_op jit(solution)/shard_map/reduce_scatter | solution.py:397
  770.7 145.7 %reduce-scatter.23.cloned.1.call-start = ((), (), s32[]{:S(2)}) async-start(), calls=%async_computation.20 | async-start | bytes 3604480 | tf_op jit(solution)/shard_map/reduce_scatter | solution.py:391
  783.0 34.1 %collective-permute-start.10 = (bf16[704,1024]{1,0:T(8,128)(2,1)}, bf16[704,1024]{1,0:T(8,128)(2,1)}, u32[]{:S(2)}, u32[]{:S(2)}) collective-permute-start(bf16[704,1024]{1,0:T(8,128)(2,1)} %constant_dynamic-slice_fusion), channel_id=1, source_target_pairs={{0,1},{1,0},{2,3},{3,2},{4,5},{5,4},{6,7},{7,6},{8,9},{9,8},{10,11... | collective-permute-start | bytes 4325384 | tf_op jit(solution)/shard_map/ppermute | solution.py:342
  821.6 169.9 %reduce-scatter.13.cloned.1.call-start = ((), (), s32[]{:S(2)}) async-start(), calls=%async_computation.13 | async-start | bytes 9437184 | tf_op jit(solution)/shard_map/reduce_scatter | solution.py:372
  838.6 227.5 %reduce-scatter.9.cloned.1.call-start = ((), (), s32[]{:S(2)}) async-start(), calls=%async_computation.11 | async-start | bytes 9437184 | tf_op jit(solution)/shard_map/reduce_scatter | solution.py:372
  849.9 285.8 %reduce-scatter.17.cloned.1.call-start = ((), (), s32[]{:S(2)}) async-start(), calls=%async_computation.17 | async-start | bytes 1310720 | tf_op jit(solution)/shard_map/reduce_scatter | solution.py:391
  856.2 13.5 %collective-permute-start.7 = (bf16[256,1024]{1,0:T(8,128)(2,1)S(1)}, bf16[256,1024]{1,0:T(8,128)(2,1)S(1)}, u32[]{:S(2)}, u32[]{:S(2)}) collective-permute-start(bf16[256,1024]{1,0:T(8,128)(2,1)S(1)} %constant_dynamic-slice_fusion.3), channel_id=1, source_target_pairs={{0,1},{1,0},{2,3},{3,2},{4,5},{5,4},{6,7},{7,6},{8,9},{9,8},{10,11... | collective-permute-start | bytes 1572872 | tf_op jit(solution)/shard_map/ppermute | solution.py:342
  871.0 349.9 %all-reduce.12.cloned.1.call-start = ((), (), s32[]{:S(2)}) async-start(), calls=%async_computation.15 | async-start | bytes 196608 | tf_op jit(solution)/shard_map/psum | solution.py:516
  872.1 12.2 collective-permute-start.8
  875.5 14.9 %collective-permute-start.9 = (bf16[256,704]{1,0:T(8,128)(2,1)}, bf16[256,704]{1,0:T(8,128)(2,1)}, u32[]{:S(2)}, u32[]{:S(2)}) collective-permute-start(bf16[256,704]{1,0:T(8,128)(2,1)} %constant_dynamic-slice_fusion.1), channel_id=1, source_target_pairs={{0,1},{1,0},{2,3},{3,2},{4,5},{5,4},{6,7},{7,6},{8,9},{9,8},{10,11... | collective-permute-start | bytes 1081352 | tf_op jit(solution)/shard_map/ppermute | solution.py:342
  893.0 5.8 copy-start.10
  895.0 26.7 %collective-permute-start.6 = (bf16[256,1152]{0,1:T(8,128)(2,1)}, bf16[256,1152]{0,1:T(8,128)(2,1)}, u32[]{:S(2)}, u32[]{:S(2)}) collective-permute-start(bf16[256,1152]{0,1:T(8,128)(2,1)} %constant_dynamic-slice_fusion.4), channel_id=1, source_target_pairs={{0,1},{1,0},{2,3},{3,2},{4,5},{5,4},{6,7},{7,6},{8,9},{9,8},{10,11... | collective-permute-start | bytes 1769480 | tf_op jit(solution)/shard_map/ppermute | solution.py:342
  900.1 91.3 %copy-start.30 = (f32[2048]{0:T(1024)S(1)}, f32[2048]{0:T(1024)}, u32[]{:S(2)}) copy-start(f32[2048]{0:T(1024)} %param.18) | copy-start | bytes 24580
  1066.0 8.2 copy-start.21
  1066.1 8.2 copy-start.22
  1066.1 8.2 copy-start.23
  1066.1 8.2 copy-start.24
  1069.6 5.5 copy-start.7
  1070.6 7.8 copy-start.20
  1072.2 59.5 %collective-permute-start.4 = (bf16[256,1024]{1,0:T(8,128)(2,1)}, bf16[256,1024]{1,0:T(8,128)(2,1)}, u32[]{:S(2)}, u32[]{:S(2)}) collective-permute-start(bf16[256,1024]{1,0:T(8,128)(2,1)} %constant_dynamic-slice_fusion.7), channel_id=1, source_target_pairs={{0,1},{1,0},{2,3},{3,2},{4,5},{5,4},{6,7},{7,6},{8,9},{9,8},{10,11... | collective-permute-start | bytes 1572872 | tf_op jit(solution)/shard_map/ppermute | solution.py:342
  1073.6 58.1 %collective-permute-start.5 = (bf16[256,1024]{1,0:T(8,128)(2,1)}, bf16[256,1024]{1,0:T(8,128)(2,1)}, u32[]{:S(2)}, u32[]{:S(2)}) collective-permute-start(bf16[256,1024]{1,0:T(8,128)(2,1)} %constant_dynamic-slice_fusion.5), channel_id=1, source_target_pairs={{0,1},{1,0},{2,3},{3,2},{4,5},{5,4},{6,7},{7,6},{8,9},{9,8},{10,11... | collective-permute-start | bytes 1572872 | tf_op jit(solution)/shard_map/ppermute | solution.py:342
  1075.1 8.4 copy-start.31
  1075.1 8.4 copy-start.32
  1075.1 8.4 copy-start.38
  1075.1 56.6 %copy-start.6 = (bf16[256,2048]{1,0:T(8,128)(2,1)S(1)}, bf16[256,2048]{1,0:T(8,128)(2,1)}, u32[]{:S(2)}) copy-start(bf16[256,2048]{1,0:T(8,128)(2,1)} %copy-done.5) | copy-start | bytes 3145732
  1075.1 56.6 %copy-start.8 = (bf16[256,2048]{1,0:T(8,128)(2,1)S(1)}, bf16[256,2048]{1,0:T(8,128)(2,1)}, u32[]{:S(2)}) copy-start(bf16[256,2048]{1,0:T(8,128)(2,1)} %copy-done.7) | copy-start | bytes 3145732
  1131.8 90.7 %copy-start.1 = (f32[3,4,2048]{2,1,0:T(4,128)S(1)}, f32[3,4,2048]{2,1,0:T(4,128)}, u32[]{:S(2)}) copy-start(f32[3,4,2048]{2,1,0:T(4,128)} %param.24) | copy-start | bytes 294916
  (4 other events, 3.9 us)
Sparse Core Ops, SparseCore 0:
  9.9 90.1 all-gather.12
  102.0 54.3 all-gather.14
  158.4 54.3 all-gather.16
  288.3 88.8 all-gather.8
  511.0 72.3 reduce-scatter.10
  589.0 54.3 all-gather.10
  645.9 60.2 reduce-scatter.18
  708.5 60.3 reduce-scatter.20
  771.3 86.0 reduce-scatter.14
  859.7 56.6 reduce-scatter.22
  920.3 71.1 reduce-scatter.12
  994.8 71.2 reduce-scatter.8
  1068.4 27.1 reduce-scatter.16
  1101.6 119.2 all-reduce.11

commit v2 on v1

--- a/solution.py
+++ b/solution.py
@@ -322,8 +322,508 @@
     return jnp.stack(cols, axis=-1), seg[:, None, :]
 
 
+SLOTS = ((0, 0, 0), (0, 0, 1), (1, 0, 0), (0, 1, 0), (1, 0, 1), (0, 1, 1), (1, 1, 0), (1, 1, 1))
+MESH = pl.DeviceIdType.MESH
+VM = pl.BlockSpec(memory_space=pltpu.VMEM)
+ANY = pl.BlockSpec(memory_space=pl.ANY)
+
+
+def slot_place(r, gx, gy):
+    dx, dy, dc = SLOTS[r]
+    hi, lo = gx // 2, gx % 2
+    hi = 1 - hi if dy else hi
+    lo = 1 - lo if dc else lo
+    return hi * 2 + lo, (1 - gy if dx else gy)
+
+
+def slot_peer(r, gx, gy):
+    px, py = slot_place(r, gx, gy)
+    return {"gx": px, "gy": py}
+
+
+def entry_barrier(peers):
+    sem = pltpu.get_barrier_semaphore()
+    for peer in peers:
+        pl.semaphore_signal(sem, inc=1, device_id=peer, device_id_type=MESH)
+    pl.semaphore_wait(sem, len(peers))
+
+
+def remote(src, dst, send, recv, peer):
+    return pltpu.make_async_remote_copy(src, dst, send, recv, device_id=peer, device_id_type=MESH)
+
+
+def nt_dot(a, b):
+    return lax.dot_general(a, b, (((1,), (1,)), ((), ())), preferred_element_type=f32)
+
+
+def nn_dot(a, b):
+    return lax.dot_general(a, b, (((1,), (0,)), ((), ())), preferred_element_type=f32)
+
+
+class Gather:
+    COPIES = 13
+
+    def __init__(self, buf, send, recv, gx, gy):
+        rows = buf.shape[1]
+        half = rows // 2
+        a, b = pl.ds(0, half), pl.ds(half, half)
+        core, xn, yn = (slot_peer(r, gx, gy) for r in (1, 2, 3))
+
+        def make(i, src, dst, part, peer):
+            return remote(buf.at[src, part], buf.at[dst, part], send.at[i], recv.at[i], peer)
+
+        self.own = [
+            make(0, 0, 2, a, xn),
+            make(1, 0, 3, a, yn),
+            make(2, 0, 2, b, xn),
+            make(3, 0, 3, b, yn),
+            remote(buf.at[0], buf.at[1], send.at[4], recv.at[4], core),
+        ]
+        self.diagonal = [make(5, 3, 6, a, xn), make(6, 2, 6, b, yn)]
+        self.cross = [
+            make(7, 2, 4, a, core),
+            make(8, 2, 4, b, core),
+            make(9, 3, 5, a, core),
+            make(10, 3, 5, b, core),
+            make(11, 6, 7, a, core),
+            make(12, 6, 7, b, core),
+        ]
+
+    def start(self):
+        for c in self.own:
+            c.start()
+
+    def step(self, i):
+        if i == 1:
+            self.own[4].wait_recv()
+        elif i == 2:
+            self.own[1].wait_recv()
+            self.diagonal[0].start()
+            self.cross[2].start()
+            self.own[0].wait_recv()
+            self.cross[0].start()
+            self.own[2].wait_recv()
+            self.diagonal[1].start()
+            self.cross[1].start()
+        elif i == 3:
+            self.own[3].wait_recv()
+            self.cross[3].start()
+        elif i == 4:
+            self.cross[0].wait_recv()
+            self.cross[1].wait_recv()
+        elif i == 5:
+            self.cross[2].wait_recv()
+            self.cross[3].wait_recv()
+        elif i == 6:
+            self.diagonal[0].wait_recv()
+            self.cross[4].start()
+            self.diagonal[1].wait_recv()
+            self.cross[5].start()
+        elif i == 7:
+            self.cross[4].wait_recv()
+            self.cross[5].wait_recv()
+
+    def finish(self):
+        for c in self.own + self.diagonal + self.cross:
+            c.wait_send()
+
+
+def mlp_kernel(
+    mixed_ref, out_ref, x_ref, gain_ref, wgu_ref, wd_ref, y_ref,
+    middle_ref, second_ref, hidden_ref, grads_ref, yrel_ref,
+    mix_in, w_out, wgu, wd, buf, ybuf, hbuf, gbuf, mid, mine,
+    load_sem, y_sem, y_out_sem, out_sem, a2a_send, a2a_recv, ag_send, ag_recv,
+):
+    gx, gy = lax.axis_index("gx"), lax.axis_index("gy")
+    ngx, ngy = 4, 2
+    me = gx * ngy + gy
+    rows = x_ref.shape[0]
+    feat = x_ref.shape[1]
+    width = mixed_ref.shape[2]
+    units = wd_ref.shape[0]
+    tile = 256
+    peers = [slot_peer(r, gx, gy) for r in range(1, 8)]
+    entry_barrier(peers)
+    sends = []
+    for i, r in enumerate((6, 7, 2, 4, 3, 5, 1)):
+        px, py = slot_place(r, gx, gy)
+        sends.append(remote(mixed_ref.at[py * ngx + px], mix_in.at[me], a2a_send.at[r], a2a_recv.at[r], slot_peer(r, gx, gy)))
+        sends[-1].start()
+    loads = [
+        pltpu.make_async_copy(mixed_ref.at[gy * ngx + gx], mine, load_sem.at[0]),
+        pltpu.make_async_copy(out_ref, w_out, load_sem.at[1]),
+        pltpu.make_async_copy(wgu_ref, wgu, load_sem.at[2]),
+        pltpu.make_async_copy(wd_ref, wd, load_sem.at[3]),
+    ]
+    for c in loads:
+        c.start()
+
+    def y_load(r, n):
+        px, py = slot_place(r, gx, gy)
+        return [
+            pltpu.make_async_copy(y_ref.at[px * ngy + h, py], ybuf.at[r % 2, :, pl.ds(h * (feat // 2), feat // 2)], y_sem.at[r % 2, h])
+            for h in range(2)
+        ]
+
+    def y_store(r):
+        return pltpu.make_async_copy(ybuf.at[r % 2], yrel_ref.at[r], y_out_sem.at[r % 2])
+
+    for c in y_load(0, 0):
+        c.start()
+    loads[0].wait()
+    mix_in[me] = mine[...]
+    for c in sends:
+        c.wait_recv()
+    loads[1].wait()
+    for h in range(ngy):
+        cols = pl.ds(h * (feat // ngy), feat // ngy)
+        total = x_ref[:, cols].astype(f32)
+        for p in range(ngx):
+            left = jnp.concatenate([mix_in[p * 2], mix_in[p * 2 + 1]], axis=1)
+            total = total + nn_dot(left, w_out[p * 2 + h])
+        mid[:, cols] = total
+    middle = mid[...]
+    rate = lax.rsqrt(jnp.mean(middle * middle, axis=-1, keepdims=True) + EPS)
+    buf[0] = (middle * rate * gain_ref[...]).astype(bf)
+    gather = Gather(buf, ag_send, ag_recv, gx, gy)
+    gather.start()
+    middle_ref[...] = mid[...]
+    loads[2].wait()
+    loads[3].wait()
+
+    def outs(r):
+        return [
+            pltpu.make_async_copy(buf.at[r], second_ref.at[r], out_sem.at[0, r % 2]),
+            pltpu.make_async_copy(hbuf.at[r % 2], hidden_ref.at[r], out_sem.at[1, r % 2]),
+            pltpu.make_async_copy(gbuf.at[r % 2], grads_ref.at[r], out_sem.at[2, r % 2]),
+        ]
+
+    for r in range(8):
+        gather.step(r)
+        if r >= 2:
+            for c in outs(r - 2):
+                c.wait()
+        if r + 1 < 8:
+            if r >= 1:
+                y_store(r - 1).wait()
+            for c in y_load(r + 1, 0):
+                c.start()
+        for c in y_load(r, 0):
+            c.wait()
+        y_store(r).start()
+
+        def body(t, _):
+            cols = pl.ds(pl.multiple_of(t * tile, tile), tile)
+            up_cols = pl.ds(pl.multiple_of(units + t * tile, tile), tile)
+            gate = nn_dot(buf[r], wgu[:, cols])
+            up = nn_dot(buf[r], wgu[:, up_cols])
+            gh = nt_dot(ybuf[r % 2], wd[cols, :])
+            s = jax.nn.sigmoid(gate)
+            act = gate * s
+            hbuf[r % 2, :, cols] = (act * up).astype(bf)
+            gbuf[r % 2, :, up_cols] = (gh * act).astype(bf)
+            gbuf[r % 2, :, cols] = (gh * up * s * (1.0 + gate * (1.0 - s))).astype(bf)
+            return 0
+
+        lax.fori_loop(0, units // tile, body, 0)
+        for c in outs(r):
+            c.start()
+    for r in (6, 7):
+        for c in outs(r):
+            c.wait()
+        y_store(r).wait()
+    gather.finish()
+    for c in sends:
+        c.wait_send()
+
+
+def mlp_forward(mixed, out_all, x_own, gain, gate_up, down, y_all, collective):
+    rows, feat = x_own.shape
+    width = mixed.shape[2]
+    units = down.shape[0]
+    sd = jax.ShapeDtypeStruct
+    return pl.pallas_call(
+        mlp_kernel,
+        in_specs=[ANY, ANY, VM, VM, ANY, ANY, ANY],
+        out_specs=[VM, ANY, ANY, ANY, ANY],
+        out_shape=[
+            sd((rows, feat), f32),
+            sd((8, rows, feat), bf),
+            sd((8, rows, units), bf),
+            sd((8, rows, 2 * units), bf),
+            sd((8, rows, feat), bf),
+        ],
+        scratch_shapes=[
+            pltpu.VMEM((8, rows, width), bf),
+            pltpu.VMEM(out_all.shape, bf),
+            pltpu.VMEM(gate_up.shape, bf),
+            pltpu.VMEM(down.shape, bf),
+            pltpu.VMEM((8, rows, feat), bf),
+            pltpu.VMEM((2, rows, feat), bf),
+            pltpu.VMEM((2, rows, units), bf),
+            pltpu.VMEM((2, rows, 2 * units), bf),
+            pltpu.VMEM((rows, feat), f32),
+            pltpu.VMEM((rows, width), bf),
+            pltpu.SemaphoreType.DMA((4,)),
+            pltpu.SemaphoreType.DMA((2, 2)),
+            pltpu.SemaphoreType.DMA((2,)),
+            pltpu.SemaphoreType.DMA((3, 2)),
+            pltpu.SemaphoreType.DMA((8,)),
+            pltpu.SemaphoreType.DMA((8,)),
+            pltpu.SemaphoreType.DMA((13,)),
+            pltpu.SemaphoreType.DMA((13,)),
+        ],
+        compiler_params=pltpu.CompilerParams(collective_id=collective, has_side_effects=True, vmem_limit_bytes=62 << 20),
+        name="mlp_forward",
+    )(mixed, out_all, x_own, gain, gate_up, down, y_all)
+
+
+class Scatter:
+    def __init__(self, give, take, acc, diag_in, last_in, s_core, r_core, s_link, r_link, gx, gy):
+        self.give, self.take, self.acc, self.diag_in, self.last_in = give, take, acc, diag_in, last_in
+        core, xn, yn = (slot_peer(r, gx, gy) for r in (1, 2, 3))
+        rows = acc.shape[1]
+        half = rows // 2
+        a, b = pl.ds(0, half), pl.ds(half, half)
+        self.a, self.b = a, b
+        self.core = [remote(give.at[n], take.at[n], s_core.at[n], r_core.at[n], core) for n in range(4)]
+
+        def link(i, src, dst, peer):
+            return remote(src, dst, s_link.at[i], r_link.at[i], peer)
+
+        self.link = [
+            link(0, acc.at[0, a], diag_in.at[0], xn),
+            link(1, acc.at[0, b], diag_in.at[1], yn),
+            link(2, acc.at[1, a], last_in.at[0, a], xn),
+            link(3, acc.at[2, b], last_in.at[1, b], yn),
+            link(4, acc.at[1, b], last_in.at[0, b], xn),
+            link(5, acc.at[2, a], last_in.at[1, a], yn),
+        ]
+
+    def run(self, product, self_acc):
+        acc = self.acc
+
+        def give_out(n, slot):
+            def put(cols, value):
+                self.give[n, :, cols] = value.astype(bf)
+
+            product(slot, put)
+            self.core[n].start()
+
+        def keep(n, slot):
+            def put(cols, value):
+                acc[n, :, cols] = value.astype(bf)
+
+            product(slot, put)
+
+        def join(n):
+            self.core[n].wait_recv()
+            acc[n] = (acc[n].astype(f32) + self.take[n].astype(f32)).astype(bf)
+
+        a, b = self.a, self.b
+        give_out(0, 7)
+        keep(0, 6)
+        give_out(1, 4)
+        join(0)
+        self.link[0].start()
+        self.link[1].start()
+        give_out(2, 5)
+        keep(1, 2)
+        join(1)
+        self.link[2].start()
+        keep(2, 3)
+        join(2)
+        self.link[3].start()
+        give_out(3, 1)
+
+        def put_self(cols, value):
+            self_acc[:, cols] = value
+
+        product(0, put_self)
+        self.link[1].wait_recv()
+        acc[1, b] = (acc[1, b].astype(f32) + self.diag_in[1].astype(f32)).astype(bf)
+        self.link[4].start()
+        self.link[0].wait_recv()
+        acc[2, a] = (acc[2, a].astype(f32) + self.diag_in[0].astype(f32)).astype(bf)
+        self.link[5].start()
+        self.core[3].wait_recv()
+        self_acc[...] += self.take[3].astype(f32)
+        for c in self.link[2:]:
+            c.wait_recv()
+        self_acc[...] += self.last_in[0].astype(f32) + self.last_in[1].astype(f32)
+
+    def finish(self):
+        for c in self.core + self.link:
+            c.wait_send()
+
+
+def scatter_scratch(rows, feat):
+    return [
+        pltpu.VMEM((4, rows, feat), bf),
+        pltpu.VMEM((4, rows, feat), bf),
+        pltpu.VMEM((3, rows, feat), bf),
+        pltpu.VMEM((2, rows // 2, feat), bf),
+        pltpu.VMEM((2, rows, feat), bf),
+        pltpu.SemaphoreType.DMA((4,)),
+        pltpu.SemaphoreType.DMA((4,)),
+        pltpu.SemaphoreType.DMA((6,)),
+        pltpu.SemaphoreType.DMA((6,)),
+    ]
+
+
+def back_kernel(
+    grads_ref, wgu_ref, out_ref, middle_ref, y_ref, gain_ref,
+    gm_ref, gmix_ref, dgain_ref,
+    give, take, acc, diag_in, last_in, s_core, r_core, s_link, r_link,
+    lhs, wgu, w_out, total, mid_low, gsend, load_sem, lhs_sem, a2a_send, a2a_recv, keep_sem,
+):
+    gx, gy = lax.axis_index("gx"), lax.axis_index("gy")
+    ngx, ngy = 4, 2
+    rows, feat = middle_ref.shape
+    width = gmix_ref.shape[2]
+    tile = 512
+    order = (7, 6, 4, 5, 2, 3, 1, 0)
+    loads = [pltpu.make_async_copy(wgu_ref, wgu, load_sem.at[0])]
+    pulls = {r: pltpu.make_async_copy(grads_ref.at[r], lhs.at[r], lhs_sem.at[r]) for r in order}
+    pulls[7].start()
+    loads[0].start()
+    for r in order[1:]:
+        pulls[r].start()
+    loads.append(pltpu.make_async_copy(out_ref, w_out, load_sem.at[1]))
+    loads[1].start()
+    entry_barrier([slot_peer(r, gx, gy) for r in range(1, 8)])
+    loads[0].wait()
+
+    def product(slot, put):
+        pulls[slot].wait()
+
+        def body(t, _):
+            cols = pl.ds(pl.multiple_of(t * tile, tile), tile)
+            put(cols, nt_dot(lhs[slot], wgu[cols, :]))
+            return 0
+
+        lax.fori_loop(0, feat // tile, body, 0)
+
+    scatter = Scatter(give, take, acc, diag_in, last_in, s_core, r_core, s_link, r_link, gx, gy)
+    scatter.run(product, total)
+    middle = middle_ref[...]
+    incoming = total[...]
+    rate = lax.rsqrt(jnp.mean(middle * middle, axis=-1, keepdims=True) + EPS)
+    scaled = gain_ref[...] * incoming
+    inner = jnp.mean(middle * scaled, axis=-1, keepdims=True)
+    dgain_ref[...] = jnp.sum((incoming * middle * rate).reshape(rows // 8, 8, feat), axis=0)
+    gm = y_ref[...].astype(f32) + rate * scaled - middle * (rate * rate * rate) * inner
+    mid_low[...] = gm.astype(bf)
+    gm_ref[...] = mid_low[...]
+    loads[1].wait()
+    v = gy * ngx + gx
+    sends = []
+    for r in (6, 7, 2, 4, 3, 5, 1, 0):
+        px, py = slot_place(r, gx, gy)
+        rows_w = pl.ds(pl.multiple_of(py * width, width), width)
+        part = nt_dot(mid_low[:, : feat // 2], w_out[px * 2, rows_w, :]) + nt_dot(mid_low[:, feat // 2 :], w_out[px * 2 + 1, rows_w, :])
+        gsend[r] = part.astype(bf)
+        if r == 0:
+            keep = pltpu.make_async_copy(gsend.at[0], gmix_ref.at[v], keep_sem)
+            keep.start()
+        else:
+            c = remote(gsend.at[r], gmix_ref.at[v], a2a_send.at[r], a2a_recv.at[r], slot_peer(r, gx, gy))
+            c.start()
+            sends.append(c)
+    keep.wait()
+    for c in sends:
+        c.wait_recv()
+    for c in sends:
+        c.wait_send()
+    scatter.finish()
+
+
+def mlp_backward(grads, gate_up, out_all, middle, y_own, gain, width, collective):
+    rows, feat = middle.shape
+    sd = jax.ShapeDtypeStruct
+    return pl.pallas_call(
+        back_kernel,
+        in_specs=[ANY, ANY, ANY, VM, VM, VM],
+        out_specs=[VM, ANY, VM],
+        out_shape=[sd((rows, feat), bf), sd((8, rows, width), bf), sd((8, feat), f32)],
+        scratch_shapes=scatter_scratch(rows, feat)
+        + [
+            pltpu.VMEM(grads.shape, bf),
+            pltpu.VMEM(gate_up.shape, bf),
+            pltpu.VMEM(out_all.shape, bf),
+            pltpu.VMEM((rows, feat), f32),
+            pltpu.VMEM((rows, feat), bf),
+            pltpu.VMEM((8, rows, width), bf),
+            pltpu.SemaphoreType.DMA((2,)),
+            pltpu.SemaphoreType.DMA((8,)),
+            pltpu.SemaphoreType.DMA((8,)),
+            pltpu.SemaphoreType.DMA((8,)),
+            pltpu.SemaphoreType.DMA,
+        ],
+        compiler_params=pltpu.CompilerParams(collective_id=collective, has_side_effects=True, vmem_limit_bytes=63 << 20),
+        name="mlp_backward",
+    )(grads, gate_up, out_all, middle, y_own, gain)
+
+
+def scatter_kernel(lhs_ref, w_ref, out_ref, give, take, acc, diag_in, last_in, s_core, r_core, s_link, r_link, lhs, w, total, load_sem, lhs_sem, *, slots, transposed):
+    gx, gy = lax.axis_index("gx"), lax.axis_index("gy")
+    rows, feat = out_ref.shape
+    tile = 512
+    load = pltpu.make_async_copy(w_ref, w, load_sem)
+
+    def source(r):
+        if slots:
+            return lhs_ref.at[r]
+        px, py = slot_place(r, gx, gy)
+        return lhs_ref.at[py * 4 + px]
+
+    order = (7, 6, 4, 5, 2, 3, 1, 0)
+    pulls = {r: pltpu.make_async_copy(source(r), lhs.at[r], lhs_sem.at[r]) for r in order}
+    pulls[7].start()
+    load.start()
+    for r in order[1:]:
+        pulls[r].start()
+    entry_barrier([slot_peer(r, gx, gy) for r in (1, 2, 3)])
+    load.wait()
+
+    def product(slot, put):
+        pulls[slot].wait()
+
+        def body(t, _):
+            cols = pl.ds(pl.multiple_of(t * tile, tile), tile)
+            put(cols, nn_dot(lhs[slot], w[:, cols]) if transposed else nt_dot(lhs[slot], w[cols, :]))
+            return 0
+
+        lax.fori_loop(0, feat // tile, body, 0)
+
+    scatter = Scatter(give, take, acc, diag_in, last_in, s_core, r_core, s_link, r_link, gx, gy)
+    scatter.run(product, total)
+    out_ref[...] = total[...]
+    scatter.finish()
+
+
+def product_scatter(lhs, w, collective, slots, transposed):
+    _, rows, depth = lhs.shape
+    feat = w.shape[1] if transposed else w.shape[0]
+    return pl.pallas_call(
+        functools.partial(scatter_kernel, slots=slots, transposed=transposed),
+        in_specs=[ANY, ANY],
+        out_specs=VM,
+        out_shape=jax.ShapeDtypeStruct((rows, feat), f32),
+        scratch_shapes=scatter_scratch(rows, feat)
+        + [
+            pltpu.VMEM(lhs.shape, bf),
+            pltpu.VMEM(w.shape, bf),
+            pltpu.VMEM((rows, feat), f32),
+            pltpu.SemaphoreType.DMA,
+            pltpu.SemaphoreType.DMA((8,)),
+        ],
+        compiler_params=pltpu.CompilerParams(collective_id=collective, has_side_effects=True, vmem_limit_bytes=60 << 20),
+        name="product_scatter",
+    )(lhs, w)
+
+
 TOKENS = ("gy", "gx")
-EVERY = ("dp", "gx", "gy")
 
 
 def dot(a, b):
@@ -364,14 +864,6 @@
     return many.transpose(2, 0, 3, 1, 4).reshape(nb, ngx * rows, ngy * width)
 
 
-def gather_rows(value):
-    return lax.all_gather(value, TOKENS, axis=0, tiled=True)
-
-
-def scatter_rows(value):
-    return lax.psum_scatter(value.astype(bf), TOKENS, scatter_dimension=0, tiled=True).astype(f32)
-
-
 def to_final(own):
     mine, other = halves(own, 1)
     return in_order(mine[None], swap(other)[None], 0)
@@ -381,22 +873,38 @@
     return lax.rsqrt(jnp.mean(value * value, axis=-1, keepdims=True) + EPS)
 
 
-def norm_back(value, rate, gain, incoming):
-    scaled = gain * incoming
-    inner = jnp.mean(value * scaled, axis=-1, keepdims=True)
-    return rate * scaled - value * (rate * rate * rate) * inner, jnp.sum(incoming * value * rate, axis=0)
-
-
 def scatter_dp(value):
     return lax.psum_scatter(value.astype(bf), "dp", scatter_dimension=0, tiled=True)
 
 
-def columns_grad(grad, ndp):
+def rows_to_dp(grad, ndp):
     rows, cols = grad.shape
     parts = grad.astype(bf).reshape(2, ndp, rows // (2 * ndp), cols).transpose(1, 0, 2, 3)
-    summed = lax.psum_scatter(parts.reshape(rows, cols), "dp", scatter_dimension=0, tiled=True)
+    summed = scatter_dp(parts.reshape(rows, cols))
     mine, other = halves(summed, 0)
     return mine, swap(other)
+
+
+def sum_axis(value, axis):
+    size = lax.axis_size(axis)
+    step = 1
+    while step < size:
+        value = value + lax.ppermute(value, axis, [(i, i ^ step) for i in range(size)])
+        step *= 2
+    return value
+
+
+def spread(value, ndp):
+    part = value.shape[0] // ndp
+    dp = lax.axis_index("dp")
+    piece = swap(lax.dynamic_slice_in_dim(value, dp * part, part, 0))
+    if ndp & (ndp - 1) or ndp > 4:
+        return lax.all_gather(piece, "dp", axis=0, tiled=True)
+    out = lax.dynamic_update_slice_in_dim(jnp.zeros(value.shape, value.dtype), piece, dp * part, 0)
+    for step in range(1, ndp):
+        got = lax.ppermute(piece, "dp", [(i, i ^ step) for i in range(ndp)])
+        out = lax.dynamic_update_slice_in_dim(out, got, (dp ^ step) * part, 0)
+    return out
 
 
 def shards(
@@ -436,9 +944,22 @@
         0,
     )
 
-    def own_columns(w):
-        mine, other = halves(w, 1)
-        return in_order(mine, swap(other), 0)
+    block = w_gate.shape[1]
+    units = -(-block // (ngy * 256)) * 256
+    unit_mine, unit_other = gy * (block - units), (1 - gy) * (block - units)
+
+    def pick(w, start, axis):
+        return lax.dynamic_slice_in_dim(w, start, units, axis)
+
+    fresh_unit = (lax.broadcasted_iota(jnp.int32, (1, units), 1) >= gy * (2 * units - block)).astype(bf)
+    gate_up = in_order(
+        jnp.concatenate([pick(w_gate, unit_mine, 1), pick(w_up, unit_mine, 1)], axis=1),
+        spread(jnp.concatenate([pick(w_gate, unit_other, 1), pick(w_up, unit_other, 1)], axis=1), ndp),
+        0,
+    ) * jnp.concatenate([fresh_unit, fresh_unit], axis=1)
+    down_w = in_order(pick(w_down, unit_mine, 0), spread(pick(w_down, unit_other, 0), ndp), 1)
+    out_all = lax.all_gather(w_out, ("gx", "gy"), axis=0, tiled=False)
+    y_all = lax.all_gather(grad_y, ("gx", "gy"), axis=0, tiled=False)
 
     aux, segrow = make_aux(segments)
     x_flat = x_all.reshape(tokens, feat)
@@ -450,61 +971,48 @@
     conv_local = lax.dynamic_slice_in_dim(conv_kernel, conv_start, width, 2)
     gain_row = head_gain[None]
     mixed, *saved = mixer_fwd(raw, aux, segrow, conv_local, gain_row)
-    mixed = mixed.reshape(tokens, width)
-
-    out_blocks = lax.all_gather(w_out, ("gx", "gy"), axis=0, tiled=False)
-    out_full = (
-        out_blocks.reshape(ngx, ngy, ngy, width, -1).transpose(2, 0, 3, 1, 4).reshape(ngx * ngy * width, feat)
+    x_own = lax.dynamic_slice_in_dim(x_flat, own_start, own_rows, 0)
+    middle, second, hidden, grads, y_rel = mlp_forward(
+        mixed.reshape(8, own_rows, width), out_all, x_own, mlp_gain[None], gate_up, down_w, y_all, 1
     )
-    y_all = gather_blocks(grad_y).reshape(tokens, feat)
-    gate_w = own_columns(w_gate)
-    up_w = own_columns(w_up)
-    down_mine, down_other = halves(w_down, 0)
-    down_w = in_order(down_mine, swap(down_other), 1)
-
-    mixed_own = lax.all_to_all(mixed, TOKENS, 0, 1, tiled=True)
-    x_own = lax.dynamic_slice_in_dim(x_flat, own_start, own_rows, 0).astype(f32)
-    middle = x_own + dot(mixed_own, out_full)
-    rate_second = rate_of(middle)
-    second = gather_rows((middle * rate_second * mlp_gain).astype(bf))
-    gate_val = dot(second, gate_w)
-    up_val = dot(second, up_w)
-    grad_hidden = dot_t(y_all, down_w)
-    sig = jax.nn.sigmoid(gate_val)
-    act = gate_val * sig
-    hidden = (act * up_val).astype(bf)
-    grad_up_val = (grad_hidden * act).astype(bf)
-    grad_gate_val = (grad_hidden * up_val * sig * (1.0 + gate_val * (1.0 - sig))).astype(bf)
-    grad_second = scatter_rows(dot_t(grad_gate_val, gate_w) + dot_t(grad_up_val, up_w))
-    norm_two, mlp_gain_grad = norm_back(middle, rate_second, mlp_gain, grad_second)
-    y_own = lax.dynamic_slice_in_dim(y_all, own_start, own_rows, 0).astype(f32)
-    grad_middle = y_own + norm_two
-    mid_low = grad_middle.astype(bf)
-    grad_mixed = lax.all_to_all(dot_t(mid_low, out_full).astype(bf), TOKENS, 1, 0, tiled=True)
+    second_flat, hidden_flat = second.reshape(tokens, feat), hidden.reshape(tokens, units)
+    grads_flat, y_flat = grads.reshape(tokens, 2 * units), y_rel.reshape(tokens, feat)
+    down_keep, down_send = halves(dot_w(hidden_flat, y_flat).astype(bf), 1)
+    down_both = jnp.stack([down_keep, swap(down_send)])
+    first, last = down_both[gy], down_both[1 - gy]
+    down_rows = jnp.concatenate([first, last[2 * units - block :]], axis=0)
+    sum_down = scatter_dp(down_rows).astype(f32)
+    grad_gu_mine, grad_gu_other = rows_to_dp(dot_w(second_flat, grads_flat), ndp)
+
+    mid_low, grad_mixed, mlp_gain_parts = mlp_backward(
+        grads, gate_up, out_all, middle, y_rel[0], mlp_gain[None], width, 2
+    )
     draw, conv_grad, gain_grad = mixer_bwd(
         raw, aux, segrow, conv_local, gain_row, saved, grad_mixed.reshape(nb, length, width)
     )
     draw = draw.reshape(tokens, -1)
-    grad_normed = scatter_rows(dot_t(draw, head_w))
-    rate_own = lax.dynamic_slice_in_dim(rate_first, own_start, own_rows, 0)
-    norm_one, norm_gain_grad = norm_back(x_own, rate_own, norm_gain, grad_normed)
-    grad_inputs = to_final((grad_middle + norm_one).astype(bf))
-
-    layer_out = to_final((middle + scatter_rows(dot(hidden, down_w))).astype(bf))
-    mid_all = gather_rows(mid_low)
-
-    down_keep, down_send = halves(dot_w(hidden, y_all).astype(bf), 1)
-    sum_down = scatter_dp(in_order(down_keep, swap(down_send), 0)).astype(f32)
-    out_keep, out_send = halves(dot_w(mixed, mid_all).astype(bf), 1)
+    grad_head_w = dot_w(normed, draw)
+    norm_gain_grad = jnp.sum(grad_head_w * head_w.astype(f32), axis=1) / norm_gain
+    head_mine, head_other = rows_to_dp(grad_head_w, ndp)
+    mid_all = lax.all_gather(mid_low, TOKENS, axis=0, tiled=True)
+    grad_normed = product_scatter(draw.reshape(8, own_rows, -1), head_w, 3, False, False)
+    x_wide_own = x_own.astype(f32)
+    rate_own = rate_of(x_wide_own)
+    scaled = norm_gain * grad_normed
+    inner = jnp.mean(x_wide_own * scaled, axis=-1, keepdims=True)
+    norm_one = rate_own * scaled - x_wide_own * (rate_own * rate_own * rate_own) * inner
+    grad_inputs = to_final((mid_low.astype(f32) + norm_one).astype(bf))
+    layer_out = to_final((middle + product_scatter(hidden, down_w, 4, True, True)).astype(bf))
+
+    out_keep, out_send = halves(dot_w(mixed.reshape(tokens, width), mid_all).astype(bf), 1)
     sum_out = scatter_dp(in_order(out_keep, swap(out_send), 0)).astype(f32)
 
-    def whole_columns(grad):
-        mine, other = columns_grad(grad, ndp)
-        return in_order(mine, other, 1).astype(f32)
-
-    sum_gate = whole_columns(dot_w(second, grad_gate_val))
-    sum_up = whole_columns(dot_w(second, grad_up_val))
-    head_mine, head_other = columns_grad(dot_w(normed, draw), ndp)
+    def unit_columns(i):
+        part = slice(i * units, (i + 1) * units)
+        both = jnp.stack([grad_gu_mine[:, part], grad_gu_other[:, part]])
+        return jnp.concatenate([both[gy], both[1 - gy][:, 2 * units - block :]], axis=1).astype(f32)
+
+    sum_gate, sum_up = unit_columns(0), unit_columns(1)
 
     def head_part(i, n):
         return in_order(head_mine[:, i : i + n], head_other[:, i : i + n], 1).astype(f32)
@@ -512,8 +1020,16 @@
     sum_query, sum_key, sum_value, sum_head_gate = (head_part(i * width, width) for i in range(4))
     sum_beta = head_part(4 * width, heads)
 
-    conv_full = lax.dynamic_update_slice_in_dim(jnp.zeros(conv_kernel.shape, f32), conv_grad, conv_start, 2)
-    norm_sum, mlp_sum, conv_sum, gain_sum = lax.psum((norm_gain_grad, mlp_gain_grad, conv_full, gain_grad), EVERY)
+    small = jnp.concatenate([conv_grad.reshape(-1), norm_gain_grad, jnp.sum(mlp_gain_parts, axis=0), gain_grad])
+    small = sum_axis(small, "dp")
+    n_conv = conv_grad.size
+    conv_full = lax.dynamic_update_slice_in_dim(
+        jnp.zeros(conv_kernel.shape, f32), small[:n_conv].reshape(conv_grad.shape), conv_start, 2
+    )
+    small = sum_axis(sum_axis(jnp.concatenate([conv_full.reshape(-1), small[n_conv:]]), "gx"), "gy")
+    n_conv = conv_full.size
+    conv_sum = small[:n_conv].reshape(conv_kernel.shape)
+    norm_sum, mlp_sum, gain_sum = jnp.split(small[n_conv:], [feat, 2 * feat])
     return (
         layer_out,
         grad_inputs,

time: 1240 us -> 1010 us (0.81)
  Pallas kernels: 89.4 us -> 335 us
  waiting for transfers between devices: 528 us -> 308 us
  matrix products: 173 us -> 68.7 us
  local copies, waits for them, and re-layouts: 221 us -> 135 us
  blocking collectives: 48.2 us -> 0 us
  other arithmetic: 129 us -> 106 us
  starting transfers between devices: 24.8 us -> 39.6 us
    pallas_call x0 -> x4, Pallas kernels: none -> 246 us  [the longest x2 115 us: product_scatter(): pl.pallas_call(functools.partial(scatter_kernel, slots=slots, transposed=...]
    reduce_scatter x6 -> x0, waiting for transfers between devices: 211 us -> none  [the longest x3 211 us: scatter_rows(): lax.psum_scatter(value.astype(bf), TOKENS, scatter_dimension=0, tiled=True)]
    psum x1 -> x0, waiting for transfers between devices: 83.4 us -> none  [shards(): lax.psum((norm_gain_grad, mlp_gain_grad, conv_full, gain_grad), EVERY)]
    reduce_scatter x2 -> x4, waiting for transfers between devices: 16.3 us -> 78 us  [scatter_dp(): lax.psum_scatter(value.astype(bf), 'dp', scatter_dimension=0, tiled=True)]
    dot_general x5 -> x0, matrix products: 58.8 us -> none  [dot_t(): lax.dot_general(a, b, (((1,), (1,)), ((), ())), preferred_element_type=f32)]
    ppermute x0 -> x11, waiting for transfers between devices: none -> 57.5 us  [the longest x6 46.2 us: spread(): got = lax.ppermute(piece, 'dp', [(i, i ^ step) for i in range(ndp)])]
    psum x1 -> x0, blocking collectives: 48.2 us -> none  [shards(): lax.psum((norm_gain_grad, mlp_gain_grad, conv_full, gain_grad), EVERY)]
    ppermute x11 -> x9, waiting for transfers between devices: 215 us -> 170 us  [swap(): return lax.ppermute(value, 'gy', [(0, 1), (1, 0)])]
  transfers between devices with their start and end apart: 27 -> 28, of which waited for: 13 -> 12; matrix products, arithmetic and copies ran while one was open for 38% -> 23% of each run, Pallas kernels for 7% -> 15%
where the time goes in v2:
time: 1010 us
  Pallas kernels  335 us (33%)
  waiting for transfers between devices  308 us (30%)
  local copies, waits for them, and re-layouts  135 us (13%)
  other arithmetic  106 us (10%)
  matrix products  68.7 us (7%)
  starting transfers between devices  39.6 us (4%)
  between operations  15.2 us (2%)
    ppermute x9, waiting for transfers between devices, swap(): return lax.ppermute(value, 'gy', [(0, 1), (1, 0)])  170 us
    pallas_call x2, Pallas kernels, product_scatter(): pl.pallas_call(functools.partial(scatter_kernel, slots=slots, transposed=...  115 us
    reduce_scatter x4, waiting for transfers between devices, scatter_dp(): lax.psum_scatter(value.astype(bf), 'dp', scatter_dimension=0, tiled=True)  78 us
    pallas_call x1, Pallas kernels, mlp_forward(): pl.pallas_call(mlp_kernel, in_specs=[ANY, ANY, VM, VM, ANY, ANY, ANY], ou...  66 us
    pallas_call x1, Pallas kernels, mlp_backward(): pl.pallas_call(back_kernel, in_specs=[ANY, ANY, ANY, VM, VM, VM], out_spe...  65 us
    pallas_call x1, Pallas kernels, mixer_bwd(): pl.pallas_call(bwd_kernel, grid=(nb, heads), in_specs=specs(length, heads...  56.5 us
    dot_general x4, matrix products, dot_w(): lax.dot_general(a, b, (((0,), (0,)), ((), ())), preferred_element_type=f32)  51.1 us
    ppermute x6, waiting for transfers between devices, spread(): got = lax.ppermute(piece, 'dp', [(i, i ^ step) for i in range(ndp)])  46.2 us
  transfers between devices with their start and end apart: 28, of which 12 were waited for; matrix products, arithmetic and copies ran while one was open for 23% of the time, Pallas kernels for 15%

profile of v2, /device:TPU:0, one launch (start us, length us, event | category | flops | bytes accessed | tf_op | source)
XLA Modules:
  0.0 1007.4 jit_solution(3320085195011803634)
XLA Ops:
  9.5 3.2 constant_dynamic-slice_fusion.9
  13.7 2.9 collective-permute-start.1
  17.5 2.5 dynamic-slice_dynamic-update-slice_fusion.7
  19.9 2.4 dynamic-slice_dynamic-update-slice_fusion.6
  25.3 1.8 constant_dynamic-slice_fusion.6
  27.2 2.0 collective-permute-start.5
  31.9 106.5 %collective-permute-done.5 = bf16[192,1024]{1,0:T(8,128)(2,1)} collective-permute-done((bf16[192,1024]{1,0:T(8,128)(2,1)}, bf16[192,1024]{1,0:T(8,128)(2,1)}, u32[]{:S(2)}, u32[]{:S(2)}) %collective-permute-start.5) | collective-permute-done | bytes 393248 | tf_op jit(solution)/shard_map/ppermute | solution.py:842
  138.4 1.8 collective-permute-start.6
  141.1 2.6 collective-permute-start.7
  147.6 2.0 copy.101
  152.3 1.4 copy.104
  161.0 9.3 stack.90.aux_ref
  172.5 3.4 collective-permute-start.3
  181.7 2.0 pad_maximum_fusion.2.wd_ref.w_ref
  183.7 20.5 %collective-permute-done.2 = bf16[256,1536]{1,0:T(8,128)(2,1)S(1)} collective-permute-done((bf16[256,1536]{1,0:T(8,128)(2,1)}, bf16[256,1536]{1,0:T(8,128)(2,1)S(1)}, u32[]{:S(2)}, u32[]{:S(2)}) %collective-permute-start.2) | collective-permute-done | bytes 786464 | tf_op jit(solution)/shard_map/ppermute | solution.py:905
  204.3 25.6 %collective-permute-done.3 = bf16[256,1536]{1,0:T(8,128)(2,1)S(1)} collective-permute-done((bf16[256,1536]{1,0:T(8,128)(2,1)}, bf16[256,1536]{1,0:T(8,128)(2,1)S(1)}, u32[]{:S(2)}, u32[]{:S(2)}) %collective-permute-start.3) | collective-permute-done | bytes 786464 | tf_op jit(solution)/shard_map/ppermute | solution.py:905
  231.3 3.7 maximum_multiply_fusion.wgu_ref
  235.0 4.2 broadcast_select_fusion.3
  239.2 18.4 %fusion.36 = (bf16[4,2,2,256,1024]{4,1,3,0,2:T(2,128)(2,1)}, f32[2,4,256,2,1024]{4,3,2,1,0:T(2,128)}) fusion(bf16[4,2,2,256,1024]{4,3,2,1,0:T(8,128)(2,1)} %bitcast.123), kind=kLoop, calls=%fused_computation.167 | loop fusion | flops 4194304 | bytes 33554432 | tf_op jit(solution)/shard_map/reshape | solution.py:863
  257.6 22.1 %reshape.184 = f32[2,1024,2048]{2,1,0:T(8,128)} reshape(f32[2,4,256,2,1024]{4,3,2,1,0:T(2,128)} %get-tuple-element.118) | data formatting | bytes 33554432 | tf_op jit(solution)/shard_map/convert_element_type | solution.py:966
  279.7 22.0 %multiply_reduce_fusion = f32[2,4,256]{2,1,0:T(4,128)S(1)} fusion(bf16[4,2,2,256,1024]{4,3,2,1,0:T(8,128)(2,1)} %bitcast.124), kind=kLoop, calls=%fused_computation.2 | loop fusion | flops 12580864 | bytes 8396800 | tf_op jit(solution)/shard_map/reduce_sum | solution.py:873
  301.8 10.3 %copy.126 = bf16[256,8,2,1024]{3,1,2,0:T(8,128)(2,1)} copy(bf16[256,8,2,1024]{3,2,1,0:T(2,128)(2,1)} %bitcast.129) | data formatting | bytes 16777216
  312.1 17.5 %fusion.q_ref.k_ref.v_ref.g_ref.b_ref = f32[2,1024,1152]{2,1,0:T(8,128)} fusion(f32[2,1024,2048]{2,1,0:T(8,128)} %reshape.184, f32[2048]{0:T(1024)S(1)} %copy-done.23, f32[2,1024]{1,0:T(2,128)S(1)} %bitcast.154, bf16[1024,1152]{1,0:T(8,128)(2,1)S(1)} %copy-done.6, bf16[1024,1152]{1,0:T(8,128)(2,1)S(1)} %get-tuple-element.121), kind=kOutput, calls=%fused_computation.5 | convolution fusion | flops 9685696512 | bytes 30949376 | tf_op jit(solution)/shard_map/dot_general | solution.py:830
  329.6 32.3 %mixer_forward.1 = (bf16[2,1024,256]{2,1,0:T(8,128)(2,1)}, bf16[2,2,1024,128]{3,2,1,0:T(8,128)(2,1)}, bf16[2,2,1024,128]{3,2,1,0:T(8,128)(2,1)}, bf16[2,2,1024,1...) custom-call(f32[2,1024,1152]{2,1,0:T(8,128)} %fusion.q_ref.k_ref.v_r, ...), custom_call_target="tpu_custom_call" | custom-call | tf_op jit(solution)/shard_map/mixer_forward/pallas_call | solution.py:140
  361.9 2.4 constant_dynamic-slice_fusion.11.x_ref
  364.3 66.0 %mlp_forward.1 = (f32[256,2048]{1,0:T(8,128)}, bf16[8,256,2048]{2,1,0:T(8,128)(2,1)}, bf16[8,256,768]{2,1,0:T(8,128)(2,1)}, bf16[8,256,1536]{2,1,0:T(8,128)(2,1)}, bf16[8,256,2048]{2,1,0:T(8,128)(2,1)}) custom-call(bf16[8,256,256]{2,1,0:T(8,128)(2,1)} %bitcast.136, bf16[8,512,1024]{2,1,0:T(8,128)(2,1)} %bitcast.127, ...), custom_call_target="tpu_custom_call" | custom-call | tf_op jit(solution)/shard_map/mlp_forward/pallas_call | solution.py:545
  430.3 2.3 slice_bitcast_fusion.y_ref
  432.6 17.0 %multiply_convert_fusion = bf16[2,4,256,2,1024]{4,3,2,1,0:T(2,128)(2,1)} fusion(f32[2,1024]{1,0:T(2,128)S(1)} %mul.229, f32[2,4,256]{2,1,0:T(4,128)S(1)} %get-tuple-element.165, bf16[4,2,2,256,1024]{4,3,2,1,0:T(8,128)(2,1)} %bitcast.125), kind=kLoop, calls=%fused_computation | loop fusion | flops 16777216 | bytes 16793600 | tf_op jit(solution)/shard_map/convert_element_type | solution.py:968
  449.5 10.2 %copy.127 = bf16[256,8,2,1024]{3,1,2,0:T(8,128)(2,1)} copy(bf16[256,8,2,1024]{3,2,1,0:T(2,128)(2,1)} %bitcast.126) | data formatting | bytes 16777216
  459.7 65.0 %mlp_backward.1 = (bf16[256,2048]{1,0:T(8,128)(2,1)}, bf16[8,256,256]{2,1,0:T(8,128)(2,1)}, f32[8,2048]{1,0:T(8,128)}) custom-call(bf16[8,256,1536]{2,1,0:T(8,128)(2,1)} %get-tuple-element.37.grads_ref, bf16[2048,1536]{1,0:T(8,128)(2,1)} %maximum_multiply_fusion.wgu_ref, bf16[8,512,1024]{2,1,0:T(8,128)(2,1)} %bitcast.128, ...), custom_call_target="tpu_custom_call" | custom-call | tf_op jit(solution)/shard_map/mlp_backward/pallas_call | solution.py:744
  524.8 56.5 %mixer_backward.1 = (bf16[2,1024,1152]{2,1,0:T(8,128)(2,1)}, f32[2,2,12,8,128]{4,3,2,1,0:T(8,128)}, f32[2,2,8,128]{3,2,1,0:T(8,128)}) custom-call(f32[2,1024,1152]{2,1,0:T(8,128)} %fusion.q_ref.k_ref.v_ref.g_ref.b_ref, f32[2,1024,1152]{2,1,0:T(8,128)} %fusion.q_ref.k_ref.v_ref.g_ref.b_ref, f32[2,1024,1152]{2,1,0:T(8,128)} %fusion.q_ref.k_ref.v_ref.g_ref.b_ref, ...), custom_call_target="tpu_custom_call" | custom-call | tf_op jit(solution)/shard_map/mixer_backward/pallas_call | solution.py:287
  581.3 18.7 %fusion.35 = (bf16[2048,1152]{1,0:T(8,128)(2,1)}, f32[2048]{0:T(1024)S(1)}) fusion(bf16[1024,1152]{1,0:T(8,128)(2,1)} %get-tuple-element.122, bf16[1024,1152]{1,0:T(8,128)(2,1)S(1)} %copy-done.4, bf16[2048,2048]{1,0:T(8,128)(2,1)} %bitcast.134, bf16[2048,1152]{1,0:T(8,128)(2,1)} %bitcast.141), kind=kOutput, calls=%fused_computation.166 | convolution fusion | flops 9680189440 | bytes 22552576 | tf_op jit(solution)/shard_map/dot_general | solution.py:838
  600.0 12.6 %copy.108 = bf16[4,2,256,1152]{2,1,0,3:T(2,128)(2,1)} copy(bf16[4,2,256,1152]{3,2,0,1:T(8,128)(2,1)} %bitcast.143) | data formatting | bytes 9437184 | tf_op jit(solution)/shard_map/transpose | solution.py:882
  612.6 8.8 reshape.179
  623.3 9.3 bitcast_convert_fusion.2
  632.6 1.5 constant_dynamic-slice_fusion
  634.1 2.0 collective-permute-start.19
  636.2 35.0 %collective-permute-done.19 = bf16[768,1024]{1,0:T(8,128)(2,1)S(1)} collective-permute-done((bf16[768,1024]{1,0:T(8,128)(2,1)}, bf16[768,1024]{1,0:T(8,128)(2,1)S(1)}, u32[]{:S(2)}, u32[]{:S(2)}) %collective-permute-start.19) | collective-permute-done | bytes 1572896 | tf_op jit(solution)/shard_map/ppermute | solution.py:842
  672.5 1.9 pad_maximum_fusion.3
  674.4 17.3 %bitcast_convert_fusion = bf16[2048,1536]{1,0:T(8,128)(2,1)S(1)} fusion(bf16[8,256,2048]{2,1,0:T(8,128)(2,1)} %get-tuple-element.52, bf16[8,256,1536]{2,1,0:T(8,128)(2,1)} %get-tuple-element.37.grads_ref), kind=kOutput, calls=%fused_computation.3 | convolution fusion | flops 12888047616 | bytes 20971520 | tf_op jit(solution)/shard_map/dot_general | solution.py:838
  691.8 3.3 copy.110
  695.2 1.6 copy-done.5
  696.8 4.3 pad_maximum_fusion.w_ref
  701.2 15.3 %collective-permute-start.11 = (f32[7296]{0:T(1024)S(1)}, f32[7296]{0:T(1024)S(1)}, u32[]{:S(2)}, u32[]{:S(2)}) collective-permute-start(f32[7296]{0:T(1024)S(1)} %pad_maximum_fusion.8), channel_id=1, source_target_pairs={{0,8},{8,0},{16,24},{24,16},{1,9},{9,1},{17,25},{25,17},{2,10},{10... | collective-permute-start | bytes 87560 | tf_op jit(solution)/shard_map/ppermute | solution.py:892
  716.5 69.7 %product_scatter.3 = f32[256,2048]{1,0:T(8,128)} custom-call(bf16[8,256,1152]{2,1,0:T(8,128)(2,1)} %bitcast.142, bf16[2048,1152]{1,0:T(8,128)(2,1)} %pad_maximum_fusion.w_ref), custom_call_target="tpu_custom_call" | custom-call | tf_op jit(solution)/shard_map/product_scatter/pallas_call | solution.py:808
  786.2 2.5 fusion.4
  789.0 2.0 fusion.8
  791.0 45.3 %product_scatter.2 = f32[256,2048]{1,0:T(8,128)} custom-call(bf16[8,256,768]{2,1,0:T(8,128)(2,1)} %get-tuple-element.36.lhs_ref, bf16[768,2048]{1,0:T(8,128)(2,1)} %pad_maximum_fusion.2.wd_ref.w_ref), custom_call_target="tpu_custom_call" | custom-call | tf_op jit(solution)/shard_map/product_scatter/pallas_call | solution.py:808
  839.5 1.8 add_convert_fusion
  841.4 2.6 collective-permute-done.14
  846.2 8.7 collective-permute-done.15
  856.7 2.4 select_bitcast_fusion.1
  859.2 6.5 collective-permute-done.9
  869.2 5.8 convolution_convert_fusion
  878.3 2.4 convert_element_type.137
  880.6 3.8 collective-permute-done.16
  884.5 2.3 broadcast_select_fusion.9
  887.8 6.4 collective-permute-done.17
  895.7 72.8 %reduce-scatter.9.cloned.1.call-done = bf16[512,1536]{1,0:T(8,128)(2,1)} async-done(((bf16[2048,1536]{1,0:T(8,128)(2,1)}), bf16[512,1536]{1,0:T(8,128)(2,1)}) %reduce-scatter.9.cloned.1.call-update) | async-done | bytes 1572880 | tf_op jit(solution)/shard_map/reduce_scatter | solution.py:877
  968.5 2.1 constant_dynamic-slice_fusion.1
  970.6 1.5 collective-permute-start.18
  978.4 11.7 %collective-permute-done.18 = bf16[256,1536]{1,0:T(8,128)(2,1)S(1)} collective-permute-done((bf16[256,1536]{1,0:T(8,128)(2,1)}, bf16[256,1536]{1,0:T(8,128)(2,1)S(1)}, u32[]{:S(2)}, u32[]{:S(2)}) %collective-permute-start.18) | collective-permute-done | bytes 786464 | tf_op jit(solution)/shard_map/ppermute | solution.py:842
  993.3 5.2 reduce-scatter.7.cloned.1.call-done
  998.5 1.8 convert_element_type.132
  (205 shorter events, 63.2 us)
Async XLA Ops:
  7.2 136.5 %copy-start = (f32[3,4,2048]{2,1,0:T(4,128)S(1)}, f32[3,4,2048]{2,1,0:T(4,128)}, u32[]{:S(2)}) copy-start(f32[3,4,2048]{2,1,0:T(4,128)} %param.24) | copy-start | bytes 294916
  7.2 232.0 %all-gather.10.cloned.1.call-start = ((), (), s32[]{:S(2)}) async-start(), calls=%async_computation.9 | async-start | bytes 9437184 | tf_op jit(solution)/shard_map/all_gather | solution.py:861
  7.9 356.4 %all-gather.12.cloned.1.call-start = ((), (), s32[]{:S(2)}) async-start(), calls=%async_computation.10 | async-start | bytes 9437184 | tf_op jit(solution)/shard_map/all_gather | solution.py:961
  8.7 355.6 %all-gather.14.cloned.1.call-start = ((), (), s32[]{:S(2)}) async-start(), calls=%async_computation.11 | async-start | bytes 9437184 | tf_op jit(solution)/shard_map/all_gather | solution.py:962
  9.4 857.5 %reduce-scatter.5.cloned.1.call-start = ((), (), s32[]{:S(2)}) async-start(), calls=%async_computation.4 | async-start | bytes 5898240 | tf_op jit(solution)/shard_map/reduce_scatter | solution.py:877
  12.7 3.9 copy-start.30
  13.7 158.0 %collective-permute-start.1 = (bf16[256,1536]{1,0:T(8,128)(2,1)}, bf16[256,1536]{1,0:T(8,128)(2,1)}, u32[]{:S(2)}, u32[]{:S(2)}) collective-permute-start(bf16[256,1536]{1,0:T(8,128)(2,1)} %fusion.14), channel_id=1, source_target_pairs={{0,1},{1,0},{2,3},{3,2},{4,5},{5,4},{6,7},{7,6},{8,9},{9,8},{10,11... | collective-permute-start | bytes 2359304 | tf_op jit(solution)/shard_map/ppermute | solution.py:842
  17.4 4.9 copy-start.18
  17.4 6.1 copy-start.19
  22.3 6.9 copy-start.28
  25.3 209.6 %collective-permute-start = (bf16[1024,1152]{1,0:T(8,128)(2,1)}, bf16[1024,1152]{1,0:T(8,128)(2,1)}, u32[]{:S(2)}, u32[]{:S(2)}) collective-permute-start(bf16[1024,1152]{1,0:T(8,128)(2,1)} %pad_dynamic-update-slice_fusion), channel_id=1, source_target_pairs={{0,1},{1,0},{2,3},{3,2},{4,5},{5,4},{6,7},{7,6},{8,9},{9,8},{10,11... | collective-permute-start | bytes 7077896 | tf_op jit(solution)/shard_map/ppermute | solution.py:842
  27.2 111.2 %collective-permute-start.5 = (bf16[192,1024]{1,0:T(8,128)(2,1)}, bf16[192,1024]{1,0:T(8,128)(2,1)}, u32[]{:S(2)}, u32[]{:S(2)}) collective-permute-start(bf16[192,1024]{1,0:T(8,128)(2,1)} %constant_dynamic-slice_fusion.6), channel_id=1, source_target_pairs={{0,1},{1,0},{2,3},{3,2},{4,5},{5,4},{6,7},{7,6},{8,9},{9,8},{10,11... | collective-permute-start | bytes 1179656 | tf_op jit(solution)/shard_map/ppermute | solution.py:842
  138.4 34.1 %collective-permute-start.6 = (bf16[192,1024]{1,0:T(8,128)(2,1)}, bf16[192,1024]{1,0:T(8,128)(2,1)}, u32[]{:S(2)}, u32[]{:S(2)}) collective-permute-start(bf16[192,1024]{1,0:T(8,128)(2,1)} %collective-permute-done.5), channel_id=1, source_target_pairs={{0,8},{8,0},{16,24},{24,16},{1,9},{9,1},{17,25},{25,17},{2,10},{10... | collective-permute-start | bytes 1179656 | tf_op jit(solution)/shard_map/ppermute | solution.py:905
  141.1 8.6 copy-start.26
  141.1 9.9 copy-start.25
  141.1 36.0 %collective-permute-start.7 = (bf16[192,1024]{1,0:T(8,128)(2,1)}, bf16[192,1024]{1,0:T(8,128)(2,1)}, u32[]{:S(2)}, u32[]{:S(2)}) collective-permute-start(bf16[192,1024]{1,0:T(8,128)(2,1)} %collective-permute-done.5), channel_id=1, source_target_pairs={{0,16},{8,24},{16,0},{24,8},{1,17},{9,25},{17,1},{25,9},{2,18},{10... | collective-permute-start | bytes 1179656 | tf_op jit(solution)/shard_map/ppermute | solution.py:905
  144.3 34.0 %collective-permute-start.8 = (bf16[192,1024]{1,0:T(8,128)(2,1)}, bf16[192,1024]{1,0:T(8,128)(2,1)}, u32[]{:S(2)}, u32[]{:S(2)}) collective-permute-start(bf16[192,1024]{1,0:T(8,128)(2,1)} %collective-permute-done.5), channel_id=1, source_target_pairs={{0,24},{8,16},{16,8},{24,0},{1,25},{9,17},{17,9},{25,1},{2,26},{10... | collective-permute-start | bytes 1179656 | tf_op jit(solution)/shard_map/ppermute | solution.py:905
  149.6 6.8 copy-start.27
  151.0 6.8 copy-start.23
  170.3 9.1 copy-start.17
  171.7 32.5 %collective-permute-start.2 = (bf16[256,1536]{1,0:T(8,128)(2,1)}, bf16[256,1536]{1,0:T(8,128)(2,1)S(1)}, u32[]{:S(2)}, u32[]{:S(2)}) collective-permute-start(bf16[256,1536]{1,0:T(8,128)(2,1)} %collective-permute-done.1), channel_id=1, source_target_pairs={{0,8},{8,0},{16,24},{24,16},{1,9},{9,1},{17,25},{25,17},{2,10},{10... | collective-permute-start | bytes 2359304 | tf_op jit(solution)/shard_map/ppermute | solution.py:905
  172.5 57.4 %collective-permute-start.3 = (bf16[256,1536]{1,0:T(8,128)(2,1)}, bf16[256,1536]{1,0:T(8,128)(2,1)S(1)}, u32[]{:S(2)}, u32[]{:S(2)}) collective-permute-start(bf16[256,1536]{1,0:T(8,128)(2,1)} %collective-permute-done.1), channel_id=1, source_target_pairs={{0,16},{8,24},{16,0},{24,8},{1,17},{9,25},{17,1},{25,9},{2,18},{10... | collective-permute-start | bytes 2359304 | tf_op jit(solution)/shard_map/ppermute | solution.py:905
  177.1 52.9 %collective-permute-start.4 = (bf16[256,1536]{1,0:T(8,128)(2,1)}, bf16[256,1536]{1,0:T(8,128)(2,1)S(1)}, u32[]{:S(2)}, u32[]{:S(2)}) collective-permute-start(bf16[256,1536]{1,0:T(8,128)(2,1)} %collective-permute-done.1), channel_id=1, source_target_pairs={{0,24},{8,16},{16,8},{24,0},{1,25},{9,17},{17,9},{25,1},{2,26},{10... | collective-permute-start | bytes 2359304 | tf_op jit(solution)/shard_map/ppermute | solution.py:905
  239.2 72.9 %copy-start.3 = (bf16[1024,1152]{1,0:T(8,128)(2,1)}, bf16[1024,1152]{1,0:T(8,128)(2,1)S(1)}, u32[]{:S(2)}) copy-start(bf16[1024,1152]{1,0:T(8,128)(2,1)S(1)} %get-tuple-element.121) | copy-start | bytes 7077892
  301.8 10.3 %copy-start.6 = (bf16[1024,1152]{1,0:T(8,128)(2,1)S(1)}, bf16[1024,1152]{1,0:T(8,128)(2,1)}, u32[]{:S(2)}) copy-start(bf16[1024,1152]{1,0:T(8,128)(2,1)} %get-tuple-element.122) | copy-start | bytes 7077892
  524.7 56.5 %copy-start.4 = (bf16[1024,1152]{1,0:T(8,128)(2,1)S(1)}, bf16[1024,1152]{1,0:T(8,128)(2,1)}, u32[]{:S(2)}) copy-start(bf16[1024,1152]{1,0:T(8,128)(2,1)} %copy-done.3) | copy-start | bytes 7077892
  621.4 1.9 copy-start.11
  621.5 247.8 %all-gather.8.cloned.1.call-start = ((), (), s32[]{:S(2)}) async-start(), calls=%async_computation.5 | async-start | bytes 9437184 | tf_op jit(solution)/shard_map/all_gather | solution.py:997
  622.1 256.2 %reduce-scatter.11.cloned.1.call-start = ((), (), s32[]{:S(2)}) async-start(), calls=%async_computation.8 | async-start | bytes 3604480 | tf_op jit(solution)/shard_map/reduce_scatter | solution.py:877
  634.1 37.0 %collective-permute-start.19 = (bf16[768,1024]{1,0:T(8,128)(2,1)}, bf16[768,1024]{1,0:T(8,128)(2,1)S(1)}, u32[]{:S(2)}, u32[]{:S(2)}) collective-permute-start(bf16[768,1024]{1,0:T(8,128)(2,1)} %get-tuple-element.125), channel_id=1, source_target_pairs={{0,1},{1,0},{2,3},{3,2},{4,5},{5,4},{6,7},{7,6},{8,9},{9,8},{10,11... | collective-permute-start | bytes 4718600 | tf_op jit(solution)/shard_map/ppermute | solution.py:842
  674.4 294.1 %reduce-scatter.9.cloned.1.call-start = ((), (), s32[]{:S(2)}) async-start(), calls=%async_computation.7 | async-start | bytes 7864320 | tf_op jit(solution)/shard_map/reduce_scatter | solution.py:877
  695.1 1.7 copy-start.5
  695.1 5.9 copy-start.22
  695.1 6.0 copy-start.29
  695.1 6.0 copy-start.24
  695.1 303.3 %reduce-scatter.7.cloned.1.call-start = ((), (), s32[]{:S(2)}) async-start(), calls=%async_computation.6 | async-start | bytes 1310720 | tf_op jit(solution)/shard_map/reduce_scatter | solution.py:877
  701.2 87.6 %collective-permute-start.11 = (f32[7296]{0:T(1024)S(1)}, f32[7296]{0:T(1024)S(1)}, u32[]{:S(2)}, u32[]{:S(2)}) collective-permute-start(f32[7296]{0:T(1024)S(1)} %pad_maximum_fusion.8), channel_id=1, source_target_pairs={{0,8},{8,0},{16,24},{24,16},{1,9},{9,1},{17,25},{25,17},{2,10},{10... | collective-permute-start | bytes 87560 | tf_op jit(solution)/shard_map/ppermute | solution.py:892
  786.2 2.8 copy-start.2
  786.2 2.8 copy-start.9
  788.8 47.6 %collective-permute-start.12 = (f32[7296]{0:T(1024)S(1)}, f32[7296]{0:T(1024)S(1)}, u32[]{:S(2)}, u32[]{:S(2)}) collective-permute-start(f32[7296]{0:T(1024)S(1)} %fusion.33), channel_id=1, source_target_pairs={{0,16},{8,24},{16,0},{24,8},{1,17},{9,25},{17,1},{25,9},{2,18},{10... | collective-permute-start | bytes 87560 | tf_op jit(solution)/shard_map/ppermute | solution.py:892
  791.0 45.6 %copy-start.10 = (bf16[256,2048]{1,0:T(8,128)(2,1)}, bf16[256,2048]{1,0:T(8,128)(2,1)S(1)}, u32[]{:S(2)}) copy-start(bf16[256,2048]{1,0:T(8,128)(2,1)S(1)} %fusion.8) | copy-start | bytes 3145732
  836.3 3.2 copy-start.7
  836.5 2.0 collective-permute-start.13
  837.4 19.3 %collective-permute-start.10 = (bf16[256,1024]{1,0:T(8,128)(2,1)}, bf16[256,1024]{1,0:T(8,128)(2,1)}, u32[]{:S(2)}, u32[]{:S(2)}) collective-permute-start(bf16[256,1024]{1,0:T(8,128)(2,1)} %constant_dynamic-slice_fusion.4), channel_id=1, source_target_pairs={{0,1},{1,0},{2,3},{3,2},{4,5},{5,4},{6,7},{7,6},{8,9},{9,8},{10,11... | collective-permute-start | bytes 1572872 | tf_op jit(solution)/shard_map/ppermute | solution.py:842
  838.5 5.4 collective-permute-start.14
  844.0 10.9 %collective-permute-start.15 = (f32[28800]{0:T(1024)S(1)}, f32[28800]{0:T(1024)S(1)}, u32[]{:S(2)}, u32[]{:S(2)}) collective-permute-start(f32[28800]{0:T(1024)S(1)} %add.199), channel_id=1, source_target_pairs={{0,1},{1,0},{2,3},{3,2},{4,5},{5,4},{6,7},{7,6},{8,9},{9,8},{10,11... | collective-permute-start | bytes 345608 | tf_op jit(solution)/shard_map/ppermute | solution.py:892
  845.0 20.7 %collective-permute-start.9 = (bf16[256,1024]{1,0:T(8,128)(2,1)S(1)}, bf16[256,1024]{1,0:T(8,128)(2,1)S(1)}, u32[]{:S(2)}, u32[]{:S(2)}) collective-permute-start(bf16[256,1024]{1,0:T(8,128)(2,1)S(1)} %constant_dynamic-slice_fusion.5), channel_id=1, source_target_pairs={{0,1},{1,0},{2,3},{3,2},{4,5},{5,4},{6,7},{7,6},{8,9},{9,8},{10,11... | collective-permute-start | bytes 1572872 | tf_op jit(solution)/shard_map/ppermute | solution.py:842
  854.9 14.3 %copy-start.8 = (bf16[2,1024,256]{2,1,0:T(8,128)(2,1)S(1)}, bf16[2,1024,256]{2,1,0:T(8,128)(2,1)}, u32[]{:S(2)}) copy-start(bf16[2,1024,256]{2,1,0:T(8,128)(2,1)} %get-tuple-element.34) | copy-start | bytes 3145732
  868.1 16.4 %collective-permute-start.16 = (bf16[256,1152]{0,1:T(8,128)(2,1)S(1)}, bf16[256,1152]{0,1:T(8,128)(2,1)}, u32[]{:S(2)}, u32[]{:S(2)}) collective-permute-start(bf16[256,1152]{0,1:T(8,128)(2,1)S(1)} %constant_dynamic-slice_fusion.3), channel_id=1, source_target_pairs={{0,1},{1,0},{2,3},{3,2},{4,5},{5,4},{6,7},{7,6},{8,9},{9,8},{10,11... | collective-permute-start | bytes 1769480 | tf_op jit(solution)/shard_map/ppermute | solution.py:842
  869.2 6.9 copy-start.12
  869.2 6.9 copy-start.13
  875.1 2.1 copy-start.14
  875.1 2.1 copy-start.15
  875.1 19.2 %collective-permute-start.17 = (bf16[256,1024]{1,0:T(8,128)(2,1)S(1)}, bf16[256,1024]{1,0:T(8,128)(2,1)S(1)}, u32[]{:S(2)}, u32[]{:S(2)}) collective-permute-start(bf16[256,1024]{1,0:T(8,128)(2,1)S(1)} %constant_dynamic-slice_fusion.2), channel_id=1, source_target_pairs={{0,1},{1,0},{2,3},{3,2},{4,5},{5,4},{6,7},{7,6},{8,9},{9,8},{10,11... | collective-permute-start | bytes 1572872 | tf_op jit(solution)/shard_map/ppermute | solution.py:842
  894.6 79.5 %copy-start.21 = (bf16[256,256]{0,1:T(8,128)(2,1)S(1)}, bf16[256,256]{0,1:T(8,128)(2,1)}, u32[]{:S(2)}) copy-start(bf16[256,256]{0,1:T(8,128)(2,1)} %get-tuple-element.133) | copy-start | bytes 393220
  895.7 80.3 %copy-start.20 = (bf16[256,256]{0,1:T(8,128)(2,1)S(1)}, bf16[256,256]{0,1:T(8,128)(2,1)}, u32[]{:S(2)}) copy-start(bf16[256,256]{0,1:T(8,128)(2,1)} %get-tuple-element.138) | copy-start | bytes 393220
  970.6 7.7 copy-start.16
  970.6 19.5 %collective-permute-start.18 = (bf16[256,1536]{1,0:T(8,128)(2,1)}, bf16[256,1536]{1,0:T(8,128)(2,1)S(1)}, u32[]{:S(2)}, u32[]{:S(2)}) collective-permute-start(bf16[256,1536]{1,0:T(8,128)(2,1)} %constant_dynamic-slice_fusion.1), channel_id=1, source_target_pairs={{0,1},{1,0},{2,3},{3,2},{4,5},{5,4},{6,7},{7,6},{8,9},{9,8},{10,11... | collective-permute-start | bytes 2359304 | tf_op jit(solution)/shard_map/ppermute | solution.py:842
  990.8 9.5 copy-start.1
Sparse Core Ops, SparseCore 0:
  9.9 90.1 all-gather.9
  102.0 65.2 all-gather.11
  169.2 54.3 all-gather.13
  621.6 99.4 reduce-scatter.4
  722.8 76.1 all-gather.7
  801.1 54.4 reduce-scatter.10
  857.9 110.5 reduce-scatter.8
  970.8 27.6 reduce-scatter.6

commit v3 on v2

--- a/solution.py
+++ b/solution.py
@@ -10,6 +10,9 @@
 bf = jnp.bfloat16
 f32 = jnp.float32
 GROUP = 8
+
+def lasting(us):
+    return pl.CostEstimate(flops=int(us * 1.15e9), bytes_accessed=1 << 20, transcendentals=0)
 
 def nn(a, b):
     return lax.dot_general(a.astype(bf), b.astype(bf), (((1,), (0,)), ((), ())), preferred_element_type=f32)
@@ -61,6 +64,10 @@
     same = aux[:, 0:1] == segrow
     return same & (row > col), same & (row >= col)
 
+def aux_columns(ref, rows):
+    block = ref[0, :, rows]
+    return jnp.concatenate([block, jnp.zeros((C - block.shape[0], C), f32)], axis=0).T
+
 def beta_column(block, h):
     lane = lax.broadcasted_iota(jnp.int32, block.shape, 1)
     return jnp.sum(jnp.where(lane == h, jax.nn.sigmoid(block), 0.0), axis=1, keepdims=True)
@@ -69,7 +76,7 @@
     start = pl.multiple_of(jnp.maximum(lo - 8, 0), 8)
     return jnp.where(lo > 0, ref[0, pl.ds(start, 8), :].astype(f32), 0.0)
 
-def fwd_kernel(q_ref, k_ref, v_ref, g_ref, b_ref, aux_ref, seg_ref, w_ref, gain_ref,
+def fwd_kernel(q_ref, k_ref, v_ref, g_ref, b_ref, aux_ref, w_ref, gain_ref,
                mixed_ref, t_ref, w_out, p_ref, f_ref, s_ref, fresh_ref, o_ref,
                q_s, u_s, b_s):
     h = pl.program_id(1)
@@ -81,12 +88,12 @@
         spans = [pl.ds(lo, C) for lo in lows]
         many, keys, right = [], [], []
         for lo, rows in zip(lows, spans):
-            aux = aux_ref[0, rows, :]
+            aux = aux_columns(aux_ref, rows)
             q = act_stage(q_ref[0, rows, :].astype(f32), prev_rows(q_ref, lo), aux, w_ref[0], True)[2]
             k = act_stage(k_ref[0, rows, :].astype(f32), prev_rows(k_ref, lo), aux, w_ref[1], True)[2]
             v = act_stage(v_ref[0, rows, :].astype(f32), prev_rows(v_ref, lo), aux, w_ref[2], False)[2]
             beta = beta_column(b_ref[0, rows, :].astype(f32), h)
-            strict, inclusive = masks(aux, seg_ref[0, 0:1, rows])
+            strict, inclusive = masks(aux, aux_ref[0, 0:1, rows])
             kb = k.astype(bf)
             qb = q.astype(bf)
             both = nt(jnp.concatenate([kb, qb], axis=0), kb)
@@ -99,7 +106,7 @@
         wus = [nn(t, r) for t, r in zip(totals, right)]
         kwus = [tn(k, wu) for k, wu in zip(keys, wus)]
         for rows, t, wu, kwu in zip(spans, totals, wus, kwus):
-            clast = aux_ref[0, rows, :][C - 1:C, 1:2]
+            clast = aux_ref[0, 1:2, rows][:, C - 1:C]
             f_ref[0, 0, rows, :] = (clast * (eye.astype(f32) - kwu[:, :C])).astype(bf)
             b_s[rows, :] = kwu[:, C:]
             t_ref[0, 0, rows, :] = t
@@ -115,7 +122,7 @@
     lax.fori_loop(0, steps, scan, jnp.zeros((C, C), f32), unroll=True)
     def stage_c(c, _):
         rows = pl.ds(pl.multiple_of(c * C, C), C)
-        aux = aux_ref[0, rows, :]
+        aux = aux_columns(aux_ref, rows)
         carried = aux[:, 1:2]
         ws = nn(jnp.concatenate([w_out[0, 0, rows, :], q_s[rows, :]], axis=0), s_ref[0, 0, rows, :])
         fresh = (u_s[rows, :] - carried * ws[:C]).astype(bf)
@@ -132,7 +139,7 @@
     return [pl.BlockSpec((1, length, 128), functools.partial(lambda t, b, h: (b, 0, t * heads + h), t)) for t in range(4)] + [
         pl.BlockSpec((1, length, 128), lambda b, h: (b, 0, 4 * heads))]
 
-def mixer_fwd(raw, aux, segrow, conv, gain):
+def mixer_fwd(raw, aux, conv, gain):
     nb, length, width = raw.shape
     heads = (width - 128) // 512
     per = pl.BlockSpec((1, 1, length, 128), lambda b, h: (b, h, 0, 0))
@@ -141,18 +148,18 @@
         fwd_kernel,
         grid=(nb, heads),
         in_specs=specs(length, heads, 0) + [
-            pl.BlockSpec((1, length, aux.shape[2]), lambda b, h: (b, 0, 0)),
-            pl.BlockSpec((1, 1, length), lambda b, h: (b, 0, 0)),
+            pl.BlockSpec((1, aux.shape[1], length), lambda b, h: (b, 0, 0)),
             pl.BlockSpec((3, conv.shape[1], 128), lambda b, h: (0, 0, h)),
             pl.BlockSpec((1, 128), lambda b, h: (0, 0)),
         ],
         out_specs=[pl.BlockSpec((1, length, 128), lambda b, h: (b, 0, h))] + [per] * 7,
         out_shape=[jax.ShapeDtypeStruct((nb, length, heads * 128), bf)] + [sh(bf)] * 6 + [sh(f32)],
         scratch_shapes=[pltpu.VMEM((length, 128), bf), pltpu.VMEM((length, 128), f32), pltpu.VMEM((length, 128), f32)],
+        cost_estimate=lasting(33),
         name="mixer_forward",
-    )(raw, raw, raw, raw, raw, aux, segrow, conv, gain)
-
-def bwd_kernel(q_ref, k_ref, v_ref, g_ref, b_ref, aux_ref, seg_ref, w_ref, gain_ref,
+    )(raw, raw, raw, raw, raw, aux, conv, gain)
+
+def bwd_kernel(q_ref, k_ref, v_ref, g_ref, b_ref, aux_ref, w_ref, gain_ref,
                t_ref, w_in, p_ref, f_ref, s_ref, fresh_ref, o_ref, dm_ref,
                draw_ref, dconv_ref, dgain_ref,
                do_s, pd_s, base_s, ds_s):
@@ -164,7 +171,7 @@
     def stage_a(c, dgain):
         lo = pl.multiple_of(c * C, C)
         rows = pl.ds(lo, C)
-        aux = aux_ref[0, rows, :]
+        aux = aux_columns(aux_ref, rows)
         carried = aux[:, 1:2]
         q = act_stage(q_ref[0, rows, :].astype(f32), prev_rows(q_ref, lo), aux, w_ref[0], True)[2]
         out = o_ref[0, 0, rows, :]
@@ -213,7 +220,7 @@
         c = steps - 1 - j
         lo = pl.multiple_of(c * C, C)
         rows = pl.ds(lo, C)
-        aux = aux_ref[0, rows, :]
+        aux = aux_columns(aux_ref, rows)
         carried = aux[:, 1:2]
         tail = aux[:, 2:3]
         xq = q_ref[0, rows, :].astype(f32)
@@ -224,7 +231,7 @@
         cv, sv, v, _, shv = act_stage(xv, prev_rows(v_ref, lo), aux, w_ref[2], False)
         bblock = b_ref[0, rows, :].astype(f32)
         beta = beta_column(bblock, h)
-        strict, inclusive = masks(aux, seg_ref[0, 0:1, rows])
+        strict, inclusive = masks(aux, aux_ref[0, 0:1, rows])
         kb = k.astype(bf)
         qb = q.astype(bf)
         st = s_ref[0, 0, rows, :]
@@ -278,7 +285,7 @@
     for n, d in enumerate(dws):
         dconv_ref[0, 0, n] = d
 
-def mixer_bwd(raw, aux, segrow, conv, gain, saved, dmixed):
+def mixer_bwd(raw, aux, conv, gain, saved, dmixed):
     nb, length, width = raw.shape
     heads = (width - 128) // 512
     taps = conv.shape[1]
@@ -288,8 +295,7 @@
         bwd_kernel,
         grid=(nb, heads),
         in_specs=specs(length, heads, 0) + [
-            pl.BlockSpec((1, length, aux.shape[2]), lambda b, h: (b, 0, 0)),
-            pl.BlockSpec((1, 1, length), lambda b, h: (b, 0, 0)),
+            pl.BlockSpec((1, aux.shape[1], length), lambda b, h: (b, 0, 0)),
             pl.BlockSpec((3, taps, 128), lambda b, h: (0, 0, h)),
             pl.BlockSpec((1, 128), lambda b, h: (0, 0)),
         ] + [per] * 7 + [pl.BlockSpec((1, length, 128), lambda b, h: (b, 0, h))],
@@ -300,8 +306,9 @@
                    jax.ShapeDtypeStruct((nb, heads, 3 * taps, 8, 128), f32),
                    jax.ShapeDtypeStruct((nb, heads, 8, 128), f32)],
         scratch_shapes=[pltpu.VMEM((length, 128), f32)] * 3 + [pltpu.VMEM((length, 128), bf)],
+        cost_estimate=lasting(2),
         name="mixer_backward",
-    )(raw, raw, raw, raw, raw, aux, segrow, conv, gain, *saved, dmixed)
+    )(raw, raw, raw, raw, raw, aux, conv, gain, *saved, dmixed)
     dconv = jnp.sum(dconv, axis=(0, 3)).reshape(heads, 3, taps, 128).transpose(1, 2, 0, 3).reshape(3, taps, heads * 128)
     return draw, dconv, jnp.sum(dgain, axis=(0, 1, 2))
 
@@ -319,7 +326,7 @@
     for i in range(1, 4):
         cols.append((jnp.pad(seg, ((0, 0), (0, i)), constant_values=-1.0)[:, i:] == seg).astype(f32))
     cols += [jnp.zeros_like(seg)] * (16 - len(cols))
-    return jnp.stack(cols, axis=-1), seg[:, None, :]
+    return jnp.stack(cols, axis=1)
 
 
 SLOTS = ((0, 0, 0), (0, 0, 1), (1, 0, 0), (0, 1, 0), (1, 0, 1), (0, 1, 1), (1, 1, 0), (1, 1, 1))
@@ -341,6 +348,15 @@
     return {"gx": px, "gy": py}
 
 
+def flipped(index, n, size):
+    out, bit = 0, 1
+    while bit < size:
+        digit = index // bit % 2
+        out = out + bit * (1 - digit if n & bit else digit)
+        bit *= 2
+    return out
+
+
 def entry_barrier(peers):
     sem = pltpu.get_barrier_semaphore()
     for peer in peers:
@@ -363,7 +379,7 @@
 class Gather:
     COPIES = 13
 
-    def __init__(self, buf, send, recv, gx, gy):
+    def __init__(self, buf, send, recv, gx, gy, over_gx=False):
         rows = buf.shape[1]
         half = rows // 2
         a, b = pl.ds(0, half), pl.ds(half, half)
@@ -379,7 +395,8 @@
             make(3, 0, 3, b, yn),
             remote(buf.at[0], buf.at[1], send.at[4], recv.at[4], core),
         ]
-        self.diagonal = [make(5, 3, 6, a, xn), make(6, 2, 6, b, yn)]
+        self.over_gx = over_gx
+        self.diagonal = [make(5, 2, 6, a, yn) if over_gx else make(5, 3, 6, a, xn), make(6, 2, 6, b, yn)]
         self.cross = [
             make(7, 2, 4, a, core),
             make(8, 2, 4, b, core),
@@ -398,9 +415,12 @@
             self.own[4].wait_recv()
         elif i == 2:
             self.own[1].wait_recv()
-            self.diagonal[0].start()
+            if not self.over_gx:
+                self.diagonal[0].start()
             self.cross[2].start()
             self.own[0].wait_recv()
+            if self.over_gx:
+                self.diagonal[0].start()
             self.cross[0].start()
             self.own[2].wait_recv()
             self.diagonal[1].start()
@@ -428,35 +448,201 @@
             c.wait_send()
 
 
-def mlp_kernel(
-    mixed_ref, out_ref, x_ref, gain_ref, wgu_ref, wd_ref, y_ref,
-    middle_ref, second_ref, hidden_ref, grads_ref, yrel_ref,
-    mix_in, w_out, wgu, wd, buf, ybuf, hbuf, gbuf, mid, mine,
-    load_sem, y_sem, y_out_sem, out_sem, a2a_send, a2a_recv, ag_send, ag_recv,
+def head_kernel(
+    x_ref, wq_ref, wk_ref, wv_ref, wg_ref, wb_ref, gate_ref, up_ref, out_ref, gain_ref,
+    normed_ref, raw_ref, hw_ref, own_ref, gu_ref, wo_ref,
+    buf, w, low, acc, ag_send, ag_recv, w_send, w_recv, load_sem, out_sem, raw_sem, hw_sem, z_send, z_recv, u_send, u_recv,
+):
+    gx, gy, dp = lax.axis_index("gx"), lax.axis_index("gy"), lax.axis_index("dp")
+    ngx = 4
+    piece = gu_ref.shape[0]
+    parts = x_ref.shape[1] // piece
+    units = gu_ref.shape[1] // 2
+    unit_other = pl.multiple_of((1 - gy) * (gate_ref.shape[1] - units), 128)
+    turn = flipped(dp, 0, parts)
+    rows_sent = pl.ds(pl.multiple_of(turn * piece, piece), piece)
+    rows = own_ref.shape[0]
+    part = x_ref.shape[1]
+    width = wq_ref.shape[1] // 2
+    weights = ((wq_ref, width), (wk_ref, width), (wv_ref, width), (wg_ref, width), (wb_ref, 128))
+    starts = [0, width, 2 * width, 3 * width, 4 * width]
+    xn = slot_peer(2, gx, gy)
+    loads = [pltpu.make_async_copy(x_ref, buf.at[0], load_sem.at[5])]
+    for i, (ref, n) in enumerate(weights):
+        src = ref.at[:, pl.ds(pl.multiple_of(gy * n, 128), n)]
+        loads.append(pltpu.make_async_copy(src, w.at[0, :, pl.ds(starts[i], n)], load_sem.at[i]))
+    for c in loads:
+        c.start()
+    peers = [slot_peer(r, gx, gy) for r in (1, 2, 3)] + [{"dp": flipped(dp, n, parts)} for n in range(1, parts)]
+    entry_barrier(peers)
+    swaps = []
+    for i, (ref, n) in enumerate(weights):
+        src = ref.at[rows_sent, pl.ds(pl.multiple_of((1 - gy) * n, 128), n)]
+        swaps.append(remote(src, w.at[1, rows_sent, pl.ds(starts[i], n)], w_send.at[i], w_recv.at[i], xn))
+        swaps[-1].start()
+    loads[0].wait()
+    gather = Gather(buf, ag_send, ag_recv, gx, gy, True)
+    gather.start()
+    extra = [
+        remote(gate_ref.at[rows_sent, pl.ds(unit_other, units)], gu_ref.at[:, pl.ds(0, units)], u_send.at[0], u_recv.at[0], xn),
+        remote(up_ref.at[rows_sent, pl.ds(unit_other, units)], gu_ref.at[:, pl.ds(units, units)], u_send.at[1], u_recv.at[1], xn),
+        remote(out_ref.at[pl.ds(pl.multiple_of((1 - gy) * width, width), width), :], wo_ref, u_send.at[2], u_recv.at[2], xn),
+    ]
+    for c in extra:
+        c.start()
+    for c in swaps:
+        c.wait_recv()
+    spread = [
+        remote(w.at[1, rows_sent], w.at[1, rows_sent], z_send.at[n], z_recv.at[n], {"dp": flipped(dp, n, parts)}) for n in range(1, parts)
+    ]
+    for c in spread:
+        c.start()
+    for c in loads[1:]:
+        c.wait()
+    keep = pltpu.make_async_copy(w.at[0], hw_ref.at[pl.ds(pl.multiple_of(gy * part, part), part)], hw_sem.at[0])
+    keep.start()
+    near = pl.ds(pl.multiple_of(gy * part, part), part)
+    far = pl.ds(pl.multiple_of((1 - gy) * part, part), part)
+    stores = []
+    blocks = []
+
+    def pair(n, first, second):
+        px, _ = slot_place(first, gx, gy)
+        for s in range(2):
+            span = pl.ds(s * rows, rows)
+            v = s * ngx + px
+            i = 2 * n + s
+            x0 = buf[first, span, :].astype(f32)
+            x1 = buf[second, span, :].astype(f32)
+            total = jnp.sum(x0 * x0, axis=-1, keepdims=True) + jnp.sum(x1 * x1, axis=-1, keepdims=True)
+            rate = lax.rsqrt(total / (2 * part) + EPS)
+            low[i, :, near] = (x0 * rate * gain_ref[:, near]).astype(bf)
+            low[i, :, far] = (x1 * rate * gain_ref[:, far]).astype(bf)
+            c = pltpu.make_async_copy(low.at[i], normed_ref.at[v], out_sem.at[i])
+            c.start()
+            stores.append(c)
+            acc[i] = nn_dot(low[i, :, near], w[0])
+            blocks.append((i, v))
+
+    for step in (1, 2, 3, 4):
+        gather.step(step)
+        if step == 2:
+            pair(0, 0, 2)
+            mine = pl.ds(pl.multiple_of(gy * rows, rows), rows)
+            own_ref[:, near] = buf[0, mine, :]
+            own_ref[:, far] = buf[2, mine, :]
+    pair(1, 1, 4)
+    gather.step(5)
+    gather.step(6)
+    pair(2, 3, 6)
+    gather.step(7)
+    pair(3, 5, 7)
+    for c in spread:
+        c.wait_recv()
+    give = pltpu.make_async_copy(w.at[1], hw_ref.at[far], hw_sem.at[1])
+    give.start()
+
+    for i, v in blocks:
+        acc[i] += nn_dot(low[i, :, far], w[1])
+        c = pltpu.make_async_copy(acc.at[i], raw_ref.at[v], raw_sem.at[i])
+        c.start()
+        stores.append(c)
+    keep.wait()
+    give.wait()
+    for c in stores:
+        c.wait()
+    for c in extra:
+        c.wait_recv()
+    for c in swaps + spread + extra:
+        c.wait_send()
+    gather.finish()
+
+
+def head_project(inputs, w_query, w_key, w_value, w_gate_head, w_beta, w_gate, w_up, w_out, gain, units, parts, collective):
+    total, part = inputs.shape
+    rows = total // 2
+    feat = 2 * part
+    cols = 2 * w_query.shape[1] + 128
+    sd = jax.ShapeDtypeStruct
+    return pl.pallas_call(
+        head_kernel,
+        in_specs=[ANY] * 9 + [VM],
+        out_specs=[ANY, ANY, ANY, VM, ANY, ANY],
+        out_shape=[
+            sd((8, rows, feat), bf),
+            sd((8, rows, cols), f32),
+            sd((feat, cols), bf),
+            sd((rows, feat), bf),
+            sd((part // parts, 2 * units), bf),
+            sd((w_out.shape[0] // 2, w_out.shape[1]), bf),
+        ],
+        scratch_shapes=[
+            pltpu.VMEM((8, total, part), bf),
+            pltpu.VMEM((2, part, cols), bf),
+            pltpu.VMEM((8, rows, feat), bf),
+            pltpu.VMEM((8, rows, cols), f32),
+            pltpu.SemaphoreType.DMA((13,)),
+            pltpu.SemaphoreType.DMA((13,)),
+            pltpu.SemaphoreType.DMA((5,)),
+            pltpu.SemaphoreType.DMA((5,)),
+            pltpu.SemaphoreType.DMA((6,)),
+            pltpu.SemaphoreType.DMA((8,)),
+            pltpu.SemaphoreType.DMA((8,)),
+            pltpu.SemaphoreType.DMA((2,)),
+            pltpu.SemaphoreType.DMA((4,)),
+            pltpu.SemaphoreType.DMA((4,)),
+            pltpu.SemaphoreType.DMA((3,)),
+            pltpu.SemaphoreType.DMA((3,)),
+        ],
+        compiler_params=pltpu.CompilerParams(collective_id=collective, has_side_effects=True, vmem_limit_bytes=60 << 20),
+        cost_estimate=lasting(80),
+        name="head_project",
+    )(inputs, w_query, w_key, w_value, w_gate_head, w_beta, w_gate, w_up, w_out, gain)
+
+
+def mlp_kernel(x_ref, gate_ref, up_ref, down_ref, y_ref, *refs, parts):
+    gu_refs, piece_ref, refs = refs[:parts], refs[parts], refs[parts + 1 :]
+    mlp_body(parts, x_ref, gate_ref, up_ref, down_ref, y_ref, gu_refs, piece_ref, *refs)
+
+
+def mlp_body(
+    parts, x_ref, gate_ref, up_ref, down_ref, y_ref, gu_refs, piece_ref,
+    second_ref, hidden_ref, grads_ref, yrel_ref, gu_out, dn_out,
+    wgu, wd, buf, ybuf, hbuf, gbuf, load_sem, w_sem, keep_sem, y_sem, y_out_sem, out_sem, ag_send, ag_recv,
 ):
     gx, gy = lax.axis_index("gx"), lax.axis_index("gy")
-    ngx, ngy = 4, 2
-    me = gx * ngy + gy
+    ngy = 2
     rows = x_ref.shape[0]
     feat = x_ref.shape[1]
-    width = mixed_ref.shape[2]
-    units = wd_ref.shape[0]
+    units = wd.shape[0]
+    half = feat // 2
     tile = 256
-    peers = [slot_peer(r, gx, gy) for r in range(1, 8)]
-    entry_barrier(peers)
-    sends = []
-    for i, r in enumerate((6, 7, 2, 4, 3, 5, 1)):
-        px, py = slot_place(r, gx, gy)
-        sends.append(remote(mixed_ref.at[py * ngx + px], mix_in.at[me], a2a_send.at[r], a2a_recv.at[r], slot_peer(r, gx, gy)))
-        sends[-1].start()
-    loads = [
-        pltpu.make_async_copy(mixed_ref.at[gy * ngx + gx], mine, load_sem.at[0]),
-        pltpu.make_async_copy(out_ref, w_out, load_sem.at[1]),
-        pltpu.make_async_copy(wgu_ref, wgu, load_sem.at[2]),
-        pltpu.make_async_copy(wd_ref, wd, load_sem.at[3]),
+    dp = lax.axis_index("dp")
+    unit_mine = pl.multiple_of(gy * (gate_ref.shape[1] - units), 128)
+    doubled = gy * (2 * units - gate_ref.shape[1])
+    load = pltpu.make_async_copy(x_ref, buf.at[0], load_sem)
+    load.start()
+    near = pl.ds(pl.multiple_of(gy * half, half), half)
+    far = pl.multiple_of((1 - gy) * half, half)
+    own_units = pl.ds(unit_mine, units)
+    w_loads = [
+        pltpu.make_async_copy(gate_ref.at[:, own_units], wgu.at[near, pl.ds(0, units)], w_sem.at[0]),
+        pltpu.make_async_copy(up_ref.at[:, own_units], wgu.at[near, pl.ds(units, units)], w_sem.at[1]),
+        pltpu.make_async_copy(down_ref.at[own_units, :], wd.at[:, near], w_sem.at[2]),
     ]
-    for c in loads:
+    w_loads.append(pltpu.make_async_copy(piece_ref, wd.at[:, pl.ds(far, half)], w_sem.at[3]))
+    for n in range(parts):
+        turn = flipped(dp, n, parts)
+        piece = half // parts
+        w_loads.append(
+            pltpu.make_async_copy(gu_refs[n], wgu.at[pl.ds(pl.multiple_of(far + turn * piece, piece), piece), :], w_sem.at[4 + n])
+        )
+    for c in w_loads:
         c.start()
+    entry_barrier([slot_peer(r, gx, gy) for r in (1, 2, 3)])
+    load.wait()
+    gather = Gather(buf, ag_send, ag_recv, gx, gy)
+    gather.start()
 
     def y_load(r, n):
         px, py = slot_place(r, gx, gy)
@@ -470,26 +656,11 @@
 
     for c in y_load(0, 0):
         c.start()
-    loads[0].wait()
-    mix_in[me] = mine[...]
-    for c in sends:
-        c.wait_recv()
-    loads[1].wait()
-    for h in range(ngy):
-        cols = pl.ds(h * (feat // ngy), feat // ngy)
-        total = x_ref[:, cols].astype(f32)
-        for p in range(ngx):
-            left = jnp.concatenate([mix_in[p * 2], mix_in[p * 2 + 1]], axis=1)
-            total = total + nn_dot(left, w_out[p * 2 + h])
-        mid[:, cols] = total
-    middle = mid[...]
-    rate = lax.rsqrt(jnp.mean(middle * middle, axis=-1, keepdims=True) + EPS)
-    buf[0] = (middle * rate * gain_ref[...]).astype(bf)
-    gather = Gather(buf, ag_send, ag_recv, gx, gy)
-    gather.start()
-    middle_ref[...] = mid[...]
-    loads[2].wait()
-    loads[3].wait()
+    for c in w_loads:
+        c.wait()
+    keeps = [pltpu.make_async_copy(wgu, gu_out, keep_sem.at[0]), pltpu.make_async_copy(wd, dn_out, keep_sem.at[1])]
+    for c in keeps:
+        c.start()
 
     def outs(r):
         return [
@@ -519,7 +690,9 @@
             up = nn_dot(buf[r], wgu[:, up_cols])
             gh = nt_dot(ybuf[r % 2], wd[cols, :])
             s = jax.nn.sigmoid(gate)
-            act = gate * s
+            keep = lax.broadcasted_iota(jnp.int32, gate.shape, 1) + t * tile >= doubled
+            act = jnp.where(keep, gate * s, 0.0)
+            up = jnp.where(keep, up, 0.0)
             hbuf[r % 2, :, cols] = (act * up).astype(bf)
             gbuf[r % 2, :, up_cols] = (gh * act).astype(bf)
             gbuf[r % 2, :, cols] = (gh * up * s * (1.0 + gate * (1.0 - s))).astype(bf)
@@ -533,49 +706,46 @@
             c.wait()
         y_store(r).wait()
     gather.finish()
-    for c in sends:
-        c.wait_send()
-
-
-def mlp_forward(mixed, out_all, x_own, gain, gate_up, down, y_all, collective):
+    for c in keeps:
+        c.wait()
+
+
+def mlp_forward(x_own, w_gate, w_up, w_down, y_all, gu_pieces, down_piece, units, collective):
     rows, feat = x_own.shape
-    width = mixed.shape[2]
-    units = down.shape[0]
+    parts = len(gu_pieces)
     sd = jax.ShapeDtypeStruct
     return pl.pallas_call(
-        mlp_kernel,
-        in_specs=[ANY, ANY, VM, VM, ANY, ANY, ANY],
-        out_specs=[VM, ANY, ANY, ANY, ANY],
+        functools.partial(mlp_kernel, parts=parts),
+        in_specs=[ANY] * (6 + parts),
+        out_specs=[ANY] * 6,
         out_shape=[
-            sd((rows, feat), f32),
             sd((8, rows, feat), bf),
             sd((8, rows, units), bf),
             sd((8, rows, 2 * units), bf),
             sd((8, rows, feat), bf),
+            sd((feat, 2 * units), bf),
+            sd((units, feat), bf),
         ],
         scratch_shapes=[
-            pltpu.VMEM((8, rows, width), bf),
-            pltpu.VMEM(out_all.shape, bf),
-            pltpu.VMEM(gate_up.shape, bf),
-            pltpu.VMEM(down.shape, bf),
+            pltpu.VMEM((feat, 2 * units), bf),
+            pltpu.VMEM((units, feat), bf),
             pltpu.VMEM((8, rows, feat), bf),
             pltpu.VMEM((2, rows, feat), bf),
             pltpu.VMEM((2, rows, units), bf),
             pltpu.VMEM((2, rows, 2 * units), bf),
-            pltpu.VMEM((rows, feat), f32),
-            pltpu.VMEM((rows, width), bf),
-            pltpu.SemaphoreType.DMA((4,)),
+            pltpu.SemaphoreType.DMA,
+            pltpu.SemaphoreType.DMA((4 + parts,)),
+            pltpu.SemaphoreType.DMA((2,)),
             pltpu.SemaphoreType.DMA((2, 2)),
             pltpu.SemaphoreType.DMA((2,)),
             pltpu.SemaphoreType.DMA((3, 2)),
-            pltpu.SemaphoreType.DMA((8,)),
-            pltpu.SemaphoreType.DMA((8,)),
             pltpu.SemaphoreType.DMA((13,)),
             pltpu.SemaphoreType.DMA((13,)),
         ],
         compiler_params=pltpu.CompilerParams(collective_id=collective, has_side_effects=True, vmem_limit_bytes=62 << 20),
+        cost_estimate=lasting(68),
         name="mlp_forward",
-    )(mixed, out_all, x_own, gain, gate_up, down, y_all)
+    )(x_own, w_gate, w_up, w_down, y_all, *gu_pieces, down_piece)
 
 
 class Scatter:
@@ -671,28 +841,103 @@
     ]
 
 
-def back_kernel(
-    grads_ref, wgu_ref, out_ref, middle_ref, y_ref, gain_ref,
-    gm_ref, gmix_ref, dgain_ref,
-    give, take, acc, diag_in, last_in, s_core, r_core, s_link, r_link,
-    lhs, wgu, w_out, total, mid_low, gsend, load_sem, lhs_sem, a2a_send, a2a_recv, keep_sem,
+def own_out_rows(out_ref, piece_ref, w, sem, gy):
+    width, part = piece_ref.shape
+    near = pl.ds(pl.multiple_of(gy * part, part), part)
+    far = pl.ds(pl.multiple_of((1 - gy) * part, part), part)
+    return [
+        pltpu.make_async_copy(out_ref.at[pl.ds(pl.multiple_of(gy * width, width), width), :], w.at[:, near], sem.at[0]),
+        pltpu.make_async_copy(piece_ref, w.at[:, far], sem.at[1]),
+    ]
+
+
+def out_kernel(
+    mixed_ref, out_ref, piece_ref, x_ref, gain_ref,
+    middle_ref, normed_ref, slots_ref,
+    give, take, acc, diag_in, last_in, s_core, r_core, s_link, r_link, lhs, w, total, load_sem, lhs_sem, keep_sem,
 ):
     gx, gy = lax.axis_index("gx"), lax.axis_index("gy")
-    ngx, ngy = 4, 2
+    feat = x_ref.shape[1]
+    tile = 512
+    loads = own_out_rows(out_ref, piece_ref, w, load_sem, gy)
+    pulls = {}
+    for r in (7, 6, 4, 5, 2, 3, 1, 0):
+        px, py = slot_place(r, gx, gy)
+        pulls[r] = pltpu.make_async_copy(mixed_ref.at[py * 4 + px], lhs.at[r], lhs_sem.at[r])
+    for c in loads + list(pulls.values()):
+        c.start()
+    entry_barrier([slot_peer(r, gx, gy) for r in (1, 2, 3)])
+    for c in loads:
+        c.wait()
+
+    def product(slot, put):
+        pulls[slot].wait()
+
+        def body(t, _):
+            cols = pl.ds(pl.multiple_of(t * tile, tile), tile)
+            put(cols, nn_dot(lhs[slot], w[:, cols]))
+            return 0
+
+        lax.fori_loop(0, feat // tile, body, 0)
+
+    scatter = Scatter(give, take, acc, diag_in, last_in, s_core, r_core, s_link, r_link, gx, gy)
+    scatter.run(product, total)
+    keep = pltpu.make_async_copy(lhs, slots_ref, keep_sem)
+    keep.start()
+    middle = x_ref[...].astype(f32) + total[...]
+    middle_ref[...] = middle
+    rate = lax.rsqrt(jnp.mean(middle * middle, axis=-1, keepdims=True) + EPS)
+    normed_ref[...] = (middle * rate * gain_ref[...]).astype(bf)
+    keep.wait()
+    scatter.finish()
+
+
+def out_project(mixed, w_out, piece, x_own, gain, collective):
+    rows, feat = x_own.shape
+    width = mixed.shape[2]
+    sd = jax.ShapeDtypeStruct
+    return pl.pallas_call(
+        out_kernel,
+        in_specs=[ANY, ANY, ANY, VM, VM],
+        out_specs=[VM, VM, ANY],
+        out_shape=[sd((rows, feat), f32), sd((rows, feat), bf), sd(mixed.shape, bf)],
+        scratch_shapes=scatter_scratch(rows, feat)
+        + [
+            pltpu.VMEM(mixed.shape, bf),
+            pltpu.VMEM((width, feat), bf),
+            pltpu.VMEM((rows, feat), f32),
+            pltpu.SemaphoreType.DMA((2,)),
+            pltpu.SemaphoreType.DMA((8,)),
+            pltpu.SemaphoreType.DMA,
+        ],
+        compiler_params=pltpu.CompilerParams(collective_id=collective, has_side_effects=True, vmem_limit_bytes=60 << 20),
+        cost_estimate=lasting(44),
+        name="out_project",
+    )(mixed, w_out, piece, x_own, gain)
+
+
+def back_kernel(
+    grads_ref, wgu_ref, out_ref, piece_ref, middle_ref, y_ref, gain_ref,
+    mid_ref, gmix_ref, dgain_ref,
+    give, take, acc, diag_in, last_in, s_core, r_core, s_link, r_link,
+    lhs, wgu, w, total, buf, gstage, y_own, load_sem, lhs_sem, ag_send, ag_recv, mid_sem, gmix_sem,
+):
+    gx, gy = lax.axis_index("gx"), lax.axis_index("gy")
     rows, feat = middle_ref.shape
-    width = gmix_ref.shape[2]
     tile = 512
+    load = pltpu.make_async_copy(wgu_ref, wgu, load_sem.at[2])
+    outs = own_out_rows(out_ref, piece_ref, w, load_sem, gy)
     order = (7, 6, 4, 5, 2, 3, 1, 0)
-    loads = [pltpu.make_async_copy(wgu_ref, wgu, load_sem.at[0])]
     pulls = {r: pltpu.make_async_copy(grads_ref.at[r], lhs.at[r], lhs_sem.at[r]) for r in order}
     pulls[7].start()
-    loads[0].start()
+    load.start()
     for r in order[1:]:
         pulls[r].start()
-    loads.append(pltpu.make_async_copy(out_ref, w_out, load_sem.at[1]))
-    loads[1].start()
-    entry_barrier([slot_peer(r, gx, gy) for r in range(1, 8)])
-    loads[0].wait()
+    outs.append(pltpu.make_async_copy(y_ref.at[0], y_own, load_sem.at[3]))
+    for c in outs:
+        c.start()
+    entry_barrier([slot_peer(r, gx, gy) for r in (1, 2, 3)])
+    load.wait()
 
     def product(slot, put):
         pulls[slot].wait()
@@ -711,58 +956,56 @@
     rate = lax.rsqrt(jnp.mean(middle * middle, axis=-1, keepdims=True) + EPS)
     scaled = gain_ref[...] * incoming
     inner = jnp.mean(middle * scaled, axis=-1, keepdims=True)
+    for c in outs:
+        c.wait()
+    buf[0] = (y_own[...].astype(f32) + rate * scaled - middle * (rate * rate * rate) * inner).astype(bf)
+    gather = Gather(buf, ag_send, ag_recv, gx, gy)
+    gather.start()
     dgain_ref[...] = jnp.sum((incoming * middle * rate).reshape(rows // 8, 8, feat), axis=0)
-    gm = y_ref[...].astype(f32) + rate * scaled - middle * (rate * rate * rate) * inner
-    mid_low[...] = gm.astype(bf)
-    gm_ref[...] = mid_low[...]
-    loads[1].wait()
-    v = gy * ngx + gx
-    sends = []
-    for r in (6, 7, 2, 4, 3, 5, 1, 0):
+    stores = []
+    for r in range(8):
+        gather.step(r)
         px, py = slot_place(r, gx, gy)
-        rows_w = pl.ds(pl.multiple_of(py * width, width), width)
-        part = nt_dot(mid_low[:, : feat // 2], w_out[px * 2, rows_w, :]) + nt_dot(mid_low[:, feat // 2 :], w_out[px * 2 + 1, rows_w, :])
-        gsend[r] = part.astype(bf)
-        if r == 0:
-            keep = pltpu.make_async_copy(gsend.at[0], gmix_ref.at[v], keep_sem)
-            keep.start()
-        else:
-            c = remote(gsend.at[r], gmix_ref.at[v], a2a_send.at[r], a2a_recv.at[r], slot_peer(r, gx, gy))
+        gstage[r] = nt_dot(buf[r], w[...]).astype(bf)
+        stores.append(pltpu.make_async_copy(gstage.at[r], gmix_ref.at[py * 4 + px], gmix_sem.at[r]))
+        stores.append(pltpu.make_async_copy(buf.at[r], mid_ref.at[r], mid_sem.at[r]))
+        for c in stores[-2:]:
             c.start()
-            sends.append(c)
-    keep.wait()
-    for c in sends:
-        c.wait_recv()
-    for c in sends:
-        c.wait_send()
+    for c in stores:
+        c.wait()
+    gather.finish()
     scatter.finish()
 
 
-def mlp_backward(grads, gate_up, out_all, middle, y_own, gain, width, collective):
+def mlp_backward(grads, gate_up, w_out, piece, middle, y_rel, gain, collective):
     rows, feat = middle.shape
+    width = piece.shape[0]
     sd = jax.ShapeDtypeStruct
     return pl.pallas_call(
         back_kernel,
-        in_specs=[ANY, ANY, ANY, VM, VM, VM],
-        out_specs=[VM, ANY, VM],
-        out_shape=[sd((rows, feat), bf), sd((8, rows, width), bf), sd((8, feat), f32)],
+        in_specs=[ANY, ANY, ANY, ANY, VM, ANY, VM],
+        out_specs=[ANY, ANY, VM],
+        out_shape=[sd((8, rows, feat), bf), sd((8, rows, width), bf), sd((8, feat), f32)],
         scratch_shapes=scatter_scratch(rows, feat)
         + [
             pltpu.VMEM(grads.shape, bf),
             pltpu.VMEM(gate_up.shape, bf),
-            pltpu.VMEM(out_all.shape, bf),
+            pltpu.VMEM((width, feat), bf),
             pltpu.VMEM((rows, feat), f32),
+            pltpu.VMEM((8, rows, feat), bf),
+            pltpu.VMEM((8, rows, width), bf),
             pltpu.VMEM((rows, feat), bf),
-            pltpu.VMEM((8, rows, width), bf),
-            pltpu.SemaphoreType.DMA((2,)),
+            pltpu.SemaphoreType.DMA((4,)),
+            pltpu.SemaphoreType.DMA((8,)),
+            pltpu.SemaphoreType.DMA((13,)),
+            pltpu.SemaphoreType.DMA((13,)),
             pltpu.SemaphoreType.DMA((8,)),
             pltpu.SemaphoreType.DMA((8,)),
-            pltpu.SemaphoreType.DMA((8,)),
-            pltpu.SemaphoreType.DMA,
         ],
         compiler_params=pltpu.CompilerParams(collective_id=collective, has_side_effects=True, vmem_limit_bytes=63 << 20),
+        cost_estimate=lasting(20),
         name="mlp_backward",
-    )(grads, gate_up, out_all, middle, y_own, gain)
+    )(grads, gate_up, w_out, piece, middle, y_rel, gain)
 
 
 def scatter_kernel(lhs_ref, w_ref, out_ref, give, take, acc, diag_in, last_in, s_core, r_core, s_link, r_link, lhs, w, total, load_sem, lhs_sem, *, slots, transposed):
@@ -819,11 +1062,9 @@
             pltpu.SemaphoreType.DMA((8,)),
         ],
         compiler_params=pltpu.CompilerParams(collective_id=collective, has_side_effects=True, vmem_limit_bytes=60 << 20),
+        cost_estimate=lasting(5),
         name="product_scatter",
     )(lhs, w)
-
-
-TOKENS = ("gy", "gx")
 
 
 def dot(a, b):
@@ -856,14 +1097,6 @@
     )
 
 
-def gather_blocks(value):
-    nb, rows, width = value.shape
-    many = lax.all_gather(value, ("gx", "gy"), axis=0, tiled=False)
-    ngx, ngy = lax.axis_size("gx"), lax.axis_size("gy")
-    many = many.reshape(ngx, ngy, nb, rows, width)
-    return many.transpose(2, 0, 3, 1, 4).reshape(nb, ngx * rows, ngy * width)
-
-
 def to_final(own):
     mine, other = halves(own, 1)
     return in_order(mine[None], swap(other)[None], 0)
@@ -877,12 +1110,15 @@
     return lax.psum_scatter(value.astype(bf), "dp", scatter_dimension=0, tiled=True)
 
 
-def rows_to_dp(grad, ndp):
-    rows, cols = grad.shape
-    parts = grad.astype(bf).reshape(2, ndp, rows // (2 * ndp), cols).transpose(1, 0, 2, 3)
-    summed = scatter_dp(parts.reshape(rows, cols))
-    mine, other = halves(summed, 0)
-    return mine, swap(other)
+def rows_to_dp(left, right):
+    part = left.shape[1] // 2
+    halves_of = [dot_w(left[:, i * part : (i + 1) * part], right).astype(bf) for i in range(2)]
+    return halves_of
+
+
+def sort_halves(parts):
+    first = lax.axis_index("gy") == 0
+    return jnp.where(first, parts[0], parts[1]), swap(jnp.where(first, parts[1], parts[0]))
 
 
 def sum_axis(value, axis):
@@ -892,19 +1128,6 @@
         value = value + lax.ppermute(value, axis, [(i, i ^ step) for i in range(size)])
         step *= 2
     return value
-
-
-def spread(value, ndp):
-    part = value.shape[0] // ndp
-    dp = lax.axis_index("dp")
-    piece = swap(lax.dynamic_slice_in_dim(value, dp * part, part, 0))
-    if ndp & (ndp - 1) or ndp > 4:
-        return lax.all_gather(piece, "dp", axis=0, tiled=True)
-    out = lax.dynamic_update_slice_in_dim(jnp.zeros(value.shape, value.dtype), piece, dp * part, 0)
-    for step in range(1, ndp):
-        got = lax.ppermute(piece, "dp", [(i, i ^ step) for i in range(ndp)])
-        out = lax.dynamic_update_slice_in_dim(out, got, (dp ^ step) * part, 0)
-    return out
 
 
 def shards(
@@ -927,74 +1150,83 @@
 ):
     ngx, ngy, ndp = lax.axis_size("gx"), lax.axis_size("gy"), lax.axis_size("dp")
     gx, gy = lax.axis_index("gx"), lax.axis_index("gy")
-    x_all = gather_blocks(inputs)
-    nb, length, feat = x_all.shape
+    nb, part_rows, part_feat = inputs.shape
+    length, feat = part_rows * ngx, part_feat * ngy
     tokens = nb * length
     own_rows = tokens // (ngx * ngy)
-    own_start = (gy * ngx + gx) * own_rows
     heads = w_beta.shape[1] // ngy
     width = w_query.shape[1] // ngy
-
-    cat = [halves(w, 1) for w in (w_query, w_key, w_value, w_gate_head)]
-    pad = ((0, 0), (0, 128 - heads))
-    beta_mine, beta_other = halves(w_beta, 1)
-    head_w = in_order(
-        jnp.concatenate([m for m, _ in cat] + [jnp.pad(beta_mine, pad)], axis=1),
-        swap(jnp.concatenate([o for _, o in cat] + [jnp.pad(beta_other, pad)], axis=1)),
-        0,
-    )
-
+    beta_w = jnp.pad(w_beta.T.reshape(ngy, heads, part_feat), ((0, 0), (0, 128 - heads), (0, 0))).reshape(ngy * 128, part_feat).T
     block = w_gate.shape[1]
     units = -(-block // (ngy * 256)) * 256
-    unit_mine, unit_other = gy * (block - units), (1 - gy) * (block - units)
-
-    def pick(w, start, axis):
-        return lax.dynamic_slice_in_dim(w, start, units, axis)
-
-    fresh_unit = (lax.broadcasted_iota(jnp.int32, (1, units), 1) >= gy * (2 * units - block)).astype(bf)
-    gate_up = in_order(
-        jnp.concatenate([pick(w_gate, unit_mine, 1), pick(w_up, unit_mine, 1)], axis=1),
-        spread(jnp.concatenate([pick(w_gate, unit_other, 1), pick(w_up, unit_other, 1)], axis=1), ndp),
-        0,
-    ) * jnp.concatenate([fresh_unit, fresh_unit], axis=1)
-    down_w = in_order(pick(w_down, unit_mine, 0), spread(pick(w_down, unit_other, 0), ndp), 1)
-    out_all = lax.all_gather(w_out, ("gx", "gy"), axis=0, tiled=False)
+    parts = ndp if ndp == 4 else 1
+    normed, raw, head_w, x_own, gu_piece, out_piece = head_project(
+        inputs.reshape(nb * part_rows, part_feat), w_query, w_key, w_value, w_gate_head, beta_w, w_gate, w_up, w_out,
+        norm_gain[None], units, parts, 5,
+    )
+    normed = normed.reshape(tokens, feat)
+    raw = raw.reshape(nb, length, -1)
+
+    def around(value):
+        return [value] + [lax.ppermute(value, "dp", [(i, i ^ n) for i in range(ndp)]) for n in range(1, parts)]
+
+    gu_pieces = around(gu_piece)
+    x_own, grad_y, w_down = lax.optimization_barrier((x_own, grad_y, w_down))
+    down_piece = swap(lax.dynamic_slice_in_dim(w_down, (1 - gy) * (block - units), units, 0))
     y_all = lax.all_gather(grad_y, ("gx", "gy"), axis=0, tiled=False)
 
-    aux, segrow = make_aux(segments)
-    x_flat = x_all.reshape(tokens, feat)
-    x_wide = x_flat.astype(f32)
-    rate_first = rate_of(x_wide)
-    normed = (x_wide * rate_first * norm_gain).astype(bf)
-    raw = dot(normed, head_w).reshape(nb, length, -1)
+    aux = make_aux(segments)
     conv_start = (gx * ngy + gy) * width
     conv_local = lax.dynamic_slice_in_dim(conv_kernel, conv_start, width, 2)
     gain_row = head_gain[None]
-    mixed, *saved = mixer_fwd(raw, aux, segrow, conv_local, gain_row)
-    x_own = lax.dynamic_slice_in_dim(x_flat, own_start, own_rows, 0)
-    middle, second, hidden, grads, y_rel = mlp_forward(
-        mixed.reshape(8, own_rows, width), out_all, x_own, mlp_gain[None], gate_up, down_w, y_all, 1
+    mixed, *saved = mixer_fwd(raw, aux, conv_local, gain_row)
+    middle, second_own, mixed_slots = out_project(
+        mixed.reshape(8, own_rows, width), w_out, out_piece, x_own, mlp_gain[None], 1
+    )
+    second, hidden, grads, y_rel, gate_up, down_w = mlp_forward(
+        second_own, w_gate, w_up, w_down, y_all, gu_pieces, down_piece, units, 6
     )
     second_flat, hidden_flat = second.reshape(tokens, feat), hidden.reshape(tokens, units)
     grads_flat, y_flat = grads.reshape(tokens, 2 * units), y_rel.reshape(tokens, feat)
-    down_keep, down_send = halves(dot_w(hidden_flat, y_flat).astype(bf), 1)
+    half = feat // 2
+    gu_first = dot_w(second_flat[:, :half], grads_flat).astype(bf)
+    hidden_flat, gu_first = lax.optimization_barrier((hidden_flat, gu_first))
+    down_grad = dot_w(hidden_flat, y_flat).astype(bf)
+    second_flat, down_grad = lax.optimization_barrier((second_flat, down_grad))
+    down_keep, down_send = halves(down_grad, 1)
     down_both = jnp.stack([down_keep, swap(down_send)])
+    gu_second = dot_w(second_flat[:, half:], grads_flat).astype(bf)
+    grads, gu_second = lax.optimization_barrier((grads, gu_second))
+    gu_sums = [scatter_dp(gu_first), scatter_dp(gu_second)]
     first, last = down_both[gy], down_both[1 - gy]
     down_rows = jnp.concatenate([first, last[2 * units - block :]], axis=0)
-    sum_down = scatter_dp(down_rows).astype(f32)
-    grad_gu_mine, grad_gu_other = rows_to_dp(dot_w(second_flat, grads_flat), ndp)
-
-    mid_low, grad_mixed, mlp_gain_parts = mlp_backward(
-        grads, gate_up, out_all, middle, y_rel[0], mlp_gain[None], width, 2
+
+    mid_slots, grad_mixed, mlp_gain_parts = mlp_backward(
+        grads, gate_up, w_out, out_piece, middle, y_rel, mlp_gain[None], 2
     )
+    grad_mixed, mid_slots, down_rows, *gu_sums = lax.optimization_barrier((grad_mixed, mid_slots, down_rows, *gu_sums))
+    down_sum = scatter_dp(down_rows)
+    mid_low = mid_slots[0]
+    out_grad = dot_w(mixed_slots.reshape(tokens, width), mid_slots.reshape(tokens, feat)).astype(bf)
+    out_keep, out_send = halves(out_grad, 1)
+    out_rows = in_order(out_keep, swap(out_send), 0)
     draw, conv_grad, gain_grad = mixer_bwd(
-        raw, aux, segrow, conv_local, gain_row, saved, grad_mixed.reshape(nb, length, width)
+        raw, aux, conv_local, gain_row, saved, grad_mixed.reshape(nb, length, width)
     )
     draw = draw.reshape(tokens, -1)
-    grad_head_w = dot_w(normed, draw)
-    norm_gain_grad = jnp.sum(grad_head_w * head_w.astype(f32), axis=1) / norm_gain
-    head_mine, head_other = rows_to_dp(grad_head_w, ndp)
-    mid_all = lax.all_gather(mid_low, TOKENS, axis=0, tiled=True)
+    draw, down_sum, out_rows = lax.optimization_barrier((draw, down_sum, out_rows))
+    out_sum = scatter_dp(out_rows)
+    main = 4 * width
+    head_grads = rows_to_dp(normed, draw[:, :main])
+    beta_grad = dot_w(normed, draw[:, main:])
+    norm_gain_grad = (
+        jnp.sum(jnp.concatenate(head_grads, axis=0).astype(f32) * head_w[:, :main].astype(f32), axis=1)
+        + jnp.sum(beta_grad * head_w[:, main:].astype(f32), axis=1)
+    ) / norm_gain
+    draw, hidden, out_sum, *head_grads = lax.optimization_barrier((draw, hidden, out_sum, *head_grads))
+    sum_down, sum_out = down_sum.astype(f32), out_sum.astype(f32)
+    grad_gu_mine, grad_gu_other = sort_halves(gu_sums)
+    head_sums = [scatter_dp(g) for g in head_grads]
     grad_normed = product_scatter(draw.reshape(8, own_rows, -1), head_w, 3, False, False)
     x_wide_own = x_own.astype(f32)
     rate_own = rate_of(x_wide_own)
@@ -1004,8 +1236,7 @@
     grad_inputs = to_final((mid_low.astype(f32) + norm_one).astype(bf))
     layer_out = to_final((middle + product_scatter(hidden, down_w, 4, True, True)).astype(bf))
 
-    out_keep, out_send = halves(dot_w(mixed.reshape(tokens, width), mid_all).astype(bf), 1)
-    sum_out = scatter_dp(in_order(out_keep, swap(out_send), 0)).astype(f32)
+    head_mine, head_other = sort_halves(head_sums)
 
     def unit_columns(i):
         part = slice(i * units, (i + 1) * units)
@@ -1018,10 +1249,17 @@
         return in_order(head_mine[:, i : i + n], head_other[:, i : i + n], 1).astype(f32)
 
     sum_query, sum_key, sum_value, sum_head_gate = (head_part(i * width, width) for i in range(4))
-    sum_beta = head_part(4 * width, heads)
-
-    small = jnp.concatenate([conv_grad.reshape(-1), norm_gain_grad, jnp.sum(mlp_gain_parts, axis=0), gain_grad])
+
+    small = jnp.concatenate(
+        [beta_grad[:, :heads].T.reshape(-1), conv_grad.reshape(-1), norm_gain_grad, jnp.sum(mlp_gain_parts, axis=0), gain_grad]
+    )
     small = sum_axis(small, "dp")
+    beta_sum, small = small[: heads * feat].reshape(heads, feat), small[heads * feat :]
+    beta_rows = feat // (ngy * ndp)
+    beta_mine, beta_other = (
+        lax.dynamic_slice_in_dim(beta_sum, (side * ndp + lax.axis_index("dp")) * beta_rows, beta_rows, 1) for side in (gy, 1 - gy)
+    )
+    sum_beta = in_order(beta_mine, swap(beta_other), 0).T
     n_conv = conv_grad.size
     conv_full = lax.dynamic_update_slice_in_dim(
         jnp.zeros(conv_kernel.shape, f32), small[:n_conv].reshape(conv_grad.shape), conv_start, 2

time: 1010 us -> 701 us (0.69)
  waiting for transfers between devices: 308 us -> 43.8 us
  Pallas kernels: 335 us -> 494 us
  local copies, waits for them, and re-layouts: 135 us -> 18.2 us
  other arithmetic: 106 us -> 35.1 us
  starting transfers between devices: 39.6 us -> 22.9 us
    pallas_call x2 -> x4, Pallas kernels: 131 us -> 306 us  [the longest x1 109 us: mlp_backward(): pl.pallas_call(back_kernel, in_specs=[ANY, ANY, ANY, ANY, VM, ANY, VM], o...]
    ppermute x9 -> x8, waiting for transfers between devices: 170 us -> 15.2 us  [swap(): return lax.ppermute(value, 'gy', [(0, 1), (1, 0)])]
    reduce_scatter x4 -> x6, waiting for transfers between devices: 78 us -> 10.5 us  [scatter_dp(): lax.psum_scatter(value.astype(bf), 'dp', scatter_dimension=0, tiled=True)]
    ppermute x6 -> x3, waiting for transfers between devices: 46.2 us -> 0.01 us  [around(): lax.ppermute(value, 'dp', [(i, i ^ n) for i in range(ndp)])]
    unnamed x80 -> x51, local copies, waits for them, and re-layouts: 35.9 us -> 3.25 us
    reduce_sum x2 -> x1, other arithmetic: 24.5 us -> 2.24 us  [rate_of(): return lax.rsqrt(jnp.mean(value * value, axis=-1, keepdims=True) + EPS)]
    convert_element_type x1 -> x0, local copies, waits for them, and re-layouts: 22.1 us -> none  [shards(): x_wide = x_flat.astype(f32)]
    another operation x11, local copies, waits for them, and re-layouts: 22.6 us -> 1.49 us  [make_aux(): return jnp.stack(cols, axis=1)]
  transfers between devices with their start and end apart: 28 -> 23, of which waited for: 12 -> 7; matrix products, arithmetic and copies ran while one was open for 23% -> 14% of each run, Pallas kernels for 15% -> 53%
where the time goes in v3:
time: 701 us; the launch traced here: 692 us
  Pallas kernels  494 us (70%)
  matrix products  62.1 us (9%)
  waiting for transfers between devices  43.8 us (6%)
  other arithmetic  35.1 us (5%)
  starting transfers between devices  22.9 us (3%)
  local copies, waits for them, and re-layouts  18.2 us (3%)
  between operations  15.4 us (2%)
    pallas_call x1, Pallas kernels, mlp_backward(): pl.pallas_call(back_kernel, in_specs=[ANY, ANY, ANY, ANY, VM, ANY, VM], o...  109 us
    pallas_call x2, Pallas kernels, product_scatter(): pl.pallas_call(functools.partial(scatter_kernel, slots=slots, transposed=...  94.1 us
    pallas_call x1, Pallas kernels, head_project(): pl.pallas_call(head_kernel, in_specs=[ANY] * 9 + [VM], out_specs=[ANY, AN...  72.8 us
    pallas_call x1, Pallas kernels, out_project(): pl.pallas_call(out_kernel, in_specs=[ANY, ANY, ANY, VM, VM], out_specs=[V...  67 us
    dot_general x7, matrix products, dot_w(): lax.dot_general(a, b, (((0,), (0,)), ((), ())), preferred_element_type=f32)  62.1 us
    pallas_call x1, Pallas kernels, mixer_bwd(): pl.pallas_call(bwd_kernel, grid=(nb, heads), in_specs=specs(length, heads...  60.4 us
    pallas_call x1, Pallas kernels, mlp_forward(): pl.pallas_call(functools.partial(mlp_kernel, parts=parts), in_specs=[ANY]...  57.8 us
    pallas_call x1, Pallas kernels, mixer_fwd(): pl.pallas_call(fwd_kernel, grid=(nb, heads), in_specs=specs(length, heads...  33 us
  transfers between devices with their start and end apart: 23, of which 7 were waited for; matrix products, arithmetic and copies ran while one was open for 14% of the time, Pallas kernels for 53%

profile of v3, /device:TPU:0, one launch (start us, length us, event | category | flops | bytes accessed | tf_op | source)
XLA Modules:
  0.0 691.5 jit_solution(14243758274249768139)
XLA Ops:
  9.0 0.9 copy.84
  9.9 72.8 %head_project.1 = (bf16[8,256,2048]{2,1,0:T(8,128)(2,1)}, f32[8,256,1152]{2,1,0:T(8,128)}, bf16[2048,1152]{1,0:T(8,128)(2,1)}, bf16[256,2048]{1,0:T(8,128)(2,1)}...) custom-call(bf16[512,1024]{1,0:T(8,128)(2,1)} %bitcast.145, bf16[1024,512]{1,0:T(8,128)(2,1)} %wq_ref.1, ...), custom_call_target="tpu_custom_call" | custom-call | flops 92000002048 | bytes 1048576 | tf_op jit(solution)/shard_map/head_project/pallas_call | solution.py:567
  82.8 8.1 %collective-permute-start = (bf16[256,1536]{1,0:T(8,128)(2,1)}, bf16[256,1536]{1,0:T(8,128)(2,1)}, u32[]{:S(2)}, u32[]{:S(2)}) collective-permute-start(bf16[256,1536]{1,0:T(8,128)(2,1)} %get-tuple-element.82.refs_0_), channel_id=1, source_target_pairs={{0,8},{8,0},{16,24},{24,16},{1,9},{9,1},{17,25},{25,17},{2,10},{10... | collective-permute-start | bytes 2359304 | tf_op jit(solution)/shard_map/ppermute | solution.py:1171
  90.9 1.0 collective-permute-start.1
  91.9 1.5 collective-permute-start.2
  93.3 1.5 constant_dynamic-slice_fusion.6
  96.2 1.4 stack.90.aux_ref
  98.2 33.0 %mixer_forward.1 = (bf16[2,1024,256]{2,1,0:T(8,128)(2,1)}, bf16[2,2,1024,128]{3,2,1,0:T(8,128)(2,1)}, bf16[2,2,1024,128]{3,2,1,0:T(8,128)(2,1)}, bf16[2,2,1024,1...) custom-call(f32[2,1024,1152]{2,1,0:T(8,128)} %bitcast.115, ...), custom_call_target="tpu_custom_call" | custom-call | flops 37950001152 | bytes 1048576 | tf_op jit(solution)/shard_map/mixer_forward/pallas_call | solution.py:147
  131.2 67.0 %out_project.1 = (f32[256,2048]{1,0:T(8,128)}, bf16[256,2048]{1,0:T(8,128)(2,1)}, bf16[8,256,256]{2,1,0:T(8,128)(2,1)}) custom-call(bf16[8,256,256]{2,1,0:T(8,128)(2,1)} %bitcast.157, bf16[512,1024]{1,0:T(8,128)(2,1)} %out_ref.5, bf16[256,1024]{1,0:T(8,128)(2,1)} %get-tuple-element.68.piece_ref, bf16[256,2048]{1,0:T(8,128)(2,1)} %get-tuple-element.70.x_ref, ...), custom_call_target="tpu_custom_call" | custom-call | flops 50600001536 | bytes 1048576 | tf_op jit(solution)/shard_map/out_project/pallas_call | solution.py:899
  198.4 1.1 copy-done.19
  199.5 57.8 %mlp_forward.1 = (bf16[8,256,2048]{2,1,0:T(8,128)(2,1)}, bf16[8,256,768]{2,1,0:T(8,128)(2,1)}, bf16[8,256,1536]{2,1,0:T(8,128)(2,1)}, bf16[8,256,2048]{2,1,0:T(8...) custom-call(bf16[256,2048]{1,0:T(8,128)(2,1)} %get-tuple-element.79.x_ref, ...), custom_call_target="tpu_custom_call" | custom-call | flops 78199996416 | bytes 1048576 | tf_op jit(solution)/shard_map/mlp_forward/pallas_call | solution.py:717
  257.3 11.4 %fusion.11 = bf16[1024,1536]{1,0:T(8,128)(2,1)} fusion(bf16[2048,1536]{1,0:T(8,128)(2,1)} %bitcast.154, bf16[2048,2048]{1,0:T(8,128)(2,1)} %bitcast.152), kind=kOutput, calls=%fused_computation.10 | convolution fusion | flops 6444023808 | bytes 13631488 | tf_op jit(solution)/shard_map/dot_general | solution.py:1079
  268.8 10.1 %convolution_convert_fusion = bf16[768,2048]{1,0:T(8,128)(2,1)S(1)} fusion(bf16[2048,768]{1,0:T(8,128)(2,1)} %bitcast.156, bf16[2048,2048]{1,0:T(8,128)(2,1)} %bitcast.151), kind=kOutput, calls=%fused_computation.17 | convolution fusion | flops 6444023808 | bytes 14680064 | tf_op jit(solution)/shard_map/dot_general | solution.py:1079
  278.9 11.4 %fusion.8 = bf16[1024,1536]{1,0:T(8,128)(2,1)} fusion(bf16[2048,1536]{1,0:T(8,128)(2,1)} %bitcast.155, bf16[2048,2048]{1,0:T(8,128)(2,1)} %bitcast.153), kind=kOutput, calls=%fused_computation.9 | convolution fusion | flops 6444023808 | bytes 13631488 | tf_op jit(solution)/shard_map/dot_general | solution.py:1079
  290.4 2.1 constant_dynamic-slice_fusion.5
  292.5 1.5 collective-permute-start.4
  294.0 108.8 %mlp_backward.1 = (bf16[8,256,2048]{2,1,0:T(8,128)(2,1)}, bf16[8,256,256]{2,1,0:T(8,128)(2,1)}, f32[8,2048]{1,0:T(8,128)}) custom-call(bf16[8,256,1536]{2,1,0:T(8,128)(2,1)} %get-tuple-element.89.grads_ref, bf16[2048,1536]{1,0:T(8,128)(2,1)} %get-tuple-element.90.wgu_ref, bf16[512,1024]{1,0:T(8,128)(2,1)} %out_ref.5, ...), custom_call_target="tpu_custom_call" | custom-call | flops 23000000512 | bytes 1048576 | tf_op jit(solution)/shard_map/mlp_backward/pallas_call | solution.py:984
  402.8 2.0 fusion.36
  405.4 1.8 pad_maximum_fusion
  407.6 5.8 fusion.16
  413.4 0.8 constant_dynamic-slice_fusion.4
  414.3 2.4 collective-permute-start.5
  416.9 60.4 %mixer_backward.1 = (bf16[2,1024,1152]{2,1,0:T(8,128)(2,1)}, f32[2,2,12,8,128]{4,3,2,1,0:T(8,128)}, f32[2,2,8,128]{3,2,1,0:T(8,128)}) custom-call(f32[2,1024,1152]{2,1,0:T(8,128)} %bitcast.120, f32[2,1024,1152]{2,1,0:T(8,128)} %bitcast.121, f32[2,1024,1152]{2,1,0:T(8,128)} %bitcast.122, f32[2,1024,1152]{2,1,0:T(8,128)} %bitcast.123, ...), custom_call_target="tpu_custom_call" | custom-call | flops 2300000000 | bytes 1048576 | tf_op jit(solution)/shard_map/mixer_backward/pallas_call | solution.py:294
  477.3 1.0 reduce_sum.65
  479.0 0.9 slice_bitcast_fusion.1
  479.9 1.3 broadcast_select_fusion.5
  481.2 1.0 pad_maximum_fusion.1
  482.3 0.9 slice_bitcast_fusion
  483.3 9.4 %fusion.23 = bf16[1024,1024]{1,0:T(8,128)(2,1)} fusion(bf16[2048,1152]{1,0:T(8,128)(2,1)} %bitcast.141, bf16[2048,2048]{1,0:T(8,128)(2,1)} %bitcast.148), kind=kOutput, calls=%fused_computation.31 | convolution fusion | flops 4296015872 | bytes 10485760 | tf_op jit(solution)/shard_map/dot_general | solution.py:1079
  492.6 8.0 %fusion.28 = bf16[1024,1024]{1,0:T(8,128)(2,1)S(1)} fusion(bf16[2048,1152]{1,0:T(8,128)(2,1)} %bitcast.142, bf16[2048,2048]{1,0:T(8,128)(2,1)} %bitcast.149), kind=kOutput, calls=%fused_computation.32 | convolution fusion | flops 4296015872 | bytes 10485760 | tf_op jit(solution)/shard_map/dot_general | solution.py:1079
  500.7 10.4 %reduce-scatter.13.cloned.1.call-done = bf16[128,1024]{1,0:T(8,128)(2,1)} async-done(((bf16[512,1024]{1,0:T(8,128)(2,1)}), bf16[128,1024]{1,0:T(8,128)(2,1)}) %reduce-scatter.13.cloned.1.call-update) | async-done | bytes 262160 | tf_op jit(solution)/shard_map/reduce_scatter | solution.py:1110
  511.4 5.8 fusion.37
  517.3 1.8 copy.70
  519.0 0.8 slice_bitcast_fusion.4
  519.9 1.4 multiply_reduce_fusion.1
  521.3 3.6 multiply_reduce_fusion
  525.5 5.6 collective-permute-done.8
  531.3 1.2 maximum_convert_fusion
  532.5 7.6 %collective-permute-done.9 = f32[11392]{0:T(1024)S(1)} collective-permute-done((f32[11392]{0:T(1024)S(1)}, f32[11392]{0:T(1024)S(1)}, u32[]{:S(2)}, u32[]{:S(2)}) %collective-permute-start.9) | collective-permute-done | bytes 45600 | tf_op jit(solution)/shard_map/ppermute | solution.py:1128
  540.7 1.5 collective-permute-start.14
  542.3 1.5 collective-permute-start.11
  543.9 1.2 maximum_convert_fusion.1
  545.1 1.3 convert_element_type.117
  546.3 1.4 collective-permute-done.11
  547.7 0.9 collective-permute-start.12
  549.2 3.4 collective-permute-done.12
  554.4 45.6 %product_scatter.2 = f32[256,2048]{1,0:T(8,128)} custom-call(bf16[8,256,768]{2,1,0:T(8,128)(2,1)} %get-tuple-element.104.lhs_ref, bf16[768,2048]{1,0:T(8,128)(2,1)} %get-tuple-element.105.w_ref), custom_call_target="tpu_custom_call" | custom-call | flops 5750000128 | bytes 1048576 | tf_op jit(solution)/shard_map/product_scatter/pallas_call | solution.py:1051
  600.1 1.9 add_convert_fusion
  602.0 0.8 constant_dynamic-slice_fusion.3
  603.6 48.4 %product_scatter.3 = f32[256,2048]{1,0:T(8,128)} custom-call(bf16[8,256,1152]{2,1,0:T(8,128)(2,1)} %bitcast.144, bf16[2048,1152]{1,0:T(8,128)(2,1)} %get-tuple-element.107.w_ref), custom_call_target="tpu_custom_call" | custom-call | flops 5750000128 | bytes 1048576 | tf_op jit(solution)/shard_map/product_scatter/pallas_call | solution.py:1051
  652.1 2.2 fusion.17
  654.4 2.0 fusion.21
  658.1 1.3 select_bitcast_fusion.3
  659.5 1.3 broadcast_select_fusion.3
  660.8 1.3 collective-permute-start.13
  662.1 1.1 pad_maximum_fusion.2
  663.2 8.3 %collective-permute-done.7 = bf16[256,1024]{1,0:T(8,128)(2,1)} collective-permute-done((bf16[256,1024]{1,0:T(8,128)(2,1)S(1)}, bf16[256,1024]{1,0:T(8,128)(2,1)}, u32[]{:S(2)}, u32[]{:S(2)}) %collective-permute-start.7) | collective-permute-done | bytes 524320 | tf_op jit(solution)/shard_map/ppermute | solution.py:1083
  671.5 1.3 select_bitcast_fusion.1
  672.8 1.1 pad_maximum_fusion.3
  673.9 6.8 collective-permute-done.13
  680.8 0.9 maximum_convert_fusion.2
  681.7 0.9 maximum_convert_fusion.3
  682.5 0.9 maximum_convert_fusion.4
  683.4 0.9 maximum_convert_fusion.5
  (143 shorter events, 12.3 us)
Async XLA Ops:
  7.2 90.4 %copy-start = (f32[3,4,2048]{2,1,0:T(4,128)S(1)}, f32[3,4,2048]{2,1,0:T(4,128)}, u32[]{:S(2)}) copy-start(f32[3,4,2048]{2,1,0:T(4,128)} %param.24) | copy-start | bytes 294916
  7.2 191.2 %all-gather.3.cloned.1.call-start = ((), (), s32[]{:S(2)}) async-start(), calls=%async_computation.12 | async-start | bytes 9437184 | tf_op jit(solution)/shard_map/all_gather | solution.py:1176
  82.7 12.6 %copy-start.18 = (s32[2,1024]{1,0:T(2,128)S(1)}, s32[2,1024]{1,0:T(2,128)}, u32[]{:S(2)}) copy-start(s32[2,1024]{1,0:T(2,128)} %param.17) | copy-start | bytes 24580
  82.7 324.5 %reduce-scatter.7.cloned.1.call-start = ((), (), s32[]{:S(2)}) async-start(), calls=%async_computation.6 | async-start | bytes 3932160 | tf_op jit(solution)/shard_map/reduce_scatter | solution.py:1110
  82.8 115.5 %collective-permute-start = (bf16[256,1536]{1,0:T(8,128)(2,1)}, bf16[256,1536]{1,0:T(8,128)(2,1)}, u32[]{:S(2)}, u32[]{:S(2)}) collective-permute-start(bf16[256,1536]{1,0:T(8,128)(2,1)} %get-tuple-element.82.refs_0_), channel_id=1, source_target_pairs={{0,8},{8,0},{16,24},{24,16},{1,9},{9,1},{17,25},{25,17},{2,10},{10... | collective-permute-start | bytes 2359304 | tf_op jit(solution)/shard_map/ppermute | solution.py:1171
  90.9 107.4 %collective-permute-start.1 = (bf16[256,1536]{1,0:T(8,128)(2,1)}, bf16[256,1536]{1,0:T(8,128)(2,1)}, u32[]{:S(2)}, u32[]{:S(2)}) collective-permute-start(bf16[256,1536]{1,0:T(8,128)(2,1)} %get-tuple-element.82.refs_0_), channel_id=1, source_target_pairs={{0,16},{8,24},{16,0},{24,8},{1,17},{9,25},{17,1},{25,9},{2,18},{10... | collective-permute-start | bytes 2359304 | tf_op jit(solution)/shard_map/ppermute | solution.py:1171
  91.9 106.4 %collective-permute-start.2 = (bf16[256,1536]{1,0:T(8,128)(2,1)}, bf16[256,1536]{1,0:T(8,128)(2,1)}, u32[]{:S(2)}, u32[]{:S(2)}) collective-permute-start(bf16[256,1536]{1,0:T(8,128)(2,1)} %get-tuple-element.82.refs_0_), channel_id=1, source_target_pairs={{0,24},{8,16},{16,8},{24,0},{1,25},{9,17},{17,9},{25,1},{2,26},{10... | collective-permute-start | bytes 2359304 | tf_op jit(solution)/shard_map/ppermute | solution.py:1171
  94.9 103.4 %collective-permute-start.3 = (bf16[768,1024]{1,0:T(8,128)(2,1)S(1)}, bf16[768,1024]{1,0:T(8,128)(2,1)S(1)}, u32[]{:S(2)}, u32[]{:S(2)}) collective-permute-start(bf16[768,1024]{1,0:T(8,128)(2,1)S(1)} %constant_dynamic-slice_fusion.6), channel_id=1, source_target_pairs={{0,1},{1,0},{2,3},{3,2},{4,5},{5,4},{6,7},{7,6},{8,9},{9,8},{10,11... | collective-permute-start | bytes 4718600 | tf_op jit(solution)/shard_map/ppermute | solution.py:1083
  198.3 1.2 copy-start.19
  268.7 138.5 %reduce-scatter.9.cloned.1.call-start = ((), (), s32[]{:S(2)}) async-start(), calls=%async_computation.7 | async-start | bytes 3932160 | tf_op jit(solution)/shard_map/reduce_scatter | solution.py:1110
  290.4 192.8 %reduce-scatter.11.cloned.1.call-start = ((), (), s32[]{:S(2)}) async-start(), calls=%async_computation.8 | async-start | bytes 3604480 | tf_op jit(solution)/shard_map/reduce_scatter | solution.py:1110
  292.5 110.2 %collective-permute-start.4 = (bf16[768,1024]{1,0:T(8,128)(2,1)}, bf16[768,1024]{1,0:T(8,128)(2,1)}, u32[]{:S(2)}, u32[]{:S(2)}) collective-permute-start(bf16[768,1024]{1,0:T(8,128)(2,1)} %get-tuple-element.119), channel_id=1, source_target_pairs={{0,1},{1,0},{2,3},{3,2},{4,5},{5,4},{6,7},{7,6},{8,9},{9,8},{10,11... | collective-permute-start | bytes 4718600 | tf_op jit(solution)/shard_map/ppermute | solution.py:1083
  402.7 2.1 copy-start.2
  405.4 2.1 copy-start.17
  405.4 2.1 copy-start.11
  407.3 103.8 %reduce-scatter.13.cloned.1.call-start = ((), (), s32[]{:S(2)}) async-start(), calls=%async_computation.9 | async-start | bytes 1310720 | tf_op jit(solution)/shard_map/reduce_scatter | solution.py:1110
  407.6 9.1 %copy-start.12 = (bf16[256,1536]{1,0:T(8,128)(2,1)S(1)}, bf16[256,1536]{1,0:T(8,128)(2,1)}, u32[]{:S(2)}) copy-start(bf16[256,1536]{1,0:T(8,128)(2,1)} %reduce-scatter.7.cloned.1.call-done) | copy-start | bytes 2359300
  407.6 9.1 %copy-start.13 = (bf16[256,1536]{1,0:T(8,128)(2,1)S(1)}, bf16[256,1536]{1,0:T(8,128)(2,1)}, u32[]{:S(2)}) copy-start(bf16[256,1536]{1,0:T(8,128)(2,1)} %reduce-scatter.9.cloned.1.call-done) | copy-start | bytes 2359300
  414.3 65.6 %collective-permute-start.5 = (bf16[256,1024]{1,0:T(8,128)(2,1)}, bf16[256,1024]{1,0:T(8,128)(2,1)}, u32[]{:S(2)}, u32[]{:S(2)}) collective-permute-start(bf16[256,1024]{1,0:T(8,128)(2,1)} %constant_dynamic-slice_fusion.4), channel_id=1, source_target_pairs={{0,1},{1,0},{2,3},{3,2},{4,5},{5,4},{6,7},{7,6},{8,9},{9,8},{10,11... | collective-permute-start | bytes 1572872 | tf_op jit(solution)/shard_map/ppermute | solution.py:1083
  416.8 65.5 %collective-permute-start.15 = (bf16[256,1536]{1,0:T(8,128)(2,1)S(1)}, bf16[256,1536]{1,0:T(8,128)(2,1)S(1)}, u32[]{:S(2)}, u32[]{:S(2)}) collective-permute-start(bf16[256,1536]{1,0:T(8,128)(2,1)S(1)} %get-tuple-element.121), channel_id=1, source_target_pairs={{0,1},{1,0},{2,3},{3,2},{4,5},{5,4},{6,7},{7,6},{8,9},{9,8},{10,11... | collective-permute-start | bytes 2359304 | tf_op jit(solution)/shard_map/ppermute | solution.py:1083
  483.2 176.2 %reduce-scatter.15.cloned.1.call-start = ((), (), s32[]{:S(2)}) async-start(), calls=%async_computation.10 | async-start | bytes 2621440 | tf_op jit(solution)/shard_map/reduce_scatter | solution.py:1110
  500.7 20.6 %copy-start.3 = (bf16[1024,1024]{1,0:T(8,128)(2,1)}, bf16[1024,1024]{1,0:T(8,128)(2,1)S(1)}, u32[]{:S(2)}) copy-start(bf16[1024,1024]{1,0:T(8,128)(2,1)S(1)} %fusion.28) | copy-start | bytes 6291460
  511.2 148.3 %reduce-scatter.17.cloned.1.call-start = ((), (), s32[]{:S(2)}) async-start(), calls=%async_computation.11 | async-start | bytes 2621440 | tf_op jit(solution)/shard_map/reduce_scatter | solution.py:1110
  521.3 3.6 copy-start.16
  521.3 3.8 copy-start.9
  521.3 3.8 copy-start.10
  525.0 15.4 %copy-start.7 = (bf16[1,256,768]{2,1,0:T(8,128)(2,1)S(1)}, bf16[1,256,768]{2,1,0:T(8,128)(2,1)}, u32[]{:S(2)}) copy-start(bf16[1,256,768]{2,1,0:T(8,128)(2,1)} %get-tuple-element.143) | copy-start | bytes 1179652
  525.0 15.4 %copy-start.8 = (bf16[1,256,768]{2,1,0:T(8,128)(2,1)S(1)}, bf16[1,256,768]{2,1,0:T(8,128)(2,1)}, u32[]{:S(2)}) copy-start(bf16[1,256,768]{2,1,0:T(8,128)(2,1)} %get-tuple-element.141) | copy-start | bytes 1179652
  525.0 6.1 collective-permute-start.8
  531.1 9.0 %collective-permute-start.9 = (f32[11392]{0:T(1024)S(1)}, f32[11392]{0:T(1024)S(1)}, u32[]{:S(2)}, u32[]{:S(2)}) collective-permute-start(f32[11392]{0:T(1024)S(1)} %add.123), channel_id=1, source_target_pairs={{0,16},{8,24},{16,0},{24,8},{1,17},{9,25},{17,1},{25,9},{2,18},{10... | collective-permute-start | bytes 136712 | tf_op jit(solution)/shard_map/ppermute | solution.py:1128
  540.2 2.0 collective-permute-start.10
  540.3 4.7 copy-start.14
  540.7 7.8 %collective-permute-start.14 = (f32[2,256]{1,0:T(2,128)S(1)}, f32[2,256]{1,0:T(2,128)S(1)}, u32[]{:S(2)}, u32[]{:S(2)}) collective-permute-start(f32[2,256]{1,0:T(2,128)S(1)} %constant_dynamic-slice_fusion), channel_id=1, source_target_pairs={{0,1},{1,0},{2,3},{3,2},{4,5},{5,4},{6,7},{7,6},{8,9},{9,8},{10,11... | collective-permute-start | bytes 6152 | tf_op jit(solution)/shard_map/ppermute | solution.py:1083
  542.3 5.4 collective-permute-start.11
  547.7 4.9 collective-permute-start.12
  554.4 45.7 %copy-start.6 = (f32[256,2048]{1,0:T(8,128)S(1)}, f32[256,2048]{1,0:T(8,128)}, u32[]{:S(2)}) copy-start(f32[256,2048]{1,0:T(8,128)} %get-tuple-element.71.middle_ref) | copy-start | bytes 6291460
  602.8 55.3 %collective-permute-start.6 = (bf16[256,1024]{1,0:T(8,128)(2,1)}, bf16[256,1024]{1,0:T(8,128)(2,1)}, u32[]{:S(2)}, u32[]{:S(2)}) collective-permute-start(bf16[256,1024]{1,0:T(8,128)(2,1)} %constant_dynamic-slice_fusion.3), channel_id=1, source_target_pairs={{0,1},{1,0},{2,3},{3,2},{4,5},{5,4},{6,7},{7,6},{8,9},{9,8},{10,11... | collective-permute-start | bytes 1572872 | tf_op jit(solution)/shard_map/ppermute | solution.py:1083
  603.6 48.4 %copy-start.5 = (bf16[256,2048]{1,0:T(8,128)(2,1)S(1)}, bf16[256,2048]{1,0:T(8,128)(2,1)}, u32[]{:S(2)}) copy-start(bf16[256,2048]{1,0:T(8,128)(2,1)} %get-tuple-element.70.x_ref) | copy-start | bytes 3145732
  652.1 2.3 copy-start.4
  654.4 2.9 copy-start.15
  656.4 15.0 %collective-permute-start.7 = (bf16[256,1024]{1,0:T(8,128)(2,1)S(1)}, bf16[256,1024]{1,0:T(8,128)(2,1)}, u32[]{:S(2)}, u32[]{:S(2)}) collective-permute-start(bf16[256,1024]{1,0:T(8,128)(2,1)S(1)} %constant_dynamic-slice_fusion.2), channel_id=1, source_target_pairs={{0,1},{1,0},{2,3},{3,2},{4,5},{5,4},{6,7},{7,6},{8,9},{9,8},{10,11... | collective-permute-start | bytes 1572872 | tf_op jit(solution)/shard_map/ppermute | solution.py:1083
  660.8 19.9 %collective-permute-start.13 = (bf16[256,1024]{1,0:T(8,128)(2,1)S(1)}, bf16[256,1024]{1,0:T(8,128)(2,1)S(1)}, u32[]{:S(2)}, u32[]{:S(2)}) collective-permute-start(bf16[256,1024]{1,0:T(8,128)(2,1)S(1)} %get-tuple-element.138), channel_id=1, source_target_pairs={{0,1},{1,0},{2,3},{3,2},{4,5},{5,4},{6,7},{7,6},{8,9},{9,8},{10,11... | collective-permute-start | bytes 1572872 | tf_op jit(solution)/shard_map/ppermute | solution.py:1083
  672.8 11.4 %copy-start.1 = (f32[3,4,2048]{2,1,0:T(4,128)S(1)}, f32[3,4,2048]{2,1,0:T(4,128)}, u32[]{:S(2)}) copy-start(f32[3,4,2048]{2,1,0:T(4,128)} %param.24) | copy-start | bytes 294916
Sparse Core Ops, SparseCore 0:
  82.8 93.0 all-gather.2
  268.9 60.1 reduce-scatter.6
  331.4 60.2 reduce-scatter.8
  407.4 57.7 reduce-scatter.10
  483.3 27.7 reduce-scatter.12
  513.4 44.5 reduce-scatter.14
  560.3 42.9 reduce-scatter.16

commit v4 on v3

--- a/solution.py
+++ b/solution.py
@@ -749,7 +749,8 @@
 
 
 class Scatter:
-    def __init__(self, give, take, acc, diag_in, last_in, s_core, r_core, s_link, r_link, gx, gy):
+    def __init__(self, give, take, acc, diag_in, last_in, s_core, r_core, s_link, r_link, gx, gy, over_gx=False):
+        self.over_gx = over_gx
         self.give, self.take, self.acc, self.diag_in, self.last_in = give, take, acc, diag_in, last_in
         core, xn, yn = (slot_peer(r, gx, gy) for r in (1, 2, 3))
         rows = acc.shape[1]
@@ -762,7 +763,7 @@
             return remote(src, dst, s_link.at[i], r_link.at[i], peer)
 
         self.link = [
-            link(0, acc.at[0, a], diag_in.at[0], xn),
+            link(0, acc.at[0, a], diag_in.at[0], yn if over_gx else xn),
             link(1, acc.at[0, b], diag_in.at[1], yn),
             link(2, acc.at[1, a], last_in.at[0, a], xn),
             link(3, acc.at[2, b], last_in.at[1, b], yn),
@@ -770,7 +771,7 @@
             link(5, acc.at[2, a], last_in.at[1, a], yn),
         ]
 
-    def run(self, product, self_acc):
+    def begin(self, product, self_acc, between=None):
         acc = self.acc
 
         def give_out(n, slot):
@@ -790,37 +791,57 @@
             self.core[n].wait_recv()
             acc[n] = (acc[n].astype(f32) + self.take[n].astype(f32)).astype(bf)
 
-        a, b = self.a, self.b
         give_out(0, 7)
         keep(0, 6)
         give_out(1, 4)
+        if between is not None:
+            between()
         join(0)
         self.link[0].start()
         self.link[1].start()
         give_out(2, 5)
         keep(1, 2)
         join(1)
-        self.link[2].start()
+        if not self.over_gx:
+            self.link[2].start()
         keep(2, 3)
         join(2)
         self.link[3].start()
+        if self.over_gx:
+            self.link[5].start()
         give_out(3, 1)
 
         def put_self(cols, value):
             self_acc[:, cols] = value
 
         product(0, put_self)
+
+    def forward(self):
+        acc, a, b = self.acc, self.a, self.b
+        if self.over_gx:
+            for i, half, onward in ((0, a, 2), (1, b, 4)):
+                self.link[i].wait_recv()
+                acc[1, half] = (acc[1, half].astype(f32) + self.diag_in[i].astype(f32)).astype(bf)
+                self.link[onward].start()
+            return
         self.link[1].wait_recv()
         acc[1, b] = (acc[1, b].astype(f32) + self.diag_in[1].astype(f32)).astype(bf)
         self.link[4].start()
         self.link[0].wait_recv()
         acc[2, a] = (acc[2, a].astype(f32) + self.diag_in[0].astype(f32)).astype(bf)
         self.link[5].start()
+
+    def end(self, self_acc):
         self.core[3].wait_recv()
         self_acc[...] += self.take[3].astype(f32)
         for c in self.link[2:]:
             c.wait_recv()
         self_acc[...] += self.last_in[0].astype(f32) + self.last_in[1].astype(f32)
+
+    def run(self, product, self_acc):
+        self.begin(product, self_acc)
+        self.forward()
+        self.end(self_acc)
 
     def finish(self):
         for c in self.core + self.link:
@@ -880,7 +901,7 @@
 
         lax.fori_loop(0, feat // tile, body, 0)
 
-    scatter = Scatter(give, take, acc, diag_in, last_in, s_core, r_core, s_link, r_link, gx, gy)
+    scatter = Scatter(give, take, acc, diag_in, last_in, s_core, r_core, s_link, r_link, gx, gy, True)
     scatter.run(product, total)
     keep = pltpu.make_async_copy(lhs, slots_ref, keep_sem)
     keep.start()
@@ -949,7 +970,7 @@
 
         lax.fori_loop(0, feat // tile, body, 0)
 
-    scatter = Scatter(give, take, acc, diag_in, last_in, s_core, r_core, s_link, r_link, gx, gy)
+    scatter = Scatter(give, take, acc, diag_in, last_in, s_core, r_core, s_link, r_link, gx, gy, True)
     scatter.run(product, total)
     middle = middle_ref[...]
     incoming = total[...]
@@ -1008,63 +1029,177 @@
     )(grads, gate_up, w_out, piece, middle, y_rel, gain)
 
 
-def scatter_kernel(lhs_ref, w_ref, out_ref, give, take, acc, diag_in, last_in, s_core, r_core, s_link, r_link, lhs, w, total, load_sem, lhs_sem, *, slots, transposed):
-    gx, gy = lax.axis_index("gx"), lax.axis_index("gy")
-    rows, feat = out_ref.shape
+def final_kernel(
+    draw_ref, hw_ref, hidden_ref, dn_ref, x_ref, mid_ref, middle_ref, other_ref, gain_ref, small_ref,
+    gin_ref, lout_ref, all_ref,
+    give1, take1, acc1, diag1, last1, sc1, rc1, sl1, rl1,
+    give2, take2, acc2, diag2, last2, sc2, rc2, sl2, rl2,
+    draw, hw, hidden, dn, x, mid, m_near, total1, total2, row_send, row_recv, z_in, z_sum, z_all,
+    load_sem, draw_sem, hidden_sem, x_sem, row_sem, z_send, z_recv, p_send, p_recv,
+    *, ndp,
+):
+    gx, gy, dp = lax.axis_index("gx"), lax.axis_index("gy"), lax.axis_index("dp")
+    me = gx * 2 + gy
+    rows, feat = middle_ref.shape
+    part = feat // 2
     tile = 512
-    load = pltpu.make_async_copy(w_ref, w, load_sem)
-
-    def source(r):
-        if slots:
-            return lhs_ref.at[r]
+    near = pl.ds(pl.multiple_of(gy * part, part), part)
+    xn = slot_peer(2, gx, gy)
+    pairs = {0: (0, 2), 2: (0, 2), 1: (1, 4), 4: (1, 4), 3: (3, 6), 6: (3, 6), 5: (5, 7), 7: (5, 7)}
+    load_hw = pltpu.make_async_copy(hw_ref, hw, load_sem.at[0])
+    load_dn = pltpu.make_async_copy(dn_ref, dn, load_sem.at[1])
+    order = (7, 5, 6, 3, 4, 1, 2, 0)
+    draws = {}
+    for r in order:
         px, py = slot_place(r, gx, gy)
-        return lhs_ref.at[py * 4 + px]
-
-    order = (7, 6, 4, 5, 2, 3, 1, 0)
-    pulls = {r: pltpu.make_async_copy(source(r), lhs.at[r], lhs_sem.at[r]) for r in order}
-    pulls[7].start()
-    load.start()
-    for r in order[1:]:
-        pulls[r].start()
-    entry_barrier([slot_peer(r, gx, gy) for r in (1, 2, 3)])
-    load.wait()
-
-    def product(slot, put):
-        pulls[slot].wait()
-
-        def body(t, _):
-            cols = pl.ds(pl.multiple_of(t * tile, tile), tile)
-            put(cols, nn_dot(lhs[slot], w[:, cols]) if transposed else nt_dot(lhs[slot], w[cols, :]))
-            return 0
-
-        lax.fori_loop(0, feat // tile, body, 0)
-
-    scatter = Scatter(give, take, acc, diag_in, last_in, s_core, r_core, s_link, r_link, gx, gy)
-    scatter.run(product, total)
-    out_ref[...] = total[...]
-    scatter.finish()
-
-
-def product_scatter(lhs, w, collective, slots, transposed):
-    _, rows, depth = lhs.shape
-    feat = w.shape[1] if transposed else w.shape[0]
+        draws[r] = pltpu.make_async_copy(draw_ref.at[py * 4 + px], draw.at[r], draw_sem.at[r])
+    hiddens = {r: pltpu.make_async_copy(hidden_ref.at[r], hidden.at[r], hidden_sem.at[r]) for r in order}
+    draws[7].start()
+    draws[5].start()
+    load_hw.start()
+    for r in order[2:]:
+        draws[r].start()
+    load_dn.start()
+    for r in order:
+        hiddens[r].start()
+    finals = [
+        pltpu.make_async_copy(x_ref, x, x_sem.at[0]),
+        pltpu.make_async_copy(mid_ref.at[0, :, near], mid.at[gy], x_sem.at[1]),
+        pltpu.make_async_copy(mid_ref.at[2, :, near], mid.at[1 - gy], x_sem.at[2]),
+    ]
+    for c in finals:
+        c.start()
+    finals.append(pltpu.make_async_copy(middle_ref.at[:, near], m_near, x_sem.at[3]))
+    finals[-1].start()
+    entry_barrier([slot_peer(r, gx, gy) for r in range(1, 8)] + [{"dp": flipped(dp, n, ndp)} for n in range(1, ndp)])
+    around = [
+        remote(small_ref, z_in.at[n], z_send.at[n], z_recv.at[n], {"dp": flipped(dp, n, ndp)}) for n in range(1, ndp)
+    ]
+    for c in around:
+        c.start()
+
+    def rows_pair(many, copies, slot, waited):
+        for r in pairs[slot]:
+            if r not in waited:
+                copies[r].wait()
+                waited.add(r)
+        first, second = pairs[slot]
+        low = first + (second - first) * gy
+        return low, first + second - low
+
+    def maker(many, copies, weights, weight_load, transposed):
+        waited = set()
+
+        def product(slot, put):
+            low, high = rows_pair(many, copies, slot, waited)
+            if weight_load is not None and "w" not in waited:
+                weight_load.wait()
+                waited.add("w")
+            _, py = slot_place(slot, gx, gy)
+
+            def body(t, _):
+                cols = pl.ds(pl.multiple_of(t * tile, tile), tile)
+                wide = pl.ds(pl.multiple_of(py * part + t * tile, tile), tile)
+                if transposed:
+                    w = weights[:, wide]
+                    value = [nn_dot(many[low], w), nn_dot(many[high], w)]
+                else:
+                    w = weights[wide, :]
+                    value = [nt_dot(many[low], w), nt_dot(many[high], w)]
+                put(cols, jnp.concatenate(value, axis=0))
+                return 0
+
+            lax.fori_loop(0, part // tile, body, 0)
+
+        return product
+
+    first = Scatter(give1, take1, acc1, diag1, last1, sc1, rc1, sl1, rl1, gx, gy)
+    second = Scatter(give2, take2, acc2, diag2, last2, sc2, rc2, sl2, rl2, gx, gy)
+    first.begin(maker(draw, draws, hw, load_hw, False), total1)
+    for c in around:
+        c.wait_recv()
+    summed = small_ref[...]
+    for n in range(1, ndp):
+        summed = summed + z_in[n]
+    z_sum[...] = summed
+    passes = [remote(z_sum, z_all.at[me], p_send.at[r], p_recv.at[r], slot_peer(r, gx, gy)) for r in range(1, 8)]
+    for c in passes:
+        c.start()
+    second.begin(maker(hidden, hiddens, dn, load_dn, True), total2, first.forward)
+    first.end(total1)
+    for c in finals:
+        c.wait()
+    wide_x = x[...].astype(f32)
+    scaled = gain_ref[:, near] * total1[...]
+    sums = [jnp.sum(wide_x * wide_x, axis=-1, keepdims=True), jnp.sum(wide_x * scaled, axis=-1, keepdims=True)]
+    lane = lax.broadcasted_iota(jnp.int32, (2 * rows, 128), 1)
+    packed = jnp.where(lane == 0, sums[0], jnp.where(lane == 1, sums[1], 0.0)).T
+    row_send[...] = packed[:8]
+    row_copy = remote(row_send, row_recv, row_sem.at[0], row_sem.at[1], xn)
+    row_copy.start()
+    second.forward()
+    second.end(total2)
+    mine = pl.ds(pl.multiple_of(gy * rows, rows), rows)
+    other = pl.ds(pl.multiple_of((1 - gy) * rows, rows), rows)
+    lout_ref[gy] = (total2[mine, :] + m_near[...]).astype(bf)
+    lout_ref[1 - gy] = (total2[other, :] + other_ref[...].astype(f32)).astype(bf)
+    row_copy.wait_recv()
+    both = jnp.concatenate([row_send[...] + row_recv[...], jnp.zeros((120, 2 * rows), f32)], axis=0).T
+    rate = lax.rsqrt(both[:, 0:1] / feat + EPS)
+    inner = both[:, 1:2] / feat
+    gin = mid[...].reshape(2 * rows, part).astype(f32) + rate * scaled - wide_x * (rate * rate * rate) * inner
+    gin_ref[...] = gin.astype(bf).reshape(2, rows, part)
+    z_all[me] = z_sum[...]
+    for c in passes:
+        c.wait_recv()
+    all_ref[...] = z_all[...]
+    for c in around + passes + [row_copy]:
+        c.wait_send()
+    first.finish()
+    second.finish()
+
+
+def final_sums(draw, head_w, hidden, down, inputs, mid, middle, other, gain, small, ndp, collective):
+    rows, feat = middle.shape
+    part = feat // 2
+    sd = jax.ShapeDtypeStruct
+    dma = pltpu.SemaphoreType.DMA
     return pl.pallas_call(
-        functools.partial(scatter_kernel, slots=slots, transposed=transposed),
-        in_specs=[ANY, ANY],
-        out_specs=VM,
-        out_shape=jax.ShapeDtypeStruct((rows, feat), f32),
-        scratch_shapes=scatter_scratch(rows, feat)
+        functools.partial(final_kernel, ndp=ndp),
+        in_specs=[ANY] * 7 + [VM] * 3,
+        out_specs=[VM] * 3,
+        out_shape=[sd((2, rows, part), bf), sd((2, rows, part), bf), sd((8, *small.shape), f32)],
+        scratch_shapes=scatter_scratch(2 * rows, part)
+        + scatter_scratch(2 * rows, part)
         + [
-            pltpu.VMEM(lhs.shape, bf),
-            pltpu.VMEM(w.shape, bf),
-            pltpu.VMEM((rows, feat), f32),
-            pltpu.SemaphoreType.DMA,
-            pltpu.SemaphoreType.DMA((8,)),
+            pltpu.VMEM(draw.shape, bf),
+            pltpu.VMEM(head_w.shape, bf),
+            pltpu.VMEM(hidden.shape, bf),
+            pltpu.VMEM(down.shape, bf),
+            pltpu.VMEM((2 * rows, part), bf),
+            pltpu.VMEM((2, rows, part), bf),
+            pltpu.VMEM((rows, part), f32),
+            pltpu.VMEM((2 * rows, part), f32),
+            pltpu.VMEM((2 * rows, part), f32),
+            pltpu.VMEM((8, 2 * rows), f32),
+            pltpu.VMEM((8, 2 * rows), f32),
+            pltpu.VMEM((ndp, *small.shape), f32),
+            pltpu.VMEM(small.shape, f32),
+            pltpu.VMEM((8, *small.shape), f32),
+            dma((2,)),
+            dma((8,)),
+            dma((8,)),
+            dma((4,)),
+            dma((2,)),
+            dma((ndp,)),
+            dma((ndp,)),
+            dma((8,)),
+            dma((8,)),
         ],
-        compiler_params=pltpu.CompilerParams(collective_id=collective, has_side_effects=True, vmem_limit_bytes=60 << 20),
+        compiler_params=pltpu.CompilerParams(collective_id=collective, has_side_effects=True, vmem_limit_bytes=63 << 20),
         cost_estimate=lasting(5),
-        name="product_scatter",
-    )(lhs, w)
+        name="final_sums",
+    )(draw, head_w, hidden, down, inputs, mid, middle, other, gain, small)
 
 
 def dot(a, b):
@@ -1097,15 +1232,6 @@
     )
 
 
-def to_final(own):
-    mine, other = halves(own, 1)
-    return in_order(mine[None], swap(other)[None], 0)
-
-
-def rate_of(value):
-    return lax.rsqrt(jnp.mean(value * value, axis=-1, keepdims=True) + EPS)
-
-
 def scatter_dp(value):
     return lax.psum_scatter(value.astype(bf), "dp", scatter_dimension=0, tiled=True)
 
@@ -1119,15 +1245,6 @@
 def sort_halves(parts):
     first = lax.axis_index("gy") == 0
     return jnp.where(first, parts[0], parts[1]), swap(jnp.where(first, parts[1], parts[0]))
-
-
-def sum_axis(value, axis):
-    size = lax.axis_size(axis)
-    step = 1
-    while step < size:
-        value = value + lax.ppermute(value, axis, [(i, i ^ step) for i in range(size)])
-        step *= 2
-    return value
 
 
 def shards(
@@ -1206,7 +1323,6 @@
     )
     grad_mixed, mid_slots, down_rows, *gu_sums = lax.optimization_barrier((grad_mixed, mid_slots, down_rows, *gu_sums))
     down_sum = scatter_dp(down_rows)
-    mid_low = mid_slots[0]
     out_grad = dot_w(mixed_slots.reshape(tokens, width), mid_slots.reshape(tokens, feat)).astype(bf)
     out_keep, out_send = halves(out_grad, 1)
     out_rows = in_order(out_keep, swap(out_send), 0)
@@ -1214,27 +1330,30 @@
         raw, aux, conv_local, gain_row, saved, grad_mixed.reshape(nb, length, width)
     )
     draw = draw.reshape(tokens, -1)
-    draw, down_sum, out_rows = lax.optimization_barrier((draw, down_sum, out_rows))
+    gu_pair = sort_halves(gu_sums)
+    middle_other = swap(lax.dynamic_slice_in_dim(middle, (1 - gy) * half, half, 1).astype(bf))
+    draw, down_sum, out_rows, middle_other, *gu_pair = lax.optimization_barrier((draw, down_sum, out_rows, middle_other, *gu_pair))
     out_sum = scatter_dp(out_rows)
     main = 4 * width
-    head_grads = rows_to_dp(normed, draw[:, :main])
-    beta_grad = dot_w(normed, draw[:, main:])
-    norm_gain_grad = (
-        jnp.sum(jnp.concatenate(head_grads, axis=0).astype(f32) * head_w[:, :main].astype(f32), axis=1)
-        + jnp.sum(beta_grad * head_w[:, main:].astype(f32), axis=1)
-    ) / norm_gain
-    draw, hidden, out_sum, *head_grads = lax.optimization_barrier((draw, hidden, out_sum, *head_grads))
+    both = rows_to_dp(normed, draw)
+    norm_gain_grad = jnp.sum(jnp.concatenate(both, axis=0).astype(f32) * head_w.astype(f32), axis=1) / norm_gain
+    beta_grad = jnp.concatenate([g[:, main : main + heads] for g in both], axis=0).astype(f32)
+    head_grads = [g[:, :main] for g in both]
+    draw, hidden, *head_grads = lax.optimization_barrier((draw, hidden, *head_grads))
+    head_sums = [scatter_dp(g) for g in head_grads]
+    hidden, out_sum = lax.optimization_barrier((hidden, out_sum))
     sum_down, sum_out = down_sum.astype(f32), out_sum.astype(f32)
-    grad_gu_mine, grad_gu_other = sort_halves(gu_sums)
-    head_sums = [scatter_dp(g) for g in head_grads]
-    grad_normed = product_scatter(draw.reshape(8, own_rows, -1), head_w, 3, False, False)
-    x_wide_own = x_own.astype(f32)
-    rate_own = rate_of(x_wide_own)
-    scaled = norm_gain * grad_normed
-    inner = jnp.mean(x_wide_own * scaled, axis=-1, keepdims=True)
-    norm_one = rate_own * scaled - x_wide_own * (rate_own * rate_own * rate_own) * inner
-    grad_inputs = to_final((mid_low.astype(f32) + norm_one).astype(bf))
-    layer_out = to_final((middle + product_scatter(hidden, down_w, 4, True, True)).astype(bf))
+    grad_gu_mine, grad_gu_other = gu_pair
+    flat = [beta_grad.T, conv_grad, norm_gain_grad, jnp.sum(mlp_gain_parts, axis=0), gain_grad]
+    counts = [v.size // 128 for v in flat]
+    small = jnp.concatenate([v.reshape(-1, 128) for v in flat])
+    small = jnp.pad(small, ((0, -small.shape[0] % 8), (0, 0)))
+    if parts == 1:
+        small = lax.psum(small, "dp")
+    grad_inputs, layer_out, gathered = final_sums(
+        draw.reshape(8, own_rows, -1), head_w, hidden, down_w, inputs.reshape(nb * part_rows, part_feat), mid_slots, middle,
+        middle_other, norm_gain[None], small, parts, 3,
+    )
 
     head_mine, head_other = sort_halves(head_sums)
 
@@ -1250,24 +1369,17 @@
 
     sum_query, sum_key, sum_value, sum_head_gate = (head_part(i * width, width) for i in range(4))
 
-    small = jnp.concatenate(
-        [beta_grad[:, :heads].T.reshape(-1), conv_grad.reshape(-1), norm_gain_grad, jnp.sum(mlp_gain_parts, axis=0), gain_grad]
-    )
-    small = sum_axis(small, "dp")
-    beta_sum, small = small[: heads * feat].reshape(heads, feat), small[heads * feat :]
+    n_beta, n_conv, n_norm, n_mlp, n_gain = counts
+    beta_parts = gathered[:, :n_beta].reshape(8, heads, feat)
     beta_rows = feat // (ngy * ndp)
-    beta_mine, beta_other = (
-        lax.dynamic_slice_in_dim(beta_sum, (side * ndp + lax.axis_index("dp")) * beta_rows, beta_rows, 1) for side in (gy, 1 - gy)
-    )
-    sum_beta = in_order(beta_mine, swap(beta_other), 0).T
-    n_conv = conv_grad.size
-    conv_full = lax.dynamic_update_slice_in_dim(
-        jnp.zeros(conv_kernel.shape, f32), small[:n_conv].reshape(conv_grad.shape), conv_start, 2
-    )
-    small = sum_axis(sum_axis(jnp.concatenate([conv_full.reshape(-1), small[n_conv:]]), "gx"), "gy")
-    n_conv = conv_full.size
-    conv_sum = small[:n_conv].reshape(conv_kernel.shape)
-    norm_sum, mlp_sum, gain_sum = jnp.split(small[n_conv:], [feat, 2 * feat])
+    beta_pair = lax.dynamic_slice(beta_parts, (gx * ngy, 0, (gy * ndp + lax.axis_index("dp")) * beta_rows), (ngy, heads, beta_rows))
+    sum_beta = beta_pair.reshape(ngy * heads, beta_rows).T
+    taps = conv_kernel.shape[1]
+    conv_sum = gathered[:, n_beta : n_beta + n_conv].reshape(8, 3, taps, width).transpose(1, 2, 0, 3).reshape(conv_kernel.shape)
+    rest = jnp.sum(gathered[:, n_beta + n_conv :], axis=0)
+    norm_sum = rest[:n_norm].reshape(feat)
+    mlp_sum = rest[n_norm : n_norm + n_mlp].reshape(feat)
+    gain_sum = rest[n_norm + n_mlp : n_norm + n_mlp + n_gain].reshape(-1)
     return (
         layer_out,
         grad_inputs,

time: 701 us -> 634 us (0.904)
  waiting for transfers between devices: 43.8 us -> 10.8 us
  Pallas kernels: 494 us -> 472 us
  other arithmetic: 35.1 us -> 24.2 us
  local copies, waits for them, and re-layouts: 18.2 us -> 27.8 us
    ppermute x5 -> x0, waiting for transfers between devices: 18 us -> none  [sum_axis(): lax.ppermute(value, axis, [(i, i ^ step) for i in range(size)])]
    reduce_scatter x6, waiting for transfers between devices: 10.5 us -> 0.03 us  [scatter_dp(): lax.psum_scatter(value.astype(bf), 'dp', scatter_dimension=0, tiled=True)]
    pallas_call x1, Pallas kernels: 109 us -> 99.3 us  [mlp_backward(): pl.pallas_call(back_kernel, in_specs=[ANY, ANY, ANY, ANY, VM, ANY, VM], o...]
    pallas_call x1, Pallas kernels: 57.8 us -> 48.9 us  [mlp_forward(): pl.pallas_call(functools.partial(mlp_kernel, parts=parts), in_specs=[ANY]...]
    slice x4 -> x9, local copies, waits for them, and re-layouts: 0.02 us -> 7.04 us  [the longest x2 3.28 us: shards(): head_grads = [g[:, :main] for g in both]]
    dot_general x7 -> x6, matrix products: 62.1 us -> 56.7 us  [dot_w(): lax.dot_general(a, b, (((0,), (0,)), ((), ())), preferred_element_type=f32)]
    ppermute x8 -> x6, waiting for transfers between devices: 15.2 us -> 10.1 us  [swap(): return lax.ppermute(value, 'gy', [(0, 1), (1, 0)])]
    pallas_call x2 -> x1, Pallas kernels: 94.1 us -> 89 us  [final_sums(): pl.pallas_call(functools.partial(final_kernel, ndp=ndp), in_specs=[ANY] *...]
  transfers between devices with their start and end apart: 23 -> 16, of which waited for: 7 -> 1; matrix products, arithmetic and copies ran while one was open for 14% -> 14% of each run, Pallas kernels for 53% -> 56%
where the time goes in v4:
time: 634 us; the launch traced here: 625 us
  Pallas kernels  472 us (74%)
  matrix products  56.7 us (9%)
  local copies, waits for them, and re-layouts  27.8 us (4%)
  other arithmetic  24.2 us (4%)
  starting transfers between devices  18.8 us (3%)
  between operations  15 us (2%)
  waiting for transfers between devices  10.8 us (2%)
    pallas_call x1, Pallas kernels, mlp_backward(): pl.pallas_call(back_kernel, in_specs=[ANY, ANY, ANY, ANY, VM, ANY, VM], o...  99.3 us
    pallas_call x1, Pallas kernels, final_sums(): pl.pallas_call(functools.partial(final_kernel, ndp=ndp), in_specs=[ANY] *...  89 us
    pallas_call x1, Pallas kernels, head_project(): pl.pallas_call(head_kernel, in_specs=[ANY] * 9 + [VM], out_specs=[ANY, AN...  72.8 us
    pallas_call x1, Pallas kernels, out_project(): pl.pallas_call(out_kernel, in_specs=[ANY, ANY, ANY, VM, VM], out_specs=[V...  68.2 us
    pallas_call x1, Pallas kernels, mixer_bwd(): pl.pallas_call(bwd_kernel, grid=(nb, heads), in_specs=specs(length, heads...  60.5 us
    dot_general x6, matrix products, dot_w(): lax.dot_general(a, b, (((0,), (0,)), ((), ())), preferred_element_type=f32)  56.7 us
    pallas_call x1, Pallas kernels, mlp_forward(): pl.pallas_call(functools.partial(mlp_kernel, parts=parts), in_specs=[ANY]...  48.9 us
    pallas_call x1, Pallas kernels, mixer_fwd(): pl.pallas_call(fwd_kernel, grid=(nb, heads), in_specs=specs(length, heads...  33 us
  transfers between devices with their start and end apart: 16, of which 1 were waited for; matrix products, arithmetic and copies ran while one was open for 14% of the time, Pallas kernels for 56%

profile of v4, /device:TPU:0, one launch (start us, length us, event | category | flops | bytes accessed | tf_op | source)
XLA Modules:
  0.0 624.9 jit_solution(2718994236899529840)
XLA Ops:
  7.2 0.7 reshape.132
  8.4 0.5 pad.33
  9.0 0.9 copy.89
  9.9 72.8 %head_project.1 = (bf16[8,256,2048]{2,1,0:T(8,128)(2,1)}, f32[8,256,1152]{2,1,0:T(8,128)}, bf16[2048,1152]{1,0:T(8,128)(2,1)}, bf16[256,2048]{1,0:T(8,128)(2,1)}...) custom-call(bf16[512,1024]{1,0:T(8,128)(2,1)} %bitcast.129, bf16[1024,512]{1,0:T(8,128)(2,1)} %wq_ref.1, ...), custom_call_target="tpu_custom_call" | custom-call | flops 92000002048 | bytes 1048576 | tf_op jit(solution)/shard_map/head_project/pallas_call | solution.py:567
  82.8 8.1 %collective-permute-start = (bf16[256,1536]{1,0:T(8,128)(2,1)}, bf16[256,1536]{1,0:T(8,128)(2,1)}, u32[]{:S(2)}, u32[]{:S(2)}) collective-permute-start(bf16[256,1536]{1,0:T(8,128)(2,1)} %get-tuple-element.88.refs_0_), channel_id=1, source_target_pairs={{0,8},{8,0},{16,24},{24,16},{1,9},{9,1},{17,25},{25,17},{2,10},{10... | collective-permute-start | bytes 2359304 | tf_op jit(solution)/shard_map/ppermute | solution.py:1288
  90.9 1.0 collective-permute-start.1
  91.9 1.5 collective-permute-start.2
  93.3 1.5 constant_dynamic-slice_fusion.3
  94.9 0.6 collective-permute-start.3
  96.3 1.4 stack.90.aux_ref
  97.7 0.6 constant_dynamic-slice_fusion.4.w_ref
  98.3 33.0 %mixer_forward.1 = (bf16[2,1024,256]{2,1,0:T(8,128)(2,1)}, bf16[2,2,1024,128]{3,2,1,0:T(8,128)(2,1)}, bf16[2,2,1024,128]{3,2,1,0:T(8,128)(2,1)}, bf16[2,2,1024,1...) custom-call(f32[2,1024,1152]{2,1,0:T(8,128)} %bitcast.114, ...), custom_call_target="tpu_custom_call" | custom-call | flops 37950001152 | bytes 1048576 | tf_op jit(solution)/shard_map/mixer_forward/pallas_call | solution.py:147
  131.4 68.2 %out_project.1 = (f32[256,2048]{1,0:T(8,128)}, bf16[256,2048]{1,0:T(8,128)(2,1)}, bf16[8,256,256]{2,1,0:T(8,128)(2,1)}) custom-call(bf16[8,256,256]{2,1,0:T(8,128)(2,1)} %bitcast.156, bf16[512,1024]{1,0:T(8,128)(2,1)} %out_ref.5, bf16[256,1024]{1,0:T(8,128)(2,1)} %get-tuple-element.82.piece_ref, bf16[256,2048]{1,0:T(8,128)(2,1)} %get-tuple-element.84.x_ref, ...), custom_call_target="tpu_custom_call" | custom-call | flops 50600001536 | bytes 1048576 | tf_op jit(solution)/shard_map/out_project/pallas_call | solution.py:920
  199.7 1.1 copy-done.16
  200.8 48.9 %mlp_forward.1 = (bf16[8,256,2048]{2,1,0:T(8,128)(2,1)}, bf16[8,256,768]{2,1,0:T(8,128)(2,1)}, bf16[8,256,1536]{2,1,0:T(8,128)(2,1)}, bf16[8,256,2048]{2,1,0:T(8...) custom-call(bf16[256,2048]{1,0:T(8,128)(2,1)} %get-tuple-element.85.x_ref, ...), custom_call_target="tpu_custom_call" | custom-call | flops 78199996416 | bytes 1048576 | tf_op jit(solution)/shard_map/mlp_forward/pallas_call | solution.py:717
  249.7 11.4 %fusion.11 = bf16[1024,1536]{1,0:T(8,128)(2,1)} fusion(bf16[2048,1536]{1,0:T(8,128)(2,1)} %bitcast.154, bf16[2048,2048]{1,0:T(8,128)(2,1)} %bitcast.152), kind=kOutput, calls=%fused_computation.10 | convolution fusion | flops 6444023808 | bytes 13631488 | tf_op jit(solution)/shard_map/dot_general | solution.py:1214
  261.2 10.1 %convolution_convert_fusion = bf16[768,2048]{1,0:T(8,128)(2,1)S(1)} fusion(bf16[2048,768]{1,0:T(8,128)(2,1)} %bitcast.127, bf16[2048,2048]{1,0:T(8,128)(2,1)} %bitcast.151), kind=kOutput, calls=%fused_computation.17 | convolution fusion | flops 6444023808 | bytes 14680064 | tf_op jit(solution)/shard_map/dot_general | solution.py:1214
  271.4 11.4 %fusion.8 = bf16[1024,1536]{1,0:T(8,128)(2,1)} fusion(bf16[2048,1536]{1,0:T(8,128)(2,1)} %bitcast.155, bf16[2048,2048]{1,0:T(8,128)(2,1)} %bitcast.153), kind=kOutput, calls=%fused_computation.9 | convolution fusion | flops 6444023808 | bytes 13631488 | tf_op jit(solution)/shard_map/dot_general | solution.py:1214
  282.9 2.1 constant_dynamic-slice_fusion.2
  284.9 0.5 collective-permute-start.4
  285.4 99.3 %mlp_backward.1 = (bf16[8,256,2048]{2,1,0:T(8,128)(2,1)}, bf16[8,256,256]{2,1,0:T(8,128)(2,1)}, f32[8,2048]{1,0:T(8,128)}) custom-call(bf16[8,256,1536]{2,1,0:T(8,128)(2,1)} %get-tuple-element.95.grads_ref, bf16[2048,1536]{1,0:T(8,128)(2,1)} %get-tuple-element.96.wgu_ref, bf16[512,1024]{1,0:T(8,128)(2,1)} %out_ref.5, ...), custom_call_target="tpu_custom_call" | custom-call | flops 23000000512 | bytes 1048576 | tf_op jit(solution)/shard_map/mlp_backward/pallas_call | solution.py:1005
  384.7 2.0 fusion.24
  386.8 0.6 fusion.22
  387.4 1.8 pad_maximum_fusion
  389.7 5.8 fusion.20
  395.6 2.4 collective-permute-start.5
  398.1 1.0 broadcast_select_fusion
  399.1 2.1 dynamic-slice_convert_fusion
  401.2 2.0 collective-permute-start.6
  403.2 60.5 %mixer_backward.1 = (bf16[2,1024,1152]{2,1,0:T(8,128)(2,1)}, f32[2,2,12,8,128]{4,3,2,1,0:T(8,128)}, f32[2,2,8,128]{3,2,1,0:T(8,128)}) custom-call(f32[2,1024,1152]{2,1,0:T(8,128)} %bitcast.119, f32[2,1024,1152]{2,1,0:T(8,128)} %bitcast.120, f32[2,1024,1152]{2,1,0:T(8,128)} %bitcast.121, f32[2,1024,1152]{2,1,0:T(8,128)} %bitcast.122, ...), custom_call_target="tpu_custom_call" | custom-call | flops 2300000000 | bytes 1048576 | tf_op jit(solution)/shard_map/mixer_backward/pallas_call | solution.py:294
  463.7 1.3 broadcast_select_fusion.5
  465.0 1.0 pad_maximum_fusion.1
  466.2 0.7 copy-done.10
  466.8 8.9 %fusion.14 = bf16[1024,1152]{1,0:T(8,128)(2,1)S(1)} fusion(bf16[2048,1152]{1,0:T(8,128)(2,1)} %bitcast.124, bf16[2048,2048]{1,0:T(8,128)(2,1)} %bitcast.149), kind=kOutput, calls=%fused_computation.11 | convolution fusion | flops 4833017856 | bytes 11272192 | tf_op jit(solution)/shard_map/dot_general | solution.py:1214
  475.7 1.6 slice.157
  477.4 8.9 %fusion.17 = bf16[1024,1152]{1,0:T(8,128)(2,1)S(1)} fusion(bf16[2048,1152]{1,0:T(8,128)(2,1)} %bitcast.125, bf16[2048,2048]{1,0:T(8,128)(2,1)} %bitcast.150), kind=kOutput, calls=%fused_computation.12 | convolution fusion | flops 4833017856 | bytes 11272192 | tf_op jit(solution)/shard_map/dot_general | solution.py:1214
  486.3 1.4 copy-done.3
  487.7 1.7 slice.159
  490.2 1.0 reduce_sum.45
  491.2 0.7 slice.160
  492.1 1.1 copy.73
  493.2 4.4 multiply_reduce_fusion
  497.7 0.6 pad.40.small_ref
  498.4 1.2 slice_bitcast_fusion
  500.4 1.3 convert_element_type.100
  501.6 1.2 maximum_convert_fusion
  502.8 1.2 maximum_convert_fusion.1
  504.0 89.0 %final_sums.1 = (bf16[2,256,1024]{2,1,0:T(8,128)(2,1)}, bf16[2,256,1024]{2,1,0:T(8,128)(2,1)}, f32[8,96,128]{2,1,0:T(8,128)}) custom-call(bf16[8,256,1152]{2,1,0:T(8,128)(2,1)} %bitcast.126, bf16[2048,1152]{1,0:T(8,128)(2,1)} %get-tuple-element.113.hw_ref, bf16[8,256,768]{2,1,0:T(8,128)(2,1)} %get-tuple-element.116.hidden_ref, ...), custom_call_target="tpu_custom_call" | custom-call | flops 5750000128 | bytes 1048576 | tf_op jit(solution)/shard_map/final_sums/pallas_call | solution.py:1167
  593.0 0.9 slice.141
  593.9 0.9 slice.144
  594.9 0.6 reshape.153
  595.6 0.6 copy.80
  596.3 0.8 convert_element_type.97
  597.1 1.3 broadcast_select_fusion.3
  598.4 1.9 collective-permute-start.8
  600.3 0.9 slice_reduce_fusion
  601.7 0.6 slice_bitcast_fusion.4
  602.3 10.1 %collective-permute-done.8 = bf16[256,1024]{1,0:T(8,128)(2,1)S(1)} collective-permute-done((bf16[256,1024]{1,0:T(8,128)(2,1)S(1)}, bf16[256,1024]{1,0:T(8,128)(2,1)S(1)}, u32[]{:S(2)}, u32[]{:S(2)}) %collective-permute-start.8) | collective-permute-done | bytes 524320 | tf_op jit(solution)/shard_map/ppermute | solution.py:1218
  612.5 0.9 maximum_convert_fusion.2
  613.4 0.9 maximum_convert_fusion.3
  614.2 0.9 maximum_convert_fusion.4
  615.1 0.9 maximum_convert_fusion.5
  615.9 1.0 copy.97
  616.9 1.0 copy.98
  (108 shorter events, 4.7 us)
Async XLA Ops:
  7.2 90.5 %copy-start = (f32[3,4,2048]{2,1,0:T(4,128)S(1)}, f32[3,4,2048]{2,1,0:T(4,128)}, u32[]{:S(2)}) copy-start(f32[3,4,2048]{2,1,0:T(4,128)} %param.24) | copy-start | bytes 294916
  7.2 192.5 %all-gather.3.cloned.1.call-start = ((), (), s32[]{:S(2)}) async-start(), calls=%async_computation.12 | async-start | bytes 9437184 | tf_op jit(solution)/shard_map/all_gather | solution.py:1293
  82.7 12.7 %copy-start.14 = (s32[2,1024]{1,0:T(2,128)S(1)}, s32[2,1024]{1,0:T(2,128)}, u32[]{:S(2)}) copy-start(s32[2,1024]{1,0:T(2,128)} %param.17) | copy-start | bytes 24580
  82.7 306.5 %reduce-scatter.7.cloned.1.call-start = ((), (), s32[]{:S(2)}) async-start(), calls=%async_computation.6 | async-start | bytes 3932160 | tf_op jit(solution)/shard_map/reduce_scatter | solution.py:1236
  82.8 116.8 %collective-permute-start = (bf16[256,1536]{1,0:T(8,128)(2,1)}, bf16[256,1536]{1,0:T(8,128)(2,1)}, u32[]{:S(2)}, u32[]{:S(2)}) collective-permute-start(bf16[256,1536]{1,0:T(8,128)(2,1)} %get-tuple-element.88.refs_0_), channel_id=1, source_target_pairs={{0,8},{8,0},{16,24},{24,16},{1,9},{9,1},{17,25},{25,17},{2,10},{10... | collective-permute-start | bytes 2359304 | tf_op jit(solution)/shard_map/ppermute | solution.py:1288
  90.9 108.7 %collective-permute-start.1 = (bf16[256,1536]{1,0:T(8,128)(2,1)}, bf16[256,1536]{1,0:T(8,128)(2,1)}, u32[]{:S(2)}, u32[]{:S(2)}) collective-permute-start(bf16[256,1536]{1,0:T(8,128)(2,1)} %get-tuple-element.88.refs_0_), channel_id=1, source_target_pairs={{0,16},{8,24},{16,0},{24,8},{1,17},{9,25},{17,1},{25,9},{2,18},{10... | collective-permute-start | bytes 2359304 | tf_op jit(solution)/shard_map/ppermute | solution.py:1288
  91.9 107.7 %collective-permute-start.2 = (bf16[256,1536]{1,0:T(8,128)(2,1)}, bf16[256,1536]{1,0:T(8,128)(2,1)}, u32[]{:S(2)}, u32[]{:S(2)}) collective-permute-start(bf16[256,1536]{1,0:T(8,128)(2,1)} %get-tuple-element.88.refs_0_), channel_id=1, source_target_pairs={{0,24},{8,16},{16,8},{24,0},{1,25},{9,17},{17,9},{25,1},{2,26},{10... | collective-permute-start | bytes 2359304 | tf_op jit(solution)/shard_map/ppermute | solution.py:1288
  94.9 104.8 %collective-permute-start.3 = (bf16[768,1024]{1,0:T(8,128)(2,1)S(1)}, bf16[768,1024]{1,0:T(8,128)(2,1)S(1)}, u32[]{:S(2)}, u32[]{:S(2)}) collective-permute-start(bf16[768,1024]{1,0:T(8,128)(2,1)S(1)} %constant_dynamic-slice_fusion.3), channel_id=1, source_target_pairs={{0,1},{1,0},{2,3},{3,2},{4,5},{5,4},{6,7},{7,6},{8,9},{9,8},{10,11... | collective-permute-start | bytes 4718600 | tf_op jit(solution)/shard_map/ppermute | solution.py:1218
  199.6 1.2 copy-start.16
  261.1 128.1 %reduce-scatter.9.cloned.1.call-start = ((), (), s32[]{:S(2)}) async-start(), calls=%async_computation.7 | async-start | bytes 3932160 | tf_op jit(solution)/shard_map/reduce_scatter | solution.py:1236
  282.8 183.3 %reduce-scatter.11.cloned.1.call-start = ((), (), s32[]{:S(2)}) async-start(), calls=%async_computation.8 | async-start | bytes 3604480 | tf_op jit(solution)/shard_map/reduce_scatter | solution.py:1236
  284.9 99.8 %collective-permute-start.4 = (bf16[768,1024]{1,0:T(8,128)(2,1)}, bf16[768,1024]{1,0:T(8,128)(2,1)}, u32[]{:S(2)}, u32[]{:S(2)}) collective-permute-start(bf16[768,1024]{1,0:T(8,128)(2,1)} %get-tuple-element.131), channel_id=1, source_target_pairs={{0,1},{1,0},{2,3},{3,2},{4,5},{5,4},{6,7},{7,6},{8,9},{9,8},{10,11... | collective-permute-start | bytes 4718600 | tf_op jit(solution)/shard_map/ppermute | solution.py:1218
  384.7 2.1 copy-start.2
  387.4 2.3 copy-start.4
  389.3 114.7 %reduce-scatter.13.cloned.1.call-start = ((), (), s32[]{:S(2)}) async-start(), calls=%async_computation.9 | async-start | bytes 1310720 | tf_op jit(solution)/shard_map/reduce_scatter | solution.py:1236
  389.7 8.3 %copy-start.7 = (bf16[256,1536]{1,0:T(8,128)(2,1)S(1)}, bf16[256,1536]{1,0:T(8,128)(2,1)}, u32[]{:S(2)}) copy-start(bf16[256,1536]{1,0:T(8,128)(2,1)} %reduce-scatter.7.cloned.1.call-done) | copy-start | bytes 2359300
  389.7 8.3 %copy-start.8 = (bf16[256,1536]{1,0:T(8,128)(2,1)S(1)}, bf16[256,1536]{1,0:T(8,128)(2,1)}, u32[]{:S(2)}) copy-start(bf16[256,1536]{1,0:T(8,128)(2,1)} %reduce-scatter.9.cloned.1.call-done) | copy-start | bytes 2359300
  395.6 68.0 %collective-permute-start.5 = (bf16[256,1024]{1,0:T(8,128)(2,1)S(1)}, bf16[256,1024]{1,0:T(8,128)(2,1)}, u32[]{:S(2)}, u32[]{:S(2)}) collective-permute-start(bf16[256,1024]{1,0:T(8,128)(2,1)S(1)} %constant_dynamic-slice_fusion.1), channel_id=1, source_target_pairs={{0,1},{1,0},{2,3},{3,2},{4,5},{5,4},{6,7},{7,6},{8,9},{9,8},{10,11... | collective-permute-start | bytes 1572872 | tf_op jit(solution)/shard_map/ppermute | solution.py:1218
  399.1 67.0 %collective-permute-start.7 = (bf16[256,1536]{1,0:T(8,128)(2,1)}, bf16[256,1536]{1,0:T(8,128)(2,1)}, u32[]{:S(2)}, u32[]{:S(2)}) collective-permute-start(bf16[256,1536]{1,0:T(8,128)(2,1)} %get-tuple-element.133), channel_id=1, source_target_pairs={{0,1},{1,0},{2,3},{3,2},{4,5},{5,4},{6,7},{7,6},{8,9},{9,8},{10,11... | collective-permute-start | bytes 2359304 | tf_op jit(solution)/shard_map/ppermute | solution.py:1218
  401.2 64.8 %collective-permute-start.6 = (bf16[256,1024]{1,0:T(8,128)(2,1)}, bf16[256,1024]{1,0:T(8,128)(2,1)S(1)}, u32[]{:S(2)}, u32[]{:S(2)}) collective-permute-start(bf16[256,1024]{1,0:T(8,128)(2,1)} %dynamic-slice_convert_fusion), channel_id=1, source_target_pairs={{0,1},{1,0},{2,3},{3,2},{4,5},{5,4},{6,7},{7,6},{8,9},{9,8},{10,11... | collective-permute-start | bytes 1572872 | tf_op jit(solution)/shard_map/ppermute | solution.py:1218
  466.0 0.8 copy-start.10
  466.1 131.0 %reduce-scatter.15.cloned.1.call-start = ((), (), s32[]{:S(2)}) async-start(), calls=%async_computation.10 | async-start | bytes 2621440 | tf_op jit(solution)/shard_map/reduce_scatter | solution.py:1236
  486.3 1.4 copy-start.3
  489.3 0.8 copy-start.12
  489.3 1.8 copy-start.15
  489.4 2.6 slice-start
  489.4 107.7 %reduce-scatter.17.cloned.1.call-start = ((), (), s32[]{:S(2)}) async-start(), calls=%async_computation.11 | async-start | bytes 2621440 | tf_op jit(solution)/shard_map/reduce_scatter | solution.py:1236
  493.2 4.4 copy-start.13
  498.4 1.9 copy-start.9
  504.0 92.2 %copy-start.11 = (bf16[128,1024]{1,0:T(8,128)(2,1)S(1)}, bf16[128,1024]{1,0:T(8,128)(2,1)}, u32[]{:S(2)}) copy-start(bf16[128,1024]{1,0:T(8,128)(2,1)} %reduce-scatter.13.cloned.1.call-done) | copy-start | bytes 786436
  598.4 17.5 %copy-start.6 = (bf16[2,256,1024]{2,1,0:T(8,128)(2,1)S(1)}, bf16[2,256,1024]{2,1,0:T(8,128)(2,1)}, u32[]{:S(2)}) copy-start(bf16[2,256,1024]{2,1,0:T(8,128)(2,1)} %get-tuple-element.185) | copy-start | bytes 3145732
  598.4 14.0 %collective-permute-start.8 = (bf16[256,1024]{1,0:T(8,128)(2,1)S(1)}, bf16[256,1024]{1,0:T(8,128)(2,1)S(1)}, u32[]{:S(2)}, u32[]{:S(2)}) collective-permute-start(bf16[256,1024]{1,0:T(8,128)(2,1)S(1)} %get-tuple-element.146), channel_id=1, source_target_pairs={{0,1},{1,0},{2,3},{3,2},{4,5},{5,4},{6,7},{7,6},{8,9},{9,8},{10,11... | collective-permute-start | bytes 1572872 | tf_op jit(solution)/shard_map/ppermute | solution.py:1218
  612.5 4.4 copy-start.5
  613.4 4.5 copy-start.1
Sparse Core Ops, SparseCore 0:
  82.9 82.4 all-gather.2
  261.3 59.3 reduce-scatter.6
  322.9 60.2 reduce-scatter.8
  389.4 58.4 reduce-scatter.10
  466.2 26.7 reduce-scatter.12
  495.3 45.6 reduce-scatter.14
  543.2 43.1 reduce-scatter.16

commit v5 on v4

--- a/solution.py
+++ b/solution.py
@@ -10,6 +10,8 @@
 bf = jnp.bfloat16
 f32 = jnp.float32
 GROUP = 8
+BACK_A = 8
+BACK_C = 4
 
 def lasting(us):
     return pl.CostEstimate(flops=int(us * 1.15e9), bytes_accessed=1 << 20, transcendentals=0)
@@ -168,37 +170,47 @@
     length = q_ref.shape[1]
     steps = length // C
     gain = gain_ref[0:1]
-    def stage_a(c, dgain):
-        lo = pl.multiple_of(c * C, C)
-        rows = pl.ds(lo, C)
-        aux = aux_columns(aux_ref, rows)
-        carried = aux[:, 1:2]
-        q = act_stage(q_ref[0, rows, :].astype(f32), prev_rows(q_ref, lo), aux, w_ref[0], True)[2]
-        out = o_ref[0, 0, rows, :]
-        g = g_ref[0, rows, :].astype(f32)
-        dm = dm_ref[0, rows, :].astype(f32)
-        s = jax.nn.sigmoid(g)
-        r = lax.rsqrt(jnp.mean(out * out, axis=-1, keepdims=True) + HEAD_EPS)
-        scaled = out * r
-        dn = dm * (g * s)
-        dg = dm * scaled * gain * (s * (1.0 + g * (1.0 - s)))
-        draw_ref[0, rows, pl.ds(pl.multiple_of((3 * heads + h) * 128, 128), 128)] = dg.astype(bf)
-        e = dn * gain
-        do = r * (e - scaled * jnp.mean(e * scaled, axis=-1, keepdims=True))
-        pd = tn(p_ref[0, 0, rows, :], do)
-        do_s[rows, :] = do
-        pd_s[rows, :] = pd
-        base_s[rows, :] = tn(jnp.concatenate([q.astype(bf), w_in[0, 0, rows, :]], axis=0),
-                             jnp.concatenate([carried * do, -carried * pd], axis=0))
-        return dgain + jnp.sum((dn * scaled).reshape(C // 8, 8, 128), axis=0)
-    dgain = lax.fori_loop(0, steps, stage_a, jnp.zeros((8, 128), f32), unroll=2)
+    def stage_a(group, dgain):
+        spans, dos, lefts, carries = [], [], [], []
+        for n in range(BACK_A):
+            lo = pl.multiple_of((group * BACK_A + n) * C, C)
+            rows = pl.ds(lo, C)
+            aux = aux_columns(aux_ref, rows)
+            q = act_stage(q_ref[0, rows, :].astype(f32), prev_rows(q_ref, lo), aux, w_ref[0], True)[2]
+            out = o_ref[0, 0, rows, :]
+            g = g_ref[0, rows, :].astype(f32)
+            dm = dm_ref[0, rows, :].astype(f32)
+            s = jax.nn.sigmoid(g)
+            r = lax.rsqrt(jnp.mean(out * out, axis=-1, keepdims=True) + HEAD_EPS)
+            scaled = out * r
+            dn = dm * (g * s)
+            dg = dm * scaled * gain * (s * (1.0 + g * (1.0 - s)))
+            draw_ref[0, rows, pl.ds(pl.multiple_of((3 * heads + h) * 128, 128), 128)] = dg.astype(bf)
+            e = dn * gain
+            do = r * (e - scaled * jnp.mean(e * scaled, axis=-1, keepdims=True))
+            do_s[rows, :] = do
+            dgain = dgain + jnp.sum((dn * scaled).reshape(C // 8, 8, 128), axis=0)
+            spans.append(rows)
+            dos.append(do)
+            lefts.append(q.astype(bf))
+            carries.append(aux[:, 1:2])
+        pds = [tn(p_ref[0, 0, rows, :], do) for rows, do in zip(spans, dos)]
+        bases = [
+            tn(jnp.concatenate([(c * do).astype(bf), (-c * pd).astype(bf)], axis=0), jnp.concatenate([q, w_in[0, 0, rows, :]], axis=0))
+            for rows, do, pd, q, c in zip(spans, dos, pds, lefts, carries)
+        ]
+        for rows, pd, base in zip(spans, pds, bases):
+            pd_s[rows, :] = pd
+            base_s[rows, :] = base
+        return dgain
+    dgain = lax.fori_loop(0, steps // BACK_A, stage_a, jnp.zeros((8, 128), f32))
     dgain_ref[0, 0] = dgain
     def scan(j, state):
         c = steps - 1 - j
         rows = pl.ds(pl.multiple_of(c * C, C), C)
         sb = state.astype(bf)
         ds_s[rows, :] = sb
-        return tn(f_ref[0, 0, rows, :], sb) + base_s[rows, :]
+        return nn(sb, f_ref[0, 0, rows, :]) + base_s[rows, :]
     lax.fori_loop(0, steps, scan, jnp.zeros((C, C), f32), unroll=True)
     row8 = lax.broadcasted_iota(jnp.int32, (8, 128), 0)
     lane = lax.broadcasted_iota(jnp.int32, (C, 128), 1)
@@ -217,71 +229,74 @@
 
     def stage_c(j, carry):
         nq, nk, nv, dws = carry
-        c = steps - 1 - j
-        lo = pl.multiple_of(c * C, C)
-        rows = pl.ds(lo, C)
-        aux = aux_columns(aux_ref, rows)
-        carried = aux[:, 1:2]
-        tail = aux[:, 2:3]
-        xq = q_ref[0, rows, :].astype(f32)
-        xk = k_ref[0, rows, :].astype(f32)
-        xv = v_ref[0, rows, :].astype(f32)
-        cq, sq, q, rq, shq = act_stage(xq, prev_rows(q_ref, lo), aux, w_ref[0], True)
-        ck, sk, k, rk, shk = act_stage(xk, prev_rows(k_ref, lo), aux, w_ref[1], True)
-        cv, sv, v, _, shv = act_stage(xv, prev_rows(v_ref, lo), aux, w_ref[2], False)
-        bblock = b_ref[0, rows, :].astype(f32)
-        beta = beta_column(bblock, h)
-        strict, inclusive = masks(aux, aux_ref[0, 0:1, rows])
-        kb = k.astype(bf)
-        qb = q.astype(bf)
-        st = s_ref[0, 0, rows, :]
-        dst = ds_s[rows, :]
-        fresh = fresh_ref[0, 0, rows, :]
-        do = do_s[rows, :]
-        gram = nt(kb, kb)
-        kk = nn(kb, jnp.concatenate([dst, st], axis=1))
-        dfresh = pd_s[rows, :] + tail * kk[:, :128]
-        x = v - carried * kk[:, 128:]
-        y = tn(t_ref[0, 0, rows, :], dfresh)
-        dx = beta * y
-        cdx = (carried * dx).astype(bf)
-        yb = y.astype(bf)
-        dob = do.astype(bf)
-        both = nt(jnp.concatenate([dob, yb], axis=0), fresh)
-        dp = jnp.where(inclusive, both[:C], 0.0)
-        da = jnp.where(strict, -both[C:], 0.0)
-        dbeta = jnp.sum(y * x, axis=-1, keepdims=True) + jnp.sum(da * gram, axis=-1, keepdims=True)
-        dg = beta * da
-        dgs = dg + dg.T
-        through = nt(jnp.concatenate([carried * do, -(carried * dx)], axis=0), st)
-        dpb = dp.astype(bf)
-        dq = through[:C] + nn(dpb, kb)
-        dk = through[C:] + tn(dpb, qb) + nt(tail * fresh.astype(f32), dst) + nn(dgs, kb)
-        dv = dx
-        db = dbeta * beta * (1.0 - beta)
-        bl = pl.ds(4 * heads * 128, 128)
-        @pl.when(h == 0)
-        def _():
-            draw_ref[0, rows, bl] = jnp.where(lane == 0, db, 0.0).astype(bf)
-        @pl.when(h > 0)
-        def _():
-            old = draw_ref[0, rows, bl]
-            draw_ref[0, rows, bl] = jnp.where(lane == h, db.astype(bf).astype(f32), old.astype(f32)).astype(bf)
-        dq = rq * (dq - q * jnp.sum(q * dq, axis=-1, keepdims=True))
-        dk = rk * (dk - k * jnp.sum(k * dk, axis=-1, keepdims=True))
-        dcq = dq * (sq * (1.0 + cq * (1.0 - sq)))
-        dck = dk * (sk * (1.0 + ck * (1.0 - sk)))
-        dcv = dv * (sv * (1.0 + cv * (1.0 - sv)))
-        rq_, wq = conv_back(dcq, nq, aux, w_ref[0], xq, shq)
-        rk_, wk = conv_back(dck, nk, aux, w_ref[1], xk, shk)
-        rv_, wv = conv_back(dcv, nv, aux, w_ref[2], xv, shv)
-        for t, val in ((0, rq_), (1, rk_), (2, rv_)):
-            draw_ref[0, rows, pl.ds(pl.multiple_of((t * heads + h) * 128, 128), 128)] = val.astype(bf)
-        dws = tuple(a + b for a, b in zip(dws, wq + wk + wv))
-        return dcq[:8], dck[:8], dcv[:8], dws
+        parts = []
+        for n in range(BACK_C):
+            lo = pl.multiple_of((steps - 1 - j * BACK_C - n) * C, C)
+            rows = pl.ds(lo, C)
+            aux = aux_columns(aux_ref, rows)
+            xq = q_ref[0, rows, :].astype(f32)
+            xk = k_ref[0, rows, :].astype(f32)
+            xv = v_ref[0, rows, :].astype(f32)
+            aq = act_stage(xq, prev_rows(q_ref, lo), aux, w_ref[0], True)
+            ak = act_stage(xk, prev_rows(k_ref, lo), aux, w_ref[1], True)
+            av = act_stage(xv, prev_rows(v_ref, lo), aux, w_ref[2], False)
+            beta = beta_column(b_ref[0, rows, :].astype(f32), h)
+            kb, qb = ak[2].astype(bf), aq[2].astype(bf)
+            parts.append((rows, aux, xq, xk, xv, aq, ak, av, beta, kb, qb))
+        grams = [nt(p[9], p[9]) for p in parts]
+        from_next = [nt(p[9], ds_s[p[0], :]) for p in parts]
+        from_state = [nn(p[9], s_ref[0, 0, p[0], :]) for p in parts]
+        ys = [tn(t_ref[0, 0, p[0], :], pd_s[p[0], :] + p[1][:, 2:3] * d) for p, d in zip(parts, from_next)]
+        boths = [
+            nt(jnp.concatenate([do_s[p[0], :].astype(bf), y.astype(bf)], axis=0), fresh_ref[0, 0, p[0], :]) for p, y in zip(parts, ys)
+        ]
+        dxs = [p[8] * y for p, y in zip(parts, ys)]
+        throughs = [
+            nt(jnp.concatenate([p[1][:, 1:2] * do_s[p[0], :], -(p[1][:, 1:2] * dx)], axis=0), s_ref[0, 0, p[0], :])
+            for p, dx in zip(parts, dxs)
+        ]
+        freshes = [nn(p[1][:, 2:3] * fresh_ref[0, 0, p[0], :].astype(f32), ds_s[p[0], :]) for p in parts]
+        dps, dgss, dbetas = [], [], []
+        for p, gram, state, y, both in zip(parts, grams, from_state, ys, boths):
+            rows, aux, beta = p[0], p[1], p[8]
+            strict, inclusive = masks(aux, aux_ref[0, 0:1, rows])
+            x = p[7][2] - aux[:, 1:2] * state
+            dps.append(jnp.where(inclusive, both[:C], 0.0).astype(bf))
+            da = jnp.where(strict, -both[C:], 0.0)
+            dbetas.append(jnp.sum(y * x, axis=-1, keepdims=True) + jnp.sum(da * gram, axis=-1, keepdims=True))
+            dg = beta * da
+            dgss.append(dg + dg.T)
+        dqs = [t[:C] + nn(dp, p[9]) for p, t, dp in zip(parts, throughs, dps)]
+        dks = [
+            t[C:] + f + tn(dp, p[10]) + nn(dgs, p[9]) for p, t, f, dp, dgs in zip(parts, throughs, freshes, dps, dgss)
+        ]
+        for p, dq, dk, dv, dbeta in zip(parts, dqs, dks, dxs, dbetas):
+            rows, aux, xq, xk, xv, (cq, sq, q, rq, shq), (ck, sk, k, rk, shk), (cv, sv, v, _, shv), beta = p[:9]
+            db = dbeta * beta * (1.0 - beta)
+            bl = pl.ds(4 * heads * 128, 128)
+            @pl.when(h == 0)
+            def _():
+                draw_ref[0, rows, bl] = jnp.where(lane == 0, db, 0.0).astype(bf)
+            @pl.when(h > 0)
+            def _():
+                old = draw_ref[0, rows, bl]
+                draw_ref[0, rows, bl] = jnp.where(lane == h, db.astype(bf).astype(f32), old.astype(f32)).astype(bf)
+            dq = rq * (dq - q * jnp.sum(q * dq, axis=-1, keepdims=True))
+            dk = rk * (dk - k * jnp.sum(k * dk, axis=-1, keepdims=True))
+            dcq = dq * (sq * (1.0 + cq * (1.0 - sq)))
+            dck = dk * (sk * (1.0 + ck * (1.0 - sk)))
+            dcv = dv * (sv * (1.0 + cv * (1.0 - sv)))
+            rq_, wq = conv_back(dcq, nq, aux, w_ref[0], xq, shq)
+            rk_, wk = conv_back(dck, nk, aux, w_ref[1], xk, shk)
+            rv_, wv = conv_back(dcv, nv, aux, w_ref[2], xv, shv)
+            for t, val in ((0, rq_), (1, rk_), (2, rv_)):
+                draw_ref[0, rows, pl.ds(pl.multiple_of((t * heads + h) * 128, 128), 128)] = val.astype(bf)
+            dws = tuple(a + b for a, b in zip(dws, wq + wk + wv))
+            nq, nk, nv = dcq[:8], dck[:8], dcv[:8]
+        return nq, nk, nv, dws
     z8 = jnp.zeros((8, 128), f32)
     taps = w_ref.shape[1]
-    _, _, _, dws = lax.fori_loop(0, steps, stage_c, (z8, z8, z8, (z8,) * (3 * taps)), unroll=2)
+    _, _, _, dws = lax.fori_loop(0, steps // BACK_C, stage_c, (z8, z8, z8, (z8,) * (3 * taps)))
     for n, d in enumerate(dws):
         dconv_ref[0, 0, n] = d
 
@@ -449,15 +464,16 @@
 
 
 def head_kernel(
-    x_ref, wq_ref, wk_ref, wv_ref, wg_ref, wb_ref, gate_ref, up_ref, out_ref, gain_ref,
+    x_ref, wq_ref, wk_ref, wv_ref, wg_ref, wb_ref, gate_ref, up_ref, down_ref, out_ref, gain_ref,
     normed_ref, raw_ref, hw_ref, own_ref, gu_ref, wo_ref,
     buf, w, low, acc, ag_send, ag_recv, w_send, w_recv, load_sem, out_sem, raw_sem, hw_sem, z_send, z_recv, u_send, u_recv,
 ):
     gx, gy, dp = lax.axis_index("gx"), lax.axis_index("gy"), lax.axis_index("dp")
     ngx = 4
-    piece = gu_ref.shape[0]
-    parts = x_ref.shape[1] // piece
     units = gu_ref.shape[1] // 2
+    parts = (x_ref.shape[1] + units // 2) // gu_ref.shape[0]
+    piece = x_ref.shape[1] // parts
+    down_piece = units // 2 // parts
     unit_other = pl.multiple_of((1 - gy) * (gate_ref.shape[1] - units), 128)
     turn = flipped(dp, 0, parts)
     rows_sent = pl.ds(pl.multiple_of(turn * piece, piece), piece)
@@ -484,8 +500,15 @@
     gather = Gather(buf, ag_send, ag_recv, gx, gy, True)
     gather.start()
     extra = [
-        remote(gate_ref.at[rows_sent, pl.ds(unit_other, units)], gu_ref.at[:, pl.ds(0, units)], u_send.at[0], u_recv.at[0], xn),
-        remote(up_ref.at[rows_sent, pl.ds(unit_other, units)], gu_ref.at[:, pl.ds(units, units)], u_send.at[1], u_recv.at[1], xn),
+        remote(gate_ref.at[rows_sent, pl.ds(unit_other, units)], gu_ref.at[pl.ds(0, piece), pl.ds(0, units)], u_send.at[0], u_recv.at[0], xn),
+        remote(up_ref.at[rows_sent, pl.ds(unit_other, units)], gu_ref.at[pl.ds(0, piece), pl.ds(units, units)], u_send.at[1], u_recv.at[1], xn),
+        remote(
+            down_ref.at[pl.ds(pl.multiple_of(unit_other + units // 2 + turn * down_piece, 32), down_piece), :],
+            gu_ref.at[pl.ds(piece, down_piece), pl.ds(0, x_ref.shape[1])],
+            u_send.at[3],
+            u_recv.at[3],
+            xn,
+        ),
         remote(out_ref.at[pl.ds(pl.multiple_of((1 - gy) * width, width), width), :], wo_ref, u_send.at[2], u_recv.at[2], xn),
     ]
     for c in extra:
@@ -558,7 +581,7 @@
     gather.finish()
 
 
-def head_project(inputs, w_query, w_key, w_value, w_gate_head, w_beta, w_gate, w_up, w_out, gain, units, parts, collective):
+def head_project(inputs, w_query, w_key, w_value, w_gate_head, w_beta, w_gate, w_up, w_down, w_out, gain, units, parts, collective):
     total, part = inputs.shape
     rows = total // 2
     feat = 2 * part
@@ -566,14 +589,14 @@
     sd = jax.ShapeDtypeStruct
     return pl.pallas_call(
         head_kernel,
-        in_specs=[ANY] * 9 + [VM],
+        in_specs=[ANY] * 10 + [VM],
         out_specs=[ANY, ANY, ANY, VM, ANY, ANY],
         out_shape=[
             sd((8, rows, feat), bf),
             sd((8, rows, cols), f32),
             sd((feat, cols), bf),
             sd((rows, feat), bf),
-            sd((part // parts, 2 * units), bf),
+            sd(((part + units // 2) // parts, 2 * units), bf),
             sd((w_out.shape[0] // 2, w_out.shape[1]), bf),
         ],
         scratch_shapes=[
@@ -591,13 +614,13 @@
             pltpu.SemaphoreType.DMA((2,)),
             pltpu.SemaphoreType.DMA((4,)),
             pltpu.SemaphoreType.DMA((4,)),
-            pltpu.SemaphoreType.DMA((3,)),
-            pltpu.SemaphoreType.DMA((3,)),
+            pltpu.SemaphoreType.DMA((4,)),
+            pltpu.SemaphoreType.DMA((4,)),
         ],
         compiler_params=pltpu.CompilerParams(collective_id=collective, has_side_effects=True, vmem_limit_bytes=60 << 20),
         cost_estimate=lasting(80),
         name="head_project",
-    )(inputs, w_query, w_key, w_value, w_gate_head, w_beta, w_gate, w_up, w_out, gain)
+    )(inputs, w_query, w_key, w_value, w_gate_head, w_beta, w_gate, w_up, w_down, w_out, gain)
 
 
 def mlp_kernel(x_ref, gate_ref, up_ref, down_ref, y_ref, *refs, parts):
@@ -630,13 +653,15 @@
         pltpu.make_async_copy(up_ref.at[:, own_units], wgu.at[near, pl.ds(units, units)], w_sem.at[1]),
         pltpu.make_async_copy(down_ref.at[own_units, :], wd.at[:, near], w_sem.at[2]),
     ]
-    w_loads.append(pltpu.make_async_copy(piece_ref, wd.at[:, pl.ds(far, half)], w_sem.at[3]))
+    w_loads.append(pltpu.make_async_copy(piece_ref, wd.at[pl.ds(0, units // 2), pl.ds(far, half)], w_sem.at[3]))
     for n in range(parts):
         turn = flipped(dp, n, parts)
         piece = half // parts
-        w_loads.append(
-            pltpu.make_async_copy(gu_refs[n], wgu.at[pl.ds(pl.multiple_of(far + turn * piece, piece), piece), :], w_sem.at[4 + n])
-        )
+        down_piece = units // 2 // parts
+        gu_rows = wgu.at[pl.ds(pl.multiple_of(far + turn * piece, piece), piece), :]
+        down_rows = wd.at[pl.ds(pl.multiple_of(units // 2 + turn * down_piece, 32), down_piece), pl.ds(far, half)]
+        w_loads.append(pltpu.make_async_copy(gu_refs[n].at[pl.ds(0, piece)], gu_rows, w_sem.at[4 + 2 * n]))
+        w_loads.append(pltpu.make_async_copy(gu_refs[n].at[pl.ds(piece, down_piece), pl.ds(0, half)], down_rows, w_sem.at[5 + 2 * n]))
     for c in w_loads:
         c.start()
     entry_barrier([slot_peer(r, gx, gy) for r in (1, 2, 3)])
@@ -734,7 +759,7 @@
             pltpu.VMEM((2, rows, units), bf),
             pltpu.VMEM((2, rows, 2 * units), bf),
             pltpu.SemaphoreType.DMA,
-            pltpu.SemaphoreType.DMA((4 + parts,)),
+            pltpu.SemaphoreType.DMA((4 + 2 * parts,)),
             pltpu.SemaphoreType.DMA((2,)),
             pltpu.SemaphoreType.DMA((2, 2)),
             pltpu.SemaphoreType.DMA((2,)),
@@ -874,7 +899,7 @@
 
 def out_kernel(
     mixed_ref, out_ref, piece_ref, x_ref, gain_ref,
-    middle_ref, normed_ref, slots_ref,
+    middle_ref, normed_ref, slots_ref, other_ref,
     give, take, acc, diag_in, last_in, s_core, r_core, s_link, r_link, lhs, w, total, load_sem, lhs_sem, keep_sem,
 ):
     gx, gy = lax.axis_index("gx"), lax.axis_index("gy")
@@ -901,12 +926,13 @@
 
         lax.fori_loop(0, feat // tile, body, 0)
 
-    scatter = Scatter(give, take, acc, diag_in, last_in, s_core, r_core, s_link, r_link, gx, gy, True)
+    scatter = Scatter(give, take, acc, diag_in, last_in, s_core, r_core, s_link, r_link, gx, gy)
     scatter.run(product, total)
     keep = pltpu.make_async_copy(lhs, slots_ref, keep_sem)
     keep.start()
     middle = x_ref[...].astype(f32) + total[...]
     middle_ref[...] = middle
+    other_ref[...] = middle_ref[:, pl.ds(pl.multiple_of((1 - gy) * (feat // 2), feat // 2), feat // 2)].astype(bf)
     rate = lax.rsqrt(jnp.mean(middle * middle, axis=-1, keepdims=True) + EPS)
     normed_ref[...] = (middle * rate * gain_ref[...]).astype(bf)
     keep.wait()
@@ -920,8 +946,8 @@
     return pl.pallas_call(
         out_kernel,
         in_specs=[ANY, ANY, ANY, VM, VM],
-        out_specs=[VM, VM, ANY],
-        out_shape=[sd((rows, feat), f32), sd((rows, feat), bf), sd(mixed.shape, bf)],
+        out_specs=[VM, VM, ANY, VM],
+        out_shape=[sd((rows, feat), f32), sd((rows, feat), bf), sd(mixed.shape, bf), sd((rows, feat // 2), bf)],
         scratch_shapes=scatter_scratch(rows, feat)
         + [
             pltpu.VMEM(mixed.shape, bf),
@@ -1236,12 +1262,6 @@
     return lax.psum_scatter(value.astype(bf), "dp", scatter_dimension=0, tiled=True)
 
 
-def rows_to_dp(left, right):
-    part = left.shape[1] // 2
-    halves_of = [dot_w(left[:, i * part : (i + 1) * part], right).astype(bf) for i in range(2)]
-    return halves_of
-
-
 def sort_halves(parts):
     first = lax.axis_index("gy") == 0
     return jnp.where(first, parts[0], parts[1]), swap(jnp.where(first, parts[1], parts[0]))
@@ -1278,7 +1298,7 @@
     units = -(-block // (ngy * 256)) * 256
     parts = ndp if ndp == 4 else 1
     normed, raw, head_w, x_own, gu_piece, out_piece = head_project(
-        inputs.reshape(nb * part_rows, part_feat), w_query, w_key, w_value, w_gate_head, beta_w, w_gate, w_up, w_out,
+        inputs.reshape(nb * part_rows, part_feat), w_query, w_key, w_value, w_gate_head, beta_w, w_gate, w_up, w_down, w_out,
         norm_gain[None], units, parts, 5,
     )
     normed = normed.reshape(tokens, feat)
@@ -1289,7 +1309,7 @@
 
     gu_pieces = around(gu_piece)
     x_own, grad_y, w_down = lax.optimization_barrier((x_own, grad_y, w_down))
-    down_piece = swap(lax.dynamic_slice_in_dim(w_down, (1 - gy) * (block - units), units, 0))
+    down_piece = swap(lax.dynamic_slice_in_dim(w_down, (1 - gy) * (block - units), units // 2, 0))
     y_all = lax.all_gather(grad_y, ("gx", "gy"), axis=0, tiled=False)
 
     aux = make_aux(segments)
@@ -1297,7 +1317,7 @@
     conv_local = lax.dynamic_slice_in_dim(conv_kernel, conv_start, width, 2)
     gain_row = head_gain[None]
     mixed, *saved = mixer_fwd(raw, aux, conv_local, gain_row)
-    middle, second_own, mixed_slots = out_project(
+    middle, second_own, mixed_slots, middle_half = out_project(
         mixed.reshape(8, own_rows, width), w_out, out_piece, x_own, mlp_gain[None], 1
     )
     second, hidden, grads, y_rel, gate_up, down_w = mlp_forward(
@@ -1331,19 +1351,17 @@
     )
     draw = draw.reshape(tokens, -1)
     gu_pair = sort_halves(gu_sums)
-    middle_other = swap(lax.dynamic_slice_in_dim(middle, (1 - gy) * half, half, 1).astype(bf))
+    middle_other = swap(middle_half)
     draw, down_sum, out_rows, middle_other, *gu_pair = lax.optimization_barrier((draw, down_sum, out_rows, middle_other, *gu_pair))
     out_sum = scatter_dp(out_rows)
     main = 4 * width
-    both = rows_to_dp(normed, draw)
-    norm_gain_grad = jnp.sum(jnp.concatenate(both, axis=0).astype(f32) * head_w.astype(f32), axis=1) / norm_gain
-    beta_grad = jnp.concatenate([g[:, main : main + heads] for g in both], axis=0).astype(f32)
-    head_grads = [g[:, :main] for g in both]
-    draw, hidden, *head_grads = lax.optimization_barrier((draw, hidden, *head_grads))
-    head_sums = [scatter_dp(g) for g in head_grads]
+    both = dot_w(normed, draw).astype(bf)
+    norm_gain_grad = jnp.sum(both.astype(f32) * head_w.astype(f32), axis=1) / norm_gain
+    beta_grad = both[:, main : main + heads].astype(f32)
+    head_grads = both[:, :main].reshape(2, half, main)
+    draw, hidden, head_grads = lax.optimization_barrier((draw, hidden, head_grads))
+    head_sums = list(lax.psum_scatter(head_grads, "dp", scatter_dimension=1, tiled=True))
     hidden, out_sum = lax.optimization_barrier((hidden, out_sum))
-    sum_down, sum_out = down_sum.astype(f32), out_sum.astype(f32)
-    grad_gu_mine, grad_gu_other = gu_pair
     flat = [beta_grad.T, conv_grad, norm_gain_grad, jnp.sum(mlp_gain_parts, axis=0), gain_grad]
     counts = [v.size // 128 for v in flat]
     small = jnp.concatenate([v.reshape(-1, 128) for v in flat])
@@ -1355,6 +1373,9 @@
         middle_other, norm_gain[None], small, parts, 3,
     )
 
+    grad_inputs, layer_out, down_sum, out_sum, *gu_pair = lax.optimization_barrier((grad_inputs, layer_out, down_sum, out_sum, *gu_pair))
+    sum_down, sum_out = down_sum.astype(f32), out_sum.astype(f32)
+    grad_gu_mine, grad_gu_other = gu_pair
     head_mine, head_other = sort_halves(head_sums)
 
     def unit_columns(i):

time: 634 us -> 596 us (0.940)
  Pallas kernels: 472 us -> 450 us
    pallas_call x1, Pallas kernels: 60.5 us -> 47.6 us  [mixer_bwd(): pl.pallas_call(bwd_kernel, grid=(nb, heads), in_specs=specs(length, heads...]
    pallas_call x1, Pallas kernels: 68.2 us -> 55.4 us  [out_project(): pl.pallas_call(out_kernel, in_specs=[ANY, ANY, ANY, VM, VM], out_specs=[V...]
    dot_general x6 -> x5, matrix products: 56.7 us -> 54.9 us  [dot_w(): lax.dot_general(a, b, (((0,), (0,)), ((), ())), preferred_element_type=f32)]
  transfers between devices with their start and end apart: 16 -> 15, of which waited for: 1 -> 2; matrix products, arithmetic and copies ran while one was open for 14% -> 13% of each run, Pallas kernels for 56% -> 55%
where the time goes in v5:
time: 596 us; the launch traced here: 587 us
  Pallas kernels  450 us (76%)
  matrix products  54.9 us (9%)
  local copies, waits for them, and re-layouts  24.2 us (4%)
  other arithmetic  19.9 us (3%)
  between operations  15 us (3%)
  starting transfers between devices  14.3 us (2%)
  waiting for transfers between devices  8.78 us (1%)
    pallas_call x1, Pallas kernels, mlp_backward(): pl.pallas_call(back_kernel, in_specs=[ANY, ANY, ANY, ANY, VM, ANY, VM], o...  99 us
    pallas_call x1, Pallas kernels, final_sums(): pl.pallas_call(functools.partial(final_kernel, ndp=ndp), in_specs=[ANY] *...  89.3 us
    pallas_call x1, Pallas kernels, head_project(): pl.pallas_call(head_kernel, in_specs=[ANY] * 10 + [VM], out_specs=[ANY, A...  77.1 us
    pallas_call x1, Pallas kernels, out_project(): pl.pallas_call(out_kernel, in_specs=[ANY, ANY, ANY, VM, VM], out_specs=[V...  55.4 us
    dot_general x5, matrix products, dot_w(): lax.dot_general(a, b, (((0,), (0,)), ((), ())), preferred_element_type=f32)  54.9 us
    pallas_call x1, Pallas kernels, mlp_forward(): pl.pallas_call(functools.partial(mlp_kernel, parts=parts), in_specs=[ANY]...  48.5 us
    pallas_call x1, Pallas kernels, mixer_bwd(): pl.pallas_call(bwd_kernel, grid=(nb, heads), in_specs=specs(length, heads...  47.6 us
    pallas_call x1, Pallas kernels, mixer_fwd(): pl.pallas_call(fwd_kernel, grid=(nb, heads), in_specs=specs(length, heads...  33 us
  transfers between devices with their start and end apart: 15, of which 2 were waited for; matrix products, arithmetic and copies ran while one was open for 13% of the time, Pallas kernels for 55%

profile of v5, /device:TPU:0, one launch (start us, length us, event | category | flops | bytes accessed | tf_op | source)
XLA Modules:
  0.0 587.2 jit_solution(8909957999606230719)
XLA Ops:
  7.2 0.7 reshape.139
  8.0 0.5 copy.62
  8.4 0.5 pad.33
  9.0 0.9 copy.91
  9.9 77.1 %head_project.1 = (bf16[8,256,2048]{2,1,0:T(8,128)(2,1)}, f32[8,256,1152]{2,1,0:T(8,128)}, bf16[2048,1152]{1,0:T(8,128)(2,1)}, bf16[256,2048]{1,0:T(8,128)(2,1)}...) custom-call(bf16[512,1024]{1,0:T(8,128)(2,1)} %bitcast.134, bf16[1024,512]{1,0:T(8,128)(2,1)} %wq_ref.1, ...), custom_call_target="tpu_custom_call" | custom-call | flops 92000002048 | bytes 1048576 | tf_op jit(solution)/shard_map/head_project/pallas_call | solution.py:590
  87.0 3.9 collective-permute-start
  90.9 1.0 collective-permute-start.1
  91.9 1.5 collective-permute-start.2
  93.4 1.2 constant_dynamic-slice_fusion.3
  94.5 0.6 collective-permute-start.3
  96.0 1.4 stack.90.aux_ref
  97.4 0.6 constant_dynamic-slice_fusion.4.w_ref
  98.0 33.0 %mixer_forward.1 = (bf16[2,1024,256]{2,1,0:T(8,128)(2,1)}, bf16[2,2,1024,128]{3,2,1,0:T(8,128)(2,1)}, bf16[2,2,1024,128]{3,2,1,0:T(8,128)(2,1)}, bf16[2,2,1024,1...) custom-call(f32[2,1024,1152]{2,1,0:T(8,128)} %bitcast.119, ...), custom_call_target="tpu_custom_call" | custom-call | flops 37950001152 | bytes 1048576 | tf_op jit(solution)/shard_map/mixer_forward/pallas_call | solution.py:149
  131.0 55.4 %out_project.1 = (f32[256,2048]{1,0:T(8,128)}, bf16[256,2048]{1,0:T(8,128)(2,1)}, bf16[8,256,256]{2,1,0:T(8,128)(2,1)}, bf16[256,1024]{1,0:T(8,128)(2,1)}) custom-call(bf16[8,256,256]{2,1,0:T(8,128)(2,1)} %bitcast.160, bf16[512,1024]{1,0:T(8,128)(2,1)} %out_ref.5, bf16[256,1024]{1,0:T(8,128)(2,1)} %get-tuple-element.88.piece_ref, ...), custom_call_target="tpu_custom_call" | custom-call | flops 50600001536 | bytes 1048576 | tf_op jit(solution)/shard_map/out_project/pallas_call | solution.py:946
  186.5 0.8 copy-done.19
  187.7 48.5 %mlp_forward.1 = (bf16[8,256,2048]{2,1,0:T(8,128)(2,1)}, bf16[8,256,768]{2,1,0:T(8,128)(2,1)}, bf16[8,256,1536]{2,1,0:T(8,128)(2,1)}, bf16[8,256,2048]{2,1,0:T(8...) custom-call(bf16[256,2048]{1,0:T(8,128)(2,1)} %get-tuple-element.91.x_ref, ...), custom_call_target="tpu_custom_call" | custom-call | flops 78199996416 | bytes 1048576 | tf_op jit(solution)/shard_map/mlp_forward/pallas_call | solution.py:742
  236.2 11.4 %fusion.7 = bf16[1024,1536]{1,0:T(8,128)(2,1)} fusion(bf16[2048,1536]{1,0:T(8,128)(2,1)} %bitcast.158, bf16[2048,2048]{1,0:T(8,128)(2,1)} %bitcast.156), kind=kOutput, calls=%fused_computation.7 | convolution fusion | flops 6444023808 | bytes 13631488 | tf_op jit(solution)/shard_map/dot_general | solution.py:1240
  247.7 10.1 %convolution_convert_fusion.1 = bf16[768,2048]{1,0:T(8,128)(2,1)S(1)} fusion(bf16[2048,768]{1,0:T(8,128)(2,1)} %bitcast.132, bf16[2048,2048]{1,0:T(8,128)(2,1)} %bitcast.155), kind=kOutput, calls=%fused_computation.12 | convolution fusion | flops 6444023808 | bytes 14680064 | tf_op jit(solution)/shard_map/dot_general | solution.py:1240
  257.9 11.5 %fusion.4 = bf16[1024,1536]{1,0:T(8,128)(2,1)} fusion(bf16[2048,1536]{1,0:T(8,128)(2,1)} %bitcast.159, bf16[2048,2048]{1,0:T(8,128)(2,1)} %bitcast.157), kind=kOutput, calls=%fused_computation.6 | convolution fusion | flops 6444023808 | bytes 13631488 | tf_op jit(solution)/shard_map/dot_general | solution.py:1240
  269.5 2.1 constant_dynamic-slice_fusion.2
  271.5 0.7 collective-permute-start.4
  272.2 99.0 %mlp_backward.1 = (bf16[8,256,2048]{2,1,0:T(8,128)(2,1)}, bf16[8,256,256]{2,1,0:T(8,128)(2,1)}, f32[8,2048]{1,0:T(8,128)}) custom-call(bf16[8,256,1536]{2,1,0:T(8,128)(2,1)} %get-tuple-element.101.grads_ref, bf16[2048,1536]{1,0:T(8,128)(2,1)} %get-tuple-element.102.wgu_ref, bf16[512,1024]{1,0:T(8,128)(2,1)} %out_ref.5, ...), custom_call_target="tpu_custom_call" | custom-call | flops 23000000512 | bytes 1048576 | tf_op jit(solution)/shard_map/mlp_backward/pallas_call | solution.py:1031
  371.3 2.0 fusion.14
  373.3 0.6 fusion.12
  373.9 1.8 pad_maximum_fusion
  375.8 0.4 reduce-scatter.12.cloned.1.call-start
  376.3 5.8 fusion.10
  382.2 2.7 collective-permute-start.5
  384.9 1.0 broadcast_select_fusion
  385.9 2.0 collective-permute-start.6
  387.9 47.6 %mixer_backward.1 = (bf16[2,1024,1152]{2,1,0:T(8,128)(2,1)}, f32[2,2,12,8,128]{4,3,2,1,0:T(8,128)}, f32[2,2,8,128]{3,2,1,0:T(8,128)}) custom-call(f32[2,1024,1152]{2,1,0:T(8,128)} %bitcast.124, f32[2,1024,1152]{2,1,0:T(8,128)} %bitcast.125, f32[2,1024,1152]{2,1,0:T(8,128)} %bitcast.126, f32[2,1024,1152]{2,1,0:T(8,128)} %bitcast.127, ...), custom_call_target="tpu_custom_call" | custom-call | flops 2300000000 | bytes 1048576 | tf_op jit(solution)/shard_map/mixer_backward/pallas_call | solution.py:309
  435.5 1.3 broadcast_select_fusion.3
  436.8 1.0 pad_maximum_fusion.1
  438.1 16.0 %multiply_reduce_fusion = (f32[2048]{0:T(1024)S(1)}, bf16[2048,1152]{1,0:T(8,128)(2,1)S(1)}) fusion(bf16[2048,1152]{1,0:T(8,128)(2,1)} %get-tuple-element.120.hw_ref, bf16[2048,2048]{1,0:T(8,128)(2,1)} %bitcast.154, bf16[2048,1152]{1,0:T(8,128)(2,1)} %bitcast.130), kind=kOutput, calls=%fused_computation | convolution fusion | flops 9675470848 | bytes 22552576 | tf_op jit(solution)/shard_map/dot_general | solution.py:1240
  454.1 3.0 slice.140
  457.1 0.5 copy-done.3
  457.7 0.8 copy-done.14
  458.7 1.1 convert_bitcast_fusion
  460.5 0.6 pad.40.small_ref
  461.1 3.7 reduce-scatter.12.cloned.1.call-done
  464.8 89.3 %final_sums.1 = (bf16[2,256,1024]{2,1,0:T(8,128)(2,1)}, bf16[2,256,1024]{2,1,0:T(8,128)(2,1)}, f32[8,96,128]{2,1,0:T(8,128)}) custom-call(bf16[8,256,1152]{2,1,0:T(8,128)(2,1)} %bitcast.131, bf16[2048,1152]{1,0:T(8,128)(2,1)} %get-tuple-element.120.hw_ref, bf16[8,256,768]{2,1,0:T(8,128)(2,1)} %get-tuple-element.123.hidden_ref, ...), custom_call_target="tpu_custom_call" | custom-call | flops 5750000128 | bytes 1048576 | tf_op jit(solution)/shard_map/final_sums/pallas_call | solution.py:1193
  554.1 0.9 slice.125
  555.1 0.7 reshape.160
  555.8 1.2 slice_bitcast_fusion
  557.3 0.9 slice_reduce_fusion
  558.6 0.5 slice_bitcast_fusion.6
  559.1 1.2 maximum_convert_fusion
  560.3 1.3 select_bitcast_fusion.1
  561.6 1.2 collective-permute-start.8
  562.8 0.7 constant_dynamic-slice_fusion
  563.5 0.9 slice.128
  564.4 0.6 reshape.161
  565.1 0.6 copy.82
  565.7 0.8 convert_element_type.89
  566.6 1.3 convert_element_type.92
  567.9 0.6 slice_bitcast_fusion.4
  568.5 1.2 maximum_convert_fusion.1
  569.7 4.9 collective-permute-done.8
  574.7 0.9 maximum_convert_fusion.2
  575.5 0.9 maximum_convert_fusion.3
  576.4 0.9 maximum_convert_fusion.4
  577.3 0.9 maximum_convert_fusion.5
  578.1 1.0 copy.99
  579.1 1.0 copy.100
  (103 shorter events, 3.4 us)
Async XLA Ops:
  7.2 90.2 %copy-start = (f32[3,4,2048]{2,1,0:T(4,128)S(1)}, f32[3,4,2048]{2,1,0:T(4,128)}, u32[]{:S(2)}) copy-start(f32[3,4,2048]{2,1,0:T(4,128)} %param.24) | copy-start | bytes 294916
  7.2 179.3 %all-gather.3.cloned.1.call-start = ((), (), s32[]{:S(2)}) async-start(), calls=%async_computation.10 | async-start | bytes 9437184 | tf_op jit(solution)/shard_map/all_gather | solution.py:1313
  9.9 85.3 %copy-start.16 = (s32[2,1024]{1,0:T(2,128)S(1)}, s32[2,1024]{1,0:T(2,128)}, u32[]{:S(2)}) copy-start(s32[2,1024]{1,0:T(2,128)} %param.17) | copy-start | bytes 24580
  87.0 288.8 %reduce-scatter.6.cloned.1.call-start = ((), (), s32[]{:S(2)}) async-start(), calls=%async_computation.5 | async-start | bytes 3932160 | tf_op jit(solution)/shard_map/reduce_scatter | solution.py:1262
  87.0 99.4 %collective-permute-start = (bf16[352,1536]{1,0:T(8,128)(2,1)}, bf16[352,1536]{1,0:T(8,128)(2,1)S(1)}, u32[]{:S(2)}, u32[]{:S(2)}) collective-permute-start(bf16[352,1536]{1,0:T(8,128)(2,1)} %get-tuple-element.94.refs_0_), channel_id=1, source_target_pairs={{0,8},{8,0},{16,24},{24,16},{1,9},{9,1},{17,25},{25,17},{2,10},{10... | collective-permute-start | bytes 3244040 | tf_op jit(solution)/shard_map/ppermute | solution.py:1308
  90.9 95.5 %collective-permute-start.1 = (bf16[352,1536]{1,0:T(8,128)(2,1)}, bf16[352,1536]{1,0:T(8,128)(2,1)}, u32[]{:S(2)}, u32[]{:S(2)}) collective-permute-start(bf16[352,1536]{1,0:T(8,128)(2,1)} %get-tuple-element.94.refs_0_), channel_id=1, source_target_pairs={{0,16},{8,24},{16,0},{24,8},{1,17},{9,25},{17,1},{25,9},{2,18},{10... | collective-permute-start | bytes 3244040 | tf_op jit(solution)/shard_map/ppermute | solution.py:1308
  91.9 94.6 %collective-permute-start.2 = (bf16[352,1536]{1,0:T(8,128)(2,1)}, bf16[352,1536]{1,0:T(8,128)(2,1)}, u32[]{:S(2)}, u32[]{:S(2)}) collective-permute-start(bf16[352,1536]{1,0:T(8,128)(2,1)} %get-tuple-element.94.refs_0_), channel_id=1, source_target_pairs={{0,24},{8,16},{16,8},{24,0},{1,25},{9,17},{17,9},{25,1},{2,26},{10... | collective-permute-start | bytes 3244040 | tf_op jit(solution)/shard_map/ppermute | solution.py:1308
  94.5 91.9 %collective-permute-start.3 = (bf16[384,1024]{1,0:T(8,128)(2,1)S(1)}, bf16[384,1024]{1,0:T(8,128)(2,1)S(1)}, u32[]{:S(2)}, u32[]{:S(2)}) collective-permute-start(bf16[384,1024]{1,0:T(8,128)(2,1)S(1)} %constant_dynamic-slice_fusion.3), channel_id=1, source_target_pairs={{0,1},{1,0},{2,3},{3,2},{4,5},{5,4},{6,7},{7,6},{8,9},{9,8},{10,11... | collective-permute-start | bytes 2359304 | tf_op jit(solution)/shard_map/ppermute | solution.py:1244
  186.4 0.9 copy-start.19
  186.4 1.2 copy-start.18
  247.7 128.1 %reduce-scatter.8.cloned.1.call-start = ((), (), s32[]{:S(2)}) async-start(), calls=%async_computation.6 | async-start | bytes 3932160 | tf_op jit(solution)/shard_map/reduce_scatter | solution.py:1262
  269.4 168.5 %reduce-scatter.10.cloned.1.call-start = ((), (), s32[]{:S(2)}) async-start(), calls=%async_computation.7 | async-start | bytes 3604480 | tf_op jit(solution)/shard_map/reduce_scatter | solution.py:1262
  271.5 99.7 %collective-permute-start.4 = (bf16[768,1024]{1,0:T(8,128)(2,1)}, bf16[768,1024]{1,0:T(8,128)(2,1)}, u32[]{:S(2)}, u32[]{:S(2)}) collective-permute-start(bf16[768,1024]{1,0:T(8,128)(2,1)} %get-tuple-element.143), channel_id=1, source_target_pairs={{0,1},{1,0},{2,3},{3,2},{4,5},{5,4},{6,7},{7,6},{8,9},{9,8},{10,11... | collective-permute-start | bytes 4718600 | tf_op jit(solution)/shard_map/ppermute | solution.py:1244
  371.3 2.1 copy-start.2
  373.9 2.3 copy-start.4
  375.8 89.0 %reduce-scatter.12.cloned.1.call-start = ((), (), s32[]{:S(2)}) async-start(), calls=%async_computation.8 | async-start | bytes 1310720 | tf_op jit(solution)/shard_map/reduce_scatter | solution.py:1262
  376.2 8.6 %copy-start.7 = (bf16[256,1536]{1,0:T(8,128)(2,1)S(1)}, bf16[256,1536]{1,0:T(8,128)(2,1)}, u32[]{:S(2)}) copy-start(bf16[256,1536]{1,0:T(8,128)(2,1)} %reduce-scatter.6.cloned.1.call-done) | copy-start | bytes 2359300
  376.3 8.6 %copy-start.8 = (bf16[256,1536]{1,0:T(8,128)(2,1)S(1)}, bf16[256,1536]{1,0:T(8,128)(2,1)}, u32[]{:S(2)}) copy-start(bf16[256,1536]{1,0:T(8,128)(2,1)} %reduce-scatter.8.cloned.1.call-done) | copy-start | bytes 2359300
  382.2 53.3 %collective-permute-start.5 = (bf16[256,1024]{1,0:T(8,128)(2,1)S(1)}, bf16[256,1024]{1,0:T(8,128)(2,1)}, u32[]{:S(2)}, u32[]{:S(2)}) collective-permute-start(bf16[256,1024]{1,0:T(8,128)(2,1)S(1)} %constant_dynamic-slice_fusion.1), channel_id=1, source_target_pairs={{0,1},{1,0},{2,3},{3,2},{4,5},{5,4},{6,7},{7,6},{8,9},{9,8},{10,11... | collective-permute-start | bytes 1572872 | tf_op jit(solution)/shard_map/ppermute | solution.py:1244
  385.9 52.0 %collective-permute-start.7 = (bf16[256,1536]{1,0:T(8,128)(2,1)}, bf16[256,1536]{1,0:T(8,128)(2,1)}, u32[]{:S(2)}, u32[]{:S(2)}) collective-permute-start(bf16[256,1536]{1,0:T(8,128)(2,1)} %get-tuple-element.145), channel_id=1, source_target_pairs={{0,1},{1,0},{2,3},{3,2},{4,5},{5,4},{6,7},{7,6},{8,9},{9,8},{10,11... | collective-permute-start | bytes 2359304 | tf_op jit(solution)/shard_map/ppermute | solution.py:1244
  385.9 52.0 %collective-permute-start.6 = (bf16[256,1024]{1,0:T(8,128)(2,1)}, bf16[256,1024]{1,0:T(8,128)(2,1)}, u32[]{:S(2)}, u32[]{:S(2)}) collective-permute-start(bf16[256,1024]{1,0:T(8,128)(2,1)} %get-tuple-element.114), channel_id=1, source_target_pairs={{0,1},{1,0},{2,3},{3,2},{4,5},{5,4},{6,7},{7,6},{8,9},{9,8},{10,11... | collective-permute-start | bytes 1572872 | tf_op jit(solution)/shard_map/ppermute | solution.py:1244
  437.9 122.4 %reduce-scatter.14.cloned.1.call-start = ((), (), s32[]{:S(2)}) async-start(), calls=%async_computation.9 | async-start | bytes 5242880 | tf_op jit(solution)/shard_map/reduce_scatter | solution.py:1363
  454.1 3.5 copy-start.3
  457.6 0.8 copy-start.14
  457.6 1.0 copy-start.11
  457.6 1.0 copy-start.17
  457.6 2.5 copy-start.15
  558.3 4.5 copy-start.12
  558.3 7.4 %copy-start.10 = (bf16[128,1024]{1,0:T(8,128)(2,1)S(1)}, bf16[128,1024]{1,0:T(8,128)(2,1)}, u32[]{:S(2)}) copy-start(bf16[128,1024]{1,0:T(8,128)(2,1)} %reduce-scatter.12.cloned.1.call-done) | copy-start | bytes 786436
  559.1 7.4 %copy-start.9 = (bf16[352,1024]{1,0:T(8,128)(2,1)S(1)}, bf16[352,1024]{1,0:T(8,128)(2,1)}, u32[]{:S(2)}) copy-start(bf16[352,1024]{1,0:T(8,128)(2,1)} %reduce-scatter.10.cloned.1.call-done) | copy-start | bytes 2162692
  561.6 13.0 %collective-permute-start.8 = (bf16[256,1024]{1,0:T(8,128)(2,1)S(1)}, bf16[256,1024]{1,0:T(8,128)(2,1)S(1)}, u32[]{:S(2)}, u32[]{:S(2)}) collective-permute-start(bf16[256,1024]{1,0:T(8,128)(2,1)S(1)} %get-tuple-element.158), channel_id=1, source_target_pairs={{0,1},{1,0},{2,3},{3,2},{4,5},{5,4},{6,7},{7,6},{8,9},{9,8},{10,11... | collective-permute-start | bytes 1572872 | tf_op jit(solution)/shard_map/ppermute | solution.py:1244
  565.0 2.8 copy-start.13
  569.7 8.5 %copy-start.6 = (bf16[2,256,1024]{2,1,0:T(8,128)(2,1)S(1)}, bf16[2,256,1024]{2,1,0:T(8,128)(2,1)}, u32[]{:S(2)}) copy-start(bf16[2,256,1024]{2,1,0:T(8,128)(2,1)} %get-tuple-element.199) | copy-start | bytes 3145732
  574.7 4.4 copy-start.5
  575.5 4.5 copy-start.1
Sparse Core Ops, SparseCore 0:
  87.1 74.0 all-gather.2
  247.8 60.2 reduce-scatter.5
  310.4 60.2 reduce-scatter.7
  375.9 58.5 reduce-scatter.9
  438.0 26.7 reduce-scatter.11
  467.0 75.5 reduce-scatter.13

commit v6 on v5

--- a/solution.py
+++ b/solution.py
@@ -1050,7 +1050,7 @@
             pltpu.SemaphoreType.DMA((8,)),
         ],
         compiler_params=pltpu.CompilerParams(collective_id=collective, has_side_effects=True, vmem_limit_bytes=63 << 20),
-        cost_estimate=lasting(20),
+        cost_estimate=lasting(1),
         name="mlp_backward",
     )(grads, gate_up, w_out, piece, middle, y_rel, gain)
 
@@ -1329,8 +1329,8 @@
     gu_first = dot_w(second_flat[:, :half], grads_flat).astype(bf)
     hidden_flat, gu_first = lax.optimization_barrier((hidden_flat, gu_first))
     down_grad = dot_w(hidden_flat, y_flat).astype(bf)
-    second_flat, down_grad = lax.optimization_barrier((second_flat, down_grad))
     down_keep, down_send = halves(down_grad, 1)
+    second_flat, down_keep, down_send = lax.optimization_barrier((second_flat, down_keep, down_send))
     down_both = jnp.stack([down_keep, swap(down_send)])
     gu_second = dot_w(second_flat[:, half:], grads_flat).astype(bf)
     grads, gu_second = lax.optimization_barrier((grads, gu_second))

time: 596 us -> 595 us (level)
  no operation moved by 1% of the time
where the time goes in v6:
time: 595 us; the launch traced here: 586 us
  Pallas kernels  450 us (76%)
  matrix products  53.2 us (9%)
  local copies, waits for them, and re-layouts  24.4 us (4%)
  other arithmetic  19.9 us (3%)
  between operations  15 us (3%)
  starting transfers between devices  14.3 us (2%)
  waiting for transfers between devices  8.85 us (1%)
    pallas_call x1, Pallas kernels, mlp_backward(): pl.pallas_call(back_kernel, in_specs=[ANY, ANY, ANY, ANY, VM, ANY, VM], o...  99 us
    pallas_call x1, Pallas kernels, final_sums(): pl.pallas_call(functools.partial(final_kernel, ndp=ndp), in_specs=[ANY] *...  89.3 us
    pallas_call x1, Pallas kernels, head_project(): pl.pallas_call(head_kernel, in_specs=[ANY] * 10 + [VM], out_specs=[ANY, A...  77.1 us
    pallas_call x1, Pallas kernels, out_project(): pl.pallas_call(out_kernel, in_specs=[ANY, ANY, ANY, VM, VM], out_specs=[V...  55.4 us
    dot_general x5, matrix products, dot_w(): lax.dot_general(a, b, (((0,), (0,)), ((), ())), preferred_element_type=f32)  53.2 us
    pallas_call x1, Pallas kernels, mlp_forward(): pl.pallas_call(functools.partial(mlp_kernel, parts=parts), in_specs=[ANY]...  48.5 us
    pallas_call x1, Pallas kernels, mixer_bwd(): pl.pallas_call(bwd_kernel, grid=(nb, heads), in_specs=specs(length, heads...  47.6 us
    pallas_call x1, Pallas kernels, mixer_fwd(): pl.pallas_call(fwd_kernel, grid=(nb, heads), in_specs=specs(length, heads...  33 us
  transfers between devices with their start and end apart: 15, of which 2 were waited for; matrix products, arithmetic and copies ran while one was open for 13% of the time, Pallas kernels for 55%

profile of v6, /device:TPU:0, one launch (start us, length us, event | category | flops | bytes accessed | tf_op | source)
XLA Modules:
  0.0 585.7 jit_solution(13162895611289478322)
XLA Ops:
  7.2 0.7 reshape.139
  8.0 0.5 copy.62
  8.4 0.5 pad.33
  9.0 0.9 copy.91
  9.9 77.1 %head_project.1 = (bf16[8,256,2048]{2,1,0:T(8,128)(2,1)}, f32[8,256,1152]{2,1,0:T(8,128)}, bf16[2048,1152]{1,0:T(8,128)(2,1)}, bf16[256,2048]{1,0:T(8,128)(2,1)}...) custom-call(bf16[512,1024]{1,0:T(8,128)(2,1)} %bitcast.140, bf16[1024,512]{1,0:T(8,128)(2,1)} %wq_ref.1, ...), custom_call_target="tpu_custom_call" | custom-call | flops 92000002048 | bytes 1048576 | tf_op jit(solution)/shard_map/head_project/pallas_call | solution.py:590
  87.0 3.9 collective-permute-start
  90.9 1.0 collective-permute-start.1
  91.9 1.5 collective-permute-start.2
  93.4 1.2 constant_dynamic-slice_fusion.4
  94.6 0.5 collective-permute-start.3
  95.9 1.4 stack.90.aux_ref
  97.4 0.6 constant_dynamic-slice_fusion.5.w_ref
  98.0 33.0 %mixer_forward.1 = (bf16[2,1024,256]{2,1,0:T(8,128)(2,1)}, bf16[2,2,1024,128]{3,2,1,0:T(8,128)(2,1)}, bf16[2,2,1024,128]{3,2,1,0:T(8,128)(2,1)}, bf16[2,2,1024,1...) custom-call(f32[2,1024,1152]{2,1,0:T(8,128)} %bitcast.118, ...), custom_call_target="tpu_custom_call" | custom-call | flops 37950001152 | bytes 1048576 | tf_op jit(solution)/shard_map/mixer_forward/pallas_call | solution.py:149
  131.0 55.4 %out_project.1 = (f32[256,2048]{1,0:T(8,128)}, bf16[256,2048]{1,0:T(8,128)(2,1)}, bf16[8,256,256]{2,1,0:T(8,128)(2,1)}, bf16[256,1024]{1,0:T(8,128)(2,1)}) custom-call(bf16[8,256,256]{2,1,0:T(8,128)(2,1)} %bitcast.163, bf16[512,1024]{1,0:T(8,128)(2,1)} %out_ref.5, bf16[256,1024]{1,0:T(8,128)(2,1)} %get-tuple-element.89.piece_ref, ...), custom_call_target="tpu_custom_call" | custom-call | flops 50600001536 | bytes 1048576 | tf_op jit(solution)/shard_map/out_project/pallas_call | solution.py:946
  186.5 0.8 copy-done.19
  187.7 48.5 %mlp_forward.1 = (bf16[8,256,2048]{2,1,0:T(8,128)(2,1)}, bf16[8,256,768]{2,1,0:T(8,128)(2,1)}, bf16[8,256,1536]{2,1,0:T(8,128)(2,1)}, bf16[8,256,2048]{2,1,0:T(8...) custom-call(bf16[256,2048]{1,0:T(8,128)(2,1)} %get-tuple-element.92.x_ref, ...), custom_call_target="tpu_custom_call" | custom-call | flops 78199996416 | bytes 1048576 | tf_op jit(solution)/shard_map/mlp_forward/pallas_call | solution.py:742
  236.2 11.4 %fusion.7 = bf16[1024,1536]{1,0:T(8,128)(2,1)} fusion(bf16[2048,1536]{1,0:T(8,128)(2,1)} %bitcast.132, bf16[2048,2048]{1,0:T(8,128)(2,1)} %bitcast.161), kind=kOutput, calls=%fused_computation.7 | convolution fusion | flops 6444023808 | bytes 13631488 | tf_op jit(solution)/shard_map/dot_general | solution.py:1240
  247.7 10.3 %convolution_convert_fusion.1 = bf16[768,2048]{1,0:T(8,128)(2,1)S(1)} fusion(bf16[2048,768]{1,0:T(8,128)(2,1)} %bitcast.138, bf16[2048,2048]{1,0:T(8,128)(2,1)} %bitcast.131), kind=kOutput, calls=%fused_computation.12 | convolution fusion | flops 6444023808 | bytes 14680064 | tf_op jit(solution)/shard_map/dot_general | solution.py:1240
  258.0 2.2 constant_dynamic-slice_fusion.2
  260.2 9.7 %fusion.4 = bf16[1024,1536]{1,0:T(8,128)(2,1)} fusion(bf16[2048,1536]{1,0:T(8,128)(2,1)S(1)} %bitcast.135, bf16[2048,2048]{1,0:T(8,128)(2,1)} %bitcast.162), kind=kOutput, calls=%fused_computation.6 | convolution fusion | flops 6444023808 | bytes 13631488 | tf_op jit(solution)/shard_map/dot_general | solution.py:1240
  269.9 0.8 collective-permute-start.4
  270.7 99.0 %mlp_backward.1 = (bf16[8,256,2048]{2,1,0:T(8,128)(2,1)}, bf16[8,256,256]{2,1,0:T(8,128)(2,1)}, f32[8,2048]{1,0:T(8,128)}) custom-call(bf16[8,256,1536]{2,1,0:T(8,128)(2,1)} %get-tuple-element.102.grads_ref, bf16[2048,1536]{1,0:T(8,128)(2,1)} %get-tuple-element.103.wgu_ref, bf16[512,1024]{1,0:T(8,128)(2,1)} %out_ref.5, ...), custom_call_target="tpu_custom_call" | custom-call | flops 1150000000 | bytes 1048576 | tf_op jit(solution)/shard_map/mlp_backward/pallas_call | solution.py:1031
  369.8 2.1 fusion.14
  371.9 0.6 fusion.12
  372.5 1.8 pad_maximum_fusion
  374.3 0.4 reduce-scatter.12.cloned.1.call-start
  374.8 5.8 fusion.10
  380.7 2.6 collective-permute-start.5
  383.3 1.0 broadcast_select_fusion
  384.3 2.0 collective-permute-start.6
  386.3 47.6 %mixer_backward.1 = (bf16[2,1024,1152]{2,1,0:T(8,128)(2,1)}, f32[2,2,12,8,128]{4,3,2,1,0:T(8,128)}, f32[2,2,8,128]{3,2,1,0:T(8,128)}) custom-call(f32[2,1024,1152]{2,1,0:T(8,128)} %bitcast.123, f32[2,1024,1152]{2,1,0:T(8,128)} %bitcast.124, f32[2,1024,1152]{2,1,0:T(8,128)} %bitcast.125, f32[2,1024,1152]{2,1,0:T(8,128)} %bitcast.126, ...), custom_call_target="tpu_custom_call" | custom-call | flops 2300000000 | bytes 1048576 | tf_op jit(solution)/shard_map/mixer_backward/pallas_call | solution.py:309
  434.0 1.3 broadcast_select_fusion.3
  435.3 1.0 pad_maximum_fusion.1
  436.6 16.0 %multiply_reduce_fusion = (f32[2048]{0:T(1024)S(1)}, bf16[2048,1152]{1,0:T(8,128)(2,1)S(1)}) fusion(bf16[2048,1152]{1,0:T(8,128)(2,1)} %get-tuple-element.122.hw_ref, bf16[2048,2048]{1,0:T(8,128)(2,1)} %bitcast.160, bf16[2048,1152]{1,0:T(8,128)(2,1)} %bitcast.136), kind=kOutput, calls=%fused_computation | convolution fusion | flops 9675470848 | bytes 22552576 | tf_op jit(solution)/shard_map/dot_general | solution.py:1240
  452.6 3.0 slice.140
  455.6 0.5 copy-done.3
  456.1 0.8 copy-done.14
  457.1 1.1 convert_bitcast_fusion
  458.9 0.6 pad.40.small_ref
  459.5 3.8 reduce-scatter.12.cloned.1.call-done
  463.3 89.3 %final_sums.1 = (bf16[2,256,1024]{2,1,0:T(8,128)(2,1)}, bf16[2,256,1024]{2,1,0:T(8,128)(2,1)}, f32[8,96,128]{2,1,0:T(8,128)}) custom-call(bf16[8,256,1152]{2,1,0:T(8,128)(2,1)} %bitcast.137, bf16[2048,1152]{1,0:T(8,128)(2,1)} %get-tuple-element.122.hw_ref, bf16[8,256,768]{2,1,0:T(8,128)(2,1)} %get-tuple-element.125.hidden_ref, ...), custom_call_target="tpu_custom_call" | custom-call | flops 5750000128 | bytes 1048576 | tf_op jit(solution)/shard_map/final_sums/pallas_call | solution.py:1193
  552.6 0.9 slice.125
  553.5 0.7 reshape.160
  554.3 1.2 slice_bitcast_fusion
  555.8 0.9 slice_reduce_fusion
  557.1 0.5 slice_bitcast_fusion.6
  557.6 1.2 maximum_convert_fusion
  558.8 1.3 select_bitcast_fusion.1
  560.1 1.2 collective-permute-start.8
  561.3 0.7 constant_dynamic-slice_fusion
  562.0 0.9 slice.128
  562.9 0.6 reshape.161
  563.6 0.6 copy.82
  564.2 0.8 convert_element_type.89
  565.1 1.3 convert_element_type.92
  566.4 0.6 slice_bitcast_fusion.4
  567.0 1.2 maximum_convert_fusion.1
  568.2 4.9 collective-permute-done.8
  573.2 0.9 maximum_convert_fusion.2
  574.1 0.9 maximum_convert_fusion.3
  574.9 0.9 maximum_convert_fusion.4
  575.8 0.9 maximum_convert_fusion.5
  576.6 1.0 copy.99
  577.6 1.0 copy.100
  (108 shorter events, 3.4 us)
Async XLA Ops:
  7.2 90.2 %copy-start = (f32[3,4,2048]{2,1,0:T(4,128)S(1)}, f32[3,4,2048]{2,1,0:T(4,128)}, u32[]{:S(2)}) copy-start(f32[3,4,2048]{2,1,0:T(4,128)} %param.24) | copy-start | bytes 294916
  7.2 179.3 %all-gather.3.cloned.1.call-start = ((), (), s32[]{:S(2)}) async-start(), calls=%async_computation.10 | async-start | bytes 9437184 | tf_op jit(solution)/shard_map/all_gather | solution.py:1313
  9.9 85.2 %copy-start.16 = (s32[2,1024]{1,0:T(2,128)S(1)}, s32[2,1024]{1,0:T(2,128)}, u32[]{:S(2)}) copy-start(s32[2,1024]{1,0:T(2,128)} %param.17) | copy-start | bytes 24580
  87.0 287.3 %reduce-scatter.6.cloned.1.call-start = ((), (), s32[]{:S(2)}) async-start(), calls=%async_computation.5 | async-start | bytes 3932160 | tf_op jit(solution)/shard_map/reduce_scatter | solution.py:1262
  87.0 99.4 %collective-permute-start = (bf16[352,1536]{1,0:T(8,128)(2,1)}, bf16[352,1536]{1,0:T(8,128)(2,1)S(1)}, u32[]{:S(2)}, u32[]{:S(2)}) collective-permute-start(bf16[352,1536]{1,0:T(8,128)(2,1)} %get-tuple-element.95.refs_0_), channel_id=1, source_target_pairs={{0,8},{8,0},{16,24},{24,16},{1,9},{9,1},{17,25},{25,17},{2,10},{10... | collective-permute-start | bytes 3244040 | tf_op jit(solution)/shard_map/ppermute | solution.py:1308
  90.9 95.5 %collective-permute-start.1 = (bf16[352,1536]{1,0:T(8,128)(2,1)}, bf16[352,1536]{1,0:T(8,128)(2,1)}, u32[]{:S(2)}, u32[]{:S(2)}) collective-permute-start(bf16[352,1536]{1,0:T(8,128)(2,1)} %get-tuple-element.95.refs_0_), channel_id=1, source_target_pairs={{0,16},{8,24},{16,0},{24,8},{1,17},{9,25},{17,1},{25,9},{2,18},{10... | collective-permute-start | bytes 3244040 | tf_op jit(solution)/shard_map/ppermute | solution.py:1308
  91.9 94.5 %collective-permute-start.2 = (bf16[352,1536]{1,0:T(8,128)(2,1)}, bf16[352,1536]{1,0:T(8,128)(2,1)}, u32[]{:S(2)}, u32[]{:S(2)}) collective-permute-start(bf16[352,1536]{1,0:T(8,128)(2,1)} %get-tuple-element.95.refs_0_), channel_id=1, source_target_pairs={{0,24},{8,16},{16,8},{24,0},{1,25},{9,17},{17,9},{25,1},{2,26},{10... | collective-permute-start | bytes 3244040 | tf_op jit(solution)/shard_map/ppermute | solution.py:1308
  94.6 91.8 %collective-permute-start.3 = (bf16[384,1024]{1,0:T(8,128)(2,1)S(1)}, bf16[384,1024]{1,0:T(8,128)(2,1)S(1)}, u32[]{:S(2)}, u32[]{:S(2)}) collective-permute-start(bf16[384,1024]{1,0:T(8,128)(2,1)S(1)} %constant_dynamic-slice_fusion.4), channel_id=1, source_target_pairs={{0,1},{1,0},{2,3},{3,2},{4,5},{5,4},{6,7},{7,6},{8,9},{9,8},{10,11... | collective-permute-start | bytes 2359304 | tf_op jit(solution)/shard_map/ppermute | solution.py:1244
  186.4 0.9 copy-start.19
  186.4 1.2 copy-start.18
  247.6 12.5 %slice-start = ((s8[6291456]{0:T(1024)(128)(4,1)}), s8[2097152]{0:T(1024)(128)(4,1)S(1)}, s32[]{:S(2)}) async-start(s8[6291456]{0:T(1024)(128)(4,1)} %bitcast.133), calls=%async_computation.11 | async-start | bytes 4194304
  247.6 126.7 %reduce-scatter.8.cloned.1.call-start = ((), (), s32[]{:S(2)}) async-start(), calls=%async_computation.6 | async-start | bytes 3932160 | tf_op jit(solution)/shard_map/reduce_scatter | solution.py:1262
  247.7 12.5 %slice-start.1 = ((s8[6291456]{0:T(1024)(128)(4,1)}), s8[4194304]{0:T(1024)(128)(4,1)S(1)}, s32[]{:S(2)}) async-start(s8[6291456]{0:T(1024)(128)(4,1)} %bitcast.133), calls=%async_computation.12 | async-start | bytes 8388608
  269.9 166.4 %reduce-scatter.10.cloned.1.call-start = ((), (), s32[]{:S(2)}) async-start(), calls=%async_computation.7 | async-start | bytes 3604480 | tf_op jit(solution)/shard_map/reduce_scatter | solution.py:1262
  269.9 99.8 %collective-permute-start.4 = (bf16[768,1024]{1,0:T(8,128)(2,1)}, bf16[768,1024]{1,0:T(8,128)(2,1)}, u32[]{:S(2)}, u32[]{:S(2)}) collective-permute-start(bf16[768,1024]{1,0:T(8,128)(2,1)} %get-tuple-element.108), channel_id=1, source_target_pairs={{0,1},{1,0},{2,3},{3,2},{4,5},{5,4},{6,7},{7,6},{8,9},{9,8},{10,11... | collective-permute-start | bytes 4718600 | tf_op jit(solution)/shard_map/ppermute | solution.py:1244
  369.8 2.1 copy-start.2
  372.5 2.3 copy-start.4
  374.3 89.0 %reduce-scatter.12.cloned.1.call-start = ((), (), s32[]{:S(2)}) async-start(), calls=%async_computation.8 | async-start | bytes 1310720 | tf_op jit(solution)/shard_map/reduce_scatter | solution.py:1262
  374.8 8.5 %copy-start.7 = (bf16[256,1536]{1,0:T(8,128)(2,1)S(1)}, bf16[256,1536]{1,0:T(8,128)(2,1)}, u32[]{:S(2)}) copy-start(bf16[256,1536]{1,0:T(8,128)(2,1)} %reduce-scatter.6.cloned.1.call-done) | copy-start | bytes 2359300
  374.8 8.5 %copy-start.8 = (bf16[256,1536]{1,0:T(8,128)(2,1)S(1)}, bf16[256,1536]{1,0:T(8,128)(2,1)}, u32[]{:S(2)}) copy-start(bf16[256,1536]{1,0:T(8,128)(2,1)} %reduce-scatter.8.cloned.1.call-done) | copy-start | bytes 2359300
  380.7 53.2 %collective-permute-start.5 = (bf16[256,1024]{1,0:T(8,128)(2,1)S(1)}, bf16[256,1024]{1,0:T(8,128)(2,1)}, u32[]{:S(2)}, u32[]{:S(2)}) collective-permute-start(bf16[256,1024]{1,0:T(8,128)(2,1)S(1)} %constant_dynamic-slice_fusion.1), channel_id=1, source_target_pairs={{0,1},{1,0},{2,3},{3,2},{4,5},{5,4},{6,7},{7,6},{8,9},{9,8},{10,11... | collective-permute-start | bytes 1572872 | tf_op jit(solution)/shard_map/ppermute | solution.py:1244
  384.3 52.0 %collective-permute-start.7 = (bf16[256,1536]{1,0:T(8,128)(2,1)}, bf16[256,1536]{1,0:T(8,128)(2,1)}, u32[]{:S(2)}, u32[]{:S(2)}) collective-permute-start(bf16[256,1536]{1,0:T(8,128)(2,1)} %get-tuple-element.147), channel_id=1, source_target_pairs={{0,1},{1,0},{2,3},{3,2},{4,5},{5,4},{6,7},{7,6},{8,9},{9,8},{10,11... | collective-permute-start | bytes 2359304 | tf_op jit(solution)/shard_map/ppermute | solution.py:1244
  384.3 52.0 %collective-permute-start.6 = (bf16[256,1024]{1,0:T(8,128)(2,1)}, bf16[256,1024]{1,0:T(8,128)(2,1)}, u32[]{:S(2)}, u32[]{:S(2)}) collective-permute-start(bf16[256,1024]{1,0:T(8,128)(2,1)} %get-tuple-element.116), channel_id=1, source_target_pairs={{0,1},{1,0},{2,3},{3,2},{4,5},{5,4},{6,7},{7,6},{8,9},{9,8},{10,11... | collective-permute-start | bytes 1572872 | tf_op jit(solution)/shard_map/ppermute | solution.py:1244
  436.4 122.5 %reduce-scatter.14.cloned.1.call-start = ((), (), s32[]{:S(2)}) async-start(), calls=%async_computation.9 | async-start | bytes 5242880 | tf_op jit(solution)/shard_map/reduce_scatter | solution.py:1363
  452.6 3.5 copy-start.3
  456.1 0.8 copy-start.14
  456.1 1.0 copy-start.11
  456.1 1.0 copy-start.17
  456.1 2.5 copy-start.15
  556.8 4.5 copy-start.12
  556.8 7.4 %copy-start.10 = (bf16[128,1024]{1,0:T(8,128)(2,1)S(1)}, bf16[128,1024]{1,0:T(8,128)(2,1)}, u32[]{:S(2)}) copy-start(bf16[128,1024]{1,0:T(8,128)(2,1)} %reduce-scatter.12.cloned.1.call-done) | copy-start | bytes 786436
  557.6 7.5 %copy-start.9 = (bf16[352,1024]{1,0:T(8,128)(2,1)S(1)}, bf16[352,1024]{1,0:T(8,128)(2,1)}, u32[]{:S(2)}) copy-start(bf16[352,1024]{1,0:T(8,128)(2,1)} %reduce-scatter.10.cloned.1.call-done) | copy-start | bytes 2162692
  560.1 13.0 %collective-permute-start.8 = (bf16[256,1024]{1,0:T(8,128)(2,1)S(1)}, bf16[256,1024]{1,0:T(8,128)(2,1)S(1)}, u32[]{:S(2)}, u32[]{:S(2)}) collective-permute-start(bf16[256,1024]{1,0:T(8,128)(2,1)S(1)} %get-tuple-element.160), channel_id=1, source_target_pairs={{0,1},{1,0},{2,3},{3,2},{4,5},{5,4},{6,7},{7,6},{8,9},{9,8},{10,11... | collective-permute-start | bytes 1572872 | tf_op jit(solution)/shard_map/ppermute | solution.py:1244
  563.5 2.8 copy-start.13
  568.2 8.5 %copy-start.6 = (bf16[2,256,1024]{2,1,0:T(8,128)(2,1)S(1)}, bf16[2,256,1024]{2,1,0:T(8,128)(2,1)}, u32[]{:S(2)}) copy-start(bf16[2,256,1024]{2,1,0:T(8,128)(2,1)} %get-tuple-element.201) | copy-start | bytes 3145732
  573.2 4.4 copy-start.5
  574.1 4.5 copy-start.1
Sparse Core Ops, SparseCore 0:
  87.1 74.0 all-gather.2
  247.8 60.2 reduce-scatter.5
  310.4 60.2 reduce-scatter.7
  374.4 58.5 reduce-scatter.9
  436.5 26.7 reduce-scatter.11
  465.5 75.5 reduce-scatter.13

commit v7 on v6

--- a/solution.py
+++ b/solution.py
@@ -135,7 +135,7 @@
         r = lax.rsqrt(jnp.mean(out * out, axis=-1, keepdims=True) + HEAD_EPS)
         mixed_ref[0, rows, :] = (out * r * gain_ref[0:1] * (g * jax.nn.sigmoid(g))).astype(bf)
         return 0
-    lax.fori_loop(0, steps, stage_c, 0, unroll=4)
+    lax.fori_loop(0, steps, stage_c, 0, unroll=8)
 
 def specs(length, heads, off):
     return [pl.BlockSpec((1, length, 128), functools.partial(lambda t, b, h: (b, 0, t * heads + h), t)) for t in range(4)] + [

time: 595 us -> 595 us (level)
  no operation moved by 1% of the time
where the time goes in v7:
time: 595 us; the launch traced here: 586 us
  Pallas kernels  450 us (76%)
  matrix products  53.2 us (9%)
  local copies, waits for them, and re-layouts  24.4 us (4%)
  other arithmetic  19.9 us (3%)
  between operations  15 us (3%)
  starting transfers between devices  14.2 us (2%)
  waiting for transfers between devices  9.15 us (2%)
    pallas_call x1, Pallas kernels, mlp_backward(): pl.pallas_call(back_kernel, in_specs=[ANY, ANY, ANY, ANY, VM, ANY, VM], o...  99 us
    pallas_call x1, Pallas kernels, final_sums(): pl.pallas_call(functools.partial(final_kernel, ndp=ndp), in_specs=[ANY] *...  89.3 us
    pallas_call x1, Pallas kernels, head_project(): pl.pallas_call(head_kernel, in_specs=[ANY] * 10 + [VM], out_specs=[ANY, A...  77.1 us
    pallas_call x1, Pallas kernels, out_project(): pl.pallas_call(out_kernel, in_specs=[ANY, ANY, ANY, VM, VM], out_specs=[V...  57.9 us
    dot_general x5, matrix products, dot_w(): lax.dot_general(a, b, (((0,), (0,)), ((), ())), preferred_element_type=f32)  53.2 us
    pallas_call x1, Pallas kernels, mlp_forward(): pl.pallas_call(functools.partial(mlp_kernel, parts=parts), in_specs=[ANY]...  48.5 us
    pallas_call x1, Pallas kernels, mixer_bwd(): pl.pallas_call(bwd_kernel, grid=(nb, heads), in_specs=specs(length, heads...  47.6 us
    pallas_call x1, Pallas kernels, mixer_fwd(): pl.pallas_call(fwd_kernel, grid=(nb, heads), in_specs=specs(length, heads...  30.3 us
  transfers between devices with their start and end apart: 15, of which 2 were waited for; matrix products, arithmetic and copies ran while one was open for 13% of the time, Pallas kernels for 55%

profile of v7, /device:TPU:0, one launch (start us, length us, event | category | flops | bytes accessed | tf_op | source)
XLA Modules:
  0.0 585.6 jit_solution(14046833409996027877)
XLA Ops:
  7.2 0.7 reshape.139
  8.0 0.5 copy.62
  8.4 0.5 pad.33
  9.0 0.9 copy.91
  9.9 77.1 %head_project.1 = (bf16[8,256,2048]{2,1,0:T(8,128)(2,1)}, f32[8,256,1152]{2,1,0:T(8,128)}, bf16[2048,1152]{1,0:T(8,128)(2,1)}, bf16[256,2048]{1,0:T(8,128)(2,1)}...) custom-call(bf16[512,1024]{1,0:T(8,128)(2,1)} %bitcast.140, bf16[1024,512]{1,0:T(8,128)(2,1)} %wq_ref.1, ...), custom_call_target="tpu_custom_call" | custom-call | flops 92000002048 | bytes 1048576 | tf_op jit(solution)/shard_map/head_project/pallas_call | solution.py:590
  87.0 3.9 collective-permute-start
  90.9 1.0 collective-permute-start.1
  91.9 1.5 collective-permute-start.2
  93.4 1.2 constant_dynamic-slice_fusion.4
  94.6 0.5 collective-permute-start.3
  95.9 1.4 stack.90.aux_ref
  97.4 0.6 constant_dynamic-slice_fusion.5.w_ref
  98.0 30.3 %mixer_forward.1 = (bf16[2,1024,256]{2,1,0:T(8,128)(2,1)}, bf16[2,2,1024,128]{3,2,1,0:T(8,128)(2,1)}, bf16[2,2,1024,128]{3,2,1,0:T(8,128)(2,1)}, bf16[2,2,1024,1...) custom-call(f32[2,1024,1152]{2,1,0:T(8,128)} %bitcast.118, ...), custom_call_target="tpu_custom_call" | custom-call | flops 37950001152 | bytes 1048576 | tf_op jit(solution)/shard_map/mixer_forward/pallas_call | solution.py:149
  128.3 57.9 %out_project.1 = (f32[256,2048]{1,0:T(8,128)}, bf16[256,2048]{1,0:T(8,128)(2,1)}, bf16[8,256,256]{2,1,0:T(8,128)(2,1)}, bf16[256,1024]{1,0:T(8,128)(2,1)}) custom-call(bf16[8,256,256]{2,1,0:T(8,128)(2,1)} %bitcast.163, bf16[512,1024]{1,0:T(8,128)(2,1)} %out_ref.5, bf16[256,1024]{1,0:T(8,128)(2,1)} %get-tuple-element.89.piece_ref, ...), custom_call_target="tpu_custom_call" | custom-call | flops 50600001536 | bytes 1048576 | tf_op jit(solution)/shard_map/out_project/pallas_call | solution.py:946
  186.3 0.8 copy-done.19
  187.4 48.5 %mlp_forward.1 = (bf16[8,256,2048]{2,1,0:T(8,128)(2,1)}, bf16[8,256,768]{2,1,0:T(8,128)(2,1)}, bf16[8,256,1536]{2,1,0:T(8,128)(2,1)}, bf16[8,256,2048]{2,1,0:T(8...) custom-call(bf16[256,2048]{1,0:T(8,128)(2,1)} %get-tuple-element.92.x_ref, ...), custom_call_target="tpu_custom_call" | custom-call | flops 78199996416 | bytes 1048576 | tf_op jit(solution)/shard_map/mlp_forward/pallas_call | solution.py:742
  235.9 11.4 %fusion.7 = bf16[1024,1536]{1,0:T(8,128)(2,1)} fusion(bf16[2048,1536]{1,0:T(8,128)(2,1)} %bitcast.132, bf16[2048,2048]{1,0:T(8,128)(2,1)} %bitcast.161), kind=kOutput, calls=%fused_computation.7 | convolution fusion | flops 6444023808 | bytes 13631488 | tf_op jit(solution)/shard_map/dot_general | solution.py:1240
  247.4 10.3 %convolution_convert_fusion.1 = bf16[768,2048]{1,0:T(8,128)(2,1)S(1)} fusion(bf16[2048,768]{1,0:T(8,128)(2,1)} %bitcast.138, bf16[2048,2048]{1,0:T(8,128)(2,1)} %bitcast.131), kind=kOutput, calls=%fused_computation.12 | convolution fusion | flops 6444023808 | bytes 14680064 | tf_op jit(solution)/shard_map/dot_general | solution.py:1240
  257.7 2.2 constant_dynamic-slice_fusion.2
  259.9 9.7 %fusion.4 = bf16[1024,1536]{1,0:T(8,128)(2,1)} fusion(bf16[2048,1536]{1,0:T(8,128)(2,1)S(1)} %bitcast.135, bf16[2048,2048]{1,0:T(8,128)(2,1)} %bitcast.162), kind=kOutput, calls=%fused_computation.6 | convolution fusion | flops 6444023808 | bytes 13631488 | tf_op jit(solution)/shard_map/dot_general | solution.py:1240
  269.7 0.8 collective-permute-start.4
  270.5 99.0 %mlp_backward.1 = (bf16[8,256,2048]{2,1,0:T(8,128)(2,1)}, bf16[8,256,256]{2,1,0:T(8,128)(2,1)}, f32[8,2048]{1,0:T(8,128)}) custom-call(bf16[8,256,1536]{2,1,0:T(8,128)(2,1)} %get-tuple-element.102.grads_ref, bf16[2048,1536]{1,0:T(8,128)(2,1)} %get-tuple-element.103.wgu_ref, bf16[512,1024]{1,0:T(8,128)(2,1)} %out_ref.5, ...), custom_call_target="tpu_custom_call" | custom-call | flops 1150000000 | bytes 1048576 | tf_op jit(solution)/shard_map/mlp_backward/pallas_call | solution.py:1031
  369.5 2.1 fusion.14
  371.6 0.6 fusion.12
  372.2 1.8 pad_maximum_fusion
  374.0 0.4 reduce-scatter.12.cloned.1.call-start
  374.5 5.8 fusion.10
  380.4 2.5 collective-permute-start.5
  382.9 1.0 broadcast_select_fusion
  383.9 2.0 collective-permute-start.6
  385.9 47.6 %mixer_backward.1 = (bf16[2,1024,1152]{2,1,0:T(8,128)(2,1)}, f32[2,2,12,8,128]{4,3,2,1,0:T(8,128)}, f32[2,2,8,128]{3,2,1,0:T(8,128)}) custom-call(f32[2,1024,1152]{2,1,0:T(8,128)} %bitcast.123, f32[2,1024,1152]{2,1,0:T(8,128)} %bitcast.124, f32[2,1024,1152]{2,1,0:T(8,128)} %bitcast.125, f32[2,1024,1152]{2,1,0:T(8,128)} %bitcast.126, ...), custom_call_target="tpu_custom_call" | custom-call | flops 2300000000 | bytes 1048576 | tf_op jit(solution)/shard_map/mixer_backward/pallas_call | solution.py:309
  433.6 1.3 broadcast_select_fusion.3
  434.9 1.0 pad_maximum_fusion.1
  436.2 16.0 %multiply_reduce_fusion = (f32[2048]{0:T(1024)S(1)}, bf16[2048,1152]{1,0:T(8,128)(2,1)S(1)}) fusion(bf16[2048,1152]{1,0:T(8,128)(2,1)} %get-tuple-element.122.hw_ref, bf16[2048,2048]{1,0:T(8,128)(2,1)} %bitcast.160, bf16[2048,1152]{1,0:T(8,128)(2,1)} %bitcast.136), kind=kOutput, calls=%fused_computation | convolution fusion | flops 9675470848 | bytes 22552576 | tf_op jit(solution)/shard_map/dot_general | solution.py:1240
  452.2 3.0 slice.140
  455.2 0.5 copy-done.3
  455.7 0.8 copy-done.14
  456.7 1.1 convert_bitcast_fusion
  458.5 0.6 pad.40.small_ref
  459.1 4.1 reduce-scatter.12.cloned.1.call-done
  463.2 89.3 %final_sums.1 = (bf16[2,256,1024]{2,1,0:T(8,128)(2,1)}, bf16[2,256,1024]{2,1,0:T(8,128)(2,1)}, f32[8,96,128]{2,1,0:T(8,128)}) custom-call(bf16[8,256,1152]{2,1,0:T(8,128)(2,1)} %bitcast.137, bf16[2048,1152]{1,0:T(8,128)(2,1)} %get-tuple-element.122.hw_ref, bf16[8,256,768]{2,1,0:T(8,128)(2,1)} %get-tuple-element.125.hidden_ref, ...), custom_call_target="tpu_custom_call" | custom-call | flops 5750000128 | bytes 1048576 | tf_op jit(solution)/shard_map/final_sums/pallas_call | solution.py:1193
  552.5 0.9 slice.125
  553.4 0.7 reshape.160
  554.2 1.2 slice_bitcast_fusion
  555.7 0.9 slice_reduce_fusion
  557.0 0.5 slice_bitcast_fusion.6
  557.5 1.2 maximum_convert_fusion
  558.7 1.3 select_bitcast_fusion.1
  560.0 1.2 collective-permute-start.8
  561.2 0.7 constant_dynamic-slice_fusion
  561.9 0.9 slice.128
  562.8 0.6 reshape.161
  563.5 0.6 copy.82
  564.1 0.8 convert_element_type.89
  565.0 1.3 convert_element_type.92
  566.3 0.6 slice_bitcast_fusion.4
  566.9 1.2 maximum_convert_fusion.1
  568.1 4.9 collective-permute-done.8
  573.1 0.9 maximum_convert_fusion.2
  574.0 0.9 maximum_convert_fusion.3
  574.8 0.9 maximum_convert_fusion.4
  575.7 0.9 maximum_convert_fusion.5
  576.5 1.0 copy.99
  577.5 1.0 copy.100
  (108 shorter events, 3.4 us)
Async XLA Ops:
  7.2 90.2 %copy-start = (f32[3,4,2048]{2,1,0:T(4,128)S(1)}, f32[3,4,2048]{2,1,0:T(4,128)}, u32[]{:S(2)}) copy-start(f32[3,4,2048]{2,1,0:T(4,128)} %param.24) | copy-start | bytes 294916
  7.2 179.1 %all-gather.3.cloned.1.call-start = ((), (), s32[]{:S(2)}) async-start(), calls=%async_computation.10 | async-start | bytes 9437184 | tf_op jit(solution)/shard_map/all_gather | solution.py:1313
  9.9 85.2 %copy-start.16 = (s32[2,1024]{1,0:T(2,128)S(1)}, s32[2,1024]{1,0:T(2,128)}, u32[]{:S(2)}) copy-start(s32[2,1024]{1,0:T(2,128)} %param.17) | copy-start | bytes 24580
  87.0 287.0 %reduce-scatter.6.cloned.1.call-start = ((), (), s32[]{:S(2)}) async-start(), calls=%async_computation.5 | async-start | bytes 3932160 | tf_op jit(solution)/shard_map/reduce_scatter | solution.py:1262
  87.0 99.2 %collective-permute-start = (bf16[352,1536]{1,0:T(8,128)(2,1)}, bf16[352,1536]{1,0:T(8,128)(2,1)S(1)}, u32[]{:S(2)}, u32[]{:S(2)}) collective-permute-start(bf16[352,1536]{1,0:T(8,128)(2,1)} %get-tuple-element.95.refs_0_), channel_id=1, source_target_pairs={{0,8},{8,0},{16,24},{24,16},{1,9},{9,1},{17,25},{25,17},{2,10},{10... | collective-permute-start | bytes 3244040 | tf_op jit(solution)/shard_map/ppermute | solution.py:1308
  90.9 95.3 %collective-permute-start.1 = (bf16[352,1536]{1,0:T(8,128)(2,1)}, bf16[352,1536]{1,0:T(8,128)(2,1)}, u32[]{:S(2)}, u32[]{:S(2)}) collective-permute-start(bf16[352,1536]{1,0:T(8,128)(2,1)} %get-tuple-element.95.refs_0_), channel_id=1, source_target_pairs={{0,16},{8,24},{16,0},{24,8},{1,17},{9,25},{17,1},{25,9},{2,18},{10... | collective-permute-start | bytes 3244040 | tf_op jit(solution)/shard_map/ppermute | solution.py:1308
  91.9 94.3 %collective-permute-start.2 = (bf16[352,1536]{1,0:T(8,128)(2,1)}, bf16[352,1536]{1,0:T(8,128)(2,1)}, u32[]{:S(2)}, u32[]{:S(2)}) collective-permute-start(bf16[352,1536]{1,0:T(8,128)(2,1)} %get-tuple-element.95.refs_0_), channel_id=1, source_target_pairs={{0,24},{8,16},{16,8},{24,0},{1,25},{9,17},{17,9},{25,1},{2,26},{10... | collective-permute-start | bytes 3244040 | tf_op jit(solution)/shard_map/ppermute | solution.py:1308
  94.6 91.6 %collective-permute-start.3 = (bf16[384,1024]{1,0:T(8,128)(2,1)S(1)}, bf16[384,1024]{1,0:T(8,128)(2,1)S(1)}, u32[]{:S(2)}, u32[]{:S(2)}) collective-permute-start(bf16[384,1024]{1,0:T(8,128)(2,1)S(1)} %constant_dynamic-slice_fusion.4), channel_id=1, source_target_pairs={{0,1},{1,0},{2,3},{3,2},{4,5},{5,4},{6,7},{7,6},{8,9},{9,8},{10,11... | collective-permute-start | bytes 2359304 | tf_op jit(solution)/shard_map/ppermute | solution.py:1244
  186.2 0.9 copy-start.19
  186.2 1.2 copy-start.18
  247.3 12.5 %slice-start = ((s8[6291456]{0:T(1024)(128)(4,1)}), s8[2097152]{0:T(1024)(128)(4,1)S(1)}, s32[]{:S(2)}) async-start(s8[6291456]{0:T(1024)(128)(4,1)} %bitcast.133), calls=%async_computation.11 | async-start | bytes 4194304
  247.4 126.6 %reduce-scatter.8.cloned.1.call-start = ((), (), s32[]{:S(2)}) async-start(), calls=%async_computation.6 | async-start | bytes 3932160 | tf_op jit(solution)/shard_map/reduce_scatter | solution.py:1262
  247.4 12.5 %slice-start.1 = ((s8[6291456]{0:T(1024)(128)(4,1)}), s8[4194304]{0:T(1024)(128)(4,1)S(1)}, s32[]{:S(2)}) async-start(s8[6291456]{0:T(1024)(128)(4,1)} %bitcast.133), calls=%async_computation.12 | async-start | bytes 8388608
  269.6 166.3 %reduce-scatter.10.cloned.1.call-start = ((), (), s32[]{:S(2)}) async-start(), calls=%async_computation.7 | async-start | bytes 3604480 | tf_op jit(solution)/shard_map/reduce_scatter | solution.py:1262
  269.7 99.8 %collective-permute-start.4 = (bf16[768,1024]{1,0:T(8,128)(2,1)}, bf16[768,1024]{1,0:T(8,128)(2,1)}, u32[]{:S(2)}, u32[]{:S(2)}) collective-permute-start(bf16[768,1024]{1,0:T(8,128)(2,1)} %get-tuple-element.108), channel_id=1, source_target_pairs={{0,1},{1,0},{2,3},{3,2},{4,5},{5,4},{6,7},{7,6},{8,9},{9,8},{10,11... | collective-permute-start | bytes 4718600 | tf_op jit(solution)/shard_map/ppermute | solution.py:1244
  369.5 2.1 copy-start.2
  372.2 2.3 copy-start.4
  374.0 89.2 %reduce-scatter.12.cloned.1.call-start = ((), (), s32[]{:S(2)}) async-start(), calls=%async_computation.8 | async-start | bytes 1310720 | tf_op jit(solution)/shard_map/reduce_scatter | solution.py:1262
  374.5 8.4 %copy-start.7 = (bf16[256,1536]{1,0:T(8,128)(2,1)S(1)}, bf16[256,1536]{1,0:T(8,128)(2,1)}, u32[]{:S(2)}) copy-start(bf16[256,1536]{1,0:T(8,128)(2,1)} %reduce-scatter.6.cloned.1.call-done) | copy-start | bytes 2359300
  374.5 8.4 %copy-start.8 = (bf16[256,1536]{1,0:T(8,128)(2,1)S(1)}, bf16[256,1536]{1,0:T(8,128)(2,1)}, u32[]{:S(2)}) copy-start(bf16[256,1536]{1,0:T(8,128)(2,1)} %reduce-scatter.8.cloned.1.call-done) | copy-start | bytes 2359300
  380.4 53.2 %collective-permute-start.5 = (bf16[256,1024]{1,0:T(8,128)(2,1)S(1)}, bf16[256,1024]{1,0:T(8,128)(2,1)}, u32[]{:S(2)}, u32[]{:S(2)}) collective-permute-start(bf16[256,1024]{1,0:T(8,128)(2,1)S(1)} %constant_dynamic-slice_fusion.1), channel_id=1, source_target_pairs={{0,1},{1,0},{2,3},{3,2},{4,5},{5,4},{6,7},{7,6},{8,9},{9,8},{10,11... | collective-permute-start | bytes 1572872 | tf_op jit(solution)/shard_map/ppermute | solution.py:1244
  383.9 52.0 %collective-permute-start.7 = (bf16[256,1536]{1,0:T(8,128)(2,1)}, bf16[256,1536]{1,0:T(8,128)(2,1)}, u32[]{:S(2)}, u32[]{:S(2)}) collective-permute-start(bf16[256,1536]{1,0:T(8,128)(2,1)} %get-tuple-element.147), channel_id=1, source_target_pairs={{0,1},{1,0},{2,3},{3,2},{4,5},{5,4},{6,7},{7,6},{8,9},{9,8},{10,11... | collective-permute-start | bytes 2359304 | tf_op jit(solution)/shard_map/ppermute | solution.py:1244
  383.9 52.0 %collective-permute-start.6 = (bf16[256,1024]{1,0:T(8,128)(2,1)}, bf16[256,1024]{1,0:T(8,128)(2,1)}, u32[]{:S(2)}, u32[]{:S(2)}) collective-permute-start(bf16[256,1024]{1,0:T(8,128)(2,1)} %get-tuple-element.116), channel_id=1, source_target_pairs={{0,1},{1,0},{2,3},{3,2},{4,5},{5,4},{6,7},{7,6},{8,9},{9,8},{10,11... | collective-permute-start | bytes 1572872 | tf_op jit(solution)/shard_map/ppermute | solution.py:1244
  436.0 122.8 %reduce-scatter.14.cloned.1.call-start = ((), (), s32[]{:S(2)}) async-start(), calls=%async_computation.9 | async-start | bytes 5242880 | tf_op jit(solution)/shard_map/reduce_scatter | solution.py:1363
  452.2 3.5 copy-start.3
  455.7 0.8 copy-start.14
  455.7 1.0 copy-start.11
  455.7 1.0 copy-start.17
  455.7 2.5 copy-start.15
  556.7 4.5 copy-start.12
  556.7 7.4 %copy-start.10 = (bf16[128,1024]{1,0:T(8,128)(2,1)S(1)}, bf16[128,1024]{1,0:T(8,128)(2,1)}, u32[]{:S(2)}) copy-start(bf16[128,1024]{1,0:T(8,128)(2,1)} %reduce-scatter.12.cloned.1.call-done) | copy-start | bytes 786436
  557.5 7.5 %copy-start.9 = (bf16[352,1024]{1,0:T(8,128)(2,1)S(1)}, bf16[352,1024]{1,0:T(8,128)(2,1)}, u32[]{:S(2)}) copy-start(bf16[352,1024]{1,0:T(8,128)(2,1)} %reduce-scatter.10.cloned.1.call-done) | copy-start | bytes 2162692
  560.0 13.0 %collective-permute-start.8 = (bf16[256,1024]{1,0:T(8,128)(2,1)S(1)}, bf16[256,1024]{1,0:T(8,128)(2,1)S(1)}, u32[]{:S(2)}, u32[]{:S(2)}) collective-permute-start(bf16[256,1024]{1,0:T(8,128)(2,1)S(1)} %get-tuple-element.160), channel_id=1, source_target_pairs={{0,1},{1,0},{2,3},{3,2},{4,5},{5,4},{6,7},{7,6},{8,9},{9,8},{10,11... | collective-permute-start | bytes 1572872 | tf_op jit(solution)/shard_map/ppermute | solution.py:1244
  563.4 2.8 copy-start.13
  568.1 8.5 %copy-start.6 = (bf16[2,256,1024]{2,1,0:T(8,128)(2,1)S(1)}, bf16[2,256,1024]{2,1,0:T(8,128)(2,1)}, u32[]{:S(2)}) copy-start(bf16[2,256,1024]{2,1,0:T(8,128)(2,1)} %get-tuple-element.201) | copy-start | bytes 3145732
  573.1 4.4 copy-start.5
  574.0 4.5 copy-start.1
Sparse Core Ops, SparseCore 0:
  87.1 76.5 all-gather.2
  247.5 60.4 reduce-scatter.5
  310.3 60.2 reduce-scatter.7
  374.1 58.7 reduce-scatter.9
  436.1 27.0 reduce-scatter.11
  465.5 75.5 reduce-scatter.13
